TPU v7x, 32 devices: a whole 2x2x4 slice. The times are simulated.
32 devices in a mesh: ctx: 8 (over z, y), fsdp: 4 (over x, core).
Axes of the slice: x: 2, y: 2, z: 4, core: 2. Of those that a mesh axis runs over, the one named last changes fastest.
Arguments:
- tokens: bfloat16 [4, 2048, 768], P('fsdp', 'ctx'), may hold values from -6 to 6
- cotangent: bfloat16 [4, 2048, 768], P('fsdp', 'ctx'), may hold values from -6 to 6
- lengths: int32 [4], P('fsdp'), may hold values from 512 to 2048, as said below
- position_block: int32 [8], replicated, may hold values from 0 to 7, each once
- routes: int32 [4, 2048, 2], P('fsdp', 'ctx'), may hold values from 0 to 7, all different within a row; in each aligned block of 256 rows (0 to 255, 256 to 511, ..., all dimensions but the last counted through in order) at most 96 rows name the same one
- gain_attn: bfloat16 [768], P('fsdp'), may hold values from 0.099609375 to 1.8984375
- w_qkv: bfloat16 [768, 2304], P('fsdp'), may hold values from -0.21875 to 0.21875
- w_out: bfloat16 [768, 768], P('fsdp'), may hold values from -3.5 to 3.5
- gain_ffn: bfloat16 [768], P('fsdp'), may hold values from 0.099609375 to 1.8984375
- w_router: bfloat16 [768, 8], P('fsdp'), may hold values from -0.15625 to 0.15625
- w_shared_in: bfloat16 [768, 4096], P('fsdp'), may hold values from -0.21875 to 0.21875
- w_shared_out: bfloat16 [2048, 768], P('fsdp'), may hold values from -0.1875 to 0.1875
- w_expert_in: bfloat16 [8, 768, 4096], P('ctx', 'fsdp'), may hold values from -0.21875 to 0.21875
- w_expert_out: bfloat16 [8, 2048, 768], P('ctx', None, 'fsdp'), may hold values from -0.1875 to 0.1875
Outputs:
- output: bfloat16 [4, 2048, 768], P('fsdp', 'ctx')
- grad_tokens: float32 [4, 2048, 768], P('fsdp', 'ctx')
- grad_gain_attn: float32 [768], P('fsdp')
- grad_qkv: float32 [768, 2304], P('fsdp')
- grad_out: float32 [768, 768], P('fsdp')
- grad_gain_ffn: float32 [768], P('fsdp')
- grad_router: float32 [768, 8], P('fsdp')
- grad_shared_in: float32 [768, 4096], P('fsdp')
- grad_shared_out: float32 [2048, 768], P('fsdp')
- grad_expert_in: float32 [8, 768, 4096], P('ctx', 'fsdp')
- grad_expert_out: float32 [8, 2048, 768], P('ctx', None, 'fsdp')
Inputs may be any that keep to these rules, and one draw needn't show every extreme that they name: `lengths`: some row has length 2048. `position_block`: each number appears once. `routes`: the two experts of a slot differ; within each row, the two-per-slot choices of an aligned block of 256 slots name no expert more than 96 times, a bound that some block reaches.
All inputs are finite; a program needn't handle non-finite values.
Results may differ from a plain program's by a relative error of at most 0.028.
Values may be sent and summed in bfloat16 or wider, within the bound.
A program may use at most 192 MiB of HBM per device.

v0:
```python
import jax
import jax.numpy as jnp
from jax import lax
from jax.sharding import PartitionSpec as P

D = 768
HEADS = 12
HEAD_DIM = 64
FF = 2048
FS = 2048


norm_eps = 1e-06
contract_rows = (((0,), (0,)), ((), ()))
contract_cols = (((1,), (1,)), ((), ()))


def rotary_tables(positions):
    halves = HEAD_DIM // 2
    inverse = 10000.0 ** (-(jnp.arange(halves, dtype=jnp.float32) * 2.0 / HEAD_DIM))
    angle_grid = positions.astype(jnp.float32)[:, None] * inverse[None, :]
    return (jnp.cos(angle_grid)[:, None, :], jnp.sin(angle_grid)[:, None, :])


def rotate(field, cos_part, sin_part):
    halves = HEAD_DIM // 2
    first_half = field[..., :halves]
    second_half = field[..., halves:]
    return jnp.concatenate(
        [
            first_half * cos_part - second_half * sin_part,
            second_half * cos_part + first_half * sin_part,
        ],
        axis=-1,
    )


def unrotate(grads, cos_part, sin_part):
    halves = HEAD_DIM // 2
    first_half = grads[..., :halves]
    second_half = grads[..., halves:]
    return jnp.concatenate(
        [
            first_half * cos_part + second_half * sin_part,
            second_half * cos_part - first_half * sin_part,
        ],
        axis=-1,
    )


def prob_grads(
    query_heads,
    key_heads,
    value_heads,
    grad_heads,
    lse_rows,
    delta_rows,
    query_pos,
    key_pos,
    length,
    scale,
):
    scores = (
        jnp.einsum("qhd,khd->hqk", query_heads, key_heads, preferred_element_type=jnp.float32)
        * scale
    )
    allowed = ((key_pos[None, :] <= query_pos[:, None]) & (key_pos[None, :] < length))[None]
    probs = jnp.where(allowed, jnp.exp(scores - lse_rows[..., None]), 0.0)
    dprobs = jnp.einsum("qhd,khd->hqk", grad_heads, value_heads, preferred_element_type=jnp.float32)
    dscores = (probs * (dprobs - delta_rows[..., None])).astype(jnp.bfloat16)
    return (dscores, probs.astype(jnp.bfloat16))


def norm_back(grad_normed, values, inv_scale, gain):
    scaled = grad_normed * gain
    total = jnp.mean(scaled * values, axis=-1, keepdims=True)
    return (
        inv_scale * scaled - values * inv_scale**3 * total,
        jnp.sum(grad_normed * values * inv_scale, axis=0),
    )


def on_device(
    tokens,
    cotangent,
    lengths,
    position_block,
    routes,
    gain_attn,
    w_qkv,
    w_out,
    gain_ffn,
    w_router,
    w_shared_in,
    w_shared_out,
    w_expert_in,
    w_expert_out,
):
    n_ctx = lax.axis_size("ctx")
    ctx_index = lax.axis_index("ctx")
    slot_dev = tokens.shape[1]
    slot_total = slot_dev * n_ctx
    local_count = w_expert_in.shape[0]
    expert_total = local_count * n_ctx
    capacity = 3 * slot_dev // expert_total
    key_block = min(slot_total, slot_dev * max(1, 512 // slot_dev))
    block_count = slot_total // key_block
    scale = HEAD_DIM ** (-0.5)
    length = lengths[0]
    key_pos = (
        position_block[:, None] * slot_dev + jnp.arange(slot_dev, dtype=jnp.int32)[None, :]
    ).reshape(slot_total)
    query_pos = lax.dynamic_slice_in_dim(key_pos, ctx_index * slot_dev, slot_dev)
    live = (query_pos < length).astype(jnp.float32)[:, None]
    gain_one, weight_qkv, weight_out, gain_two, weight_router, shared_in, shared_out = (
        lax.all_gather(gain_attn, "fsdp", axis=0, tiled=True),
        lax.all_gather(w_qkv, "fsdp", axis=0, tiled=True),
        lax.all_gather(w_out, "fsdp", axis=0, tiled=True),
        lax.all_gather(gain_ffn, "fsdp", axis=0, tiled=True),
        lax.all_gather(w_router, "fsdp", axis=0, tiled=True),
        lax.all_gather(w_shared_in, "fsdp", axis=0, tiled=True),
        lax.all_gather(w_shared_out, "fsdp", axis=0, tiled=True),
    )
    gain_one = gain_one.astype(jnp.float32)
    gain_two = gain_two.astype(jnp.float32)
    resid_in = tokens[0].astype(jnp.float32)
    inv_one = lax.rsqrt(jnp.mean(resid_in * resid_in, axis=-1, keepdims=True) + norm_eps)
    attn_in = (resid_in * inv_one * gain_one).astype(jnp.bfloat16)
    projected = jnp.dot(attn_in, weight_qkv, preferred_element_type=jnp.float32)
    cos_part, sin_part = rotary_tables(query_pos)
    queries = rotate(
        projected[:, :D].reshape(slot_dev, HEADS, HEAD_DIM), cos_part, sin_part
    ).astype(jnp.bfloat16)
    keys_rot = rotate(
        projected[:, D : 2 * D].reshape(slot_dev, HEADS, HEAD_DIM), cos_part, sin_part
    ).astype(jnp.bfloat16)
    values_own = projected[:, 2 * D :].astype(jnp.bfloat16)
    local_kv = jnp.concatenate([keys_rot.reshape(slot_dev, D), values_own], axis=1)
    all_kv = lax.all_gather(local_kv, "ctx", axis=0, tiled=True)
    kv_blocks = all_kv.reshape(block_count, key_block, 2 * D)
    pos_blocks = key_pos.reshape(block_count, key_block)

    def forward_step(carry, pieces):
        running_max, running_sum, running_acc = carry
        block_kv, block_pos = pieces
        block_keys = block_kv[:, :D].reshape(key_block, HEADS, HEAD_DIM)
        block_values = block_kv[:, D:].reshape(key_block, HEADS, HEAD_DIM)
        scores = (
            jnp.einsum("qhd,khd->hqk", queries, block_keys, preferred_element_type=jnp.float32)
            * scale
        )
        allowed = ((block_pos[None, :] <= query_pos[:, None]) & (block_pos[None, :] < length))[None]
        scores = jnp.where(allowed, scores, -1e30)
        new_max = jnp.maximum(running_max, jnp.max(scores, axis=-1))
        weights = jnp.where(allowed, jnp.exp(scores - new_max[..., None]), 0.0)
        factor = jnp.exp(running_max - new_max)
        running_sum = running_sum * factor + jnp.sum(weights, axis=-1)
        running_acc = running_acc * factor[..., None] + jnp.einsum(
            "hqk,khd->hqd",
            weights.astype(jnp.bfloat16),
            block_values,
            preferred_element_type=jnp.float32,
        )
        return ((new_max, running_sum, running_acc), None)

    start_state = (
        jnp.full((HEADS, slot_dev), -1e30, jnp.float32),
        jnp.zeros((HEADS, slot_dev), jnp.float32),
        jnp.zeros((HEADS, slot_dev, HEAD_DIM), jnp.float32),
    )
    final_state, unused = lax.scan(forward_step, start_state, (kv_blocks, pos_blocks))
    final_max, final_sum, final_acc = final_state
    attn_heads = (final_acc / final_sum[..., None]).transpose(1, 0, 2)
    log_total = final_max + jnp.log(final_sum)
    attn_out = attn_heads.reshape(slot_dev, D).astype(jnp.bfloat16)
    residual = resid_in + jnp.dot(attn_out, weight_out, preferred_element_type=jnp.float32)
    inv_two = lax.rsqrt(jnp.mean(residual * residual, axis=-1, keepdims=True) + norm_eps)
    ffn_in = (residual * inv_two * gain_two).astype(jnp.bfloat16)
    logits = jnp.dot(ffn_in, weight_router, preferred_element_type=jnp.float32)
    pair_expert = routes[0].reshape(2 * slot_dev)
    expert_hot = (
        pair_expert[:, None] == jnp.arange(expert_total, dtype=jnp.int32)[None, :]
    ).astype(jnp.int32)
    route_hot = expert_hot.reshape(slot_dev, 2, expert_total).astype(jnp.float32)
    chosen = jnp.sum(logits[:, None, :] * route_hot, axis=-1)
    gates = jax.nn.softmax(chosen, axis=-1)
    shared_mid = jnp.dot(ffn_in, shared_in, preferred_element_type=jnp.float32)
    shared_gate = shared_mid[:, :FS]
    shared_up = shared_mid[:, FS:]
    shared_sig = jax.nn.sigmoid(shared_gate)
    shared_act = (shared_gate * shared_sig * shared_up).astype(jnp.bfloat16)
    shared_res = jnp.dot(shared_act, shared_out, preferred_element_type=jnp.float32)
    earlier = jnp.cumsum(expert_hot, axis=0) - expert_hot
    slot_index = jnp.sum(earlier * expert_hot, axis=-1)
    target = pair_expert * capacity + slot_index
    pick = (
        target[:, None] == jnp.arange(expert_total * capacity, dtype=jnp.int32)[None, :]
    ).astype(jnp.bfloat16)
    token_pick = jnp.sum(pick.reshape(slot_dev, 2, expert_total * capacity), axis=1)
    outgoing = lax.dot_general(
        token_pick, ffn_in, contract_rows, preferred_element_type=jnp.float32
    ).astype(jnp.bfloat16)
    wide_in, wide_out = (
        lax.all_gather(w_expert_in, "fsdp", axis=1, tiled=True),
        lax.all_gather(w_expert_out, "fsdp", axis=2, tiled=True),
    )

    def to_experts(block):
        return (
            block.reshape(n_ctx, local_count, capacity, D)
            .transpose(1, 0, 2, 3)
            .reshape(local_count, n_ctx * capacity, D)
        )

    def to_sources(block):
        return (
            block.reshape(local_count, n_ctx, capacity, D)
            .transpose(1, 0, 2, 3)
            .reshape(n_ctx * local_count, capacity, D)
        )

    arrived = lax.all_to_all(
        outgoing.reshape(expert_total, capacity, D), "ctx", split_axis=0, concat_axis=0, tiled=True
    )
    expert_rows = to_experts(arrived)
    expert_mid = jnp.einsum(
        "end,edf->enf", expert_rows, wide_in, preferred_element_type=jnp.float32
    )
    expert_gate_part = expert_mid[..., :FF]
    expert_up = expert_mid[..., FF:]
    expert_sigmoid = jax.nn.sigmoid(expert_gate_part)
    expert_act = (expert_gate_part * expert_sigmoid * expert_up).astype(jnp.bfloat16)
    expert_res = jnp.einsum(
        "enf,efd->end", expert_act, wide_out, preferred_element_type=jnp.float32
    ).astype(jnp.bfloat16)
    came_back = lax.all_to_all(
        to_sources(expert_res), "ctx", split_axis=0, concat_axis=0, tiled=True
    )
    pair_res = jnp.dot(
        pick, came_back.reshape(expert_total * capacity, D), preferred_element_type=jnp.float32
    ).reshape(slot_dev, 2, D)
    mixture = jnp.sum(gates[..., None] * pair_res, axis=1)
    output = (live * (residual + shared_res + mixture)).astype(jnp.bfloat16)
    grad_res = cotangent[0].astype(jnp.float32) * live
    grad_gate = jnp.sum(grad_res[:, None, :] * pair_res, axis=-1)
    grad_chosen = gates * (grad_gate - jnp.sum(gates * grad_gate, axis=-1, keepdims=True))
    grad_logits = jnp.sum(grad_chosen[..., None] * route_hot, axis=1).astype(jnp.bfloat16)
    grad_pairs = (
        (gates[..., None] * grad_res[:, None, :]).astype(jnp.bfloat16).reshape(2 * slot_dev, D)
    )
    grad_slots = lax.dot_general(
        pick, grad_pairs, contract_rows, preferred_element_type=jnp.float32
    ).astype(jnp.bfloat16)
    grad_arrived = lax.all_to_all(
        grad_slots.reshape(expert_total, capacity, D),
        "ctx",
        split_axis=0,
        concat_axis=0,
        tiled=True,
    )
    grad_rows = to_experts(grad_arrived)
    grad_activation = jnp.einsum(
        "end,efd->enf", grad_rows, wide_out, preferred_element_type=jnp.float32
    )
    grad_wide_out = jnp.einsum(
        "enf,end->efd", expert_act, grad_rows, preferred_element_type=jnp.float32
    )
    grad_expert_gate = (
        grad_activation
        * expert_up
        * expert_sigmoid
        * (1.0 + expert_gate_part * (1.0 - expert_sigmoid))
    )
    grad_expert_up = grad_activation * expert_gate_part * expert_sigmoid
    grad_middle = jnp.concatenate([grad_expert_gate, grad_expert_up], axis=-1).astype(jnp.bfloat16)
    grad_wide_in = jnp.einsum(
        "end,enf->edf", expert_rows, grad_middle, preferred_element_type=jnp.float32
    )
    grad_inrows = jnp.einsum(
        "enf,edf->end", grad_middle, wide_in, preferred_element_type=jnp.float32
    ).astype(jnp.bfloat16)
    grad_sent = lax.all_to_all(
        to_sources(grad_inrows), "ctx", split_axis=0, concat_axis=0, tiled=True
    )
    grad_from_experts = jnp.dot(
        token_pick,
        grad_sent.reshape(expert_total * capacity, D),
        preferred_element_type=jnp.float32,
    )
    expert_in_grad, expert_out_grad = (
        lax.psum_scatter(
            grad_wide_in.astype(jnp.bfloat16), "fsdp", scatter_dimension=1, tiled=True
        ).astype(jnp.float32),
        lax.psum_scatter(
            grad_wide_out.astype(jnp.bfloat16), "fsdp", scatter_dimension=2, tiled=True
        ).astype(jnp.float32),
    )
    grad_shared_res = grad_res.astype(jnp.bfloat16)
    grad_shared_act = lax.dot_general(
        grad_shared_res, shared_out, contract_cols, preferred_element_type=jnp.float32
    )
    grad_weight_so = lax.dot_general(
        shared_act, grad_shared_res, contract_rows, preferred_element_type=jnp.float32
    )
    grad_sgate = grad_shared_act * shared_up * shared_sig * (1.0 + shared_gate * (1.0 - shared_sig))
    grad_sup = grad_shared_act * shared_gate * shared_sig
    grad_smid = jnp.concatenate([grad_sgate, grad_sup], axis=-1).astype(jnp.bfloat16)
    grad_weight_si = lax.dot_general(
        ffn_in, grad_smid, contract_rows, preferred_element_type=jnp.float32
    )
    grad_weight_router = lax.dot_general(
        ffn_in, grad_logits, contract_rows, preferred_element_type=jnp.float32
    )
    grad_ffn_in = lax.dot_general(
        grad_smid, shared_in, contract_cols, preferred_element_type=jnp.float32
    )
    grad_ffn_in = (
        grad_ffn_in
        + lax.dot_general(
            grad_logits, weight_router, contract_cols, preferred_element_type=jnp.float32
        )
        + grad_from_experts
    )
    grad_norm_two, grad_gain_two = norm_back(grad_ffn_in, residual, inv_two, gain_two)
    grad_residual = grad_res + grad_norm_two
    grad_branch = grad_residual.astype(jnp.bfloat16)
    grad_weight_out = lax.dot_general(
        attn_out, grad_branch, contract_rows, preferred_element_type=jnp.float32
    )
    grad_heads = (
        lax.dot_general(grad_branch, weight_out, contract_cols, preferred_element_type=jnp.float32)
        .astype(jnp.bfloat16)
        .reshape(slot_dev, HEADS, HEAD_DIM)
    )
    delta_slots = jnp.sum(grad_heads.astype(jnp.float32) * attn_heads, axis=-1)
    delta_rows = delta_slots.T

    def grad_step(grad_acc, pieces):
        block_kv, block_pos = pieces
        block_keys = block_kv[:, :D].reshape(key_block, HEADS, HEAD_DIM)
        block_values = block_kv[:, D:].reshape(key_block, HEADS, HEAD_DIM)
        dscores, wprobs = prob_grads(
            queries,
            block_keys,
            block_values,
            grad_heads,
            log_total,
            delta_rows,
            query_pos,
            block_pos,
            length,
            scale,
        )
        grad_acc = grad_acc + jnp.einsum(
            "hqk,khd->hqd", dscores, block_keys, preferred_element_type=jnp.float32
        )
        grad_keys = (
            jnp.einsum("hqk,qhd->khd", dscores, queries, preferred_element_type=jnp.float32) * scale
        )
        grad_values = jnp.einsum(
            "hqk,qhd->khd", wprobs, grad_heads, preferred_element_type=jnp.float32
        )
        return (
            grad_acc,
            jnp.concatenate(
                [grad_keys.reshape(key_block, D), grad_values.reshape(key_block, D)], axis=1
            ),
        )

    grad_query_sum, kv_terms = lax.scan(
        grad_step, jnp.zeros((HEADS, slot_dev, HEAD_DIM), jnp.float32), (kv_blocks, pos_blocks)
    )
    own_kv = lax.psum_scatter(
        kv_terms.reshape(slot_total, 2 * D).astype(jnp.bfloat16),
        "ctx",
        scatter_dimension=0,
        tiled=True,
    ).astype(jnp.float32)
    grad_local_keys = own_kv[:, :D].reshape(slot_dev, HEADS, HEAD_DIM)
    grad_values_own = own_kv[:, D:]
    grad_query_rot = (
        (grad_query_sum * scale).transpose(1, 0, 2).astype(jnp.bfloat16).astype(jnp.float32)
    )
    grad_query_raw = unrotate(grad_query_rot, cos_part, sin_part)
    grad_key_raw = unrotate(
        grad_local_keys.astype(jnp.bfloat16).astype(jnp.float32), cos_part, sin_part
    )
    grad_projected = jnp.concatenate(
        [grad_query_raw.reshape(slot_dev, D), grad_key_raw.reshape(slot_dev, D), grad_values_own],
        axis=1,
    ).astype(jnp.bfloat16)
    grad_weight_qkv = lax.dot_general(
        attn_in, grad_projected, contract_rows, preferred_element_type=jnp.float32
    )
    grad_attn_in = lax.dot_general(
        grad_projected, weight_qkv, contract_cols, preferred_element_type=jnp.float32
    )
    grad_norm_one, grad_gain_one = norm_back(grad_attn_in, resid_in, inv_one, gain_one)
    grad_inputs = grad_residual + grad_norm_one
    dense_terms = (
        lax.psum_scatter(
            grad_gain_one.astype(jnp.bfloat16), "fsdp", scatter_dimension=0, tiled=True
        ).astype(jnp.float32),
        lax.psum_scatter(
            grad_weight_qkv.astype(jnp.bfloat16), "fsdp", scatter_dimension=0, tiled=True
        ).astype(jnp.float32),
        lax.psum_scatter(
            grad_weight_out.astype(jnp.bfloat16), "fsdp", scatter_dimension=0, tiled=True
        ).astype(jnp.float32),
        lax.psum_scatter(
            grad_gain_two.astype(jnp.bfloat16), "fsdp", scatter_dimension=0, tiled=True
        ).astype(jnp.float32),
        lax.psum_scatter(
            grad_weight_router.astype(jnp.bfloat16), "fsdp", scatter_dimension=0, tiled=True
        ).astype(jnp.float32),
        lax.psum_scatter(
            grad_weight_si.astype(jnp.bfloat16), "fsdp", scatter_dimension=0, tiled=True
        ).astype(jnp.float32),
        lax.psum_scatter(
            grad_weight_so.astype(jnp.bfloat16), "fsdp", scatter_dimension=0, tiled=True
        ).astype(jnp.float32),
    )
    dense_sums = (
        lax.psum(dense_terms[0].astype(jnp.bfloat16), "ctx").astype(jnp.float32),
        lax.psum(dense_terms[1].astype(jnp.bfloat16), "ctx").astype(jnp.float32),
        lax.psum(dense_terms[2].astype(jnp.bfloat16), "ctx").astype(jnp.float32),
        lax.psum(dense_terms[3].astype(jnp.bfloat16), "ctx").astype(jnp.float32),
        lax.psum(dense_terms[4].astype(jnp.bfloat16), "ctx").astype(jnp.float32),
        lax.psum(dense_terms[5].astype(jnp.bfloat16), "ctx").astype(jnp.float32),
        lax.psum(dense_terms[6].astype(jnp.bfloat16), "ctx").astype(jnp.float32),
    )
    return (
        output[None],
        grad_inputs[None],
        dense_sums[0],
        dense_sums[1],
        dense_sums[2],
        dense_sums[3],
        dense_sums[4],
        dense_sums[5],
        dense_sums[6],
        expert_in_grad,
        expert_out_grad,
    )


def solution(mesh):
    placed = (
        P("fsdp", "ctx", None),
        P("fsdp", "ctx", None),
        P("fsdp"),
        P(),
        P("fsdp", "ctx", None),
        P("fsdp"),
        P("fsdp", None),
        P("fsdp", None),
        P("fsdp"),
        P("fsdp", None),
        P("fsdp", None),
        P("fsdp", None),
        P("ctx", "fsdp", None),
        P("ctx", None, "fsdp"),
    )
    return jax.shard_map(
        on_device,
        mesh=mesh,
        in_specs=placed,
        out_specs=(
            P("fsdp", "ctx", None),
            P("fsdp", "ctx", None),
            P("fsdp"),
            P("fsdp", None),
            P("fsdp", None),
            P("fsdp"),
            P("fsdp", None),
            P("fsdp", None),
            P("fsdp", None),
            P("ctx", "fsdp", None),
            P("ctx", None, "fsdp"),
        ),
        check_vma=False,
    )
```

profile of v0, /device:TPU:0, one launch (start us, length us, event | category | flops | bytes accessed | tf_op | source)
XLA Modules:
  0.0 1029.6 jit_solution(17480993784199968676)
XLA Ops:
  11.7 8.3 all-reduce.7
  24.7 18.3 %all-gather.9.cloned.1.call-done = bf16[768,2304]{1,0:T(8,128)(2,1)} async-done(((bf16[192,2304]{1,0:T(8,128)(2,1)}), bf16[768,2304]{1,0:T(8,128)(2,1)}) %all-gather.9.cloned.1.call-update) | async-done | bytes 3538960 | tf_op jit(solution)/shard_map/all_gather | solution.py:117
  43.1 3.3 fusion.85
  56.1 92.2 %all-gather.11.cloned.1.call-done = bf16[2048,1536]{1,0:T(8,128)(2,1)} async-done(((bf16[256,1536]{1,0:T(8,128)(2,1)}), bf16[2048,1536]{1,0:T(8,128)(2,1)}) %all-gather.11.cloned.1.call-update) | async-done | bytes 6291472 | tf_op jit(solution)/shard_map/all_gather | solution.py:139
  148.4 8.6 copy.97
  157.0 57.0 %while.28 = (s32[]{:T(128)}, f32[12,256]{1,0:T(8,128)S(1)}, f32[12,256]{1,0:T(8,128)S(1)}, f32[12,256,64]{1,2,0:T(8,128)S(1)}, s32[4,512]{1,0:T(4,128)}, /*index...) while((s32[]{:T(128)}, f32[12,256]{1,0:T(8,128)S(1)}, ...), condition=%wide.region_4.5_spmd.clone, body=%wide.region_1.4_spmd.clone.sunk | while | flops 423968256 | bytes 54599840 | solution.py:171
  161.0 3.8 fusion.179
  164.8 4.4 fusion.180
  175.3 3.8 fusion.179
  179.2 4.4 fusion.180
  189.5 3.8 fusion.179
  193.3 4.4 fusion.180
  203.7 3.8 fusion.179
  207.6 4.5 fusion.180
  219.8 4.3 all-to-all-start
  224.1 5.4 all-gather
  238.6 3.4 fusion.48
  242.0 11.0 %all-to-all-done = bf16[8,96,768]{2,1,0:T(8,128)(2,1)} async-done(((bf16[8,96,768]{2,1,0:T(8,128)(2,1)}), bf16[8,96,768]{2,1,0:T(8,128)(2,1)}, u32[]{:S(2)}, u32[]{:S(2)}) %all-to-all-start) | async-done | bytes 1179680 | tf_op jit(solution)/shard_map/all_to_all | solution.py:222
  252.9 3.6 all-to-all-start.2
  257.3 10.1 convolution_bitcast_fusion
  267.5 17.9 %all-to-all-done.2 = bf16[8,96,768]{2,1,0:T(8,128)(2,1)S(1)} async-done(((bf16[8,96,768]{2,1,0:T(8,128)(2,1)}), bf16[8,96,768]{2,1,0:T(8,128)(2,1)S(1)}, u32[]{:S(2)}, u32[]{:S(2)}) %all-to-all-start.2) | async-done | bytes 1179680 | tf_op jit(solution)/shard_map/all_to_all | solution.py:254
  285.3 10.6 %fusion.39 = (bf16[768,2048]{1,0:T(8,128)(2,1)}, bf16[768,2048]{1,0:T(8,128)(2,1)}, bf16[1,768,2048]{2,1,0:T(8,128)(2,1)S(1)}) fusion(f32[1,768,4096]{2,1,0:T(8,128)} %convolution_bitcast_fusion, bf16[768,768]{1,0:T(8,128)(2,1)S(1)} %bitcast.307, bf16[1,2048,768]{1,2,0:T(8,128)(2,1)} %all-gather.21.cloned.1.call-done), kind=kOutput, calls=%fused_computation.67 | convolution fusion | flops 2441084928 | bytes 26345472 | tf_op jit(solution)/shard_map/end,efd->enf/dot_general | solution.py:262
  295.9 3.7 fusion.49
  299.6 4.1 all-to-all-start.1
  303.7 6.8 fusion.107
  310.6 8.9 fusion.54
  319.5 12.9 %all-to-all-done.1 = bf16[8,96,768]{2,1,0:T(8,128)(2,1)S(1)} async-done(((bf16[8,96,768]{2,1,0:T(8,128)(2,1)}), bf16[8,96,768]{2,1,0:T(8,128)(2,1)S(1)}, u32[]{:S(2)}, u32[]{:S(2)}) %all-to-all-start.1) | async-done | bytes 1179680 | tf_op jit(solution)/shard_map/all_to_all | solution.py:236
  333.4 3.6 all-to-all-start.3
  337.7 5.7 multiply_convert_fusion.2
  343.4 6.3 fusion.57
  352.3 13.5 %all-to-all-done.3 = bf16[8,96,768]{2,1,0:T(8,128)(2,1)S(1)} async-done(((bf16[8,96,768]{2,1,0:T(8,128)(2,1)}), bf16[8,96,768]{2,1,0:T(8,128)(2,1)S(1)}, u32[]{:S(2)}, u32[]{:S(2)}) %all-to-all-start.3) | async-done | bytes 1179680 | tf_op jit(solution)/shard_map/all_to_all | solution.py:282
  373.1 83.8 %while.29 = (s32[]{:T(128)}, f32[12,256,64]{1,2,0:T(8,128)}, bf16[4,512,1536]{2,1,0:T(8,128)(2,1)}, s32[4,512]{1,0:T(4,128)}, s32[256]{0:T(256)}, /*index=5*/s32...) while((s32[]{:T(128)}, f32[12,256,64]{1,2,0:T(8,128)}, ...), condition=%wide.region_20.21_spmd.clone, body=%wide.region_19.20_spmd.clone.sunk | while | flops 1026949632 | bytes 54801124 | solution.py:370
  378.2 3.1 fusion.195
  388.6 2.7 constant_dynamic-update-slice_fusion.2
  391.3 2.7 convolution_add_fusion.4
  398.9 3.1 fusion.195
  412.0 2.9 convolution_add_fusion.4
  419.9 3.1 fusion.195
  430.3 2.7 constant_dynamic-update-slice_fusion.2
  432.9 2.9 convolution_add_fusion.4
  440.9 3.1 fusion.195
  451.2 2.7 constant_dynamic-update-slice_fusion.2
  453.9 2.9 convolution_add_fusion.4
  458.2 2.8 convolution_convert_fusion.4
  463.8 6.1 convolution_convert_fusion
  471.9 102.1 %reduce-scatter.13.cloned.1.call-done = bf16[256,1536]{1,0:T(8,128)(2,1)} async-done(((bf16[2048,1536]{1,0:T(8,128)(2,1)}), bf16[256,1536]{1,0:T(8,128)(2,1)}) %reduce-scatter.13.cloned.1.call-update) | async-done | bytes 786448 | tf_op jit(solution)/shard_map/reduce_scatter | solution.py:373
  580.1 4.5 convolution_convert_fusion.2
  586.3 6.6 fusion.40
  592.9 15.8 %copy.120 = bf16[1,2048,768]{1,0,2:T(2,128)(2,1)} copy(bf16[1,2048,768]{2,1,0:T(8,128)(2,1)} %fusion.40) | data formatting | bytes 6291456
  608.7 6.5 copy.145
  615.3 11.0 %fusion.31 = bf16[1,768,4096]{2,1,0:T(8,128)(2,1)} fusion(bf16[768,768]{1,0:T(8,128)(2,1)} %bitcast.16, bf16[768,2048]{1,0:T(8,128)(2,1)} %get-tuple-element.385, bf16[768,2048]{1,0:T(8,128)(2,1)} %get-tuple-element.384), kind=kOutput, calls=%fused_computation.55 | convolution fusion | flops 4847566848 | bytes 13762560 | tf_op jit(solution)/shard_map/end,enf->edf/dot_general | solution.py:276
  626.6 16.0 %reduce-scatter.17.cloned.1.call-done = bf16[192,768]{1,0:T(8,128)(2,1)} async-done(((bf16[768,768]{1,0:T(8,128)(2,1)}), bf16[192,768]{1,0:T(8,128)(2,1)}) %reduce-scatter.17.cloned.1.call-update) | async-done | bytes 294928 | tf_op jit(solution)/shard_map/reduce_scatter | solution.py:407
  642.7 60.9 %reduce-scatter.19.cloned.1.call-done = bf16[192,4096]{1,0:T(8,128)(2,1)} async-done(((bf16[768,4096]{1,0:T(8,128)(2,1)}), bf16[192,4096]{1,0:T(8,128)(2,1)}) %reduce-scatter.19.cloned.1.call-update) | async-done | bytes 1572880 | tf_op jit(solution)/shard_map/reduce_scatter | solution.py:416
  703.6 43.0 %reduce-scatter.15.cloned.1.call-done = bf16[192,2304]{1,0:T(8,128)(2,1)} async-done(((bf16[768,2304]{1,0:T(8,128)(2,1)}), bf16[192,2304]{1,0:T(8,128)(2,1)}) %reduce-scatter.15.cloned.1.call-update) | async-done | bytes 884752 | tf_op jit(solution)/shard_map/reduce_scatter | solution.py:404
  747.3 3.8 fusion.62
  751.2 18.3 %reduce-scatter.25.cloned.1.call-done = bf16[192,8]{1,0:T(8,128)(2,1)} async-done(((bf16[768,8]{1,0:T(8,128)(2,1)}), bf16[192,8]{1,0:T(8,128)(2,1)}) %reduce-scatter.25.cloned.1.call-update) | async-done | bytes 3088
  770.3 39.5 %reduce-scatter.27.cloned.1.call-done = bf16[192,2048]{1,0:T(8,128)(2,1)} async-done(((bf16[768,2048]{1,0:T(8,128)(2,1)}), bf16[192,2048]{1,0:T(8,128)(2,1)}) %reduce-scatter.27.cloned.1.call-update) | async-done | bytes 786448
  811.9 3.1 copy.121
  817.5 53.2 %reduce-scatter.23.cloned.1.call-done = bf16[1,192,4096]{2,1,0:T(8,128)(2,1)} async-done(((bf16[1,768,4096]{2,1,0:T(8,128)(2,1)}), bf16[1,192,4096]{2,1,0:T(8,128)(2,1)}) %reduce-scatter.23.cloned.1.call-update) | async-done | bytes 1572880 | tf_op jit(solution)/shard_map/reduce_scatter | solution.py:291
  870.7 3.6 convert_element_type.277
  875.6 5.8 all-reduce.6
  881.5 23.1 %all-reduce.4 = (bf16[192]{0:T(256)(128)(2,1)S(1)}, bf16[192]{0:T(256)(128)(2,1)S(1)}, bf16[192,8]{0,1:T(8,128)(2,1)S(1)}) all-reduce(bf16[192]{0:T(256)(128)(2,1)S(1)} %dynamic-slice.3, bf16[192]{0:T(256)(128)(2,1)S(1)} %dynamic-slice.5, bf16[192,8]{0,1:T(8,128)(2,1)S(1)} %copy.119), channel_id=1, replica_groups=mesh['ctx'=8,'fsdp'=4] {'ctx'}, use_global_device_ids=true, to_apply=%region_25.26 | all-reduce | flops 1920 | bytes 7680 | tf_op jit(solution)/shard_map/psum | solution.py:424
  907.5 108.1 %all-reduce.10.cloned.1.call-done = (bf16[192,2304]{1,0:T(8,128)(2,1)}, bf16[192,768]{1,0:T(8,128)(2,1)}, bf16[192,4096]{1,0:T(8,128)(2,1)}, bf16[512,768]{1,0:T(8,128)(2,1)}) async-done(((bf16[192,2304]{1,0:T(8,128)(2,1)}, bf16[192,768]{1,0:T(8,128)(2,1)}, bf16[192,4096]{1,0:T(8,128)(2,1)}, bf16[512,768]{1,0:T(8,128)(2,1)}), (bf16[192,2304]{1,0:T(8,128)(2,1)}, bf16[192,768]{1,0:T(8,128)(2,1)}, ...) | async-done | bytes 3538960 | tf_op jit(solution)/shard_map/psum | solution.py:425
  1015.6 3.6 convert_element_type.272
  (393 shorter events, 146.7 us)
Async XLA Ops:
  7.2 35.9 %all-gather.9.cloned.1.call-start = ((), (), s32[]{:S(2)}) async-start(), calls=%async_computation.12 | async-start | bytes 4423680 | tf_op jit(solution)/shard_map/all_gather | solution.py:117
  7.9 140.5 %all-gather.11.cloned.1.call-start = ((), (), s32[]{:S(2)}) async-start(), calls=%async_computation.13 | async-start | bytes 7077888 | tf_op jit(solution)/shard_map/all_gather | solution.py:139
  20.0 26.3 %copy-start.49 = (f32[768]{0:T(1024)}, f32[768]{0:T(1024)S(1)}, u32[]{:S(2)}) copy-start(f32[768]{0:T(1024)S(1)} %convert_element_type.226) | copy-start | bytes 9220
  24.5 21.8 %copy-start.65 = (f32[256]{0:T(256)}, f32[256]{0:T(256)S(1)}, u32[]{:S(2)}) copy-start(f32[256]{0:T(256)S(1)} %get-tuple-element.409) | copy-start | bytes 3076
  24.7 22.3 %copy-start.40 = (f32[256,32]{0,1:T(8,128)}, f32[256,32]{0,1:T(8,128)S(1)}, u32[]{:S(2)}) copy-start(f32[256,32]{0,1:T(8,128)S(1)} %get-tuple-element.406) | copy-start | bytes 98308
  24.7 22.3 %copy-start.42 = (f32[256,32]{0,1:T(8,128)}, f32[256,32]{0,1:T(8,128)S(1)}, u32[]{:S(2)}) copy-start(f32[256,32]{0,1:T(8,128)S(1)} %get-tuple-element.407) | copy-start | bytes 98308
  49.2 6.9 copy-start.34
  49.2 165.0 %all-gather.13.cloned.1.call-start = ((), (), s32[]{:S(2)}) async-start(), calls=%async_computation.14 | async-start | bytes 1474560 | tf_op jit(solution)/shard_map/all_gather | solution.py:118
  49.9 207.4 %all-gather.19.cloned.1.call-start = ((), (), s32[]{:S(2)}) async-start(), calls=%async_computation.17 | async-start | bytes 7864320 | tf_op jit(solution)/shard_map/all_gather | solution.py:204
  50.5 217.0 %all-gather.21.cloned.1.call-start = ((), (), s32[]{:S(2)}) async-start(), calls=%async_computation.18 | async-start | bytes 3932160 | tf_op jit(solution)/shard_map/all_gather | solution.py:205
  51.1 252.6 %all-gather.15.cloned.1.call-start = ((), (), s32[]{:S(2)}) async-start(), calls=%async_computation.15 | async-start | bytes 7864320 | tf_op jit(solution)/shard_map/all_gather | solution.py:121
  55.4 162.8 %copy-start.19 = (bf16[256,768]{1,0:T(8,128)(2,1)}, bf16[256,768]{1,0:T(8,128)(2,1)S(1)}, u32[]{:S(2)}) copy-start(bf16[256,768]{1,0:T(8,128)(2,1)S(1)} %fusion.63) | copy-start | bytes 1179652
  157.0 58.0 %copy-start.9 = (bf16[1,256,768]{2,1,0:T(8,128)(2,1)S(1)}, bf16[1,256,768]{2,1,0:T(8,128)(2,1)}, u32[]{:S(2)}) copy-start(bf16[1,256,768]{2,1,0:T(8,128)(2,1)} %param.18) | copy-start | bytes 1179652
  164.8 4.6 copy-start
  179.2 4.6 copy-start
  193.3 4.7 copy-start
  207.6 4.7 copy-start
  216.9 151.8 %copy-start.5 = (f32[256,768]{1,0:T(8,128)}, f32[256,768]{1,0:T(8,128)S(1)}, u32[]{:S(2)}) copy-start(f32[256,768]{1,0:T(8,128)S(1)} %get-tuple-element.415) | copy-start | bytes 2359300
  216.9 7.2 copy-start.73
  216.9 14.0 %copy-start.14 = (bf16[1,256,768]{2,1,0:T(8,128)(2,1)S(1)}, bf16[1,256,768]{2,1,0:T(8,128)(2,1)}, u32[]{:S(2)}) copy-start(bf16[1,256,768]{2,1,0:T(8,128)(2,1)} %param.19) | copy-start | bytes 1179652
  216.9 14.0 %copy-start.62 = (f32[256]{0:T(256)S(1)}, f32[256]{0:T(256)}, u32[]{:S(2)}) copy-start(f32[256]{0:T(256)} %get-tuple-element.376) | copy-start | bytes 3076
  217.5 13.5 %copy-start.61 = (f32[256]{0:T(256)}, f32[256]{0:T(256)S(1)}, u32[]{:S(2)}) copy-start(f32[256]{0:T(256)S(1)} %get-tuple-element.411) | copy-start | bytes 3076
  218.3 85.4 %copy-start.3 = (bf16[256,768]{1,0:T(8,128)(2,1)}, bf16[256,768]{1,0:T(8,128)(2,1)S(1)}, u32[]{:S(2)}) copy-start(bf16[256,768]{1,0:T(8,128)(2,1)S(1)} %multiply_convert_fusion.7) | copy-start | bytes 1179652
  219.8 33.1 %all-to-all-start = ((bf16[8,96,768]{2,1,0:T(8,128)(2,1)}), bf16[8,96,768]{2,1,0:T(8,128)(2,1)}, u32[]{:S(2)}, u32[]{:S(2)}) async-start(bf16[8,96,768]{2,1,0:T(8,128)(2,1)} %bitcast.15), calls=%async_computation | async-start | bytes 2359296 | tf_op jit(solution)/shard_map/all_to_all | solution.py:222
  238.3 14.7 %copy-start.69 = (f32[256,2]{0,1:T(2,128)}, f32[256,2]{0,1:T(2,128)S(1)}, u32[]{:S(2)}) copy-start(f32[256,2]{0,1:T(2,128)S(1)} %fusion.92) | copy-start | bytes 6148
  252.9 32.4 %all-to-all-start.2 = ((bf16[8,96,768]{2,1,0:T(8,128)(2,1)}), bf16[8,96,768]{2,1,0:T(8,128)(2,1)S(1)}, u32[]{:S(2)}, u32[]{:S(2)}) async-start(bf16[8,96,768]{2,1,0:T(8,128)(2,1)} %bitcast.311), calls=%async_computation.2 | async-start | bytes 2359296 | tf_op jit(solution)/shard_map/all_to_all | solution.py:254
  256.6 81.1 %all-gather.17.cloned.1.call-start = ((), (), s32[]{:S(2)}) async-start(), calls=%async_computation.16 | async-start | bytes 3932160 | tf_op jit(solution)/shard_map/all_gather | solution.py:122
  285.3 10.6 %copy-start.25 = (bf16[8,96,768]{2,1,0:T(8,128)(2,1)}, bf16[8,96,768]{2,1,0:T(8,128)(2,1)S(1)}, u32[]{:S(2)}) copy-start(bf16[8,96,768]{2,1,0:T(8,128)(2,1)S(1)} %all-to-all-done.2) | copy-start | bytes 3538948
  285.3 10.6 %copy-start.75 = (bf16[1,2048,768]{1,2,0:T(8,128)(2,1)S(1)}, bf16[1,2048,768]{1,2,0:T(8,128)(2,1)}, u32[]{:S(2)}) copy-start(bf16[1,2048,768]{1,2,0:T(8,128)(2,1)} %all-gather.21.cloned.1.call-done) | copy-start | bytes 9437188
  299.6 32.8 %all-to-all-start.1 = ((bf16[8,96,768]{2,1,0:T(8,128)(2,1)}), bf16[8,96,768]{2,1,0:T(8,128)(2,1)S(1)}, u32[]{:S(2)}, u32[]{:S(2)}) async-start(bf16[8,96,768]{2,1,0:T(8,128)(2,1)} %bitcast.312), calls=%async_computation.1 | async-start | bytes 2359296 | tf_op jit(solution)/shard_map/all_to_all | solution.py:236
  303.7 6.8 copy-start.77
  303.7 6.8 copy-start.78
  310.6 26.5 %copy-start.29 = (f32[12,256]{1,0:T(8,128)S(1)}, f32[12,256]{1,0:T(8,128)}, u32[]{:S(2)}) copy-start(f32[12,256]{1,0:T(8,128)} %copy-done.28) | copy-start | bytes 36868
  310.6 27.1 %copy-start.63 = (f32[256]{0:T(256)S(1)}, f32[256]{0:T(256)}, u32[]{:S(2)}) copy-start(f32[256]{0:T(256)} %get-tuple-element.376) | copy-start | bytes 3076
  333.4 32.4 %all-to-all-start.3 = ((bf16[8,96,768]{2,1,0:T(8,128)(2,1)}), bf16[8,96,768]{2,1,0:T(8,128)(2,1)S(1)}, u32[]{:S(2)}, u32[]{:S(2)}) async-start(bf16[8,96,768]{2,1,0:T(8,128)(2,1)} %bitcast.310), calls=%async_computation.3 | async-start | bytes 2359296 | tf_op jit(solution)/shard_map/all_to_all | solution.py:282
  337.0 237.1 %reduce-scatter.13.cloned.1.call-start = ((), (), s32[]{:S(2)}) async-start(), calls=%async_computation.19 | async-start | bytes 7077888 | tf_op jit(solution)/shard_map/reduce_scatter | solution.py:373
  343.4 6.3 copy-start.31
  343.4 6.3 copy-start.32
  343.4 6.4 copy-start.24
  343.4 6.4 copy-start.27
  343.4 6.4 copy-start.68
  343.4 6.4 copy-start.70
  349.7 16.0 %copy-start.20 = (bf16[256,768]{1,0:T(8,128)(2,1)S(1)}, bf16[256,768]{1,0:T(8,128)(2,1)}, u32[]{:S(2)}) copy-start(bf16[256,768]{1,0:T(8,128)(2,1)} %copy-done.19) | copy-start | bytes 1179652
  349.8 16.5 %copy-start.45 = (bf16[768,8]{0,1:T(8,128)(2,1)S(1)}, bf16[768,8]{0,1:T(8,128)(2,1)}, u32[]{:S(2)}) copy-start(bf16[768,8]{0,1:T(8,128)(2,1)} %reshape.537) | copy-start | bytes 36868
  349.8 16.5 %copy-start.48 = (f32[768]{0:T(1024)S(1)}, f32[768]{0:T(1024)}, u32[]{:S(2)}) copy-start(f32[768]{0:T(1024)} %convert_element_type.232) | copy-start | bytes 9220
  351.6 17.0 %copy-start.15 = (bf16[1,256,768]{2,1,0:T(8,128)(2,1)S(1)}, bf16[1,256,768]{2,1,0:T(8,128)(2,1)}, u32[]{:S(2)}) copy-start(bf16[1,256,768]{2,1,0:T(8,128)(2,1)} %param.19) | copy-start | bytes 1179652
  456.9 169.7 %reduce-scatter.21.cloned.1.call-start = ((), (), s32[]{:S(2)}) async-start(), calls=%async_computation.23 | async-start | bytes 3932160 | tf_op jit(solution)/shard_map/reduce_scatter | solution.py:419
  461.0 181.7 %reduce-scatter.17.cloned.1.call-start = ((), (), s32[]{:S(2)}) async-start(), calls=%async_computation.21 | async-start | bytes 1474560 | tf_op jit(solution)/shard_map/reduce_scatter | solution.py:407
  463.7 239.9 %reduce-scatter.19.cloned.1.call-start = ((), (), s32[]{:S(2)}) async-start(), calls=%async_computation.22 | async-start | bytes 7864320 | tf_op jit(solution)/shard_map/reduce_scatter | solution.py:416
  469.8 107.3 %copy-start.41 = (f32[256,32]{0,1:T(8,128)S(1)}, f32[256,32]{0,1:T(8,128)}, u32[]{:S(2)}) copy-start(f32[256,32]{0,1:T(8,128)} %copy-done.40) | copy-start | bytes 98308
  469.9 107.3 %copy-start.43 = (f32[256,32]{0,1:T(8,128)S(1)}, f32[256,32]{0,1:T(8,128)}, u32[]{:S(2)}) copy-start(f32[256,32]{0,1:T(8,128)} %copy-done.42) | copy-start | bytes 98308
  469.9 276.8 %reduce-scatter.15.cloned.1.call-start = ((), (), s32[]{:S(2)}) async-start(), calls=%async_computation.20 | async-start | bytes 4423680 | tf_op jit(solution)/shard_map/reduce_scatter | solution.py:404
  580.0 4.6 copy-start.37
  584.6 184.8 %reduce-scatter.25.cloned.1.call-start = ((), (), s32[]{:S(2)}) async-start(), calls=%async_computation.25 | async-start | bytes 245760
  586.3 223.5 %reduce-scatter.27.cloned.1.call-start = ((), (), s32[]{:S(2)}) async-start(), calls=%async_computation.26 | async-start | bytes 3932160
  615.2 255.5 %reduce-scatter.23.cloned.1.call-start = ((), (), s32[]{:S(2)}) async-start(), calls=%async_computation.24 | async-start | bytes 7864320 | tf_op jit(solution)/shard_map/reduce_scatter | solution.py:291
  626.3 121.1 %copy-start.6 = (f32[256,768]{1,0:T(8,128)S(1)}, f32[256,768]{1,0:T(8,128)}, u32[]{:S(2)}) copy-start(f32[256,768]{1,0:T(8,128)} %copy-done.5) | copy-start | bytes 2359300
  626.3 389.3 %all-reduce.10.cloned.1.call-start = ((), (), s32[]{:S(2)}) async-start(), calls=%async_computation.27 | async-start | bytes 7077888 | tf_op jit(solution)/shard_map/psum | solution.py:425
  815.0 59.3 %copy-start.11 = (bf16[1,256,768]{2,1,0:T(8,128)(2,1)S(1)}, bf16[1,256,768]{2,1,0:T(8,128)(2,1)}, u32[]{:S(2)}) copy-start(bf16[1,256,768]{2,1,0:T(8,128)(2,1)} %param.18) | copy-start | bytes 1179652
  815.0 59.3 %copy-start.36 = (bf16[256,768]{1,0:T(8,128)(2,1)S(1)}, bf16[256,768]{1,0:T(8,128)(2,1)}, u32[]{:S(2)}) copy-start(bf16[256,768]{1,0:T(8,128)(2,1)} %copy.111) | copy-start | bytes 1179652
  815.0 59.3 %copy-start.38 = (bf16[256,768]{1,0:T(8,128)(2,1)S(1)}, bf16[256,768]{1,0:T(8,128)(2,1)}, u32[]{:S(2)}) copy-start(bf16[256,768]{1,0:T(8,128)(2,1)} %copy-done.37) | copy-start | bytes 1179652
  815.0 59.3 %copy-start.39 = (bf16[256,768]{1,0:T(8,128)(2,1)S(1)}, bf16[256,768]{1,0:T(8,128)(2,1)}, u32[]{:S(2)}) copy-start(bf16[256,768]{1,0:T(8,128)(2,1)} %get-tuple-element.401) | copy-start | bytes 1179652
  874.3 32.0 %copy-start.72 = (f32[256]{0:T(256)S(1)}, f32[256]{0:T(256)}, u32[]{:S(2)}) copy-start(f32[256]{0:T(256)} %get-tuple-element.408) | copy-start | bytes 3076
  1015.6 4.9 copy-start.35
  (47 other events, 81.3 us)
Sparse Core Ops, SparseCore 0:
  9.6 33.4 all-gather.8
  49.3 99.0 all-gather.10
  149.9 15.6 all-gather.12
  167.0 46.3 all-gather.18
  214.8 28.6 all-gather.20
  244.9 46.3 all-gather.14
  292.9 28.5 all-gather.16
  457.0 117.0 reduce-scatter.12
  576.6 37.0 reduce-scatter.20
  616.9 25.7 reduce-scatter.16
  645.2 58.3 reduce-scatter.18
  706.2 40.3 reduce-scatter.14
  749.6 19.7 reduce-scatter.24
  771.8 37.9 reduce-scatter.26
  812.3 58.3 reduce-scatter.22
  874.5 141.0 all-reduce.9
where the time goes:
time: 1040 us; the launch traced here: 1030 us
  waiting for transfers between devices  611 us (59%)
  matrix products  170 us (16%)
  local copies, waits for them, and re-layouts  96.4 us (9%)
  other arithmetic  74.8 us (7%)
  blocking collectives  42.6 us (4%)
  between operations  17.3 us (2%)
  starting transfers between devices  16.7 us (2%)
    psum x1, waiting for transfers between devices, on_device(): lax.psum(dense_terms[1].astype(jnp.bfloat16), 'ctx').astype(jnp.float32)  108 us
    reduce_scatter x1, waiting for transfers between devices, on_device(): lax.psum_scatter(kv_terms.reshape(slot_total, 2 * D).astype(jnp.bfloat16)...  102 us
    all_gather x1, waiting for transfers between devices, on_device(): all_kv = lax.all_gather(local_kv, 'ctx', axis=0, tiled=True)  92.2 us
    unnamed x18, waiting for transfers between devices  61.6 us
    reduce_scatter x1, waiting for transfers between devices, on_device(): lax.psum_scatter(grad_weight_si.astype(jnp.bfloat16), 'fsdp', scatter_dim...  60.9 us
    reduce_scatter x1, waiting for transfers between devices, on_device(): lax.psum_scatter(grad_wide_in.astype(jnp.bfloat16), 'fsdp', scatter_dimen...  53.2 us
    unnamed x172, local copies, waits for them, and re-layouts  52.9 us
    reduce_scatter x1, waiting for transfers between devices, on_device(): lax.psum_scatter(grad_weight_qkv.astype(jnp.bfloat16), 'fsdp', scatter_di...  43 us
  transfers between devices with their start and end apart: 20, of which 14 were waited for; matrix products, arithmetic and copies ran while one was open for 22% of the time, Pallas kernels for 0%

commit v1 on v0

v1 whole, which is shorter than its diff:
```python
import functools

import jax
import jax.numpy as jnp
from jax import lax
from jax.experimental import pallas as pl
from jax.experimental.pallas import tpu as pltpu
from jax.sharding import PartitionSpec as P

D = 768
HEADS = 12
HEAD_DIM = 64
FF = 2048
FS = 2048
LANES = 128
CHUNK = 256
PACKED = 3 * D + LANES
norm_eps = 1e-06
F32 = jnp.float32
BF16 = jnp.bfloat16


def dot(a, b):
    return jnp.dot(a, b, preferred_element_type=F32)


def dot_nt(a, b):
    return lax.dot_general(a, b, (((1,), (1,)), ((), ())), preferred_element_type=F32)


def dot_tn(a, b):
    return lax.dot_general(a, b, (((0,), (0,)), ((), ())), preferred_element_type=F32)


def call(kernel, outs, *, flops, nbytes, limit=56, **kw):
    return pl.pallas_call(
        kernel,
        out_shape=outs,
        compiler_params=pltpu.CompilerParams(vmem_limit_bytes=limit << 20),
        cost_estimate=pl.CostEstimate(
            flops=int(flops), bytes_accessed=int(nbytes), transcendentals=0
        ),
        **kw,
    )


def shape(dims, dtype):
    return jax.ShapeDtypeStruct(dims, dtype)


def lanes_of(rows, width=LANES):
    return lax.broadcasted_iota(jnp.int32, (rows, width), 1)


def first_heads(n_ctx, slot_dev):
    share = HEADS * slot_dev // n_ctx
    return [min(share * d // slot_dev, HEADS - 2) for d in range(n_ctx)]


def partner(t, lane):
    return jnp.where(lane % 64 < 32, pltpu.roll(t, 96, 1), pltpu.roll(t, 32, 1))


def in_parts(v):
    high = v.astype(BF16)
    rest = v - high.astype(F32)
    mid = rest.astype(BF16)
    low = (rest - mid.astype(F32)).astype(BF16)
    return high.astype(F32), mid.astype(F32), low.astype(F32)


def part_lanes(v, lane):
    high, mid, low = in_parts(v)
    zero = jnp.zeros((), F32)
    return jnp.where(
        lane == 0, high, jnp.where(lane == 1, mid, jnp.where(lane == 2, low, zero))
    ).astype(BF16)


def picks(target_ref, places):
    rows = target_ref.shape[0]
    place = lanes_of(rows, places)
    return tuple(
        jnp.where(place == target_ref[:, k : k + 1], 1.0, 0.0).astype(BF16) for k in range(2)
    )


def qkv_kernel(heads, experts, x_ref, w_ref, cos_ref, sin_ref, send_ref, in_ref, tail_ref):
    x = x_ref[...].astype(F32)
    tail = w_ref[:, 3 * D :].astype(F32).T
    tail_ref[...] = tail
    inv = lax.rsqrt(jnp.mean(x * x, axis=-1, keepdims=True) + norm_eps)
    attn_in = (x * inv * tail[experts : experts + 1, :]).astype(BF16)
    in_ref[...] = attn_in
    lane = lanes_of(x.shape[0])
    cos, sin = cos_ref[...], sin_ref[...]
    for part in range(3):
        y = dot(attn_in, w_ref[:, part * D : (part + 1) * D])
        groups = []
        for g in range(D // LANES):
            t = y[:, g * LANES : (g + 1) * LANES]
            if part < 2:
                t = t * cos + partner(t, lane) * sin
            groups.append(t)
        turned = [pltpu.roll(t, 64, 1) for t in groups]
        for d, head in enumerate(heads):
            g = head // 2
            if head % 2 == 0:
                packet = groups[g]
            else:
                packet = jnp.where(lane < 64, turned[g], turned[g + 1])
            send_ref[d, :, part * LANES : (part + 1) * LANES] = packet.astype(BF16)


def stack_rows(stack_ref, block, lane):
    rows = block.shape[0]
    zero = jnp.zeros((), block.dtype)
    stack_ref[0:rows, :] = jnp.where(lane < 64, block, zero)
    stack_ref[rows : 2 * rows, :] = jnp.where(lane >= 64, block, zero)


def unstack_rows(stack_ref, block, offset, lane):
    rows = stack_ref.shape[0] // 2
    stack_ref[...] = jnp.zeros_like(stack_ref)
    stack_ref[pl.ds(offset, block.shape[0]), :] = block
    return jnp.where(lane < 64, stack_ref[0:rows, :], stack_ref[rows : 2 * rows, :])


def key_limits(share, rows, q_block, offset, length):
    row = lax.broadcasted_iota(jnp.int32, (1, share), 1) + offset
    row = jnp.where(row >= rows, row - rows, row)
    return jnp.minimum(q_block * rows + row + 1, length)


def attend_kernel(n, share, sc, recv_ref, out_ref, keep_ref, lse_ref, stack, scores, back):
    q_block = pl.program_id(0)
    rows = recv_ref.shape[1]
    offset = pl.multiple_of(sc[n], 64)
    length = sc[n + 1]
    lane = lanes_of(rows)
    stack_rows(stack, recv_ref[sc[q_block], :, 0:LANES] * 0.125, lane)
    query = stack[pl.ds(offset, share), :]
    limit = key_limits(share, rows, q_block, offset, length)
    key_row = lax.broadcasted_iota(jnp.int32, (rows, share), 0)
    blocks = jnp.minimum(q_block + 1, (length + rows - 1) // rows)

    def score_step(j, top):
        keys = recv_ref[sc[j], :, LANES : 2 * LANES]
        s = dot_nt(keys, query)
        s = jnp.where(key_row < limit - j * rows, s, -1e30)
        scores[j] = s
        return jnp.maximum(top, jnp.max(s, axis=0, keepdims=True))

    top = lax.fori_loop(0, blocks, score_step, jnp.full((1, share), -1e30, F32))

    def value_step(j, carry):
        total, acc = carry
        weights = jnp.exp(scores[j] - top)
        total = total + jnp.sum(weights, axis=0, keepdims=True)
        values = recv_ref[sc[j], :, 2 * LANES : 3 * LANES]
        return total, acc + dot_tn(values, weights.astype(BF16))

    total, acc = lax.fori_loop(
        0, blocks, value_step, (jnp.zeros((1, share), F32), jnp.zeros((LANES, share), F32))
    )
    acc = acc / total
    keep_ref[0] = acc
    lse_ref[0] = top + jnp.log(total)
    out_ref[0] = unstack_rows(back, acc.T, offset, lane).astype(BF16)


def attend_back_kernel(
    n, share, sc, recv_ref, grad_ref, keep_ref, lse_ref, out_ref, stack, gstack, dkeys, dvalues, back
):
    q_block = pl.program_id(0)
    rows = recv_ref.shape[1]
    offset = pl.multiple_of(sc[n], 64)
    length = sc[n + 1]
    lane = lanes_of(rows)
    source = sc[q_block]

    @pl.when(q_block == 0)
    def _():
        dkeys[...] = jnp.zeros_like(dkeys)
        dvalues[...] = jnp.zeros_like(dvalues)

    stack_rows(stack, recv_ref[source, :, 0:LANES] * 0.125, lane)
    query = stack[pl.ds(offset, share), :]
    stack_rows(gstack, grad_ref[source], lane)
    grad = gstack[pl.ds(offset, share), :]
    lse = lse_ref[0]
    delta = jnp.sum(grad.astype(F32).T * keep_ref[0], axis=0, keepdims=True)
    limit = key_limits(share, rows, q_block, offset, length)
    key_row = lax.broadcasted_iota(jnp.int32, (rows, share), 0)
    blocks = jnp.minimum(q_block + 1, (length + rows - 1) // rows)

    def step(j, acc):
        keys = recv_ref[sc[j], :, LANES : 2 * LANES]
        values = recv_ref[sc[j], :, 2 * LANES : 3 * LANES]
        s = dot_nt(keys, query)
        weights = jnp.exp(jnp.where(key_row < limit - j * rows, s, -1e30) - lse)
        dweights = dot_nt(values, grad)
        dscores = (weights * (dweights - delta)).astype(BF16)
        dkeys[j] += dot(dscores, query)
        dvalues[j] += dot(weights.astype(BF16), grad)
        return acc + dot_tn(keys, dscores)

    acc = lax.fori_loop(0, blocks, step, jnp.zeros((LANES, share), F32))
    dquery = unstack_rows(back, acc.T * 0.125, offset, lane)
    out_ref[source, :, 0:LANES] = dquery.astype(BF16)

    @pl.when(q_block == n - 1)
    def _():
        def flush(j, carry):
            out_ref[sc[j], :, LANES : 2 * LANES] = dkeys[j].astype(BF16)
            out_ref[sc[j], :, 2 * LANES : 3 * LANES] = dvalues[j].astype(BF16)
            return carry

        lax.fori_loop(0, n, flush, 0)


def middle_kernel(
    heads,
    experts,
    came_ref,
    w_ref,
    x_ref,
    tail_ref,
    routes_ref,
    target_ref,
    residual_ref,
    in_ref,
    gates_ref,
    send_ref,
):
    total = x_ref[...].astype(F32)
    for d, head in enumerate(heads):
        total = total + dot(came_ref[d], w_ref[64 * head : 64 * head + LANES, :])
    residual_ref[...] = total
    inv = lax.rsqrt(jnp.mean(total * total, axis=-1, keepdims=True) + norm_eps)
    ffn_in = (total * inv * tail_ref[experts + 1 : experts + 2, :]).astype(BF16)
    in_ref[...] = ffn_in
    logits = dot_nt(ffn_in, tail_ref[...].astype(BF16))
    lane = lanes_of(logits.shape[0])
    chosen = [
        jnp.sum(jnp.where(lane == routes_ref[:, k : k + 1], logits, 0.0), axis=-1, keepdims=True)
        for k in range(2)
    ]
    top = jnp.maximum(chosen[0], chosen[1])
    raised = [jnp.exp(c - top) for c in chosen]
    gates = [r / (raised[0] + raised[1]) for r in raised]
    gates_ref[...] = jnp.where(lane == 0, gates[0], gates[1])
    pick = picks(target_ref, send_ref.shape[0])
    send_ref[:, 0:D] = dot_tn(pick[0] + pick[1], ffn_in).astype(BF16)
    send_ref[:, D:] = (
        dot_tn(pick[0], part_lanes(gates[0], lane)) + dot_tn(pick[1], part_lanes(gates[1], lane))
    ).astype(BF16)


def gated(g, u, da):
    sig = 1.0 / (1.0 + jnp.exp(-g))
    silu = g * sig
    return silu * u, da * u * sig * (1.0 + g * (1.0 - sig)), da * silu


def shared_kernel(
    x_ref, dy_ref, wg_ref, wu_ref, wo_ref, res_ref, dx_ref, mid_ref, dwo_ref, res_acc, dx_acc
):
    c = pl.program_id(0)

    @pl.when(c == 0)
    def _():
        res_acc[...] = jnp.zeros_like(res_acc)
        dx_acc[...] = jnp.zeros_like(dx_acc)

    x, dy = x_ref[...], dy_ref[...]
    wg, wu, wo = wg_ref[...], wu_ref[...], wo_ref[...]
    act, dg, du = gated(dot(x, wg), dot(x, wu), dot_nt(dy, wo))
    act, dg, du = act.astype(BF16), dg.astype(BF16), du.astype(BF16)
    res_acc[...] += dot(act, wo)
    dx_acc[...] += dot_nt(dg, wg) + dot_nt(du, wu)
    mid_ref[0] = dg
    mid_ref[1] = du
    dwo_ref[...] = dot_tn(act, dy).astype(BF16)

    @pl.when(c == pl.num_programs(0) - 1)
    def _():
        res_ref[...] = res_acc[...]
        dx_ref[...] = dx_acc[...]


def shared_grad_kernel(x_ref, mid_ref, out_ref, xt):
    @pl.when((pl.program_id(0) == 0) & (pl.program_id(1) == 0))
    def _():
        xt[...] = x_ref[...].T

    out_ref[...] = dot(xt[...], mid_ref[0]).astype(BF16)


def expert_kernel(
    x_ref, dy_ref, wg_ref, wu_ref, wt_ref, dx_ref, res_ref, mid_ref, dx_acc, res_acc, dgate
):
    c = pl.program_id(0)

    @pl.when(c == 0)
    def _():
        res_acc[...] = jnp.zeros_like(res_acc)
        dx_acc[...] = jnp.zeros_like(dx_acc)
        dgate[...] = jnp.zeros_like(dgate)

    x, dy = x_ref[:, 0:D], dy_ref[...]
    gate = jnp.sum(x_ref[:, D:].astype(F32), axis=-1, keepdims=True)
    wg, wu, wt = wg_ref[...], wu_ref[...], wt_ref[...]
    da = dot(dy, wt)
    act, dg, du = gated(dot(x, wg), dot(x, wu), da * gate)
    dgate[...] += jnp.sum(act * da, axis=-1, keepdims=True)
    mid_ref[2] = (act * gate).astype(BF16)
    act, dg, du = act.astype(BF16), dg.astype(BF16), du.astype(BF16)
    res_acc[...] += dot_nt(act, wt)
    dx_acc[...] += dot_nt(dg, wg) + dot_nt(du, wu)
    mid_ref[0] = dg
    mid_ref[1] = du

    @pl.when(c == pl.num_programs(0) - 1)
    def _():
        res_ref[...] = res_acc[...].astype(BF16)
        dx_ref[:, 0:D] = dx_acc[...].astype(BF16)
        dx_ref[:, D:] = part_lanes(dgate[:, 0:1], lanes_of(dgate.shape[0]))


def expert_grad_kernel(x_ref, dy_ref, mid_ref, out_ref, xt, dyt):
    @pl.when((pl.program_id(0) == 0) & (pl.program_id(1) == 0))
    def _():
        xt[...] = x_ref[...].T
        dyt[...] = dy_ref[...].T

    @pl.when(pl.program_id(0) < 2)
    def _():
        out_ref[...] = dot(xt[...], mid_ref[0]).astype(BF16)

    @pl.when(pl.program_id(0) == 2)
    def _():
        out_ref[...] = dot(dyt[...], mid_ref[0]).astype(BF16)


def combine_kernel(
    heads,
    experts,
    came_ref,
    dx_ref,
    residual_ref,
    dout_ref,
    gates_ref,
    routes_ref,
    target_ref,
    tail_ref,
    w_ref,
    send_ref,
    dres_ref,
    branch_ref,
    dlogits_ref,
    dgain_ref,
):
    pick = picks(target_ref, came_ref.shape[0])
    gates = [gates_ref[:, k : k + 1] for k in range(2)]
    parts = came_ref[:, D:]
    dgate = [jnp.sum(dot(pick[k], parts), axis=-1, keepdims=True) for k in range(2)]
    mean = gates[0] * dgate[0] + gates[1] * dgate[1]
    lane = lanes_of(pick[0].shape[0])
    dlogits = sum(
        jnp.where(lane == routes_ref[:, k : k + 1], gates[k] * (dgate[k] - mean), 0.0)
        for k in range(2)
    ).astype(BF16)
    dlogits_ref[...] = dlogits
    tail = tail_ref[...]
    dffn = dot(pick[0] + pick[1], came_ref[:, 0:D]) + dx_ref[...] + dot(dlogits, tail.astype(BF16))
    residual = residual_ref[...]
    inv = lax.rsqrt(jnp.mean(residual * residual, axis=-1, keepdims=True) + norm_eps)
    scaled = dffn * tail[experts + 1 : experts + 2, :]
    total = jnp.mean(scaled * residual, axis=-1, keepdims=True)
    dres = dout_ref[...].astype(F32) + inv * scaled - residual * inv * inv * inv * total
    dres_ref[...] = dres
    dgain_ref[...] = jnp.sum(dffn * residual * inv, axis=0, keepdims=True)
    branch = dres.astype(BF16)
    branch_ref[...] = branch
    for d, head in enumerate(heads):
        send_ref[d] = dot_nt(branch, w_ref[64 * head : 64 * head + LANES, :]).astype(BF16)


def dense_grad_kernel(heads, came_ref, branch_ref, in_ref, dlogits_ref, kept_ref, out_ref, router_ref, acc):
    acc[...] = jnp.zeros_like(acc)
    branch = branch_ref[...]
    for d, head in enumerate(heads):
        acc[64 * head : 64 * head + LANES, :] += dot_tn(came_ref[d], branch)
    out_ref[...] = acc[...].astype(BF16)
    router_ref[...] = dot_tn(in_ref[...], dlogits_ref[...])


def last_kernel(
    heads,
    experts,
    recv_ref,
    cos_ref,
    sin_ref,
    in_ref,
    x_ref,
    w_ref,
    tail_ref,
    dres_ref,
    router_ref,
    dgain_ref,
    out_ref,
    pack_ref,
    dproj,
):
    lane = lanes_of(x_ref.shape[0])
    cos, sin = cos_ref[...], sin_ref[...]
    for part in range(3):
        groups = [jnp.zeros(lane.shape, F32) for _ in range(D // LANES)]
        for d, head in enumerate(heads):
            g = head // 2
            packet = recv_ref[d, :, part * LANES : (part + 1) * LANES].astype(F32)
            if head % 2 == 0:
                groups[g] = groups[g] + packet
            else:
                packet = pltpu.roll(packet, 64, 1)
                groups[g] = groups[g] + jnp.where(lane >= 64, packet, 0.0)
                groups[g + 1] = groups[g + 1] + jnp.where(lane < 64, packet, 0.0)
        for g, t in enumerate(groups):
            if part < 2:
                t = t.astype(BF16).astype(F32)
                t = t * cos - partner(t, lane) * sin
            dproj[:, part * D + g * LANES : part * D + (g + 1) * LANES] = t.astype(BF16)
    dnorm = dot_nt(dproj[...], w_ref[:, 0 : 3 * D])
    x = x_ref[...].astype(F32)
    gain = tail_ref[experts : experts + 1, :]
    inv = lax.rsqrt(jnp.mean(x * x, axis=-1, keepdims=True) + norm_eps)
    scaled = dnorm * gain
    total = jnp.mean(scaled * x, axis=-1, keepdims=True)
    out_ref[...] = dres_ref[...] + inv * scaled - x * inv * inv * inv * total
    dgain_one = jnp.sum(dnorm * x * inv, axis=0, keepdims=True)
    row = lax.broadcasted_iota(jnp.int32, (LANES, D), 0)
    gains = jnp.where(row == experts, dgain_one, jnp.where(row == experts + 1, dgain_ref[...], 0.0))
    pack_ref[:, 3 * D :] = (router_ref[...] + gains.T).astype(BF16)
    turned = in_ref[...].T
    for part in range(3):
        pack_ref[:, part * D : (part + 1) * D] = dot(
            turned, dproj[:, part * D : (part + 1) * D]
        ).astype(BF16)


def output_kernel(residual_ref, shared_ref, gates_ref, target_ref, live_ref, came_ref, out_ref):
    pick = picks(target_ref, came_ref.shape[0])
    came = came_ref[...]
    mixture = gates_ref[:, 0:1] * dot(pick[0], came) + gates_ref[:, 1:2] * dot(pick[1], came)
    out_ref[...] = (live_ref[...] * (residual_ref[...] + shared_ref[...] + mixture)).astype(BF16)


def on_device(
    tokens,
    cotangent,
    lengths,
    position_block,
    routes,
    gain_attn,
    w_qkv,
    w_out,
    gain_ffn,
    w_router,
    w_shared_in,
    w_shared_out,
    w_expert_in,
    w_expert_out,
):
    n_ctx = lax.axis_size("ctx")
    ctx_index = lax.axis_index("ctx")
    rows = tokens.shape[1]
    local = w_qkv.shape[0]
    experts = w_router.shape[1]
    capacity = 3 * rows // experts
    places = experts * capacity
    share = HEADS * rows // n_ctx
    heads = first_heads(n_ctx, rows)
    gather = functools.partial(lax.all_gather, axis_name="fsdp", axis=0, tiled=True)
    exchange = functools.partial(
        lax.all_to_all, axis_name="ctx", split_axis=0, concat_axis=0, tiled=True
    )
    x = tokens[0]
    length = lengths[0]

    first_pack = jnp.concatenate(
        [
            w_qkv,
            w_router,
            gain_attn[:, None],
            gain_ffn[:, None],
            jnp.zeros((local, LANES - experts - 2), BF16),
        ],
        axis=1,
    )
    qkv_pack = gather(first_pack)
    mid_pack = gather(jnp.concatenate([w_out, w_shared_in], axis=1))
    shared_out = gather(w_shared_out)
    expert_pack = gather(jnp.concatenate([w_expert_in[0], w_expert_out[0].T], axis=1))

    query_pos = position_block[ctx_index] * rows + jnp.arange(rows, dtype=jnp.int32)
    live = (query_pos < length).astype(F32)[:, None]
    halves = HEAD_DIM // 2
    inverse = 10000.0 ** (-(jnp.arange(halves, dtype=F32) * 2.0 / HEAD_DIM))
    angles = query_pos.astype(F32)[:, None] * inverse[None, :]
    cos, sin = jnp.cos(angles), jnp.sin(angles)
    cos = jnp.concatenate([cos, cos, cos, cos], axis=1)
    sin = jnp.concatenate([-sin, sin, -sin, sin], axis=1)

    order = jnp.sum(
        jnp.where(
            position_block[None, :] == jnp.arange(n_ctx, dtype=jnp.int32)[:, None],
            jnp.arange(n_ctx, dtype=jnp.int32)[None, :],
            0,
        ),
        axis=1,
    )
    head_of = jnp.minimum(share * ctx_index // rows, HEADS - 2)
    offset = share * ctx_index - rows * head_of
    scalars = jnp.concatenate(
        [order, jnp.stack([offset.astype(jnp.int32), length.astype(jnp.int32)])]
    )

    pairs = routes[0].reshape(2 * rows)
    hot = (pairs[:, None] == jnp.arange(experts, dtype=jnp.int32)[None, :]).astype(jnp.int32)
    earlier = jnp.cumsum(hot, axis=0) - hot
    target = (pairs * capacity + jnp.sum(earlier * hot, axis=-1)).reshape(rows, 2)
    dout = (cotangent[0].astype(F32) * live).astype(BF16)
    place = jnp.arange(places, dtype=jnp.int32)
    token_pick = (
        (target[:, 0:1] == place[None, :]) | (target[:, 1:2] == place[None, :])
    ).astype(BF16)
    dy_rows = exchange(dot_tn(token_pick, dout).astype(BF16).reshape(n_ctx, -1, D))
    dy_rows = dy_rows.reshape(places, D)

    send, attn_in, tail = call(
        functools.partial(qkv_kernel, heads, experts),
        (
            shape((n_ctx, rows, 3 * LANES), BF16),
            shape((rows, D), BF16),
            shape((LANES, D), F32),
        ),
        flops=2 * rows * D * 3 * D,
        nbytes=6 << 20,
    )(x, qkv_pack, cos, sin)
    recv = exchange(send)

    packet = pl.BlockSpec((n_ctx, rows, 3 * LANES), lambda i, sc: (0, 0, 0))
    block_of = lambda i, sc: (i, 0, 0)
    attended, kept, lse = call(
        functools.partial(attend_kernel, n_ctx, share),
        (
            shape((n_ctx, rows, LANES), BF16),
            shape((n_ctx, LANES, share), F32),
            shape((n_ctx, 1, share), F32),
        ),
        flops=2 * share * rows * n_ctx * n_ctx * LANES * 2,
        nbytes=5 << 20,
        grid_spec=pltpu.PrefetchScalarGridSpec(
            num_scalar_prefetch=1,
            grid=(n_ctx,),
            in_specs=[packet],
            out_specs=[
                pl.BlockSpec((1, rows, LANES), lambda i, sc: (sc[i], 0, 0)),
                pl.BlockSpec((1, LANES, share), block_of),
                pl.BlockSpec((1, 1, share), block_of),
            ],
            scratch_shapes=[
                pltpu.VMEM((2 * rows, LANES), BF16),
                pltpu.VMEM((n_ctx, rows, share), F32),
                pltpu.VMEM((2 * rows, LANES), F32),
            ],
        ),
    )(scalars, recv)
    came = exchange(attended)

    whole = pl.BlockSpec(memory_space=pltpu.VMEM)
    out_block = pl.BlockSpec((D, D), lambda i: (0, 0))

    def full(*dims):
        return pl.BlockSpec(dims, lambda i: (0,) * len(dims))

    residual, ffn_in, gates, outgoing = call(
        functools.partial(middle_kernel, heads, experts),
        (
            shape((rows, D), F32),
            shape((rows, D), BF16),
            shape((rows, LANES), F32),
            shape((places, D + LANES), BF16),
        ),
        flops=2 * rows * D * (D + 1024 + 2 * places),
        nbytes=5 << 20,
        grid=(1,),
        in_specs=[
            full(n_ctx, rows, LANES),
            out_block,
            full(rows, D),
            full(LANES, D),
            full(rows, 2),
            full(rows, 2),
        ],
        out_specs=[
            full(rows, D),
            full(rows, D),
            full(rows, LANES),
            full(places, D + LANES),
        ],
    )(came, mid_pack, x, tail, routes[0], target)
    x_rows = exchange(outgoing.reshape(n_ctx, -1, D + LANES)).reshape(places, D + LANES)

    lead = D // CHUNK
    steps = FS // CHUNK
    shared_res, shared_dx, shared_mid, grad_so = call(
        shared_kernel,
        (
            shape((rows, D), F32),
            shape((rows, D), F32),
            shape((2, rows, FS), BF16),
            shape((FS, D), BF16),
        ),
        flops=2 * rows * D * FS * 7,
        nbytes=14 << 20,
        grid=(steps,),
        in_specs=[
            full(rows, D),
            full(rows, D),
            pl.BlockSpec((D, CHUNK), lambda c: (0, lead + c)),
            pl.BlockSpec((D, CHUNK), lambda c: (0, lead + steps + c)),
            pl.BlockSpec((CHUNK, D), lambda c: (c, 0)),
        ],
        out_specs=[
            full(rows, D),
            full(rows, D),
            pl.BlockSpec((2, rows, CHUNK), lambda c: (0, 0, c)),
            pl.BlockSpec((CHUNK, D), lambda c: (c, 0)),
        ],
        scratch_shapes=[pltpu.VMEM((rows, D), F32), pltpu.VMEM((rows, D), F32)],
    )(ffn_in, dout, mid_pack, mid_pack, shared_out)
    dense_pack = call(
        shared_grad_kernel,
        shape((D, D + 2 * FS), BF16),
        flops=2 * rows * D * FS * 2,
        nbytes=9 << 20,
        grid=(2, steps),
        in_specs=[
            pl.BlockSpec((rows, D), lambda i, c: (0, 0)),
            pl.BlockSpec((1, rows, CHUNK), lambda i, c: (i, 0, c)),
        ],
        out_specs=pl.BlockSpec((D, CHUNK), lambda i, c: (0, lead + i * steps + c)),
        scratch_shapes=[pltpu.VMEM((D, rows), BF16)],
    )(ffn_in, shared_mid)

    wide = FF // CHUNK
    expert_dx, expert_res, expert_mid = call(
        expert_kernel,
        (
            shape((places, D + LANES), BF16),
            shape((places, D), BF16),
            shape((3, places, FF), BF16),
        ),
        flops=2 * places * D * FF * 6,
        nbytes=24 << 20,
        grid=(wide,),
        in_specs=[
            full(places, D + LANES),
            full(places, D),
            pl.BlockSpec((D, CHUNK), lambda c: (0, c)),
            pl.BlockSpec((D, CHUNK), lambda c: (0, wide + c)),
            pl.BlockSpec((D, CHUNK), lambda c: (0, 2 * wide + c)),
        ],
        out_specs=[
            full(places, D + LANES),
            full(places, D),
            pl.BlockSpec((3, places, CHUNK), lambda c: (0, 0, c)),
        ],
        scratch_shapes=[
            pltpu.VMEM((places, D), F32),
            pltpu.VMEM((places, D), F32),
            pltpu.VMEM((places, LANES), F32),
        ],
    )(x_rows, dy_rows, expert_pack, expert_pack, expert_pack)
    dx_came = exchange(expert_dx.reshape(n_ctx, -1, D + LANES)).reshape(places, D + LANES)
    expert_grad = call(
        expert_grad_kernel,
        shape((D, 3 * FF), BF16),
        flops=2 * places * D * FF * 3,
        nbytes=21 << 20,
        grid=(3, wide),
        in_specs=[
            pl.BlockSpec((places, D), lambda i, c: (0, 0)),
            pl.BlockSpec((places, D), lambda i, c: (0, 0)),
            pl.BlockSpec((1, places, CHUNK), lambda i, c: (i, 0, c)),
        ],
        out_specs=pl.BlockSpec((D, CHUNK), lambda i, c: (0, i * wide + c)),
        scratch_shapes=[pltpu.VMEM((D, places), BF16), pltpu.VMEM((D, places), BF16)],
    )(x_rows, dy_rows, expert_mid)

    branch_send, dres, branch, dlogits, dgain_two = call(
        functools.partial(combine_kernel, heads, experts),
        (
            shape((n_ctx, rows, LANES), BF16),
            shape((rows, D), F32),
            shape((rows, D), BF16),
            shape((rows, LANES), BF16),
            shape((1, D), F32),
        ),
        flops=2 * rows * D * (places + 1024),
        nbytes=6 << 20,
        grid=(1,),
        in_specs=[
            full(places, D + LANES),
            full(rows, D),
            full(rows, D),
            full(rows, D),
            full(rows, LANES),
            full(rows, 2),
            full(rows, 2),
            full(LANES, D),
            out_block,
        ],
        out_specs=[
            full(n_ctx, rows, LANES),
            full(rows, D),
            full(rows, D),
            full(rows, LANES),
            full(1, D),
        ],
    )(dx_came, shared_dx, residual, dout, gates, routes[0], target, tail, mid_pack)
    branch_recv = exchange(branch_send)

    dense_pack, grad_router = call(
        functools.partial(dense_grad_kernel, heads),
        (shape((D, D + 2 * FS), BF16), shape((D, LANES), F32)),
        flops=2 * rows * D * (1024 + LANES),
        nbytes=4 << 20,
        grid=(1,),
        in_specs=[
            full(n_ctx, rows, LANES),
            full(rows, D),
            full(rows, D),
            full(rows, LANES),
            pl.BlockSpec(memory_space=pl.ANY),
        ],
        out_specs=[out_block, full(D, LANES)],
        scratch_shapes=[pltpu.VMEM((D, D), F32)],
        input_output_aliases={4: 0},
    )(came, branch, ffn_in, dlogits, dense_pack)

    dsend = call(
        functools.partial(attend_back_kernel, n_ctx, share),
        shape((n_ctx, rows, 3 * LANES), BF16),
        flops=2 * share * rows * n_ctx * n_ctx * LANES * 3,
        nbytes=8 << 20,
        grid_spec=pltpu.PrefetchScalarGridSpec(
            num_scalar_prefetch=1,
            grid=(n_ctx,),
            in_specs=[
                packet,
                pl.BlockSpec((n_ctx, rows, LANES), lambda i, sc: (0, 0, 0)),
                pl.BlockSpec((1, LANES, share), block_of),
                pl.BlockSpec((1, 1, share), block_of),
            ],
            out_specs=packet,
            scratch_shapes=[
                pltpu.VMEM((2 * rows, LANES), BF16),
                pltpu.VMEM((2 * rows, LANES), BF16),
                pltpu.VMEM((n_ctx, rows, LANES), F32),
                pltpu.VMEM((n_ctx, rows, LANES), F32),
                pltpu.VMEM((2 * rows, LANES), F32),
            ],
        ),
    )(scalars, recv, branch_recv, kept, lse)
    drecv = exchange(dsend)

    grad_x, last_pack = call(
        functools.partial(last_kernel, heads, experts),
        (shape((rows, D), F32), shape((D, PACKED), BF16)),
        flops=2 * rows * D * 3 * D * 2,
        nbytes=14 << 20,
        in_specs=[whole] * 10,
        out_specs=[whole, whole],
        scratch_shapes=[pltpu.VMEM((rows, 3 * D), BF16)],
    )(drecv, cos, sin, attn_in, x, qkv_pack, tail, dres, grad_router, dgain_two)

    res_came = exchange(expert_res.reshape(n_ctx, -1, D)).reshape(places, D)
    output = call(
        output_kernel,
        shape((rows, D), BF16),
        flops=2 * rows * D * places * 2,
        nbytes=5 << 20,
    )(residual, shared_res, gates, target, live, res_came)

    scatter = functools.partial(
        lax.psum_scatter, axis_name="fsdp", scatter_dimension=0, tiled=True
    )
    expert_sum = scatter(expert_grad)
    dense_part, so_part = scatter(dense_pack), scatter(grad_so)
    dense_sum, so_sum = lax.psum((dense_part, so_part), "ctx")
    last_sum = lax.psum(scatter(last_pack), "ctx")
    last_sum = last_sum.astype(F32)
    dense_sum = dense_sum.astype(F32)
    expert_sum = expert_sum.astype(F32)
    small = last_sum[:, 3 * D :]
    return (
        output[None],
        grad_x[None],
        small[:, experts],
        last_sum[:, 0 : 3 * D],
        dense_sum[:, 0:D],
        small[:, experts + 1],
        small[:, 0:experts],
        dense_sum[:, D:],
        so_sum.astype(F32),
        expert_sum[None, :, 0 : 2 * FF],
        expert_sum[:, 2 * FF :].T[None],
    )


def solution(mesh):
    row_spec = P("fsdp", "ctx", None)
    flat = P("fsdp", None)
    return jax.shard_map(
        on_device,
        mesh=mesh,
        in_specs=(
            row_spec,
            row_spec,
            P("fsdp"),
            P(),
            row_spec,
            P("fsdp"),
            flat,
            flat,
            P("fsdp"),
            flat,
            flat,
            flat,
            P("ctx", "fsdp", None),
            P("ctx", None, "fsdp"),
        ),
        out_specs=(
            row_spec,
            row_spec,
            P("fsdp"),
            flat,
            flat,
            P("fsdp"),
            flat,
            flat,
            flat,
            P("ctx", "fsdp", None),
            P("ctx", None, "fsdp"),
        ),
        check_vma=False,
    )
```

time: 1040 us -> 715 us (0.69); the launches traced: 1030 us -> 717 us
  waiting for transfers between devices: 611 us -> 437 us
  matrix products: 170 us -> 1.87 us
  Pallas kernels: 0 us -> 147 us
  local copies, waits for them, and re-layouts: 96.4 us -> 24 us
  other arithmetic: 74.8 us -> 10.9 us
  blocking collectives: 42.6 us -> 56.1 us
    dot_general x53 -> x1, matrix products: 170 us -> 1.87 us  [dot_tn(): lax.dot_general(a, b, (((0,), (0,)), ((), ())), preferred_element_type=F32)]
    pallas_call x0 -> x12, Pallas kernels: none -> 147 us  [the longest x1 24.3 us: on_device(): call(functools.partial(attend_back_kernel, n_ctx, share), shape((n_ctx, r...]
    reduce_scatter x6 -> x4, waiting for transfers between devices: 275 us -> 157 us  [the longest x1 76.1 us: on_device(): expert_sum = scatter(expert_grad)]
    all_gather x7 -> x4, waiting for transfers between devices: 111 us -> 26.9 us  [the longest x1 26.8 us: on_device(): qkv_pack = gather(first_pack)]
    unnamed x18 -> x9, waiting for transfers between devices: 61.6 us -> 1.33 us
    all_to_all x0 -> x2, blocking collectives: none -> 56.1 us  [the longest x1 37.3 us: on_device(): exchange(outgoing.reshape(n_ctx, -1, D + LANES)).reshape(places, D + LANES)]
    all_to_all x4 -> x6, waiting for transfers between devices: 55.1 us -> 110 us  [the longest x1 33.9 us: on_device(): recv = exchange(send)]
    unnamed x172 -> x39, local copies, waits for them, and re-layouts: 52.9 us -> 8.33 us
  transfers between devices with their start and end apart: 20 -> 15, of which waited for: 14 -> 10; matrix products, arithmetic and copies ran while one was open for 22% -> 2% of each run, Pallas kernels for 0% -> 21%
where the time goes in v1:
time: 715 us; the launch traced here: 717 us
  waiting for transfers between devices  437 us (61%)
  Pallas kernels  147 us (21%)
  blocking collectives  56.1 us (8%)
  starting transfers between devices  24.5 us (3%)
  local copies, waits for them, and re-layouts  24 us (3%)
  between operations  15.5 us (2%)
  other arithmetic  10.9 us (2%)
    psum x1, waiting for transfers between devices, on_device(): dense_sum, so_sum = lax.psum((dense_part, so_part), 'ctx')  141 us
    reduce_scatter x1, waiting for transfers between devices, on_device(): expert_sum = scatter(expert_grad)  76.1 us
    reduce_scatter x2, waiting for transfers between devices, on_device(): dense_part, so_part = (scatter(dense_pack), scatter(grad_so))  69 us
    all_to_all x1, blocking collectives, on_device(): exchange(outgoing.reshape(n_ctx, -1, D + LANES)).reshape(places, D + LANES)  37.3 us
    all_to_all x1, waiting for transfers between devices, on_device(): recv = exchange(send)  33.9 us
    all_gather x1, waiting for transfers between devices, on_device(): qkv_pack = gather(first_pack)  26.8 us
    pallas_call x1, Pallas kernels, on_device(): call(functools.partial(attend_back_kernel, n_ctx, share), shape((n_ctx, r...  24.3 us
    pallas_call x1, Pallas kernels, on_device(): call(expert_kernel, (shape((places, D + LANES), BF16), shape((places, D),...  23.4 us
  transfers between devices with their start and end apart: 15, of which 10 were waited for; matrix products, arithmetic and copies ran while one was open for 2% of the time, Pallas kernels for 21%

profile of v1, /device:TPU:0, one launch (start us, length us, event | category | flops | bytes accessed | tf_op | source)
XLA Modules:
  0.0 716.6 jit_solution(10515286101047541029)
XLA Ops:
  7.2 0.9 broadcast_in_dim.51
  8.1 0.7 broadcast_in_dim.52
  8.9 0.8 copy.43
  9.7 2.0 concatenate.19
  11.9 1.4 pad_maximum_fusion.1
  13.3 1.3 copy-done.10
  14.6 1.6 pad_maximum_fusion
  16.2 0.6 copy-done.17
  16.9 0.6 dynamic_slice.3
  18.1 0.5 fusion.6
  18.7 1.0 pad_maximum_fusion.2
  19.7 26.8 %all-gather.5.cloned.1.call-done.w_ref = bf16[768,2432]{1,0:T(8,128)(2,1)} async-done(((bf16[192,2432]{1,0:T(8,128)(2,1)}), bf16[768,2432]{1,0:T(8,128)(2,1)}) %all-gather.5.cloned.1.call-update) | async-done | bytes 3735568 | tf_op jit(solution)/shard_map/all_gather | solution.py:501
  46.5 5.0 shard_map.221
  51.5 5.7 all-to-all-start
  58.3 1.1 reduce-window.6
  59.4 0.2 slice_reduce_fusion.4
  60.0 0.6 pad_add_fusion.sc
  60.7 33.9 %all-to-all-done.recv_ref = bf16[8,256,384]{2,1,0:T(8,128)(2,1)S(1)} async-done(((bf16[8,256,384]{2,1,0:T(8,128)(2,1)}), bf16[8,256,384]{2,1,0:T(8,128)(2,1)S(1)}, u32[]{:S(2)}, u32[]{:S(2)}) %all-to-all-start) | async-done | bytes 1572896 | tf_op jit(solution)/shard_map/all_to_all | solution.py:551
  94.6 1.1 copy-done.9
  95.7 21.0 %shard_map.222 = (bf16[8,256,128]{2,1,0:T(8,128)(2,1)}, f32[8,128,384]{2,1,0:T(8,128)}, f32[8,1,384]{2,1,0:T(1,128)}) custom-call(s32[10]{0:T(128)} %pad_add_fusion.sc, bf16[8,256,384]{2,1,0:T(8,128)(2,1)} %copy-done.9), custom_call_target="tpu_custom_call" | custom-call | flops 3221225472 | bytes 5242880 | tf_op jit(solution)/shard_map/pallas_call | solution.py:555
  116.7 3.8 all-to-all-start.1
  120.5 0.2 slice_reduce_fusion.1
  120.8 1.9 convolution_convert_fusion
  122.7 12.9 %all-to-all-done.1.came_ref = bf16[8,256,128]{2,1,0:T(8,128)(2,1)S(1)} async-done(((bf16[8,256,128]{2,1,0:T(8,128)(2,1)}), bf16[8,256,128]{2,1,0:T(8,128)(2,1)S(1)}, u32[]{:S(2)}, u32[]{:S(2)}) %all-to-all-start.1) | async-done | bytes 524320 | tf_op jit(solution)/shard_map/all_to_all | solution.py:580
  135.6 3.6 all-to-all-start.3
  139.3 0.5 all-gather.9.cloned.1.call-update
  139.8 5.2 shard_map.223
  145.0 23.0 %all-to-all-done.3 = bf16[8,96,768]{2,1,0:T(8,128)(2,1)S(1)} async-done(((bf16[8,96,768]{2,1,0:T(8,128)(2,1)}), bf16[8,96,768]{2,1,0:T(8,128)(2,1)S(1)}, u32[]{:S(2)}, u32[]{:S(2)}) %all-to-all-start.3) | async-done | bytes 1179680 | tf_op jit(solution)/shard_map/all_to_all | solution.py:538
  168.0 37.3 %all_to_all.40 = bf16[8,96,896]{2,1,0:T(8,128)(2,1)} all-to-all(bf16[8,96,896]{2,1,0:T(8,128)(2,1)} %bitcast.51), channel_id=1, replica_groups=mesh['ctx'=8,'fsdp'=4] {'ctx'}, dimensions={0} | all-to-all | bytes 2752512 | tf_op jit(solution)/shard_map/all_to_all | solution.py:614
  205.4 23.4 %shard_map.225 = (bf16[768,896]{1,0:T(8,128)(2,1)}, bf16[768,768]{1,0:T(8,128)(2,1)}, bf16[3,768,2048]{2,1,0:T(8,128)(2,1)}) custom-call(bf16[768,896]{1,0:T(8,128)(2,1)} %bitcast.48, bf16[768,768]{1,0:T(8,128)(2,1)} %bitcast.52, bf16[768,6144]{1,0:T(8,128)(2,1)} %all-gather.11.cloned.1.call-done.wg_ref.wu_ref.wt_ref, ...), custom_call_target="tpu_custom_call" | custom-call | flops 14495514624 | bytes 25165824 | tf_op jit(solution)/shard_map/pallas_call | solution.py:659
  228.8 3.6 all-to-all-start.5
  232.4 0.2 reduce-scatter.9.cloned.1.call-start
  232.6 12.8 %shard_map.224 = (f32[256,768]{1,0:T(8,128)}, f32[256,768]{1,0:T(8,128)}, bf16[2,256,2048]{2,1,0:T(8,128)(2,1)}, bf16[2048,768]{1,0:T(8,128)(2,1)}) custom-call(bf16[256,768]{1,0:T(8,128)(2,1)} %get-tuple-element.41.x_ref.in_ref, bf16[256,768]{1,0:T(8,128)(2,1)} %copy-done.7, bf16[768,4864]{1,0:T(8,128)(2,1)} %all-gather.7.cloned.1.call-done.w_ref.wg_ref.wu_ref, ...), custom_call_target="tpu_custom_call" | custom-call | flops 5637144576 | bytes 14680064 | tf_op jit(solution)/shard_map/pallas_call | solution.py:618
  245.4 18.8 %all-to-all-done.5 = bf16[8,96,896]{2,1,0:T(8,128)(2,1)S(1)} async-done(((bf16[8,96,896]{2,1,0:T(8,128)(2,1)}), bf16[8,96,896]{2,1,0:T(8,128)(2,1)S(1)}, u32[]{:S(2)}, u32[]{:S(2)}) %all-to-all-start.5) | async-done | bytes 1376288 | tf_op jit(solution)/shard_map/all_to_all | solution.py:687
  264.2 1.1 copy-done.2
  265.3 5.9 shard_map.227
  271.2 18.7 %all_to_all.41.grad_ref = bf16[8,256,128]{2,1,0:T(8,128)(2,1)} all-to-all(bf16[8,256,128]{2,1,0:T(8,128)(2,1)} %get-tuple-element.48), channel_id=1, replica_groups=mesh['ctx'=8,'fsdp'=4] {'ctx'}, dimensions={0} | all-to-all | bytes 1048576 | tf_op jit(solution)/shard_map/all_to_all | solution.py:734
  289.9 24.3 %shard_map.228 = bf16[8,256,384]{2,1,0:T(8,128)(2,1)} custom-call(s32[10]{0:T(128)} %pad_add_fusion.sc, bf16[8,256,384]{2,1,0:T(8,128)(2,1)} %copy-done.9, bf16[8,256,128]{2,1,0:T(8,128)(2,1)} %all_to_all.41.grad_ref, f32[8,128,384]{2,1,0:T(8,128)} %get-tuple-element.49.keep_ref, f32[8,1,384]{2,1,0:T(1,128)} %get-tuple-element.50.lse_ref), custom_call_target="tpu_custom_call" | custom-call | flops 4831838208 | bytes 8388608 | tf_op jit(solution)/shard_map/pallas_call | solution.py:754
  314.2 3.6 all-to-all-start.7
  317.9 12.3 %shard_map.229.kept_ref = bf16[768,4864]{1,0:T(8,128)(2,1)} custom-call(bf16[256,768]{1,0:T(8,128)(2,1)} %get-tuple-element.41.x_ref.in_ref, bf16[2,256,2048]{2,1,0:T(8,128)(2,1)} %get-tuple-element.55.mid_ref), custom_call_target="tpu_custom_call" | custom-call | flops 1610612736 | bytes 9437184 | tf_op jit(solution)/shard_map/pallas_call | solution.py:644
  330.2 3.0 shard_map.230
  333.3 21.7 %all-to-all-done.7.recv_ref = bf16[8,256,384]{2,1,0:T(8,128)(2,1)S(1)} async-done(((bf16[8,256,384]{2,1,0:T(8,128)(2,1)}), bf16[8,256,384]{2,1,0:T(8,128)(2,1)S(1)}, u32[]{:S(2)}, u32[]{:S(2)}) %all-to-all-start.7) | async-done | bytes 1572896 | tf_op jit(solution)/shard_map/all_to_all | solution.py:778
  355.0 1.1 copy-done.1
  356.1 7.9 %shard_map.231 = (f32[256,768]{1,0:T(8,128)}, bf16[768,2432]{1,0:T(8,128)(2,1)}) custom-call(bf16[8,256,384]{2,1,0:T(8,128)(2,1)} %copy-done.1, f32[256,128]{1,0:T(8,128)} %get-tuple-element.117.cos_ref, f32[256,128]{1,0:T(8,128)} %get-tuple-element.118.sin_ref, bf16[256,768]{1,0:T(8,128)(2,1)} %get-tuple-element.51.in_ref, bf16[256,768]{1,0:T(8,128)(2,1)} %bitcast.46, ...), custom_call_target="tpu_custom_call" | custom-call | flops 1811939328 | bytes 14680064 | tf_op jit(solution)/shard_map/pallas_call | solution.py:780
  364.1 0.7 reduce-scatter.7.cloned.1.call-update
  364.8 23.0 %shard_map.232 = bf16[768,6144]{1,0:T(8,128)(2,1)} custom-call(bf16[768,896]{1,0:T(8,128)(2,1)} %bitcast.49, bf16[768,768]{1,0:T(8,128)(2,1)} %bitcast.53, bf16[3,768,2048]{2,1,0:T(8,128)(2,1)} %get-tuple-element.62.mid_ref), custom_call_target="tpu_custom_call" | custom-call | flops 7247757312 | bytes 22020096 | tf_op jit(solution)/shard_map/pallas_call | solution.py:688
  387.9 3.7 all-to-all-start.4
  391.7 12.3 %reduce-scatter.5.cloned.1.call-done = bf16[192,2432]{1,0:T(8,128)(2,1)} async-done(((bf16[768,2432]{1,0:T(8,128)(2,1)}), bf16[192,2432]{1,0:T(8,128)(2,1)}) %reduce-scatter.5.cloned.1.call-update) | async-done | bytes 933904 | tf_op jit(solution)/shard_map/reduce_scatter | solution.py:804
  404.0 68.9 %reduce-scatter.7.cloned.1.call-done = bf16[192,4864]{1,0:T(8,128)(2,1)} async-done(((bf16[768,4864]{1,0:T(8,128)(2,1)}), bf16[192,4864]{1,0:T(8,128)(2,1)}) %reduce-scatter.7.cloned.1.call-update) | async-done | bytes 1867792 | tf_op jit(solution)/shard_map/reduce_scatter | solution.py:802
  473.0 0.7 fusion.5.live_ref
  473.7 1.0 copy-done.6
  474.7 3.5 shard_map.226
  478.2 76.1 %reduce-scatter.11.cloned.1.call-done = bf16[192,6144]{1,0:T(8,128)(2,1)} async-done(((bf16[768,6144]{1,0:T(8,128)(2,1)}), bf16[192,6144]{1,0:T(8,128)(2,1)}) %reduce-scatter.11.cloned.1.call-update) | async-done | bytes 2359312 | tf_op jit(solution)/shard_map/reduce_scatter | solution.py:801
  554.2 2.2 convert_element_type.64
  556.4 1.3 slice_bitcast_fusion.1
  557.7 1.9 slice_bitcast_fusion
  559.5 140.7 %all-reduce.3.cloned.1.call-done = (bf16[192,4864]{1,0:T(8,128)(2,1)}, bf16[192,2432]{1,0:T(8,128)(2,1)}, bf16[512,768]{1,0:T(8,128)(2,1)}) async-done(((bf16[192,4864]{1,0:T(8,128)(2,1)}, bf16[192,2432]{1,0:T(8,128)(2,1)}, bf16[512,768]{1,0:T(8,128)(2,1)}), (bf16[192,4864]{1,0:T(8,128)(2,1)}, bf16[192,2432]{1,0:T(8,128)(2,1)}, bf16[512,768]{1,0:T(8,128)(2,1)})) %all-reduce.3.cloned.1.call-update) | async-done | bytes 3588112 | tf_op jit(solution)/shard_map/psum | solution.py:803
  700.2 1.8 slice.57
  702.1 3.5 slice.60
  705.6 1.3 slice.56
  707.0 0.7 copy.51
  707.7 0.3 copy-done.13
  708.0 1.3 convert_element_type.63
  709.3 0.8 slice_reduce_fusion.2
  (66 shorter events, 1.7 us)
Async XLA Ops:
  7.2 4.7 copy-start.8
  7.2 4.7 copy-start.15
  7.2 39.3 %all-gather.5.cloned.1.call-start = ((), (), s32[]{:S(2)}) async-start(), calls=%async_computation.12 | async-start | bytes 4669440 | tf_op jit(solution)/shard_map/all_gather | solution.py:501
  11.8 128.0 %all-gather.7.cloned.1.call-start = ((), (), s32[]{:S(2)}) async-start(), calls=%async_computation.13 | async-start | bytes 9338880 | tf_op jit(solution)/shard_map/all_gather | solution.py:502
  11.9 1.5 copy-start.12
  13.2 1.4 copy-start.10
  13.3 192.1 %all-gather.11.cloned.1.call-start = ((), (), s32[]{:S(2)}) async-start(), calls=%async_computation.15 | async-start | bytes 11796480 | tf_op jit(solution)/shard_map/all_gather | solution.py:504
  16.2 0.7 copy-start.17
  51.5 5.7 copy-start.16
  51.5 43.1 %all-to-all-start = ((bf16[8,256,384]{2,1,0:T(8,128)(2,1)}), bf16[8,256,384]{2,1,0:T(8,128)(2,1)S(1)}, u32[]{:S(2)}, u32[]{:S(2)}) async-start(bf16[8,256,384]{2,1,0:T(8,128)(2,1)} %get-tuple-element.37), calls=%async_computation | async-start | bytes 3145728 | tf_op jit(solution)/shard_map/all_to_all | solution.py:551
  57.3 63.1 %copy-start.4 = (s32[1,256,2]{2,1,0:T(8,128)}, s32[1,256,2]{2,1,0:T(8,128)S(1)}, u32[]{:S(2)}) copy-start(s32[1,256,2]{2,1,0:T(8,128)S(1)} %copy.47) | copy-start | bytes 6148
  94.6 1.1 copy-start.9
  116.7 4.0 copy-start.14
  116.7 18.9 %all-to-all-start.1 = ((bf16[8,256,128]{2,1,0:T(8,128)(2,1)}), bf16[8,256,128]{2,1,0:T(8,128)(2,1)S(1)}, u32[]{:S(2)}, u32[]{:S(2)}) async-start(bf16[8,256,128]{2,1,0:T(8,128)(2,1)} %get-tuple-element.38), calls=%async_computation.1 | async-start | bytes 1048576 | tf_op jit(solution)/shard_map/all_to_all | solution.py:580
  120.5 15.1 %copy-start.3 = (s32[256,2]{1,0:T(8,128)}, s32[256,2]{1,0:T(8,128)S(1)}, u32[]{:S(2)}) copy-start(s32[256,2]{1,0:T(8,128)S(1)} %multiply_add_fusion.target_ref) | copy-start | bytes 6148
  120.8 14.7 %copy-start.7 = (bf16[256,768]{1,0:T(8,128)(2,1)}, bf16[256,768]{1,0:T(8,128)(2,1)S(1)}, u32[]{:S(2)}) copy-start(bf16[256,768]{1,0:T(8,128)(2,1)S(1)} %fusion.dy_ref.dout_ref) | copy-start | bytes 1179652
  135.6 4.3 copy-start.5
  135.6 32.4 %all-to-all-start.3 = ((bf16[8,96,768]{2,1,0:T(8,128)(2,1)}), bf16[8,96,768]{2,1,0:T(8,128)(2,1)S(1)}, u32[]{:S(2)}, u32[]{:S(2)}) async-start(bf16[8,96,768]{2,1,0:T(8,128)(2,1)} %bitcast.54), calls=%async_computation.3 | async-start | bytes 2359296 | tf_op jit(solution)/shard_map/all_to_all | solution.py:538
  139.2 93.4 %all-gather.9.cloned.1.call-start = ((), (), s32[]{:S(2)}) async-start(), calls=%async_computation.14 | async-start | bytes 3932160 | tf_op jit(solution)/shard_map/all_gather | solution.py:503
  168.0 37.4 %copy-start.11 = (bf16[8,96,768]{2,1,0:T(8,128)(2,1)}, bf16[8,96,768]{2,1,0:T(8,128)(2,1)S(1)}, u32[]{:S(2)}) copy-start(bf16[8,96,768]{2,1,0:T(8,128)(2,1)S(1)} %all-to-all-done.3) | copy-start | bytes 3538948
  228.8 35.4 %all-to-all-start.5 = ((bf16[8,96,896]{2,1,0:T(8,128)(2,1)}), bf16[8,96,896]{2,1,0:T(8,128)(2,1)S(1)}, u32[]{:S(2)}, u32[]{:S(2)}) async-start(bf16[8,96,896]{2,1,0:T(8,128)(2,1)} %bitcast.50), calls=%async_computation.5 | async-start | bytes 2752512 | tf_op jit(solution)/shard_map/all_to_all | solution.py:687
  232.4 159.3 %reduce-scatter.9.cloned.1.call-start = ((), (), s32[]{:S(2)}) async-start(), calls=%async_computation.18 | async-start | bytes 3932160 | tf_op jit(solution)/shard_map/reduce_scatter | solution.py:802
  264.2 1.1 copy-start.2
  314.2 40.8 %all-to-all-start.7 = ((bf16[8,256,384]{2,1,0:T(8,128)(2,1)}), bf16[8,256,384]{2,1,0:T(8,128)(2,1)S(1)}, u32[]{:S(2)}, u32[]{:S(2)}) async-start(bf16[8,256,384]{2,1,0:T(8,128)(2,1)} %shard_map.228), calls=%async_computation.7 | async-start | bytes 3145728 | tf_op jit(solution)/shard_map/all_to_all | solution.py:778
  317.8 86.2 %reduce-scatter.5.cloned.1.call-start = ((), (), s32[]{:S(2)}) async-start(), calls=%async_computation.16 | async-start | bytes 4669440 | tf_op jit(solution)/shard_map/reduce_scatter | solution.py:804
  355.0 1.1 copy-start.1
  364.0 108.9 %reduce-scatter.7.cloned.1.call-start = ((), (), s32[]{:S(2)}) async-start(), calls=%async_computation.17 | async-start | bytes 9338880 | tf_op jit(solution)/shard_map/reduce_scatter | solution.py:802
  364.8 189.4 %reduce-scatter.11.cloned.1.call-start = ((), (), s32[]{:S(2)}) async-start(), calls=%async_computation.19 | async-start | bytes 11796480 | tf_op jit(solution)/shard_map/reduce_scatter | solution.py:801
  387.9 85.8 %all-to-all-start.4 = ((bf16[8,96,768]{2,1,0:T(8,128)(2,1)}), bf16[8,96,768]{2,1,0:T(8,128)(2,1)S(1)}, u32[]{:S(2)}, u32[]{:S(2)}) async-start(bf16[8,96,768]{2,1,0:T(8,128)(2,1)} %bitcast.15), calls=%async_computation.4 | async-start | bytes 2359296 | tf_op jit(solution)/shard_map/all_to_all | solution.py:790
  391.6 308.6 %all-reduce.3.cloned.1.call-start = ((), (), s32[]{:S(2)}) async-start(), calls=%async_computation.20 | async-start | bytes 7176192 | tf_op jit(solution)/shard_map/psum | solution.py:803
  473.7 1.0 copy-start.6
  702.1 3.5 copy-start
  706.9 1.1 copy-start.13
Sparse Core Ops, SparseCore 0:
  11.9 34.5 all-gather.4
  48.6 53.0 all-gather.6
  103.9 64.2 all-gather.10
  169.6 28.5 all-gather.8
  245.6 38.1 reduce-scatter.8
  364.2 39.8 reduce-scatter.4
  406.6 66.3 reduce-scatter.6
  475.7 78.4 reduce-scatter.10
  558.6 141.6 all-reduce.2

commit v2 on v1

--- a/solution.py
+++ b/solution.py
@@ -83,6 +83,28 @@
     return tuple(
         jnp.where(place == target_ref[:, k : k + 1], 1.0, 0.0).astype(BF16) for k in range(2)
     )
+
+
+def start_kernel(experts, capacity, routes_ref, cot_ref, live_ref, target_ref, dout_ref, send_ref):
+    rows = routes_ref.shape[0]
+    lane = lanes_of(rows)
+    hot = [jnp.where(lane == routes_ref[:, k : k + 1], 1.0, 0.0) for k in range(2)]
+    below = jnp.where(
+        lanes_of(rows, rows) < lax.broadcasted_iota(jnp.int32, (rows, rows), 0), 1.0, 0.0
+    )
+    earlier = dot(below.astype(BF16), (hot[0] + hot[1]).astype(BF16))
+    place = [
+        routes_ref[:, k : k + 1] * capacity
+        + jnp.sum(hot[k] * earlier, axis=-1, keepdims=True).astype(jnp.int32)
+        for k in range(2)
+    ]
+    for k in range(2):
+        target_ref[:, k : k + 1] = place[k]
+    dout = (cot_ref[...].astype(F32) * live_ref[...]).astype(BF16)
+    dout_ref[...] = dout
+    spot = lanes_of(rows, send_ref.shape[0])
+    pick = jnp.where((spot == place[0]) | (spot == place[1]), 1.0, 0.0).astype(BF16)
+    send_ref[...] = dot_tn(pick, dout).astype(BF16)
 
 
 def qkv_kernel(heads, experts, x_ref, w_ref, cos_ref, sin_ref, send_ref, in_ref, tail_ref):
@@ -263,8 +285,25 @@
     return silu * u, da * u * sig * (1.0 + g * (1.0 - sig)), da * silu
 
 
+def store_shards(sc, first_row, value, keep_ref, give_ref):
+    half, shard, _ = keep_ref.shape
+    piece = min(shard, value.shape[0])
+    for u in range(value.shape[0] // piece):
+        row = first_row + u * piece
+        j = sc[row // shard]
+        inside = pl.multiple_of(row % shard, piece)
+
+        @pl.when(j < half)
+        def _():
+            keep_ref[j, pl.ds(inside, piece), :] = value[u * piece : (u + 1) * piece]
+
+        @pl.when(j >= half)
+        def _():
+            give_ref[j - half, pl.ds(inside, piece), :] = value[u * piece : (u + 1) * piece]
+
+
 def shared_kernel(
-    x_ref, dy_ref, wg_ref, wu_ref, wo_ref, res_ref, dx_ref, mid_ref, dwo_ref, res_acc, dx_acc
+    sc, x_ref, dy_ref, wg_ref, wu_ref, wo_ref, res_ref, dx_ref, mid_ref, keep_ref, give_ref, res_acc, dx_acc
 ):
     c = pl.program_id(0)
 
@@ -281,7 +320,7 @@
     dx_acc[...] += dot_nt(dg, wg) + dot_nt(du, wu)
     mid_ref[0] = dg
     mid_ref[1] = du
-    dwo_ref[...] = dot_tn(act, dy).astype(BF16)
+    store_shards(sc, c * CHUNK, dot_tn(act, dy).astype(BF16), keep_ref, give_ref)
 
     @pl.when(c == pl.num_programs(0) - 1)
     def _():
@@ -289,12 +328,27 @@
         dx_ref[...] = dx_acc[...]
 
 
-def shared_grad_kernel(x_ref, mid_ref, out_ref, xt):
+def turn_shards(sc, x, raw, xt):
+    raw[...] = x.T
+    shard = raw.shape[0] // sc.shape[0]
+    for j in range(sc.shape[0]):
+        row = pl.multiple_of(sc[j] * shard, 16)
+        xt[j * shard : (j + 1) * shard, :] = raw[pl.ds(row, shard), :]
+
+
+def split_shards(value, keep_ref, give_ref):
+    half, shard, _ = keep_ref.shape
+    for j in range(half):
+        keep_ref[j] = value[j * shard : (j + 1) * shard]
+        give_ref[j] = value[(half + j) * shard : (half + j + 1) * shard]
+
+
+def shared_grad_kernel(sc, x_ref, mid_ref, keep_ref, give_ref, raw, xt):
     @pl.when((pl.program_id(0) == 0) & (pl.program_id(1) == 0))
     def _():
-        xt[...] = x_ref[...].T
-
-    out_ref[...] = dot(xt[...], mid_ref[0]).astype(BF16)
+        turn_shards(sc, x_ref[...], raw, xt)
+
+    split_shards(dot(xt[...], mid_ref[0]).astype(BF16), keep_ref, give_ref)
 
 
 def expert_kernel(
@@ -328,19 +382,19 @@
         dx_ref[:, D:] = part_lanes(dgate[:, 0:1], lanes_of(dgate.shape[0]))
 
 
-def expert_grad_kernel(x_ref, dy_ref, mid_ref, out_ref, xt, dyt):
+def expert_grad_kernel(sc, x_ref, dy_ref, mid_ref, keep_ref, give_ref, raw, xt, dyt):
     @pl.when((pl.program_id(0) == 0) & (pl.program_id(1) == 0))
     def _():
-        xt[...] = x_ref[...].T
-        dyt[...] = dy_ref[...].T
+        turn_shards(sc, x_ref[...], raw, xt)
+        turn_shards(sc, dy_ref[...], raw, dyt)
 
     @pl.when(pl.program_id(0) < 2)
     def _():
-        out_ref[...] = dot(xt[...], mid_ref[0]).astype(BF16)
+        split_shards(dot(xt[...], mid_ref[0]).astype(BF16), keep_ref, give_ref)
 
     @pl.when(pl.program_id(0) == 2)
     def _():
-        out_ref[...] = dot(dyt[...], mid_ref[0]).astype(BF16)
+        split_shards(dot(dyt[...], mid_ref[0]).astype(BF16), keep_ref, give_ref)
 
 
 def combine_kernel(
@@ -387,18 +441,26 @@
         send_ref[d] = dot_nt(branch, w_ref[64 * head : 64 * head + LANES, :]).astype(BF16)
 
 
-def dense_grad_kernel(heads, came_ref, branch_ref, in_ref, dlogits_ref, kept_ref, out_ref, router_ref, acc):
+def dense_grad_kernel(
+    heads, sc, came_ref, branch_ref, in_ref, dlogits_ref, k_ref, g_ref, keep_ref, give_ref, router_ref, acc
+):
     acc[...] = jnp.zeros_like(acc)
     branch = branch_ref[...]
     for d, head in enumerate(heads):
         acc[64 * head : 64 * head + LANES, :] += dot_tn(came_ref[d], branch)
-    out_ref[...] = acc[...].astype(BF16)
+    half, shard, _ = keep_ref.shape
+    for j in range(half):
+        row = pl.multiple_of(sc[j] * shard, 16)
+        keep_ref[j] = acc[pl.ds(row, shard), :].astype(BF16)
+        row = pl.multiple_of(sc[half + j] * shard, 16)
+        give_ref[j] = acc[pl.ds(row, shard), :].astype(BF16)
     router_ref[...] = dot_tn(in_ref[...], dlogits_ref[...])
 
 
 def last_kernel(
     heads,
     experts,
+    sc,
     recv_ref,
     cos_ref,
     sin_ref,
@@ -412,6 +474,9 @@
     out_ref,
     pack_ref,
     dproj,
+    raw,
+    turned,
+    small,
 ):
     lane = lanes_of(x_ref.shape[0])
     cos, sin = cos_ref[...], sin_ref[...]
@@ -441,12 +506,188 @@
     dgain_one = jnp.sum(dnorm * x * inv, axis=0, keepdims=True)
     row = lax.broadcasted_iota(jnp.int32, (LANES, D), 0)
     gains = jnp.where(row == experts, dgain_one, jnp.where(row == experts + 1, dgain_ref[...], 0.0))
-    pack_ref[:, 3 * D :] = (router_ref[...] + gains.T).astype(BF16)
-    turned = in_ref[...].T
+    small[...] = router_ref[...] + gains.T
+    turn_shards(sc, in_ref[...], raw, turned)
+    shards, shard, _ = pack_ref.shape
     for part in range(3):
-        pack_ref[:, part * D : (part + 1) * D] = dot(
-            turned, dproj[:, part * D : (part + 1) * D]
-        ).astype(BF16)
+        value = dot(turned[...], dproj[:, part * D : (part + 1) * D]).astype(BF16)
+        for j in range(shards):
+            pack_ref[j, :, part * D : (part + 1) * D] = value[j * shard : (j + 1) * shard]
+    for j in range(shards):
+        row = pl.multiple_of(sc[j] * shard, 16)
+        pack_ref[j, :, 3 * D :] = small[pl.ds(row, shard), :].astype(BF16)
+
+
+def ring_split(rows, columns, pieces):
+    down = 1
+    while 2 * down <= pieces and rows % (32 * down) == 0:
+        down *= 2
+    across = pieces // down
+    width = -(-columns // (LANES * across)) * LANES
+    return down, across, rows // down, width
+
+
+def ring_place(position, n):
+    half = n // 2
+    return jnp.where(position < half, 2 * position, 2 * (n - 1 - position) + 1)
+
+
+def tail_kernel(
+    n,
+    members,
+    splits,
+    a_ref,
+    b_ref,
+    c_ref,
+    a_out,
+    b_out,
+    c_out,
+    *scratch,
+):
+    own, back, full = scratch[0:3], scratch[3:6], scratch[6:9]
+    levels = members.bit_length() - 1
+    caught, sums = scratch[9 : 9 + levels], scratch[9 + levels : 9 + 2 * levels]
+    send_sem, recv_sem, level_send, level_recv = scratch[9 + 2 * levels :]
+    ctx, fsdp = lax.axis_index("ctx"), lax.axis_index("fsdp")
+    here = jnp.where(ctx % 2 == 0, ctx // 2, n - 1 - ctx // 2)
+    ahead = (ring_place(lax.rem(here + 1, n), n), fsdp)
+    behind = (ring_place(lax.rem(here + n - 1, n), n), fsdp)
+    mates = [(ctx, fsdp + (1 << b) - 2 * (1 << b) * (fsdp // (1 << b) % 2)) for b in range(levels)]
+
+    barrier = pltpu.get_barrier_semaphore()
+    for peer in [ahead, behind] + mates:
+        pl.semaphore_signal(barrier, inc=1, device_id=peer, device_id_type=pl.DeviceIdType.MESH)
+    pl.semaphore_wait(barrier, 2 + levels)
+
+    def level_copy(b):
+        count = members >> (b + 1)
+        source = c_ref.at[pl.ds(count, count)] if b == 0 else sums[b - 1].at[pl.ds(count, count)]
+        return pltpu.make_async_remote_copy(
+            src_ref=source,
+            dst_ref=caught[b],
+            send_sem=level_send.at[b],
+            recv_sem=level_recv.at[b],
+            device_id=mates[b],
+            device_id_type=pl.DeviceIdType.MESH,
+        )
+
+    def level_add(b):
+        count = members >> (b + 1)
+        level_copy(b).wait_recv()
+        before = c_ref if b == 0 else sums[b - 1]
+        for j in range(count):
+            sums[b][j] = (before[j].astype(F32) + caught[b][j].astype(F32)).astype(BF16)
+
+    def load(i, ref):
+        down, across, height, width = splits[i]
+        for p in range(down * across):
+            r, c = p // across, p % across
+            have = max(0, min(width, ref.shape[1] - c * width))
+            if have > 0:
+                own[i][p, :, 0:have] = ref[r * height : (r + 1) * height, c * width : c * width + have]
+            if have < width:
+                own[i][p, :, have:] = jnp.zeros((height, width - have), BF16)
+
+    def save(i, ref):
+        down, across, height, width = splits[i]
+        for p in range(down * across):
+            r, c = p // across, p % across
+            have = max(0, min(width, ref.shape[1] - c * width))
+            if have > 0:
+                ref[r * height : (r + 1) * height, c * width : c * width + have] = full[i][p, :, 0:have]
+
+    def chunk(direction, steps):
+        if direction == 0:
+            return lax.rem(here + 4 * n - steps, n)
+        return n + lax.rem(here + steps, n)
+
+    def copy(i, direction, step, source, target, slot):
+        return pltpu.make_async_remote_copy(
+            src_ref=source[i].at[slot],
+            dst_ref=target[i].at[slot],
+            send_sem=send_sem.at[i, direction, step],
+            recv_sem=recv_sem.at[i, direction, step],
+            device_id=ahead if direction == 0 else behind,
+            device_id_type=pl.DeviceIdType.MESH,
+        )
+
+    def first(i):
+        for direction in range(2):
+            copy(i, direction, 0, own, back, chunk(direction, 1)).start()
+
+    def reduce_step(i, s):
+        for direction in range(2):
+            slot = chunk(direction, 1 + s)
+            copy(i, direction, s - 1, own, back, slot).wait_recv()
+            back[i][slot] = (back[i][slot].astype(F32) + own[i][slot].astype(F32)).astype(BF16)
+            copy(i, direction, s, back, back, slot).start()
+
+    def turn(i):
+        for direction in range(2):
+            slot = chunk(direction, n)
+            copy(i, direction, n - 2, own, back, slot).wait_recv()
+            full[i][slot] = (back[i][slot].astype(F32) + own[i][slot].astype(F32)).astype(BF16)
+            copy(i, direction, n - 1, full, full, slot).start()
+
+    def gather_step(i, s):
+        for direction in range(2):
+            slot = chunk(direction, s)
+            copy(i, direction, n - 2 + s, full, full, slot).wait_recv()
+            copy(i, direction, n - 1 + s, full, full, slot).start()
+
+    def end(i):
+        for direction in range(2):
+            slot = chunk(direction, n - 1)
+            copy(i, direction, 2 * n - 3, full, full, slot).wait_recv()
+
+    def both(body, low, high):
+        lax.fori_loop(low, high, lambda s, carry: (body(s), carry)[1], 0)
+
+    level_copy(0).start()
+    load(0, a_ref)
+    first(0)
+    load(1, b_ref)
+    first(1)
+
+    def early(s):
+        reduce_step(0, s)
+        reduce_step(1, s)
+
+    early(1)
+    for b in range(levels):
+        level_add(b)
+        if b + 1 < levels:
+            level_copy(b + 1).start()
+            if b == 0:
+                both(early, 2, n - 1)
+                turn(0)
+                turn(1)
+    load(2, sums[levels - 1].at[0])
+    first(2)
+
+    def joint(s):
+        gather_step(0, s)
+        gather_step(1, s)
+        reduce_step(2, s)
+
+    both(joint, 1, n - 1)
+    end(0)
+    end(1)
+    turn(2)
+    save(0, a_out)
+    save(1, b_out)
+    both(lambda s: gather_step(2, s), 1, n - 1)
+    end(2)
+    save(2, c_out)
+    for b in range(levels):
+        level_copy(b).wait_send()
+
+    def drain(s):
+        for i in range(3):
+            for direction in range(2):
+                copy(i, direction, s, own, back, 0).wait_send()
+
+    both(drain, 0, 2 * n - 2)
 
 
 def output_kernel(residual_ref, shared_ref, gates_ref, target_ref, live_ref, came_ref, out_ref):
@@ -479,6 +720,7 @@
     experts = w_router.shape[1]
     capacity = 3 * rows // experts
     places = experts * capacity
+    members = D // local
     share = HEADS * rows // n_ctx
     heads = first_heads(n_ctx, rows)
     gather = functools.partial(lax.all_gather, axis_name="fsdp", axis=0, tiled=True)
@@ -499,9 +741,17 @@
         axis=1,
     )
     qkv_pack = gather(first_pack)
-    mid_pack = gather(jnp.concatenate([w_out, w_shared_in], axis=1))
+    out_weight = gather(w_out)
+    weights = gather(
+        jnp.concatenate([w_shared_in, w_expert_in[0], w_expert_out[0].T], axis=1)
+    )
     shared_out = gather(w_shared_out)
-    expert_pack = gather(jnp.concatenate([w_expert_in[0], w_expert_out[0].T], axis=1))
+    fsdp_index = lax.axis_index("fsdp")
+    bits = members.bit_length() - 1
+    mirrored = [int(format(j, "b").zfill(bits)[::-1], 2) for j in range(members)]
+    shard_at = fsdp_index ^ jnp.array(mirrored, jnp.int32)
+    spots = fsdp_index ^ jnp.arange(members, dtype=jnp.int32)
+    spot_of = sum(((spots >> b) & 1) << (bits - 1 - b) for b in range(bits))
 
     query_pos = position_block[ctx_index] * rows + jnp.arange(rows, dtype=jnp.int32)
     live = (query_pos < length).astype(F32)[:, None]
@@ -526,17 +776,13 @@
         [order, jnp.stack([offset.astype(jnp.int32), length.astype(jnp.int32)])]
     )
 
-    pairs = routes[0].reshape(2 * rows)
-    hot = (pairs[:, None] == jnp.arange(experts, dtype=jnp.int32)[None, :]).astype(jnp.int32)
-    earlier = jnp.cumsum(hot, axis=0) - hot
-    target = (pairs * capacity + jnp.sum(earlier * hot, axis=-1)).reshape(rows, 2)
-    dout = (cotangent[0].astype(F32) * live).astype(BF16)
-    place = jnp.arange(places, dtype=jnp.int32)
-    token_pick = (
-        (target[:, 0:1] == place[None, :]) | (target[:, 1:2] == place[None, :])
-    ).astype(BF16)
-    dy_rows = exchange(dot_tn(token_pick, dout).astype(BF16).reshape(n_ctx, -1, D))
-    dy_rows = dy_rows.reshape(places, D)
+    target, dout, dy_send = call(
+        functools.partial(start_kernel, experts, capacity),
+        (shape((rows, 2), jnp.int32), shape((rows, D), BF16), shape((places, D), BF16)),
+        flops=2 * rows * D * places,
+        nbytes=3 << 20,
+    )(routes[0], cotangent[0], live)
+    dy_rows = exchange(dy_send.reshape(n_ctx, -1, D)).reshape(places, D)
 
     send, attn_in, tail = call(
         functools.partial(qkv_kernel, heads, experts),
@@ -548,6 +794,7 @@
         flops=2 * rows * D * 3 * D,
         nbytes=6 << 20,
     )(x, qkv_pack, cos, sin)
+    send, dy_rows = lax.optimization_barrier((send, dy_rows))
     recv = exchange(send)
 
     packet = pl.BlockSpec((n_ctx, rows, 3 * LANES), lambda i, sc: (0, 0, 0))
@@ -580,10 +827,10 @@
     came = exchange(attended)
 
     whole = pl.BlockSpec(memory_space=pltpu.VMEM)
-    out_block = pl.BlockSpec((D, D), lambda i: (0, 0))
+    out_block = pl.BlockSpec((D, D), lambda *at: (0, 0))
 
     def full(*dims):
-        return pl.BlockSpec(dims, lambda i: (0,) * len(dims))
+        return pl.BlockSpec(dims, lambda *at: (0,) * len(dims))
 
     residual, ffn_in, gates, outgoing = call(
         functools.partial(middle_kernel, heads, experts),
@@ -610,50 +857,63 @@
             full(rows, LANES),
             full(places, D + LANES),
         ],
-    )(came, mid_pack, x, tail, routes[0], target)
+    )(came, out_weight, x, tail, routes[0], target)
     x_rows = exchange(outgoing.reshape(n_ctx, -1, D + LANES)).reshape(places, D + LANES)
 
     lead = D // CHUNK
     steps = FS // CHUNK
-    shared_res, shared_dx, shared_mid, grad_so = call(
+    half = members // 2
+
+    def split(rows_each, columns):
+        return (shape((half, rows_each, columns), BF16),) * 2
+
+    shared_res, shared_dx, shared_mid, so_keep, so_give = call(
         shared_kernel,
         (
             shape((rows, D), F32),
             shape((rows, D), F32),
             shape((2, rows, FS), BF16),
-            shape((FS, D), BF16),
-        ),
+        )
+        + split(FS // members, D),
         flops=2 * rows * D * FS * 7,
         nbytes=14 << 20,
-        grid=(steps,),
-        in_specs=[
-            full(rows, D),
-            full(rows, D),
-            pl.BlockSpec((D, CHUNK), lambda c: (0, lead + c)),
-            pl.BlockSpec((D, CHUNK), lambda c: (0, lead + steps + c)),
-            pl.BlockSpec((CHUNK, D), lambda c: (c, 0)),
-        ],
-        out_specs=[
-            full(rows, D),
-            full(rows, D),
-            pl.BlockSpec((2, rows, CHUNK), lambda c: (0, 0, c)),
-            pl.BlockSpec((CHUNK, D), lambda c: (c, 0)),
-        ],
-        scratch_shapes=[pltpu.VMEM((rows, D), F32), pltpu.VMEM((rows, D), F32)],
-    )(ffn_in, dout, mid_pack, mid_pack, shared_out)
-    dense_pack = call(
+        grid_spec=pltpu.PrefetchScalarGridSpec(
+            num_scalar_prefetch=1,
+            grid=(steps,),
+            in_specs=[
+                full(rows, D),
+                full(rows, D),
+                pl.BlockSpec((D, CHUNK), lambda c, sc: (0, c)),
+                pl.BlockSpec((D, CHUNK), lambda c, sc: (0, steps + c)),
+                pl.BlockSpec((CHUNK, D), lambda c, sc: (c, 0)),
+            ],
+            out_specs=[
+                full(rows, D),
+                full(rows, D),
+                pl.BlockSpec((2, rows, CHUNK), lambda c, sc: (0, 0, c)),
+                full(half, FS // members, D),
+                full(half, FS // members, D),
+            ],
+            scratch_shapes=[pltpu.VMEM((rows, D), F32), pltpu.VMEM((rows, D), F32)],
+        ),
+    )(spot_of, ffn_in, dout, weights, weights, shared_out)
+    column = pl.BlockSpec((half, local, CHUNK), lambda i, c, sc: (0, 0, lead + i * steps + c))
+    dense_keep, dense_give = call(
         shared_grad_kernel,
-        shape((D, D + 2 * FS), BF16),
+        split(local, D + 2 * FS),
         flops=2 * rows * D * FS * 2,
         nbytes=9 << 20,
-        grid=(2, steps),
-        in_specs=[
-            pl.BlockSpec((rows, D), lambda i, c: (0, 0)),
-            pl.BlockSpec((1, rows, CHUNK), lambda i, c: (i, 0, c)),
-        ],
-        out_specs=pl.BlockSpec((D, CHUNK), lambda i, c: (0, lead + i * steps + c)),
-        scratch_shapes=[pltpu.VMEM((D, rows), BF16)],
-    )(ffn_in, shared_mid)
+        grid_spec=pltpu.PrefetchScalarGridSpec(
+            num_scalar_prefetch=1,
+            grid=(2, steps),
+            in_specs=[
+                full(rows, D),
+                pl.BlockSpec((1, rows, CHUNK), lambda i, c, sc: (i, 0, c)),
+            ],
+            out_specs=[column, column],
+            scratch_shapes=[pltpu.VMEM((D, rows), BF16), pltpu.VMEM((D, rows), BF16)],
+        ),
+    )(shard_at, ffn_in, shared_mid)
 
     wide = FF // CHUNK
     expert_dx, expert_res, expert_mid = call(
@@ -669,9 +929,9 @@
         in_specs=[
             full(places, D + LANES),
             full(places, D),
-            pl.BlockSpec((D, CHUNK), lambda c: (0, c)),
-            pl.BlockSpec((D, CHUNK), lambda c: (0, wide + c)),
-            pl.BlockSpec((D, CHUNK), lambda c: (0, 2 * wide + c)),
+            pl.BlockSpec((D, CHUNK), lambda c: (0, 2 * steps + c)),
+            pl.BlockSpec((D, CHUNK), lambda c: (0, 2 * steps + wide + c)),
+            pl.BlockSpec((D, CHUNK), lambda c: (0, 2 * steps + 2 * wide + c)),
         ],
         out_specs=[
             full(places, D + LANES),
@@ -683,22 +943,26 @@
             pltpu.VMEM((places, D), F32),
             pltpu.VMEM((places, LANES), F32),
         ],
-    )(x_rows, dy_rows, expert_pack, expert_pack, expert_pack)
+    )(x_rows, dy_rows, weights, weights, weights)
     dx_came = exchange(expert_dx.reshape(n_ctx, -1, D + LANES)).reshape(places, D + LANES)
-    expert_grad = call(
+    wide_column = pl.BlockSpec((half, local, CHUNK), lambda i, c, sc: (0, 0, i * wide + c))
+    expert_keep, expert_give = call(
         expert_grad_kernel,
-        shape((D, 3 * FF), BF16),
+        split(local, 3 * FF),
         flops=2 * places * D * FF * 3,
         nbytes=21 << 20,
-        grid=(3, wide),
-        in_specs=[
-            pl.BlockSpec((places, D), lambda i, c: (0, 0)),
-            pl.BlockSpec((places, D), lambda i, c: (0, 0)),
-            pl.BlockSpec((1, places, CHUNK), lambda i, c: (i, 0, c)),
-        ],
-        out_specs=pl.BlockSpec((D, CHUNK), lambda i, c: (0, i * wide + c)),
-        scratch_shapes=[pltpu.VMEM((D, places), BF16), pltpu.VMEM((D, places), BF16)],
-    )(x_rows, dy_rows, expert_mid)
+        grid_spec=pltpu.PrefetchScalarGridSpec(
+            num_scalar_prefetch=1,
+            grid=(3, wide),
+            in_specs=[
+                full(places, D),
+                full(places, D),
+                pl.BlockSpec((1, places, CHUNK), lambda i, c, sc: (i, 0, c)),
+            ],
+            out_specs=[wide_column, wide_column],
+            scratch_shapes=[pltpu.VMEM((D, places), BF16) for _ in range(3)],
+        ),
+    )(shard_at, x_rows, dy_rows, expert_mid)
 
     branch_send, dres, branch, dlogits, dgain_two = call(
         functools.partial(combine_kernel, heads, experts),
@@ -730,26 +994,31 @@
             full(rows, LANES),
             full(1, D),
         ],
-    )(dx_came, shared_dx, residual, dout, gates, routes[0], target, tail, mid_pack)
+    )(dx_came, shared_dx, residual, dout, gates, routes[0], target, tail, out_weight)
     branch_recv = exchange(branch_send)
 
-    dense_pack, grad_router = call(
+    front = pl.BlockSpec((half, local, D), lambda i, sc: (0, 0, 0))
+    dense_keep, dense_give, grad_router = call(
         functools.partial(dense_grad_kernel, heads),
-        (shape((D, D + 2 * FS), BF16), shape((D, LANES), F32)),
+        split(local, D + 2 * FS) + (shape((D, LANES), F32),),
         flops=2 * rows * D * (1024 + LANES),
         nbytes=4 << 20,
-        grid=(1,),
-        in_specs=[
-            full(n_ctx, rows, LANES),
-            full(rows, D),
-            full(rows, D),
-            full(rows, LANES),
-            pl.BlockSpec(memory_space=pl.ANY),
-        ],
-        out_specs=[out_block, full(D, LANES)],
-        scratch_shapes=[pltpu.VMEM((D, D), F32)],
-        input_output_aliases={4: 0},
-    )(came, branch, ffn_in, dlogits, dense_pack)
+        grid_spec=pltpu.PrefetchScalarGridSpec(
+            num_scalar_prefetch=1,
+            grid=(1,),
+            in_specs=[
+                full(n_ctx, rows, LANES),
+                full(rows, D),
+                full(rows, D),
+                full(rows, LANES),
+                pl.BlockSpec(memory_space=pl.ANY),
+                pl.BlockSpec(memory_space=pl.ANY),
+            ],
+            out_specs=[front, front, full(D, LANES)],
+            scratch_shapes=[pltpu.VMEM((D, D), F32)],
+        ),
+        input_output_aliases={5: 0, 6: 1},
+    )(shard_at, came, branch, ffn_in, dlogits, dense_keep, dense_give)
 
     dsend = call(
         functools.partial(attend_back_kernel, n_ctx, share),
@@ -779,13 +1048,33 @@
 
     grad_x, last_pack = call(
         functools.partial(last_kernel, heads, experts),
-        (shape((rows, D), F32), shape((D, PACKED), BF16)),
+        (shape((rows, D), F32), shape((members, local, PACKED), BF16)),
         flops=2 * rows * D * 3 * D * 2,
         nbytes=14 << 20,
-        in_specs=[whole] * 10,
-        out_specs=[whole, whole],
-        scratch_shapes=[pltpu.VMEM((rows, 3 * D), BF16)],
-    )(drecv, cos, sin, attn_in, x, qkv_pack, tail, dres, grad_router, dgain_two)
+        grid_spec=pltpu.PrefetchScalarGridSpec(
+            num_scalar_prefetch=1,
+            grid=(1,),
+            in_specs=[
+                full(n_ctx, rows, 3 * LANES),
+                full(rows, LANES),
+                full(rows, LANES),
+                full(rows, D),
+                full(rows, D),
+                full(D, PACKED),
+                full(LANES, D),
+                full(rows, D),
+                full(D, LANES),
+                full(1, D),
+            ],
+            out_specs=[full(rows, D), full(members, local, PACKED)],
+            scratch_shapes=[
+                pltpu.VMEM((rows, 3 * D), BF16),
+                pltpu.VMEM((D, rows), BF16),
+                pltpu.VMEM((D, rows), BF16),
+                pltpu.VMEM((D, LANES), F32),
+            ],
+        ),
+    )(shard_at, drecv, cos, sin, attn_in, x, qkv_pack, tail, dres, grad_router, dgain_two)
 
     res_came = exchange(expert_res.reshape(n_ctx, -1, D)).reshape(places, D)
     output = call(
@@ -795,16 +1084,44 @@
         nbytes=5 << 20,
     )(residual, shared_res, gates, target, live, res_came)
 
-    scatter = functools.partial(
-        lax.psum_scatter, axis_name="fsdp", scatter_dimension=0, tiled=True
-    )
-    expert_sum = scatter(expert_grad)
-    dense_part, so_part = scatter(dense_pack), scatter(grad_so)
-    dense_sum, so_sum = lax.psum((dense_part, so_part), "ctx")
-    last_sum = lax.psum(scatter(last_pack), "ctx")
+    def reduce_shards(keep, give):
+        terms = [keep]
+        for b in range(bits):
+            if b > 0:
+                count = members >> (b + 1)
+                give = sum(t[count:].astype(F32) for t in terms).astype(BF16)
+                terms = [t[:count] for t in terms]
+            came_in = lax.ppermute(give, "fsdp", [(i, i ^ (1 << b)) for i in range(members)])
+            terms.append(came_in)
+        return sum(t[0].astype(F32) for t in terms)
+
+    dense_part = reduce_shards(dense_keep, dense_give).astype(BF16)
+    so_part = reduce_shards(so_keep, so_give).astype(BF16)
+    expert_sum = reduce_shards(expert_keep, expert_give)
+
+    sizes = [dense_part.shape, so_part.shape, (local, PACKED)]
+    splits = [ring_split(r, c, 2 * n_ctx) for r, c in sizes]
+    tiles = [(2 * n_ctx, height, width) for _, _, height, width in splits]
+    levels = [(members >> (b + 1), local, PACKED) for b in range(bits)]
+    dense_sum, so_sum, last_sum = pl.pallas_call(
+        functools.partial(tail_kernel, n_ctx, members, splits),
+        out_shape=tuple(shape(size, BF16) for size in sizes),
+        in_specs=[whole] * 3,
+        out_specs=[whole] * 3,
+        scratch_shapes=[pltpu.VMEM(t, BF16) for t in tiles + tiles + tiles + levels + levels]
+        + [
+            pltpu.SemaphoreType.DMA((3, 2, 2 * n_ctx - 2)),
+            pltpu.SemaphoreType.DMA((3, 2, 2 * n_ctx - 2)),
+            pltpu.SemaphoreType.DMA((bits,)),
+            pltpu.SemaphoreType.DMA((bits,)),
+        ],
+        compiler_params=pltpu.CompilerParams(
+            collective_id=0, has_side_effects=True, vmem_limit_bytes=56 << 20
+        ),
+        cost_estimate=pl.CostEstimate(flops=0, bytes_accessed=200 << 20, transcendentals=0),
+    )(dense_part, so_part, last_pack)
     last_sum = last_sum.astype(F32)
     dense_sum = dense_sum.astype(F32)
-    expert_sum = expert_sum.astype(F32)
     small = last_sum[:, 3 * D :]
     return (
         output[None],

time: 715 us -> 564 us (0.79)
  waiting for transfers between devices: 437 us -> 187 us
  Pallas kernels: 147 us -> 256 us
  blocking collectives: 56.1 us -> 21.1 us
  other arithmetic: 10.9 us -> 26.4 us
  starting transfers between devices: 24.5 us -> 34.6 us
    reduce_scatter x4 -> x0, waiting for transfers between devices: 157 us -> none  [the longest x1 76.1 us: on_device(): expert_sum = scatter(expert_grad)]
    psum x1 -> x0, waiting for transfers between devices: 141 us -> none  [on_device(): dense_sum, so_sum = lax.psum((dense_part, so_part), 'ctx')]
    pallas_call x3 -> x5, Pallas kernels: 38.4 us -> 146 us  [the longest x1 103 us: on_device(): pl.pallas_call(functools.partial(tail_kernel, n_ctx, members, splits), ou...]
    ppermute x0 -> x6, waiting for transfers between devices: none -> 64.4 us  [reduce_shards(): lax.ppermute(give, 'fsdp', [(i, i ^ 1 << b) for i in range(members)])]
    all_to_all x1 -> x0, blocking collectives: 37.3 us -> none  [on_device(): exchange(outgoing.reshape(n_ctx, -1, D + LANES)).reshape(places, D + LANES)]
    all_to_all x1, waiting for transfers between devices: 18.8 us -> 0.01 us  [on_device(): exchange(expert_dx.reshape(n_ctx, -1, D + LANES)).reshape(places, D + LANES)]
    all_to_all x1 -> x2, waiting for transfers between devices: 23 us -> 39.2 us  [the longest x1 32.6 us: on_device(): exchange(outgoing.reshape(n_ctx, -1, D + LANES)).reshape(places, D + LANES)]
    convert_element_type x3 -> x5, other arithmetic: 2.32 us -> 13.8 us  [the longest x3 8.08 us: reduce_shards(): give = sum((t[count:].astype(F32) for t in terms)).astype(BF16)]
  transfers between devices with their start and end apart: 15 -> 17, of which waited for: 10 -> 9; matrix products, arithmetic and copies ran while one was open for 2% -> 5% of each run, Pallas kernels for 21% -> 27%
where the time goes in v2:
time: 564 us; the launch traced here: 563 us
  Pallas kernels  256 us (45%)
  waiting for transfers between devices  187 us (33%)
  starting transfers between devices  34.6 us (6%)
  other arithmetic  26.4 us (5%)
  local copies, waits for them, and re-layouts  23.5 us (4%)
  blocking collectives  21.1 us (4%)
  between operations  15.3 us (3%)
    pallas_call x1, Pallas kernels, on_device(): pl.pallas_call(functools.partial(tail_kernel, n_ctx, members, splits), ou...  103 us
    ppermute x6, waiting for transfers between devices, reduce_shards(): lax.ppermute(give, 'fsdp', [(i, i ^ 1 << b) for i in range(members)])  64.4 us
    all_to_all x1, waiting for transfers between devices, on_device(): recv = exchange(send)  36.4 us
    all_to_all x1, waiting for transfers between devices, on_device(): exchange(outgoing.reshape(n_ctx, -1, D + LANES)).reshape(places, D + LANES)  32.6 us
    pallas_call x1, Pallas kernels, on_device(): call(expert_kernel, (shape((places, D + LANES), BF16), shape((places, D),...  23.5 us
    pallas_call x1, Pallas kernels, on_device(): call(expert_grad_kernel, split(local, 3 * FF), flops=2 * places * D * FF...  23.4 us
    pallas_call x1, Pallas kernels, on_device(): call(functools.partial(attend_back_kernel, n_ctx, share), shape((n_ctx, r...  23.4 us
    all_to_all x1, blocking collectives, on_device(): branch_recv = exchange(branch_send)  21.1 us
  transfers between devices with their start and end apart: 17, of which 9 were waited for; matrix products, arithmetic and copies ran while one was open for 5% of the time, Pallas kernels for 27%

profile of v2, /device:TPU:0, one launch (start us, length us, event | category | flops | bytes accessed | tf_op | source)
XLA Modules:
  0.0 563.5 jit_solution(13096732875786466575)
XLA Ops:
  7.2 0.9 broadcast_in_dim.48
  8.1 0.7 broadcast_in_dim.49
  8.9 0.8 copy.41
  9.7 2.0 concatenate.16
  11.9 0.7 all-gather.7.cloned.1.call-update
  12.6 3.0 pad_maximum_fusion
  16.3 0.8 copy.45
  17.1 0.6 dynamic_slice.3
  18.4 0.7 fusion.2.live_ref
  19.0 3.2 shard_map.231
  22.2 7.3 %all-to-all-start = ((bf16[8,96,768]{2,1,0:T(8,128)(2,1)}), bf16[8,96,768]{2,1,0:T(8,128)(2,1)S(1)}, u32[]{:S(2)}, u32[]{:S(2)}) async-start(bf16[8,96,768]{2,1,0:T(8,128)(2,1)} %bitcast.45), calls=%async_computation | async-start | bytes 2359296 | tf_op jit(solution)/shard_map/all_to_all | solution.py:785
  30.1 1.0 pad_maximum_fusion.1
  31.1 15.4 %all-gather.5.cloned.1.call-done.w_ref = bf16[768,2432]{1,0:T(8,128)(2,1)} async-done(((bf16[192,2432]{1,0:T(8,128)(2,1)}), bf16[768,2432]{1,0:T(8,128)(2,1)}) %all-gather.5.cloned.1.call-update) | async-done | bytes 3735568 | tf_op jit(solution)/shard_map/all_gather | solution.py:743
  46.5 5.0 shard_map.230
  51.5 6.6 %all-to-all-done = bf16[8,96,768]{2,1,0:T(8,128)(2,1)S(1)} async-done(((bf16[8,96,768]{2,1,0:T(8,128)(2,1)}), bf16[8,96,768]{2,1,0:T(8,128)(2,1)S(1)}, u32[]{:S(2)}, u32[]{:S(2)}) %all-to-all-start) | async-done | bytes 1179680 | tf_op jit(solution)/shard_map/all_to_all | solution.py:785
  58.1 1.0 copy-done.11
  59.2 3.6 all-to-all-start.1
  62.9 0.6 pad_add_fusion.sc
  63.5 36.4 %all-to-all-done.1.recv_ref = bf16[8,256,384]{2,1,0:T(8,128)(2,1)S(1)} async-done(((bf16[8,256,384]{2,1,0:T(8,128)(2,1)}), bf16[8,256,384]{2,1,0:T(8,128)(2,1)S(1)}, u32[]{:S(2)}, u32[]{:S(2)}) %all-to-all-start.1) | async-done | bytes 1572896 | tf_op jit(solution)/shard_map/all_to_all | solution.py:798
  100.0 1.1 copy-done.6
  101.1 20.0 %shard_map.232 = (bf16[8,256,128]{2,1,0:T(8,128)(2,1)}, f32[8,128,384]{2,1,0:T(8,128)}, f32[8,1,384]{2,1,0:T(1,128)}) custom-call(s32[10]{0:T(128)} %pad_add_fusion.sc, bf16[8,256,384]{2,1,0:T(8,128)(2,1)} %copy-done.6), custom_call_target="tpu_custom_call" | custom-call | flops 3221225472 | bytes 5242880 | tf_op jit(solution)/shard_map/pallas_call | solution.py:802
  121.2 3.6 all-to-all-start.2
  124.8 15.9 %all-to-all-done.2.came_ref = bf16[8,256,128]{2,1,0:T(8,128)(2,1)S(1)} async-done(((bf16[8,256,128]{2,1,0:T(8,128)(2,1)}), bf16[8,256,128]{2,1,0:T(8,128)(2,1)S(1)}, u32[]{:S(2)}, u32[]{:S(2)}) %all-to-all-start.2) | async-done | bytes 524320 | tf_op jit(solution)/shard_map/all_to_all | solution.py:827
  140.7 0.8 copy-done.5
  141.5 5.2 shard_map.233
  146.6 3.7 all-to-all-start.3
  150.9 32.6 %all-to-all-done.3 = bf16[8,96,896]{2,1,0:T(8,128)(2,1)S(1)} async-done(((bf16[8,96,896]{2,1,0:T(8,128)(2,1)}), bf16[8,96,896]{2,1,0:T(8,128)(2,1)S(1)}, u32[]{:S(2)}, u32[]{:S(2)}) %all-to-all-start.3) | async-done | bytes 1376288 | tf_op jit(solution)/shard_map/all_to_all | solution.py:861
  183.5 1.1 copy-done.10
  184.6 23.5 %shard_map.235 = (bf16[768,896]{1,0:T(8,128)(2,1)}, bf16[768,768]{1,0:T(8,128)(2,1)}, bf16[3,768,2048]{2,1,0:T(8,128)(2,1)}) custom-call(bf16[768,896]{1,0:T(8,128)(2,1)} %bitcast.39, bf16[768,768]{1,0:T(8,128)(2,1)} %bitcast.43, bf16[768,10240]{1,0:T(8,128)(2,1)} %all-gather.9.cloned.1.call-done.wg_ref.wu_ref.wt_ref, ...), custom_call_target="tpu_custom_call" | custom-call | flops 14495514624 | bytes 25165824 | tf_op jit(solution)/shard_map/pallas_call | solution.py:919
  208.1 3.9 all-to-all-start.5
  212.5 23.4 %shard_map.243 = (bf16[2,192,6144]{2,1,0:T(8,128)(2,1)}, bf16[2,192,6144]{2,1,0:T(8,128)(2,1)}) custom-call(s32[4]{0:T(128)} %broadcast_xor_fusion.sc, bf16[768,896]{1,0:T(8,128)(2,1)} %bitcast.40, bf16[768,768]{1,0:T(8,128)(2,1)} %bitcast.44, bf16[3,768,2048]{2,1,0:T(8,128)(2,1)} %get-tuple-element.88.mid_ref), custom_call_target="tpu_custom_call" | custom-call | flops 7247757312 | bytes 22020096 | tf_op jit(solution)/shard_map/pallas_call | solution.py:949
  236.5 14.0 %shard_map.234 = (f32[256,768]{1,0:T(8,128)}, f32[256,768]{1,0:T(8,128)}, bf16[2,256,2048]{2,1,0:T(8,128)(2,1)}, bf16[2,512,768]{2,1,0:T(8,128)(2,1)}, bf16[2,512,768]{2,1,0:T(8,128)(2,1)}) custom-call(s32[4]{0:T(128)} %shift-left_add_fusion.sc, bf16[256,768]{1,0:T(8,128)(2,1)} %get-tuple-element.58.x_ref.in_ref, ...), custom_call_target="tpu_custom_call" | custom-call | flops 5637144576 | bytes 14680064 | tf_op jit(solution)/shard_map/pallas_call | solution.py:870
  250.5 1.1 copy-done.3
  251.6 5.9 %shard_map.237 = (bf16[8,256,128]{2,1,0:T(8,128)(2,1)}, f32[256,768]{1,0:T(8,128)}, bf16[256,768]{1,0:T(8,128)(2,1)}, bf16[256,128]{1,0:T(8,128)(2,1)}, f32[1,768]{1,0:T(1,128)}) custom-call(bf16[768,896]{1,0:T(8,128)(2,1)} %bitcast.33, f32[256,768]{1,0:T(8,128)} %get-tuple-element.66.dx_ref, f32[256,768]{1,0:T(8,128)} %get-tuple-element.57.residual_ref, ...), custom_call_target="tpu_custom_call" | custom-call | flops 704643072 | bytes 6291456 | tf_op jit(solution)/shard_map/pallas_call | solution.py:967
  257.5 21.1 %all_to_all.40.grad_ref = bf16[8,256,128]{2,1,0:T(8,128)(2,1)} all-to-all(bf16[8,256,128]{2,1,0:T(8,128)(2,1)} %get-tuple-element.67), channel_id=1, replica_groups=mesh['ctx'=8,'fsdp'=4] {'ctx'}, dimensions={0} | all-to-all | bytes 1048576 | tf_op jit(solution)/shard_map/all_to_all | solution.py:998
  278.6 3.6 all-to-all-start.4
  282.3 13.1 %shard_map.239 = (bf16[2,192,4864]{2,1,0:T(8,128)(2,1)}, bf16[2,192,4864]{2,1,0:T(8,128)(2,1)}) custom-call(s32[4]{0:T(128)} %broadcast_xor_fusion.sc, bf16[256,768]{1,0:T(8,128)(2,1)} %get-tuple-element.58.x_ref.in_ref, bf16[2,256,2048]{2,1,0:T(8,128)(2,1)} %get-tuple-element.74.mid_ref), custom_call_target="tpu_custom_call" | custom-call | flops 1610612736 | bytes 9437184 | tf_op jit(solution)/shard_map/pallas_call | solution.py:901
  295.3 3.8 shard_map.240
  299.6 23.4 %shard_map.238 = bf16[8,256,384]{2,1,0:T(8,128)(2,1)} custom-call(s32[10]{0:T(128)} %pad_add_fusion.sc, bf16[8,256,384]{2,1,0:T(8,128)(2,1)} %copy-done.6, bf16[8,256,128]{2,1,0:T(8,128)(2,1)} %all_to_all.40.grad_ref, f32[8,128,384]{2,1,0:T(8,128)} %get-tuple-element.68.keep_ref, f32[8,1,384]{2,1,0:T(1,128)} %get-tuple-element.69.lse_ref), custom_call_target="tpu_custom_call" | custom-call | flops 4831838208 | bytes 8388608 | tf_op jit(solution)/shard_map/pallas_call | solution.py:1023
  323.1 6.0 %all-to-all-start.7 = ((bf16[8,256,384]{2,1,0:T(8,128)(2,1)}), bf16[8,256,384]{2,1,0:T(8,128)(2,1)S(1)}, u32[]{:S(2)}, u32[]{:S(2)}) async-start(bf16[8,256,384]{2,1,0:T(8,128)(2,1)} %shard_map.238), calls=%async_computation.7 | async-start | bytes 3145728 | tf_op jit(solution)/shard_map/all_to_all | solution.py:1047
  329.1 1.6 add_convert_fusion.4
  330.6 0.8 collective-permute-start.3
  331.4 4.6 add_convert_fusion
  336.0 1.3 collective-permute-start.5
  337.3 3.5 shard_map.236
  340.8 10.0 %collective-permute-done.3 = bf16[1,512,768]{2,1,0:T(8,128)(2,1)S(1)} collective-permute-done((bf16[1,512,768]{2,1,0:T(8,128)(2,1)S(1)}, bf16[1,512,768]{2,1,0:T(8,128)(2,1)S(1)}, u32[]{:S(2)}, u32[]{:S(2)}) %collective-permute-start.3) | collective-permute-done | bytes 786464 | tf_op jit(solution)/shard_map/ppermute | solution.py:1094
  350.8 2.3 fusion.1.b_ref
  353.1 14.4 %all-to-all-done.7.recv_ref = bf16[8,256,384]{2,1,0:T(8,128)(2,1)S(1)} async-done(((bf16[8,256,384]{2,1,0:T(8,128)(2,1)}), bf16[8,256,384]{2,1,0:T(8,128)(2,1)S(1)}, u32[]{:S(2)}, u32[]{:S(2)}) %all-to-all-start.7) | async-done | bytes 1572896 | tf_op jit(solution)/shard_map/all_to_all | solution.py:1047
  367.6 1.1 copy-done.2
  368.7 8.9 %shard_map.241 = (f32[256,768]{1,0:T(8,128)}, bf16[4,192,2432]{2,1,0:T(8,128)(2,1)}) custom-call(s32[4]{0:T(128)} %broadcast_xor_fusion.sc, bf16[8,256,384]{2,1,0:T(8,128)(2,1)} %copy-done.2, f32[256,128]{1,0:T(8,128)} %get-tuple-element.140.cos_ref, f32[256,128]{1,0:T(8,128)} %get-tuple-element.141.sin_ref, bf16[256,768]{1,0:T(8,128)(2,1)} %get-tuple-element.70.in_ref, ...), custom_call_target="tpu_custom_call" | custom-call | flops 1811939328 | bytes 14680064 | tf_op jit(solution)/shard_map/pallas_call | solution.py:1049
  377.7 1.9 add_convert_fusion.2
  379.7 21.8 %collective-permute-done.5 = bf16[1,192,6144]{2,1,0:T(8,128)(2,1)} collective-permute-done((bf16[1,192,6144]{2,1,0:T(8,128)(2,1)}, bf16[1,192,6144]{2,1,0:T(8,128)(2,1)}, u32[]{:S(2)}, u32[]{:S(2)}) %collective-permute-start.5) | collective-permute-done | bytes 2359328 | tf_op jit(solution)/shard_map/ppermute | solution.py:1094
  401.5 4.3 add_bitcast_fusion
  405.8 1.2 slice_bitcast_fusion.1
  407.0 1.9 slice_bitcast_fusion
  408.9 32.5 %collective-permute-done.1 = bf16[1,192,4864]{2,1,0:T(8,128)(2,1)S(1)} collective-permute-done((bf16[1,192,4864]{2,1,0:T(8,128)(2,1)S(1)}, bf16[1,192,4864]{2,1,0:T(8,128)(2,1)S(1)}, u32[]{:S(2)}, u32[]{:S(2)}) %collective-permute-start.1) | collective-permute-done | bytes 1867808 | tf_op jit(solution)/shard_map/ppermute | solution.py:1094
  441.4 3.4 fusion.a_ref
  444.9 102.6 %shard_map.242 = (bf16[192,4864]{1,0:T(8,128)(2,1)}, bf16[512,768]{1,0:T(8,128)(2,1)}, bf16[192,2432]{1,0:T(8,128)(2,1)}) custom-call(bf16[192,4864]{1,0:T(8,128)(2,1)} %fusion.a_ref, bf16[512,768]{1,0:T(8,128)(2,1)} %fusion.1.b_ref, bf16[4,192,2432]{2,1,0:T(8,128)(2,1)} %get-tuple-element.84.c_ref), custom_call_target="tpu_custom_call" | custom-call | bytes 209715200 | tf_op jit(solution)/shard_map/pallas_call | solution.py:1106
  547.4 1.8 slice.90
  549.2 3.5 slice.93
  552.8 1.3 slice.89
  554.2 0.7 copy.46
  554.9 1.3 convert_element_type.119
  556.2 0.8 slice_reduce_fusion
  (54 shorter events, 3.2 us)
Async XLA Ops:
  7.2 5.4 copy-start.8
  7.2 5.4 copy-start.9
  7.2 39.3 %all-gather.5.cloned.1.call-start = ((), (), s32[]{:S(2)}) async-start(), calls=%async_computation.8 | async-start | bytes 4669440 | tf_op jit(solution)/shard_map/all_gather | solution.py:743
  11.8 113.0 %all-gather.7.cloned.1.call-start = ((), (), s32[]{:S(2)}) async-start(), calls=%async_computation.9 | async-start | bytes 1474560 | tf_op jit(solution)/shard_map/all_gather | solution.py:744
  12.6 170.9 %all-gather.9.cloned.1.call-start = ((), (), s32[]{:S(2)}) async-start(), calls=%async_computation.10 | async-start | bytes 19660800 | tf_op jit(solution)/shard_map/all_gather | solution.py:745
  15.6 0.7 copy-start.13
  15.6 1.5 copy-start.14
  22.2 35.9 %all-to-all-start = ((bf16[8,96,768]{2,1,0:T(8,128)(2,1)}), bf16[8,96,768]{2,1,0:T(8,128)(2,1)S(1)}, u32[]{:S(2)}, u32[]{:S(2)}) async-start(bf16[8,96,768]{2,1,0:T(8,128)(2,1)} %bitcast.45), calls=%async_computation | async-start | bytes 2359296 | tf_op jit(solution)/shard_map/all_to_all | solution.py:785
  58.1 1.0 copy-start.11
  59.2 40.8 %all-to-all-start.1 = ((bf16[8,256,384]{2,1,0:T(8,128)(2,1)}), bf16[8,256,384]{2,1,0:T(8,128)(2,1)S(1)}, u32[]{:S(2)}, u32[]{:S(2)}) async-start(bf16[8,256,384]{2,1,0:T(8,128)(2,1)} %get-tuple-element.53), calls=%async_computation.1 | async-start | bytes 3145728 | tf_op jit(solution)/shard_map/all_to_all | solution.py:798
  100.0 1.1 copy-start.6
  121.2 19.5 %all-to-all-start.2 = ((bf16[8,256,128]{2,1,0:T(8,128)(2,1)}), bf16[8,256,128]{2,1,0:T(8,128)(2,1)S(1)}, u32[]{:S(2)}, u32[]{:S(2)}) async-start(bf16[8,256,128]{2,1,0:T(8,128)(2,1)} %get-tuple-element.54), calls=%async_computation.2 | async-start | bytes 1048576 | tf_op jit(solution)/shard_map/all_to_all | solution.py:827
  140.7 0.8 copy-start.5
  146.6 36.8 %all-to-all-start.3 = ((bf16[8,96,896]{2,1,0:T(8,128)(2,1)}), bf16[8,96,896]{2,1,0:T(8,128)(2,1)S(1)}, u32[]{:S(2)}, u32[]{:S(2)}) async-start(bf16[8,96,896]{2,1,0:T(8,128)(2,1)} %bitcast.42), calls=%async_computation.3 | async-start | bytes 2752512 | tf_op jit(solution)/shard_map/all_to_all | solution.py:861
  150.3 86.1 %all-gather.11.cloned.1.call-start = ((), (), s32[]{:S(2)}) async-start(), calls=%async_computation.11 | async-start | bytes 3932160 | tf_op jit(solution)/shard_map/all_gather | solution.py:748
  183.5 1.1 copy-start.10
  208.1 3.9 copy-start.15
  208.1 42.4 %all-to-all-start.5 = ((bf16[8,96,896]{2,1,0:T(8,128)(2,1)}), bf16[8,96,896]{2,1,0:T(8,128)(2,1)S(1)}, u32[]{:S(2)}, u32[]{:S(2)}) async-start(bf16[8,96,896]{2,1,0:T(8,128)(2,1)} %bitcast.41), calls=%async_computation.5 | async-start | bytes 2752512 | tf_op jit(solution)/shard_map/all_to_all | solution.py:947
  235.9 95.5 %collective-permute-start.4 = (bf16[2,192,6144]{2,1,0:T(8,128)(2,1)}, bf16[2,192,6144]{2,1,0:T(8,128)(2,1)}, u32[]{:S(2)}, u32[]{:S(2)}) collective-permute-start(bf16[2,192,6144]{2,1,0:T(8,128)(2,1)} %get-tuple-element.90), channel_id=1, source_target_pairs={{0,1},{1,0},{2,3},{3,2},{4,5},{5,4},{6,7},{7,6},{8,9},{9,8},{10,11... | collective-permute-start | bytes 14155784 | tf_op jit(solution)/shard_map/ppermute | solution.py:1094
  250.5 1.1 copy-start.3
  278.6 44.4 %all-to-all-start.4 = ((bf16[8,96,768]{2,1,0:T(8,128)(2,1)}), bf16[8,96,768]{2,1,0:T(8,128)(2,1)S(1)}, u32[]{:S(2)}, u32[]{:S(2)}) async-start(bf16[8,96,768]{2,1,0:T(8,128)(2,1)} %bitcast.13), calls=%async_computation.4 | async-start | bytes 2359296 | tf_op jit(solution)/shard_map/all_to_all | solution.py:1079
  282.2 46.8 %collective-permute-start.2 = (bf16[2,512,768]{2,1,0:T(8,128)(2,1)}, bf16[2,512,768]{2,1,0:T(8,128)(2,1)}, u32[]{:S(2)}, u32[]{:S(2)}) collective-permute-start(bf16[2,512,768]{2,1,0:T(8,128)(2,1)} %get-tuple-element.83), channel_id=1, source_target_pairs={{0,1},{1,0},{2,3},{3,2},{4,5},{5,4},{6,7},{7,6},{8,9},{9,8},{10,11... | collective-permute-start | bytes 4718600 | tf_op jit(solution)/shard_map/ppermute | solution.py:1094
  299.2 78.5 %collective-permute-start = (bf16[2,192,4864]{2,1,0:T(8,128)(2,1)}, bf16[2,192,4864]{2,1,0:T(8,128)(2,1)}, u32[]{:S(2)}, u32[]{:S(2)}) collective-permute-start(bf16[2,192,4864]{2,1,0:T(8,128)(2,1)} %get-tuple-element.81), channel_id=1, source_target_pairs={{0,1},{1,0},{2,3},{3,2},{4,5},{5,4},{6,7},{7,6},{8,9},{9,8},{10,11... | collective-permute-start | bytes 11206664 | tf_op jit(solution)/shard_map/ppermute | solution.py:1094
  323.1 7.6 %copy-start.4 = (bf16[8,96,768]{2,1,0:T(8,128)(2,1)}, bf16[8,96,768]{2,1,0:T(8,128)(2,1)S(1)}, u32[]{:S(2)}) copy-start(bf16[8,96,768]{2,1,0:T(8,128)(2,1)S(1)} %all-to-all-done.4) | copy-start | bytes 3538948
  323.1 44.5 %all-to-all-start.7 = ((bf16[8,256,384]{2,1,0:T(8,128)(2,1)}), bf16[8,256,384]{2,1,0:T(8,128)(2,1)S(1)}, u32[]{:S(2)}, u32[]{:S(2)}) async-start(bf16[8,256,384]{2,1,0:T(8,128)(2,1)} %shard_map.238), calls=%async_computation.7 | async-start | bytes 3145728 | tf_op jit(solution)/shard_map/all_to_all | solution.py:1047
  330.6 20.2 %collective-permute-start.3 = (bf16[1,512,768]{2,1,0:T(8,128)(2,1)S(1)}, bf16[1,512,768]{2,1,0:T(8,128)(2,1)S(1)}, u32[]{:S(2)}, u32[]{:S(2)}) collective-permute-start(bf16[1,512,768]{2,1,0:T(8,128)(2,1)S(1)} %add_convert_fusion.4), channel_id=1, source_target_pairs={{0,2},{1,3},{2,0},{3,1},{4,6},{5,7},{6,4},{7,5},{8,10},{9,11},{10,... | collective-permute-start | bytes 2359304 | tf_op jit(solution)/shard_map/ppermute | solution.py:1094
  336.0 14.8 %copy-start.7 = (bf16[2,512,768]{2,1,0:T(8,128)(2,1)S(1)}, bf16[2,512,768]{2,1,0:T(8,128)(2,1)}, u32[]{:S(2)}) copy-start(bf16[2,512,768]{2,1,0:T(8,128)(2,1)} %get-tuple-element.82) | copy-start | bytes 4718596
  336.0 65.5 %collective-permute-start.5 = (bf16[1,192,6144]{2,1,0:T(8,128)(2,1)}, bf16[1,192,6144]{2,1,0:T(8,128)(2,1)}, u32[]{:S(2)}, u32[]{:S(2)}) collective-permute-start(bf16[1,192,6144]{2,1,0:T(8,128)(2,1)} %add_convert_fusion), channel_id=1, source_target_pairs={{0,2},{1,3},{2,0},{3,1},{4,6},{5,7},{6,4},{7,5},{8,10},{9,11},{10,... | collective-permute-start | bytes 7077896 | tf_op jit(solution)/shard_map/ppermute | solution.py:1094
  367.6 1.1 copy-start.2
  368.7 9.0 %copy-start = (bf16[2,192,4864]{2,1,0:T(8,128)(2,1)S(1)}, bf16[2,192,4864]{2,1,0:T(8,128)(2,1)}, u32[]{:S(2)}) copy-start(bf16[2,192,4864]{2,1,0:T(8,128)(2,1)} %get-tuple-element.80) | copy-start | bytes 11206660
  379.6 61.8 %collective-permute-start.1 = (bf16[1,192,4864]{2,1,0:T(8,128)(2,1)S(1)}, bf16[1,192,4864]{2,1,0:T(8,128)(2,1)S(1)}, u32[]{:S(2)}, u32[]{:S(2)}) collective-permute-start(bf16[1,192,4864]{2,1,0:T(8,128)(2,1)S(1)} %add_convert_fusion.2), channel_id=1, source_target_pairs={{0,2},{1,3},{2,0},{3,1},{4,6},{5,7},{6,4},{7,5},{8,10},{9,11},{10,... | collective-permute-start | bytes 5603336 | tf_op jit(solution)/shard_map/ppermute | solution.py:1094
  549.2 3.5 copy-start.1
  552.8 2.1 copy-start.12
Sparse Core Ops, SparseCore 0:
  11.9 34.5 all-gather.4
  48.1 17.4 all-gather.6
  67.2 99.9 all-gather.8
  168.6 28.5 all-gather.10

commit v3 on v1

--- a/solution.py
+++ b/solution.py
@@ -44,6 +44,18 @@
     )
 
 
+def comm_call(kernel, outs, number, *, nbytes, limit=60, **kw):
+    return pl.pallas_call(
+        kernel,
+        out_shape=outs,
+        compiler_params=pltpu.CompilerParams(
+            collective_id=number, has_side_effects=True, vmem_limit_bytes=limit << 20
+        ),
+        cost_estimate=pl.CostEstimate(flops=0, bytes_accessed=int(nbytes), transcendentals=0),
+        **kw,
+    )
+
+
 def shape(dims, dtype):
     return jax.ShapeDtypeStruct(dims, dtype)
 
@@ -83,6 +95,28 @@
     return tuple(
         jnp.where(place == target_ref[:, k : k + 1], 1.0, 0.0).astype(BF16) for k in range(2)
     )
+
+
+def start_kernel(experts, capacity, routes_ref, cot_ref, live_ref, target_ref, dout_ref, send_ref):
+    rows = routes_ref.shape[0]
+    lane = lanes_of(rows)
+    hot = [jnp.where(lane == routes_ref[:, k : k + 1], 1.0, 0.0) for k in range(2)]
+    below = jnp.where(
+        lanes_of(rows, rows) < lax.broadcasted_iota(jnp.int32, (rows, rows), 0), 1.0, 0.0
+    )
+    earlier = dot(below.astype(BF16), (hot[0] + hot[1]).astype(BF16))
+    place = [
+        routes_ref[:, k : k + 1] * capacity
+        + jnp.sum(hot[k] * earlier, axis=-1, keepdims=True).astype(jnp.int32)
+        for k in range(2)
+    ]
+    for k in range(2):
+        target_ref[:, k : k + 1] = place[k]
+    dout = (cot_ref[...].astype(F32) * live_ref[...]).astype(BF16)
+    dout_ref[...] = dout
+    spot = lanes_of(rows, send_ref.shape[0])
+    pick = jnp.where((spot == place[0]) | (spot == place[1]), 1.0, 0.0).astype(BF16)
+    send_ref[...] = dot_tn(pick, dout).astype(BF16)
 
 
 def qkv_kernel(heads, experts, x_ref, w_ref, cos_ref, sin_ref, send_ref, in_ref, tail_ref):
@@ -263,8 +297,25 @@
     return silu * u, da * u * sig * (1.0 + g * (1.0 - sig)), da * silu
 
 
+def store_shards(sc, first_row, value, keep_ref, give_ref):
+    half, shard, _ = keep_ref.shape
+    piece = min(shard, value.shape[0])
+    for u in range(value.shape[0] // piece):
+        row = first_row + u * piece
+        j = sc[row // shard]
+        inside = pl.multiple_of(row % shard, piece)
+
+        @pl.when(j < half)
+        def _():
+            keep_ref[j, pl.ds(inside, piece), :] = value[u * piece : (u + 1) * piece]
+
+        @pl.when(j >= half)
+        def _():
+            give_ref[j - half, pl.ds(inside, piece), :] = value[u * piece : (u + 1) * piece]
+
+
 def shared_kernel(
-    x_ref, dy_ref, wg_ref, wu_ref, wo_ref, res_ref, dx_ref, mid_ref, dwo_ref, res_acc, dx_acc
+    sc, x_ref, dy_ref, wg_ref, wu_ref, wo_ref, res_ref, dx_ref, mid_ref, keep_ref, give_ref, res_acc, dx_acc
 ):
     c = pl.program_id(0)
 
@@ -281,7 +332,7 @@
     dx_acc[...] += dot_nt(dg, wg) + dot_nt(du, wu)
     mid_ref[0] = dg
     mid_ref[1] = du
-    dwo_ref[...] = dot_tn(act, dy).astype(BF16)
+    store_shards(sc, c * CHUNK, dot_tn(act, dy).astype(BF16), keep_ref, give_ref)
 
     @pl.when(c == pl.num_programs(0) - 1)
     def _():
@@ -289,12 +340,27 @@
         dx_ref[...] = dx_acc[...]
 
 
-def shared_grad_kernel(x_ref, mid_ref, out_ref, xt):
+def turn_shards(sc, x, raw, xt):
+    raw[...] = x.T
+    shard = raw.shape[0] // sc.shape[0]
+    for j in range(sc.shape[0]):
+        row = pl.multiple_of(sc[j] * shard, 16)
+        xt[j * shard : (j + 1) * shard, :] = raw[pl.ds(row, shard), :]
+
+
+def split_shards(value, keep_ref, give_ref):
+    half, shard, _ = keep_ref.shape
+    for j in range(half):
+        keep_ref[j] = value[j * shard : (j + 1) * shard]
+        give_ref[j] = value[(half + j) * shard : (half + j + 1) * shard]
+
+
+def shared_grad_kernel(sc, x_ref, mid_ref, keep_ref, give_ref, raw, xt):
     @pl.when((pl.program_id(0) == 0) & (pl.program_id(1) == 0))
     def _():
-        xt[...] = x_ref[...].T
-
-    out_ref[...] = dot(xt[...], mid_ref[0]).astype(BF16)
+        turn_shards(sc, x_ref[...], raw, xt)
+
+    split_shards(dot(xt[...], mid_ref[0]).astype(BF16), keep_ref, give_ref)
 
 
 def expert_kernel(
@@ -326,21 +392,6 @@
         res_ref[...] = res_acc[...].astype(BF16)
         dx_ref[:, 0:D] = dx_acc[...].astype(BF16)
         dx_ref[:, D:] = part_lanes(dgate[:, 0:1], lanes_of(dgate.shape[0]))
-
-
-def expert_grad_kernel(x_ref, dy_ref, mid_ref, out_ref, xt, dyt):
-    @pl.when((pl.program_id(0) == 0) & (pl.program_id(1) == 0))
-    def _():
-        xt[...] = x_ref[...].T
-        dyt[...] = dy_ref[...].T
-
-    @pl.when(pl.program_id(0) < 2)
-    def _():
-        out_ref[...] = dot(xt[...], mid_ref[0]).astype(BF16)
-
-    @pl.when(pl.program_id(0) == 2)
-    def _():
-        out_ref[...] = dot(dyt[...], mid_ref[0]).astype(BF16)
 
 
 def combine_kernel(
@@ -387,18 +438,202 @@
         send_ref[d] = dot_nt(branch, w_ref[64 * head : 64 * head + LANES, :]).astype(BF16)
 
 
-def dense_grad_kernel(heads, came_ref, branch_ref, in_ref, dlogits_ref, kept_ref, out_ref, router_ref, acc):
+def ring_split(rows, columns, pieces):
+    down = 1
+    while 2 * down <= pieces and rows % (32 * down) == 0:
+        down *= 2
+    across = pieces // down
+    width = -(-columns // (LANES * across)) * LANES
+    return down, across, rows // down, width
+
+
+def ring_place(position, n):
+    half = n // 2
+    return jnp.where(position < half, 2 * position, 2 * (n - 1 - position) + 1)
+
+
+def flipped(index, mask):
+    for b in range(mask.bit_length()):
+        if mask >> b & 1:
+            index = index + (1 << b) - 2 * (1 << b) * (index // (1 << b) % 2)
+    return index
+
+
+def mirrored(members):
+    bits = members.bit_length() - 1
+    return [int(format(j, "b").zfill(bits)[::-1], 2) for j in range(members)]
+
+
+def shard_rows(members, shard):
+    fsdp = lax.axis_index("fsdp")
+    return [pl.multiple_of(flipped(fsdp, m) * shard, 16) for m in mirrored(members)]
+
+
+def remote(source, target, send_sem, recv_sem, peer):
+    return pltpu.make_async_remote_copy(
+        src_ref=source,
+        dst_ref=target,
+        send_sem=send_sem,
+        recv_sem=recv_sem,
+        device_id=peer,
+        device_id_type=pl.DeviceIdType.MESH,
+    )
+
+
+def greet(peers):
+    barrier = pltpu.get_barrier_semaphore()
+    for peer in peers:
+        pl.semaphore_signal(barrier, inc=1, device_id=peer, device_id_type=pl.DeviceIdType.MESH)
+    pl.semaphore_wait(barrier, len(peers))
+
+
+def mates_of(members):
+    ctx, fsdp = lax.axis_index("ctx"), lax.axis_index("fsdp")
+    return [(ctx, flipped(fsdp, 1 << b)) for b in range(members.bit_length() - 1)]
+
+
+def row_peers(n):
+    ctx, fsdp = lax.axis_index("ctx"), lax.axis_index("fsdp")
+    return [(lax.rem(ctx + d, n), fsdp) for d in range(1, n)]
+
+
+def loop(body, low, high):
+    lax.fori_loop(low, high, lambda s, carry: (body(s), carry)[1], 0)
+
+
+def add_into(target, j, other):
+    target[j] = (target[j].astype(F32) + other[j].astype(F32)).astype(BF16)
+
+
+def back_exchange_kernel(
+    n,
+    members,
+    heads,
+    send_ref,
+    x_ref,
+    dy_ref,
+    came_ref,
+    branch_ref,
+    in_ref,
+    dlogits_ref,
+    mid_ref,
+    recv_ref,
+    sum_ref,
+    out_grad_ref,
+    router_ref,
+    give,
+    caught,
+    crossed,
+    raw,
+    xt,
+    dyt,
+    acc,
+    mids,
+    send_sem,
+    recv_sem,
+    own_sem,
+    give_sem,
+    caught_sem,
+    cross_sem,
+    mid_sem,
+):
+    ctx = lax.axis_index("ctx")
+    peers = row_peers(n)
+    mates = mates_of(members)
+    mate, far = mates[0], mates[1]
+    greet(peers + [mate, far])
+    own = pltpu.make_async_copy(send_ref.at[ctx], recv_ref.at[ctx], own_sem)
+    own.start()
+    copies = [
+        remote(send_ref.at[p[0]], recv_ref.at[ctx], send_sem.at[d], recv_sem.at[d], p)
+        for d, p in enumerate(peers)
+    ]
+    for c in copies:
+        c.start()
+
+    steps = mid_ref.shape[2] // CHUNK
+    parts = mid_ref.shape[0]
+
+    def fetch(i, c, slot):
+        column = pl.multiple_of(c * CHUNK, CHUNK)
+        return pltpu.make_async_copy(
+            mid_ref.at[i, :, pl.ds(column, CHUNK)], mids.at[slot], mid_sem.at[slot]
+        )
+
+    fetch(0, 0, 0).start()
+    shard = D // members
+    half = members // 2
+    rows = shard_rows(members, shard)
+
+    def turned(value, target):
+        raw[...] = value.T
+        for j in range(members):
+            target[j * shard : (j + 1) * shard, :] = raw[pl.ds(rows[j], shard), :]
+
+    turned(x_ref[:, 0:D], xt)
+    turned(dy_ref[...], dyt)
+
+    def swap(i):
+        return remote(give.at[i], caught.at[i], give_sem.at[i], caught_sem.at[i], mate)
+
+    quarter = members // 4
+    cross = remote(
+        sum_ref.at[0, pl.ds(quarter, quarter)], crossed, cross_sem.at[0], cross_sem.at[1], far
+    )
+    for i in range(parts):
+        left = xt if i < 2 else dyt
+
+        def step(c, left=left, i=i):
+            slot = lax.rem(c, 2)
+            fetch(i, c, slot).wait()
+
+            @pl.when(c + 1 < steps)
+            def _():
+                fetch(i, c + 1, 1 - slot).start()
+
+            value = dot(left[...], mids[slot]).astype(BF16)
+            column = pl.ds(pl.multiple_of(c * CHUNK, CHUNK), CHUNK)
+            for j in range(half):
+                sum_ref[i, j, :, column] = value[j * shard : (j + 1) * shard]
+                give[i, j, :, column] = value[(half + j) * shard : (half + j + 1) * shard]
+
+        loop(step, 0, steps)
+        if i + 1 < parts:
+            fetch(i + 1, 0, 0).start()
+        swap(i).start()
+        if i > 0:
+            swap(i - 1).wait_recv()
+            for j in range(half):
+                add_into(sum_ref.at[i - 1], j, caught.at[i - 1])
+        if i == 1:
+            cross.start()
+
     acc[...] = jnp.zeros_like(acc)
     branch = branch_ref[...]
     for d, head in enumerate(heads):
         acc[64 * head : 64 * head + LANES, :] += dot_tn(came_ref[d], branch)
-    out_ref[...] = acc[...].astype(BF16)
+    for j in range(members):
+        out_grad_ref[j] = acc[pl.ds(rows[j], shard), :].astype(BF16)
     router_ref[...] = dot_tn(in_ref[...], dlogits_ref[...])
+    swap(parts - 1).wait_recv()
+    for j in range(half):
+        add_into(sum_ref.at[parts - 1], j, caught.at[parts - 1])
+    for c in copies:
+        c.wait()
+    own.wait()
+    cross.wait()
+    for j in range(quarter):
+        add_into(sum_ref.at[0], j, crossed)
+    for i in range(parts):
+        swap(i).wait_send()
 
 
 def last_kernel(
+    n,
+    members,
     heads,
     experts,
+    splits,
     recv_ref,
     cos_ref,
     sin_ref,
@@ -407,12 +642,141 @@
     w_ref,
     tail_ref,
     dres_ref,
+    out_grad_ref,
     router_ref,
     dgain_ref,
-    out_ref,
-    pack_ref,
-    dproj,
+    a_ref,
+    a_other,
+    b_ref,
+    b_other,
+    e_ref,
+    x_out,
+    a_out,
+    b_out,
+    c_out,
+    e_out,
+    *scratch,
 ):
+    bits = members.bit_length() - 1
+    streams = len(splits)
+    own, back, full = (scratch[k * streams : (k + 1) * streams] for k in range(3))
+    scratch = scratch[3 * streams :]
+    caught, e_caught = scratch[0:bits], scratch[bits : 2 * bits - 1]
+    dproj, raw, turned, small, pack = scratch[2 * bits - 1 : 2 * bits + 4]
+    send_sem, recv_sem, level_send, level_recv, e_send, e_recv = scratch[2 * bits + 4 :]
+    ctx, fsdp = lax.axis_index("ctx"), lax.axis_index("fsdp")
+    here = jnp.where(ctx % 2 == 0, ctx // 2, n - 1 - ctx // 2)
+    ahead = (ring_place(lax.rem(here + 1, n), n), fsdp)
+    behind = (ring_place(lax.rem(here + n - 1, n), n), fsdp)
+    mates = mates_of(members)
+    greet([ahead, behind] + mates)
+    shard = D // members
+    parts = e_ref.shape[0]
+
+    def level_copy(b):
+        count = members >> (b + 1)
+        return remote(
+            pack.at[pl.ds(count, count)], caught[b], level_send.at[b], level_recv.at[b], mates[b]
+        )
+
+    def level_add(b):
+        level_copy(b).wait_recv()
+        for j in range(members >> (b + 1)):
+            add_into(pack, j, caught[b])
+
+    def e_copy(i, b):
+        count = members >> (b + 1)
+        source = e_ref if b == 1 or (b == 2 and i == 0) else e_caught[b - 2]
+        return remote(
+            source.at[i, pl.ds(count, count)],
+            e_caught[b - 1].at[i],
+            e_send.at[i, b - 1],
+            e_recv.at[i, b - 1],
+            mates[b],
+        )
+
+    def e_add(i, b):
+        e_copy(i, b).wait_recv()
+        source = e_ref if b == 1 or (b == 2 and i == 0) else e_caught[b - 2]
+        for j in range(members >> (b + 1)):
+            total = source[i, j].astype(F32) + e_caught[b - 1][i, j].astype(F32)
+            if b == bits - 1:
+                e_out[i] = total.astype(BF16)
+            else:
+                e_caught[b - 1][i, j] = total.astype(BF16)
+
+    def tiles(i):
+        down, across, height, width = splits[i][0:4]
+        columns = splits[i][4]
+        for p in range(down * across):
+            r, c = p // across, p % across
+            yield p, r * height, height, c * width, max(0, min(width, columns - c * width)), width
+
+    def load(i, ref, skip=0, other=None):
+        for p, top, height, start, have, width in tiles(i):
+            if have > 0:
+                value = ref[top : top + height, skip + start : skip + start + have]
+                if other is not None:
+                    added = other[top : top + height, skip + start : skip + start + have]
+                    value = (value.astype(F32) + added.astype(F32)).astype(BF16)
+                own[i][p, :, 0:have] = value
+            if have < width:
+                own[i][p, :, have:] = jnp.zeros((height, width - have), BF16)
+
+    def save(i, ref, skip=0):
+        for p, top, height, start, have, width in tiles(i):
+            if have > 0:
+                ref[top : top + height, skip + start : skip + start + have] = full[i][p, :, 0:have]
+
+    def chunk(direction, steps):
+        if direction == 0:
+            return lax.rem(here + 4 * n - steps, n)
+        return n + lax.rem(here + steps, n)
+
+    def copy(i, direction, step, source, target, slot):
+        return remote(
+            source[i].at[slot],
+            target[i].at[slot],
+            send_sem.at[i, direction, step],
+            recv_sem.at[i, direction, step],
+            ahead if direction == 0 else behind,
+        )
+
+    def first(i):
+        for direction in range(2):
+            copy(i, direction, 0, own, back, chunk(direction, 1)).start()
+
+    def reduce_step(i, s):
+        for direction in range(2):
+            slot = chunk(direction, 1 + s)
+            copy(i, direction, s - 1, own, back, slot).wait_recv()
+            add_into(back[i], slot, own[i])
+            copy(i, direction, s, back, back, slot).start()
+
+    def turn(i):
+        for direction in range(2):
+            slot = chunk(direction, n)
+            copy(i, direction, n - 2, own, back, slot).wait_recv()
+            full[i][slot] = (back[i][slot].astype(F32) + own[i][slot].astype(F32)).astype(BF16)
+            copy(i, direction, n - 1, full, full, slot).start()
+
+    def gather_step(i, s):
+        for direction in range(2):
+            slot = chunk(direction, s)
+            copy(i, direction, n - 2 + s, full, full, slot).wait_recv()
+            copy(i, direction, n - 1 + s, full, full, slot).start()
+
+    def end(i):
+        for direction in range(2):
+            copy(i, direction, 2 * n - 3, full, full, chunk(direction, n - 1)).wait_recv()
+
+    dense, late = [0, 1], list(range(2, streams))
+    e_copy(1, 1).start()
+    load(0, a_ref, other=a_other)
+    first(0)
+    load(1, b_ref, other=b_other)
+    first(1)
+
     lane = lanes_of(x_ref.shape[0])
     cos, sin = cos_ref[...], sin_ref[...]
     for part in range(3):
@@ -431,22 +795,120 @@
                 t = t.astype(BF16).astype(F32)
                 t = t * cos - partner(t, lane) * sin
             dproj[:, part * D + g * LANES : part * D + (g + 1) * LANES] = t.astype(BF16)
+    rows = shard_rows(members, shard)
+    raw[...] = in_ref[...].T
+    for j in range(members):
+        turned[j * shard : (j + 1) * shard, :] = raw[pl.ds(rows[j], shard), :]
+    for part in range(3):
+        value = dot(turned[...], dproj[:, part * D : (part + 1) * D]).astype(BF16)
+        for j in range(members):
+            pack[j, :, part * D : (part + 1) * D] = value[j * shard : (j + 1) * shard]
     dnorm = dot_nt(dproj[...], w_ref[:, 0 : 3 * D])
     x = x_ref[...].astype(F32)
     gain = tail_ref[experts : experts + 1, :]
     inv = lax.rsqrt(jnp.mean(x * x, axis=-1, keepdims=True) + norm_eps)
-    scaled = dnorm * gain
-    total = jnp.mean(scaled * x, axis=-1, keepdims=True)
-    out_ref[...] = dres_ref[...] + inv * scaled - x * inv * inv * inv * total
     dgain_one = jnp.sum(dnorm * x * inv, axis=0, keepdims=True)
     row = lax.broadcasted_iota(jnp.int32, (LANES, D), 0)
     gains = jnp.where(row == experts, dgain_one, jnp.where(row == experts + 1, dgain_ref[...], 0.0))
-    pack_ref[:, 3 * D :] = (router_ref[...] + gains.T).astype(BF16)
-    turned = in_ref[...].T
-    for part in range(3):
-        pack_ref[:, part * D : (part + 1) * D] = dot(
-            turned, dproj[:, part * D : (part + 1) * D]
-        ).astype(BF16)
+    small[...] = router_ref[...] + gains.T
+    for j in range(members):
+        pack[j, :, 3 * D : PACKED] = small[pl.ds(rows[j], shard), :].astype(BF16)
+        pack[j, :, PACKED:] = out_grad_ref[j]
+    level_copy(0).start()
+    scaled = dnorm * gain
+    total = jnp.mean(scaled * x, axis=-1, keepdims=True)
+    x_out[...] = dres_ref[...] + inv * scaled - x * inv * inv * inv * total
+
+    def early(s):
+        for i in dense:
+            reduce_step(i, s)
+
+    def dense_gather(s):
+        for i in dense:
+            gather_step(i, s)
+
+    loop(early, 1, 3)
+    level_add(0)
+    level_copy(1).start()
+    loop(early, 3, n - 1)
+    for i in dense:
+        turn(i)
+    loop(dense_gather, 1, n // 2 + 1)
+    for b in range(1, bits):
+        level_add(b)
+        if b + 1 < bits:
+            level_copy(b + 1).start()
+    for i in range(2, parts):
+        e_copy(i, 1).start()
+    skip = 0
+    for i in late:
+        load(i, pack.at[0], skip)
+        skip += splits[i][4]
+        first(i)
+    rest = n - 2 - n // 2
+
+    def joint(s):
+        for i in late:
+            reduce_step(i, s)
+        for i in dense:
+            gather_step(i, s + n // 2)
+
+    def late_reduce(s):
+        for i in late:
+            reduce_step(i, s)
+
+    loop(joint, 1, rest + 1)
+    for i in dense:
+        end(i)
+    loop(late_reduce, rest + 1, n - 1)
+    for i in late:
+        turn(i)
+    save(0, a_out)
+    save(1, b_out)
+    e_add(1, 1)
+
+    def finish(s):
+        for i in late:
+            gather_step(i, s)
+
+    loop(finish, 1, n - 1)
+    for i in late:
+        end(i)
+    skip = 0
+    for i in late:
+        save(i, c_out, skip)
+        skip += splits[i][4]
+    for i in range(2, parts):
+        e_add(i, 1)
+    if bits == 2:
+        e_out[0] = e_ref[0, 0]
+    for b in range(2, bits):
+        for i in range(parts):
+            e_copy(i, b).start()
+        for i in range(parts):
+            e_add(i, b)
+    for b in range(bits):
+        level_copy(b).wait_send()
+    for b in range(1, bits):
+        for i in range(1 if b == 1 else 0, parts):
+            e_copy(i, b).wait_send()
+
+    def drain(s):
+        for i in range(streams):
+            for direction in range(2):
+                copy(i, direction, s, own, back, 0).wait_send()
+
+    loop(drain, 0, 2 * n - 2)
+
+
+def widen_kernel(late_ref, a_ref, b_ref, e_ref, qkv_out, w_out, a_out, b_out, in_out, back_out):
+    qkv_out[...] = late_ref[:, 0 : 3 * D].astype(F32)
+    w_out[...] = late_ref[:, PACKED:].astype(F32)
+    a_out[...] = a_ref[...].astype(F32)
+    b_out[...] = b_ref[...].astype(F32)
+    in_out[:, 0:FF] = e_ref[0].astype(F32)
+    in_out[:, FF:] = e_ref[1].astype(F32)
+    back_out[...] = e_ref[2].astype(F32).T
 
 
 def output_kernel(residual_ref, shared_ref, gates_ref, target_ref, live_ref, came_ref, out_ref):
@@ -479,6 +941,7 @@
     experts = w_router.shape[1]
     capacity = 3 * rows // experts
     places = experts * capacity
+    members = D // local
     share = HEADS * rows // n_ctx
     heads = first_heads(n_ctx, rows)
     gather = functools.partial(lax.all_gather, axis_name="fsdp", axis=0, tiled=True)
@@ -499,9 +962,16 @@
         axis=1,
     )
     qkv_pack = gather(first_pack)
-    mid_pack = gather(jnp.concatenate([w_out, w_shared_in], axis=1))
+    out_weight = gather(w_out)
+    weights = gather(
+        jnp.concatenate([w_shared_in, w_expert_in[0], w_expert_out[0].T], axis=1)
+    )
     shared_out = gather(w_shared_out)
-    expert_pack = gather(jnp.concatenate([w_expert_in[0], w_expert_out[0].T], axis=1))
+    fsdp_index = lax.axis_index("fsdp")
+    bits = members.bit_length() - 1
+    shard_at = fsdp_index ^ jnp.array(mirrored(members), jnp.int32)
+    spots = fsdp_index ^ jnp.arange(members, dtype=jnp.int32)
+    spot_of = sum(((spots >> b) & 1) << (bits - 1 - b) for b in range(bits))
 
     query_pos = position_block[ctx_index] * rows + jnp.arange(rows, dtype=jnp.int32)
     live = (query_pos < length).astype(F32)[:, None]
@@ -526,17 +996,13 @@
         [order, jnp.stack([offset.astype(jnp.int32), length.astype(jnp.int32)])]
     )
 
-    pairs = routes[0].reshape(2 * rows)
-    hot = (pairs[:, None] == jnp.arange(experts, dtype=jnp.int32)[None, :]).astype(jnp.int32)
-    earlier = jnp.cumsum(hot, axis=0) - hot
-    target = (pairs * capacity + jnp.sum(earlier * hot, axis=-1)).reshape(rows, 2)
-    dout = (cotangent[0].astype(F32) * live).astype(BF16)
-    place = jnp.arange(places, dtype=jnp.int32)
-    token_pick = (
-        (target[:, 0:1] == place[None, :]) | (target[:, 1:2] == place[None, :])
-    ).astype(BF16)
-    dy_rows = exchange(dot_tn(token_pick, dout).astype(BF16).reshape(n_ctx, -1, D))
-    dy_rows = dy_rows.reshape(places, D)
+    target, dout, dy_send = call(
+        functools.partial(start_kernel, experts, capacity),
+        (shape((rows, 2), jnp.int32), shape((rows, D), BF16), shape((places, D), BF16)),
+        flops=2 * rows * D * places,
+        nbytes=3 << 20,
+    )(routes[0], cotangent[0], live)
+    dy_rows = exchange(dy_send.reshape(n_ctx, -1, D)).reshape(places, D)
 
     send, attn_in, tail = call(
         functools.partial(qkv_kernel, heads, experts),
@@ -548,6 +1014,7 @@
         flops=2 * rows * D * 3 * D,
         nbytes=6 << 20,
     )(x, qkv_pack, cos, sin)
+    send, dy_rows = lax.optimization_barrier((send, dy_rows))
     recv = exchange(send)
 
     packet = pl.BlockSpec((n_ctx, rows, 3 * LANES), lambda i, sc: (0, 0, 0))
@@ -580,10 +1047,10 @@
     came = exchange(attended)
 
     whole = pl.BlockSpec(memory_space=pltpu.VMEM)
-    out_block = pl.BlockSpec((D, D), lambda i: (0, 0))
+    out_block = pl.BlockSpec((D, D), lambda *at: (0, 0))
 
     def full(*dims):
-        return pl.BlockSpec(dims, lambda i: (0,) * len(dims))
+        return pl.BlockSpec(dims, lambda *at: (0,) * len(dims))
 
     residual, ffn_in, gates, outgoing = call(
         functools.partial(middle_kernel, heads, experts),
@@ -610,50 +1077,62 @@
             full(rows, LANES),
             full(places, D + LANES),
         ],
-    )(came, mid_pack, x, tail, routes[0], target)
+    )(came, out_weight, x, tail, routes[0], target)
     x_rows = exchange(outgoing.reshape(n_ctx, -1, D + LANES)).reshape(places, D + LANES)
 
-    lead = D // CHUNK
     steps = FS // CHUNK
-    shared_res, shared_dx, shared_mid, grad_so = call(
+    half = members // 2
+
+    def split(rows_each, columns):
+        return (shape((half, rows_each, columns), BF16),) * 2
+
+    shared_res, shared_dx, shared_mid, so_keep, so_give = call(
         shared_kernel,
         (
             shape((rows, D), F32),
             shape((rows, D), F32),
             shape((2, rows, FS), BF16),
-            shape((FS, D), BF16),
-        ),
+        )
+        + split(FS // members, D),
         flops=2 * rows * D * FS * 7,
         nbytes=14 << 20,
-        grid=(steps,),
-        in_specs=[
-            full(rows, D),
-            full(rows, D),
-            pl.BlockSpec((D, CHUNK), lambda c: (0, lead + c)),
-            pl.BlockSpec((D, CHUNK), lambda c: (0, lead + steps + c)),
-            pl.BlockSpec((CHUNK, D), lambda c: (c, 0)),
-        ],
-        out_specs=[
-            full(rows, D),
-            full(rows, D),
-            pl.BlockSpec((2, rows, CHUNK), lambda c: (0, 0, c)),
-            pl.BlockSpec((CHUNK, D), lambda c: (c, 0)),
-        ],
-        scratch_shapes=[pltpu.VMEM((rows, D), F32), pltpu.VMEM((rows, D), F32)],
-    )(ffn_in, dout, mid_pack, mid_pack, shared_out)
-    dense_pack = call(
+        grid_spec=pltpu.PrefetchScalarGridSpec(
+            num_scalar_prefetch=1,
+            grid=(steps,),
+            in_specs=[
+                full(rows, D),
+                full(rows, D),
+                pl.BlockSpec((D, CHUNK), lambda c, sc: (0, c)),
+                pl.BlockSpec((D, CHUNK), lambda c, sc: (0, steps + c)),
+                pl.BlockSpec((CHUNK, D), lambda c, sc: (c, 0)),
+            ],
+            out_specs=[
+                full(rows, D),
+                full(rows, D),
+                pl.BlockSpec((2, rows, CHUNK), lambda c, sc: (0, 0, c)),
+                full(half, FS // members, D),
+                full(half, FS // members, D),
+            ],
+            scratch_shapes=[pltpu.VMEM((rows, D), F32), pltpu.VMEM((rows, D), F32)],
+        ),
+    )(spot_of, ffn_in, dout, weights, weights, shared_out)
+    column = pl.BlockSpec((half, local, CHUNK), lambda i, c, sc: (0, 0, i * steps + c))
+    dense_keep, dense_give = call(
         shared_grad_kernel,
-        shape((D, D + 2 * FS), BF16),
+        split(local, 2 * FS),
         flops=2 * rows * D * FS * 2,
         nbytes=9 << 20,
-        grid=(2, steps),
-        in_specs=[
-            pl.BlockSpec((rows, D), lambda i, c: (0, 0)),
-            pl.BlockSpec((1, rows, CHUNK), lambda i, c: (i, 0, c)),
-        ],
-        out_specs=pl.BlockSpec((D, CHUNK), lambda i, c: (0, lead + i * steps + c)),
-        scratch_shapes=[pltpu.VMEM((D, rows), BF16)],
-    )(ffn_in, shared_mid)
+        grid_spec=pltpu.PrefetchScalarGridSpec(
+            num_scalar_prefetch=1,
+            grid=(2, steps),
+            in_specs=[
+                full(rows, D),
+                pl.BlockSpec((1, rows, CHUNK), lambda i, c, sc: (i, 0, c)),
+            ],
+            out_specs=[column, column],
+            scratch_shapes=[pltpu.VMEM((D, rows), BF16), pltpu.VMEM((D, rows), BF16)],
+        ),
+    )(shard_at, ffn_in, shared_mid)
 
     wide = FF // CHUNK
     expert_dx, expert_res, expert_mid = call(
@@ -669,9 +1148,9 @@
         in_specs=[
             full(places, D + LANES),
             full(places, D),
-            pl.BlockSpec((D, CHUNK), lambda c: (0, c)),
-            pl.BlockSpec((D, CHUNK), lambda c: (0, wide + c)),
-            pl.BlockSpec((D, CHUNK), lambda c: (0, 2 * wide + c)),
+            pl.BlockSpec((D, CHUNK), lambda c: (0, 2 * steps + c)),
+            pl.BlockSpec((D, CHUNK), lambda c: (0, 2 * steps + wide + c)),
+            pl.BlockSpec((D, CHUNK), lambda c: (0, 2 * steps + 2 * wide + c)),
         ],
         out_specs=[
             full(places, D + LANES),
@@ -683,23 +1162,11 @@
             pltpu.VMEM((places, D), F32),
             pltpu.VMEM((places, LANES), F32),
         ],
-    )(x_rows, dy_rows, expert_pack, expert_pack, expert_pack)
+    )(x_rows, dy_rows, weights, weights, weights)
     dx_came = exchange(expert_dx.reshape(n_ctx, -1, D + LANES)).reshape(places, D + LANES)
-    expert_grad = call(
-        expert_grad_kernel,
-        shape((D, 3 * FF), BF16),
-        flops=2 * places * D * FF * 3,
-        nbytes=21 << 20,
-        grid=(3, wide),
-        in_specs=[
-            pl.BlockSpec((places, D), lambda i, c: (0, 0)),
-            pl.BlockSpec((places, D), lambda i, c: (0, 0)),
-            pl.BlockSpec((1, places, CHUNK), lambda i, c: (i, 0, c)),
-        ],
-        out_specs=pl.BlockSpec((D, CHUNK), lambda i, c: (0, i * wide + c)),
-        scratch_shapes=[pltpu.VMEM((D, places), BF16), pltpu.VMEM((D, places), BF16)],
-    )(x_rows, dy_rows, expert_mid)
-
+    shared_dx, dense_keep, dense_give, so_keep, so_give = lax.optimization_barrier(
+        (shared_dx, dense_keep, dense_give, so_keep, so_give)
+    )
     branch_send, dres, branch, dlogits, dgain_two = call(
         functools.partial(combine_kernel, heads, experts),
         (
@@ -730,26 +1197,41 @@
             full(rows, LANES),
             full(1, D),
         ],
-    )(dx_came, shared_dx, residual, dout, gates, routes[0], target, tail, mid_pack)
+    )(dx_came, shared_dx, residual, dout, gates, routes[0], target, tail, out_weight)
     branch_recv = exchange(branch_send)
 
-    dense_pack, grad_router = call(
-        functools.partial(dense_grad_kernel, heads),
-        (shape((D, D + 2 * FS), BF16), shape((D, LANES), F32)),
-        flops=2 * rows * D * (1024 + LANES),
-        nbytes=4 << 20,
-        grid=(1,),
-        in_specs=[
-            full(n_ctx, rows, LANES),
-            full(rows, D),
-            full(rows, D),
-            full(rows, LANES),
-            pl.BlockSpec(memory_space=pl.ANY),
-        ],
-        out_specs=[out_block, full(D, LANES)],
-        scratch_shapes=[pltpu.VMEM((D, D), F32)],
-        input_output_aliases={4: 0},
-    )(came, branch, ffn_in, dlogits, dense_pack)
+    def halve(terms, give, b):
+        count = members >> (b + 1)
+        if give is None:
+            give = sum(t[count:].astype(F32) for t in terms).astype(BF16)
+            terms = [t[:count] for t in terms]
+        came_in = lax.ppermute(give, "fsdp", [(i, i ^ (1 << b)) for i in range(members)])
+        return terms + [came_in]
+
+    def upper(terms, b):
+        count = members >> (b + 1)
+        give = sum(t[count:].astype(F32) for t in terms).astype(BF16)
+        return [t[:count] for t in terms], give
+
+    def gathered(terms):
+        return sum(t.astype(F32) for t in terms).astype(BF16)
+
+    def rest_of(terms, give):
+        keep = gathered(terms)
+        for b in range(1, bits):
+            came_in = halve([], give, b)[0]
+            if b + 1 < bits:
+                keep, give = (
+                    gathered(t) for t in zip(*[(u[: u.shape[0] // 2], u[u.shape[0] // 2 :]) for u in (keep, came_in)])
+                )
+        return keep[0], came_in[0]
+
+    dense_terms, dense_give = upper(halve([dense_keep], dense_give, 0), 1)
+    so_terms, so_give = upper(halve([so_keep], so_give, 0), 1)
+    branch_recv, expert_res = lax.optimization_barrier((branch_recv, expert_res))
+    recv, dense_give, so_give = lax.optimization_barrier((recv, dense_give, so_give))
+    dense_part, dense_other = rest_of(dense_terms, dense_give)
+    so_part, so_other = rest_of(so_terms, so_give)
 
     dsend = call(
         functools.partial(attend_back_kernel, n_ctx, share),
@@ -775,17 +1257,90 @@
             ],
         ),
     )(scalars, recv, branch_recv, kept, lse)
-    drecv = exchange(dsend)
-
-    grad_x, last_pack = call(
-        functools.partial(last_kernel, heads, experts),
-        (shape((rows, D), F32), shape((D, PACKED), BF16)),
-        flops=2 * rows * D * 3 * D * 2,
-        nbytes=14 << 20,
-        in_specs=[whole] * 10,
-        out_specs=[whole, whole],
-        scratch_shapes=[pltpu.VMEM((rows, 3 * D), BF16)],
-    )(drecv, cos, sin, attn_in, x, qkv_pack, tail, dres, grad_router, dgain_two)
+    drecv, expert_sum, out_grad, grad_router = comm_call(
+        functools.partial(back_exchange_kernel, n_ctx, members, heads),
+        (
+            shape((n_ctx, rows, 3 * LANES), BF16),
+            shape((3, half, local, FF), BF16),
+            shape((members, local, D), BF16),
+            shape((D, LANES), F32),
+        ),
+        1,
+        in_specs=[whole] * 7 + [pl.BlockSpec(memory_space=pl.ANY)],
+        out_specs=[whole] * 4,
+        scratch_shapes=[
+            pltpu.VMEM((3, half, local, FF), BF16),
+            pltpu.VMEM((3, half, local, FF), BF16),
+            pltpu.VMEM((members // 4, local, FF), BF16),
+            pltpu.VMEM((D, places), BF16),
+            pltpu.VMEM((D, places), BF16),
+            pltpu.VMEM((D, places), BF16),
+            pltpu.VMEM((D, D), F32),
+            pltpu.VMEM((2, places, CHUNK), BF16),
+            pltpu.SemaphoreType.DMA((n_ctx - 1,)),
+            pltpu.SemaphoreType.DMA((n_ctx - 1,)),
+            pltpu.SemaphoreType.DMA,
+            pltpu.SemaphoreType.DMA((3,)),
+            pltpu.SemaphoreType.DMA((3,)),
+            pltpu.SemaphoreType.DMA((2,)),
+            pltpu.SemaphoreType.DMA((2,)),
+        ],
+        nbytes=120 << 20,
+    )(dsend, x_rows, dy_rows, came, branch, ffn_in, dlogits, expert_mid)
+
+    late_width = PACKED + D
+    first_width = late_width // 2 // LANES * LANES
+    sizes = [(local, 2 * FS), (FS // members, D)]
+    sizes += [(local, first_width), (local, late_width - first_width)]
+    splits = [ring_split(r, c, 2 * n_ctx) + (c,) for r, c in sizes]
+    tiles = [(2 * n_ctx, t[2], t[3]) for t in splits]
+    grad_x, dense_sum, so_sum, last_sum, expert_sum = comm_call(
+        functools.partial(last_kernel, n_ctx, members, heads, experts, splits),
+        (
+            shape((rows, D), F32),
+            shape((local, 2 * FS), BF16),
+            shape((FS // members, D), BF16),
+            shape((local, late_width), BF16),
+            shape((3, local, FF), BF16),
+        ),
+        0,
+        in_specs=[whole] * 16,
+        out_specs=[whole] * 5,
+        scratch_shapes=[pltpu.VMEM(t, BF16) for t in tiles * 3]
+        + [pltpu.VMEM((members >> (b + 1), local, late_width), BF16) for b in range(bits)]
+        + [pltpu.VMEM((3, members >> (b + 1), local, FF), BF16) for b in range(1, bits)]
+        + [
+            pltpu.VMEM((rows, 3 * D), BF16),
+            pltpu.VMEM((D, rows), BF16),
+            pltpu.VMEM((D, rows), BF16),
+            pltpu.VMEM((D, LANES), F32),
+            pltpu.VMEM((members, local, late_width), BF16),
+            pltpu.SemaphoreType.DMA((4, 2, 2 * n_ctx - 2)),
+            pltpu.SemaphoreType.DMA((4, 2, 2 * n_ctx - 2)),
+            pltpu.SemaphoreType.DMA((bits,)),
+            pltpu.SemaphoreType.DMA((bits,)),
+            pltpu.SemaphoreType.DMA((3, max(1, bits - 1))),
+            pltpu.SemaphoreType.DMA((3, max(1, bits - 1))),
+        ],
+        nbytes=200 << 20,
+    )(
+        drecv,
+        cos,
+        sin,
+        attn_in,
+        x,
+        qkv_pack,
+        tail,
+        dres,
+        out_grad,
+        grad_router,
+        dgain_two,
+        dense_part,
+        dense_other,
+        so_part,
+        so_other,
+        expert_sum,
+    )
 
     res_came = exchange(expert_res.reshape(n_ctx, -1, D)).reshape(places, D)
     output = call(
@@ -795,29 +1350,32 @@
         nbytes=5 << 20,
     )(residual, shared_res, gates, target, live, res_came)
 
-    scatter = functools.partial(
-        lax.psum_scatter, axis_name="fsdp", scatter_dimension=0, tiled=True
-    )
-    expert_sum = scatter(expert_grad)
-    dense_part, so_part = scatter(dense_pack), scatter(grad_so)
-    dense_sum, so_sum = lax.psum((dense_part, so_part), "ctx")
-    last_sum = lax.psum(scatter(last_pack), "ctx")
-    last_sum = last_sum.astype(F32)
-    dense_sum = dense_sum.astype(F32)
-    expert_sum = expert_sum.astype(F32)
-    small = last_sum[:, 3 * D :]
+    small = last_sum[:, 3 * D : PACKED].astype(F32)
+    grad_qkv, grad_out, grad_si, grad_so, grad_ei, grad_eo = call(
+        widen_kernel,
+        (
+            shape((local, 3 * D), F32),
+            shape((local, D), F32),
+            shape((local, 2 * FS), F32),
+            shape((FS // members, D), F32),
+            shape((local, 2 * FF), F32),
+            shape((FF, local), F32),
+        ),
+        flops=0,
+        nbytes=21 << 20,
+    )(last_sum, dense_sum, so_sum, expert_sum)
     return (
         output[None],
         grad_x[None],
         small[:, experts],
-        last_sum[:, 0 : 3 * D],
-        dense_sum[:, 0:D],
+        grad_qkv,
+        grad_out,
         small[:, experts + 1],
         small[:, 0:experts],
-        dense_sum[:, D:],
-        so_sum.astype(F32),
-        expert_sum[None, :, 0 : 2 * FF],
-        expert_sum[:, 2 * FF :].T[None],
+        grad_si,
+        grad_so,
+        grad_ei[None],
+        grad_eo[None],
     )
 
 

time: 715 us -> 491 us (0.69)
  waiting for transfers between devices: 437 us -> 123 us
  Pallas kernels: 147 us -> 287 us
  blocking collectives: 56.1 us -> 0 us
  starting transfers between devices: 24.5 us -> 32.7 us
    reduce_scatter x4 -> x0, waiting for transfers between devices: 157 us -> none  [the longest x1 76.1 us: on_device(): expert_sum = scatter(expert_grad)]
    psum x1 -> x0, waiting for transfers between devices: 141 us -> none  [on_device(): dense_sum, so_sum = lax.psum((dense_part, so_part), 'ctx')]
    pallas_call x4 -> x5, Pallas kernels: 46.2 us -> 184 us  [the longest x1 113 us: on_device(): comm_call(functools.partial(last_kernel, n_ctx, members, heads, experts,...]
    all_to_all x2 -> x0, blocking collectives: 56.1 us -> none  [the longest x1 37.3 us: on_device(): exchange(outgoing.reshape(n_ctx, -1, D + LANES)).reshape(places, D + LANES)]
    all_to_all x1, waiting for transfers between devices: 18.8 us -> 5.38 us  [on_device(): exchange(expert_dx.reshape(n_ctx, -1, D + LANES)).reshape(places, D + LANES)]
    all_gather x1, waiting for transfers between devices: 26.8 us -> 15.4 us  [on_device(): qkv_pack = gather(first_pack)]
    squeeze x0 -> x2, other arithmetic: none -> 8.73 us  [rest_of(): return (keep[0], came_in[0])]
    all_to_all x2 -> x3, starting transfers between devices: 7.23 us -> 14.7 us  [the longest x1 7.34 us: on_device(): dy_rows = exchange(dy_send.reshape(n_ctx, -1, D)).reshape(places, D)]
  transfers between devices with their start and end apart: 15 -> 15, of which waited for: 10 -> 7; matrix products, arithmetic and copies ran while one was open for 2% -> 4% of each run, Pallas kernels for 21% -> 58%
where the time goes in v3:
time: 491 us; the launch traced here: 492 us
  Pallas kernels  287 us (58%)
  waiting for transfers between devices  123 us (25%)
  starting transfers between devices  32.7 us (7%)
  local copies, waits for them, and re-layouts  18.3 us (4%)
  other arithmetic  16 us (3%)
  between operations  15.3 us (3%)
    pallas_call x1, Pallas kernels, on_device(): comm_call(functools.partial(last_kernel, n_ctx, members, heads, experts,...  113 us
    pallas_call x1, Pallas kernels, on_device(): comm_call(functools.partial(back_exchange_kernel, n_ctx, members, heads),...  46.7 us
    all_to_all x1, waiting for transfers between devices, on_device(): recv = exchange(send)  35.9 us
    all_to_all x1, waiting for transfers between devices, on_device(): exchange(outgoing.reshape(n_ctx, -1, D + LANES)).reshape(places, D + LANES)  32.4 us
    pallas_call x1, Pallas kernels, on_device(): call(functools.partial(attend_back_kernel, n_ctx, share), shape((n_ctx, r...  24.8 us
    pallas_call x1, Pallas kernels, on_device(): call(expert_kernel, (shape((places, D + LANES), BF16), shape((places, D),...  23.4 us
    pallas_call x1, Pallas kernels, on_device(): call(functools.partial(attend_kernel, n_ctx, share), (shape((n_ctx, rows,...  21.4 us
    all_gather x1, waiting for transfers between devices, on_device(): qkv_pack = gather(first_pack)  15.4 us
  transfers between devices with their start and end apart: 15, of which 7 were waited for; matrix products, arithmetic and copies ran while one was open for 4% of the time, Pallas kernels for 58%

profile of v3, /device:TPU:0, one launch (start us, length us, event | category | flops | bytes accessed | tf_op | source)
XLA Modules:
  0.0 492.1 jit_solution(10059895856060921022)
XLA Ops:
  7.2 0.0 all-gather.5.cloned.1.call-start
  7.2 0.7 broadcast_in_dim.48
  8.0 0.7 broadcast_in_dim.49
  8.7 0.8 copy.42
  9.6 2.2 concatenate.16
  11.8 0.0 all-gather.7.cloned.1.call-start
  11.9 0.7 all-gather.7.cloned.1.call-update
  12.6 0.0 all-gather.9.cloned.1.call-start
  12.6 3.0 pad_maximum_fusion
  16.3 0.8 copy.46
  17.1 0.6 dynamic_slice.3
  18.4 0.7 fusion.2.live_ref
  19.0 3.2 shard_map.231
  22.2 7.3 %all-to-all-start = ((bf16[8,96,768]{2,1,0:T(8,128)(2,1)}), bf16[8,96,768]{2,1,0:T(8,128)(2,1)S(1)}, u32[]{:S(2)}, u32[]{:S(2)}) async-start(bf16[8,96,768]{2,1,0:T(8,128)(2,1)} %bitcast.46), calls=%async_computation | async-start | bytes 2359296 | tf_op jit(solution)/shard_map/all_to_all | solution.py:1005
  29.6 0.5 fusion.3
  30.1 1.0 pad_maximum_fusion.1
  31.1 15.4 %all-gather.5.cloned.1.call-done.w_ref = bf16[768,2432]{1,0:T(8,128)(2,1)} async-done(((bf16[192,2432]{1,0:T(8,128)(2,1)}), bf16[768,2432]{1,0:T(8,128)(2,1)}) %all-gather.5.cloned.1.call-update) | async-done | bytes 3735568 | tf_op jit(solution)/shard_map/all_gather | solution.py:964
  46.5 5.0 %shard_map.230 = (bf16[8,256,384]{2,1,0:T(8,128)(2,1)}, bf16[256,768]{1,0:T(8,128)(2,1)}, f32[128,768]{1,0:T(8,128)}) custom-call(bf16[256,768]{1,0:T(8,128)(2,1)} %bitcast.40, bf16[768,2432]{1,0:T(8,128)(2,1)} %all-gather.5.cloned.1.call-done.w_ref, f32[256,128]{1,0:T(8,128)} %get-tuple-element.174.cos_ref, f32[256,128]{1,0:T(8,128)} %get-tuple-element.175.sin_ref), custom_call_target="tpu_custom_call" | custom-call | flops 905969664 | bytes 6291456 | tf_op jit(solution)/shard_map/pallas_call | solution.py:1007
  51.5 6.6 %all-to-all-done = bf16[8,96,768]{2,1,0:T(8,128)(2,1)S(1)} async-done(((bf16[8,96,768]{2,1,0:T(8,128)(2,1)}), bf16[8,96,768]{2,1,0:T(8,128)(2,1)S(1)}, u32[]{:S(2)}, u32[]{:S(2)}) %all-to-all-start) | async-done | bytes 1179680 | tf_op jit(solution)/shard_map/all_to_all | solution.py:1005
  58.1 1.0 copy-done.2
  59.2 4.3 all-to-all-start.1
  63.5 0.1 select_reduce_fusion
  63.6 0.6 pad_add_fusion.sc
  64.2 35.9 %all-to-all-done.1.recv_ref = bf16[8,256,384]{2,1,0:T(8,128)(2,1)} async-done(((bf16[8,256,384]{2,1,0:T(8,128)(2,1)}), bf16[8,256,384]{2,1,0:T(8,128)(2,1)}, u32[]{:S(2)}, u32[]{:S(2)}) %all-to-all-start.1) | async-done | bytes 1572896 | tf_op jit(solution)/shard_map/all_to_all | solution.py:1018
  100.1 21.4 %shard_map.232 = (bf16[8,256,128]{2,1,0:T(8,128)(2,1)}, f32[8,128,384]{2,1,0:T(8,128)}, f32[8,1,384]{2,1,0:T(1,128)}) custom-call(s32[10]{0:T(128)} %pad_add_fusion.sc, bf16[8,256,384]{2,1,0:T(8,128)(2,1)} %all-to-all-done.1.recv_ref), custom_call_target="tpu_custom_call" | custom-call | flops 3221225472 | bytes 5242880 | tf_op jit(solution)/shard_map/pallas_call | solution.py:1022
  121.5 3.6 all-to-all-start.2
  125.2 0.0 all-gather.11.cloned.1.call-start
  125.2 0.5 all-gather.11.cloned.1.call-update
  125.8 14.1 %all-to-all-done.2.came_ref = bf16[8,256,128]{2,1,0:T(8,128)(2,1)S(1)} async-done(((bf16[8,256,128]{2,1,0:T(8,128)(2,1)}), bf16[8,256,128]{2,1,0:T(8,128)(2,1)S(1)}, u32[]{:S(2)}, u32[]{:S(2)}) %all-to-all-start.2) | async-done | bytes 524320 | tf_op jit(solution)/shard_map/all_to_all | solution.py:1047
  139.8 0.8 copy-done.4
  140.6 5.2 %shard_map.233 = (f32[256,768]{1,0:T(8,128)}, bf16[256,768]{1,0:T(8,128)(2,1)}, f32[256,128]{1,0:T(8,128)}, bf16[768,896]{1,0:T(8,128)(2,1)}) custom-call(bf16[8,256,128]{2,1,0:T(8,128)(2,1)} %copy-done.4, bf16[768,768]{1,0:T(8,128)(2,1)} %all-gather.7.cloned.1.call-done.w_ref, bf16[256,768]{1,0:T(8,128)(2,1)} %bitcast.41, ...), custom_call_target="tpu_custom_call" | custom-call | flops 1308622848 | bytes 5242880 | tf_op jit(solution)/shard_map/pallas_call | solution.py:1055
  145.8 3.8 all-to-all-start.3
  149.6 0.5 shift-left_add_fusion
  150.1 32.4 %all-to-all-done.3 = bf16[8,96,896]{2,1,0:T(8,128)(2,1)S(1)} async-done(((bf16[8,96,896]{2,1,0:T(8,128)(2,1)}), bf16[8,96,896]{2,1,0:T(8,128)(2,1)S(1)}, u32[]{:S(2)}, u32[]{:S(2)}) %all-to-all-start.3) | async-done | bytes 1376288 | tf_op jit(solution)/shard_map/all_to_all | solution.py:1081
  182.5 1.1 copy-done
  183.7 23.4 %shard_map.235 = (bf16[768,896]{1,0:T(8,128)(2,1)}, bf16[768,768]{1,0:T(8,128)(2,1)}, bf16[3,768,2048]{2,1,0:T(8,128)(2,1)}) custom-call(bf16[768,896]{1,0:T(8,128)(2,1)} %bitcast.30, bf16[768,768]{1,0:T(8,128)(2,1)} %bitcast.33, bf16[768,10240]{1,0:T(8,128)(2,1)} %all-gather.9.cloned.1.call-done.wg_ref.wu_ref.wt_ref, ...), custom_call_target="tpu_custom_call" | custom-call | flops 14495514624 | bytes 25165824 | tf_op jit(solution)/shard_map/pallas_call | solution.py:1138
  207.0 3.8 all-to-all-start.4
  210.8 0.0 all-gather.11.cloned.1.call-done.wo_ref
  210.8 14.1 %shard_map.234 = (f32[256,768]{1,0:T(8,128)}, f32[256,768]{1,0:T(8,128)}, bf16[2,256,2048]{2,1,0:T(8,128)(2,1)}, bf16[2,512,768]{2,1,0:T(8,128)(2,1)}, bf16[2,512,768]{2,1,0:T(8,128)(2,1)}) custom-call(s32[4]{0:T(128)} %get-tuple-element.176.sc, bf16[256,768]{1,0:T(8,128)(2,1)} %get-tuple-element.73.x_ref.in_ref, ...), custom_call_target="tpu_custom_call" | custom-call | flops 5637144576 | bytes 14680064 | tf_op jit(solution)/shard_map/pallas_call | solution.py:1089
  224.9 12.9 %shard_map.236 = (bf16[2,192,4096]{2,1,0:T(8,128)(2,1)}, bf16[2,192,4096]{2,1,0:T(8,128)(2,1)}) custom-call(s32[4]{0:T(128)} %get-tuple-element.177.sc, bf16[256,768]{1,0:T(8,128)(2,1)} %get-tuple-element.73.x_ref.in_ref, bf16[2,256,2048]{2,1,0:T(8,128)(2,1)} %get-tuple-element.81.mid_ref), custom_call_target="tpu_custom_call" | custom-call | flops 1610612736 | bytes 9437184 | tf_op jit(solution)/shard_map/pallas_call | solution.py:1120
  237.8 0.5 collective-permute-start.1
  238.3 5.4 %all-to-all-done.4 = bf16[8,96,896]{2,1,0:T(8,128)(2,1)S(1)} async-done(((bf16[8,96,896]{2,1,0:T(8,128)(2,1)}), bf16[8,96,896]{2,1,0:T(8,128)(2,1)S(1)}, u32[]{:S(2)}, u32[]{:S(2)}) %all-to-all-start.4) | async-done | bytes 1376288 | tf_op jit(solution)/shard_map/all_to_all | solution.py:1166
  243.7 1.1 copy-done.1
  244.8 6.0 %shard_map.237 = (bf16[8,256,128]{2,1,0:T(8,128)(2,1)}, f32[256,768]{1,0:T(8,128)}, bf16[256,768]{1,0:T(8,128)(2,1)}, bf16[256,128]{1,0:T(8,128)(2,1)}, f32[1,768]{1,0:T(1,128)}) custom-call(bf16[768,896]{1,0:T(8,128)(2,1)} %bitcast.32, f32[256,768]{1,0:T(8,128)} %get-tuple-element.86.dx_ref, f32[256,768]{1,0:T(8,128)} %get-tuple-element.72.residual_ref, ...), custom_call_target="tpu_custom_call" | custom-call | flops 704643072 | bytes 6291456 | tf_op jit(solution)/shard_map/pallas_call | solution.py:1170
  250.7 3.6 all-to-all-start.5
  254.4 2.9 fusion.1
  257.3 11.7 %all-to-all-done.5.grad_ref = bf16[8,256,128]{2,1,0:T(8,128)(2,1)S(1)} async-done(((bf16[8,256,128]{2,1,0:T(8,128)(2,1)}), bf16[8,256,128]{2,1,0:T(8,128)(2,1)S(1)}, u32[]{:S(2)}, u32[]{:S(2)}) %all-to-all-start.5) | async-done | bytes 524320 | tf_op jit(solution)/shard_map/all_to_all | solution.py:1201
  269.0 0.8 copy-done.11
  269.8 3.6 all-to-all-start.6
  273.5 5.8 %fusion = (bf16[192,4096]{1,0:T(8,128)(2,1)}, bf16[1,192,4096]{2,1,0:T(8,128)(2,1)}) fusion(bf16[2,192,4096]{2,1,0:T(8,128)(2,1)} %collective-permute-done, bf16[2,192,4096]{2,1,0:T(8,128)(2,1)} %get-tuple-element.90), kind=kLoop, calls=%fused_computation.3 | loop fusion | flops 6291456 | bytes 9437184 | tf_op jit(solution)/shard_map/squeeze | solution.py:1227
  279.3 2.0 collective-permute-start.3
  281.3 24.8 %shard_map.239.send_ref = bf16[8,256,384]{2,1,0:T(8,128)(2,1)} custom-call(s32[10]{0:T(128)} %pad_add_fusion.sc, bf16[8,256,384]{2,1,0:T(8,128)(2,1)} %all-to-all-done.1.recv_ref, bf16[8,256,128]{2,1,0:T(8,128)(2,1)} %copy-done.11, f32[8,128,384]{2,1,0:T(8,128)} %get-tuple-element.96.keep_ref, f32[8,1,384]{2,1,0:T(1,128)} %get-tuple-element.97.lse_ref), custom_call_target="tpu_custom_call" | custom-call | flops 4831838208 | bytes 8388608 | tf_op jit(solution)/shard_map/pallas_call | solution.py:1236
  306.2 46.7 %shard_map.240 = (bf16[8,256,384]{2,1,0:T(8,128)(2,1)}, bf16[3,2,192,2048]{3,2,1,0:T(8,128)(2,1)}, bf16[4,192,768]{2,1,0:T(8,128)(2,1)}, f32[768,128]{1,0:T(8,128)}) custom-call(bf16[8,256,384]{2,1,0:T(8,128)(2,1)} %shard_map.239.send_ref, bf16[768,896]{1,0:T(8,128)(2,1)} %bitcast.31, bf16[768,768]{1,0:T(8,128)(2,1)} %bitcast.34, ...), custom_call_target="tpu_custom_call" | custom-call | bytes 125829120 | tf_op jit(solution)/shard_map/pallas_call | solution.py:1260
  352.9 0.8 copy-done.9
  353.8 0.5 copy-done.5
  354.3 113.0 %shard_map.241 = (f32[256,768]{1,0:T(8,128)}, bf16[192,4096]{1,0:T(8,128)(2,1)}, bf16[512,768]{1,0:T(8,128)(2,1)}, bf16[192,3200]{1,0:T(8,128)(2,1)}, bf16[3,192,2048]{2,1,0:T(8,128)(2,1)}) custom-call(bf16[8,256,384]{2,1,0:T(8,128)(2,1)} %get-tuple-element.101.recv_ref, f32[256,128]{1,0:T(8,128)} %get-tuple-element.174.cos_ref, ...), custom_call_target="tpu_custom_call" | custom-call | bytes 209715200 | tf_op jit(solution)/shard_map/pallas_call | solution.py:1297
  467.3 7.7 %shard_map.242 = (f32[192,2304]{1,0:T(8,128)}, f32[192,768]{1,0:T(8,128)}, f32[192,4096]{1,0:T(8,128)}, f32[512,768]{1,0:T(8,128)}, f32[192,4096]{1,0:T(8,128)}, /*index=5*/f32[2048,192]{1,0:T(8,128)}) custom-call(bf16[192,3200]{1,0:T(8,128)(2,1)} %get-tuple-element.111.late_ref, bf16[192,4096]{1,0:T(8,128)(2,1)} %get-tuple-element.112.a_ref, ...), custom_call_target="tpu_custom_call" | custom-call | bytes 22020096 | tf_op jit(solution)/shard_map/pallas_call | solution.py:1354
  475.0 2.8 copy.48
  477.8 0.8 slice_convert_fusion
  478.6 0.7 copy.47
  479.3 0.8 slice_reduce_fusion
  480.1 1.1 copy-done.3
  481.1 3.5 shard_map.238
  484.7 0.9 copy.51
  (36 shorter events, 0.2 us)
Async XLA Ops:
  7.2 39.4 %all-gather.5.cloned.1.call-start = ((), (), s32[]{:S(2)}) async-start(), calls=%async_computation.7 | async-start | bytes 4669440 | tf_op jit(solution)/shard_map/all_gather | solution.py:964
  9.6 3.0 copy-start.7
  9.6 3.0 copy-start.8
  11.8 113.9 %all-gather.7.cloned.1.call-start = ((), (), s32[]{:S(2)}) async-start(), calls=%async_computation.8 | async-start | bytes 1474560 | tf_op jit(solution)/shard_map/all_gather | solution.py:965
  12.6 170.0 %all-gather.9.cloned.1.call-start = ((), (), s32[]{:S(2)}) async-start(), calls=%async_computation.9 | async-start | bytes 19660800 | tf_op jit(solution)/shard_map/all_gather | solution.py:966
  15.7 0.7 copy-start.12
  15.7 1.5 copy-start.14
  22.2 35.9 %all-to-all-start = ((bf16[8,96,768]{2,1,0:T(8,128)(2,1)}), bf16[8,96,768]{2,1,0:T(8,128)(2,1)S(1)}, u32[]{:S(2)}, u32[]{:S(2)}) async-start(bf16[8,96,768]{2,1,0:T(8,128)(2,1)} %bitcast.46), calls=%async_computation | async-start | bytes 2359296 | tf_op jit(solution)/shard_map/all_to_all | solution.py:1005
  58.1 1.0 copy-start.2
  59.2 40.9 %all-to-all-start.1 = ((bf16[8,256,384]{2,1,0:T(8,128)(2,1)}), bf16[8,256,384]{2,1,0:T(8,128)(2,1)}, u32[]{:S(2)}, u32[]{:S(2)}) async-start(bf16[8,256,384]{2,1,0:T(8,128)(2,1)} %get-tuple-element.68), calls=%async_computation.1 | async-start | bytes 3145728 | tf_op jit(solution)/shard_map/all_to_all | solution.py:1018
  121.5 18.3 %all-to-all-start.2 = ((bf16[8,256,128]{2,1,0:T(8,128)(2,1)}), bf16[8,256,128]{2,1,0:T(8,128)(2,1)S(1)}, u32[]{:S(2)}, u32[]{:S(2)}) async-start(bf16[8,256,128]{2,1,0:T(8,128)(2,1)} %get-tuple-element.69), calls=%async_computation.2 | async-start | bytes 1048576 | tf_op jit(solution)/shard_map/all_to_all | solution.py:1047
  125.2 85.7 %all-gather.11.cloned.1.call-start = ((), (), s32[]{:S(2)}) async-start(), calls=%async_computation.10 | async-start | bytes 3932160 | tf_op jit(solution)/shard_map/all_gather | solution.py:969
  139.8 0.8 copy-start.4
  145.8 3.8 copy-start.13
  145.8 36.7 %all-to-all-start.3 = ((bf16[8,96,896]{2,1,0:T(8,128)(2,1)}), bf16[8,96,896]{2,1,0:T(8,128)(2,1)S(1)}, u32[]{:S(2)}, u32[]{:S(2)}) async-start(bf16[8,96,896]{2,1,0:T(8,128)(2,1)} %bitcast.44), calls=%async_computation.3 | async-start | bytes 2752512 | tf_op jit(solution)/shard_map/all_to_all | solution.py:1081
  182.5 1.1 copy-start
  207.0 36.6 %all-to-all-start.4 = ((bf16[8,96,896]{2,1,0:T(8,128)(2,1)}), bf16[8,96,896]{2,1,0:T(8,128)(2,1)S(1)}, u32[]{:S(2)}, u32[]{:S(2)}) async-start(bf16[8,96,896]{2,1,0:T(8,128)(2,1)} %bitcast.43), calls=%async_computation.4 | async-start | bytes 2752512 | tf_op jit(solution)/shard_map/all_to_all | solution.py:1166
  237.8 35.7 %collective-permute-start = (bf16[2,192,4096]{2,1,0:T(8,128)(2,1)}, bf16[2,192,4096]{2,1,0:T(8,128)(2,1)}, u32[]{:S(2)}, u32[]{:S(2)}) collective-permute-start(bf16[2,192,4096]{2,1,0:T(8,128)(2,1)} %get-tuple-element.91), channel_id=1, source_target_pairs={{0,1},{1,0},{2,3},{3,2},{4,5},{5,4},{6,7},{7,6},{8,9},{9,8},{10,11... | collective-permute-start | bytes 9437192 | tf_op jit(solution)/shard_map/ppermute | solution.py:1208
  237.8 16.6 %collective-permute-start.1 = (bf16[2,512,768]{2,1,0:T(8,128)(2,1)}, bf16[2,512,768]{2,1,0:T(8,128)(2,1)}, u32[]{:S(2)}, u32[]{:S(2)}) collective-permute-start(bf16[2,512,768]{2,1,0:T(8,128)(2,1)} %get-tuple-element.93), channel_id=1, source_target_pairs={{0,1},{1,0},{2,3},{3,2},{4,5},{5,4},{6,7},{7,6},{8,9},{9,8},{10,11... | collective-permute-start | bytes 4718600 | tf_op jit(solution)/shard_map/ppermute | solution.py:1208
  243.7 1.1 copy-start.1
  244.8 9.6 %copy-start.6 = (bf16[2,512,768]{2,1,0:T(8,128)(2,1)S(1)}, bf16[2,512,768]{2,1,0:T(8,128)(2,1)}, u32[]{:S(2)}) copy-start(bf16[2,512,768]{2,1,0:T(8,128)(2,1)} %get-tuple-element.92) | copy-start | bytes 4718596
  250.7 18.3 %all-to-all-start.5 = ((bf16[8,256,128]{2,1,0:T(8,128)(2,1)}), bf16[8,256,128]{2,1,0:T(8,128)(2,1)S(1)}, u32[]{:S(2)}, u32[]{:S(2)}) async-start(bf16[8,256,128]{2,1,0:T(8,128)(2,1)} %get-tuple-element.87), calls=%async_computation.5 | async-start | bytes 1048576 | tf_op jit(solution)/shard_map/all_to_all | solution.py:1201
  269.0 0.8 copy-start.11
  269.8 210.3 %all-to-all-start.6 = ((bf16[8,96,768]{2,1,0:T(8,128)(2,1)}), bf16[8,96,768]{2,1,0:T(8,128)(2,1)S(1)}, u32[]{:S(2)}, u32[]{:S(2)}) async-start(bf16[8,96,768]{2,1,0:T(8,128)(2,1)} %bitcast.45), calls=%async_computation.6 | async-start | bytes 2359296 | tf_op jit(solution)/shard_map/all_to_all | solution.py:1345
  279.3 73.6 %collective-permute-start.2 = (bf16[1,192,4096]{2,1,0:T(8,128)(2,1)}, bf16[1,192,4096]{2,1,0:T(8,128)(2,1)S(1)}, u32[]{:S(2)}, u32[]{:S(2)}) collective-permute-start(bf16[1,192,4096]{2,1,0:T(8,128)(2,1)} %get-tuple-element.107), channel_id=1, source_target_pairs={{0,2},{1,3},{2,0},{3,1},{4,6},{5,7},{6,4},{7,5},{8,10},{9,11},{10,... | collective-permute-start | bytes 4718600 | tf_op jit(solution)/shard_map/ppermute | solution.py:1208
  279.3 73.6 %collective-permute-start.3 = (bf16[1,512,768]{2,1,0:T(8,128)(2,1)}, bf16[1,512,768]{2,1,0:T(8,128)(2,1)S(1)}, u32[]{:S(2)}, u32[]{:S(2)}) collective-permute-start(bf16[1,512,768]{2,1,0:T(8,128)(2,1)} %get-tuple-element.108), channel_id=1, source_target_pairs={{0,2},{1,3},{2,0},{3,1},{4,6},{5,7},{6,4},{7,5},{8,10},{9,11},{10,... | collective-permute-start | bytes 2359304 | tf_op jit(solution)/shard_map/ppermute | solution.py:1208
  352.9 0.9 copy-start.9
  352.9 1.4 copy-start.5
  480.1 1.1 copy-start.3
  481.1 3.6 copy-start.10
Sparse Core Ops, SparseCore 0:
  11.9 34.5 all-gather.4
  48.1 17.4 all-gather.6
  67.2 99.9 all-gather.8
  168.6 28.5 all-gather.10

commit v4 on v3

--- a/solution.py
+++ b/solution.py
@@ -297,72 +297,6 @@
     return silu * u, da * u * sig * (1.0 + g * (1.0 - sig)), da * silu
 
 
-def store_shards(sc, first_row, value, keep_ref, give_ref):
-    half, shard, _ = keep_ref.shape
-    piece = min(shard, value.shape[0])
-    for u in range(value.shape[0] // piece):
-        row = first_row + u * piece
-        j = sc[row // shard]
-        inside = pl.multiple_of(row % shard, piece)
-
-        @pl.when(j < half)
-        def _():
-            keep_ref[j, pl.ds(inside, piece), :] = value[u * piece : (u + 1) * piece]
-
-        @pl.when(j >= half)
-        def _():
-            give_ref[j - half, pl.ds(inside, piece), :] = value[u * piece : (u + 1) * piece]
-
-
-def shared_kernel(
-    sc, x_ref, dy_ref, wg_ref, wu_ref, wo_ref, res_ref, dx_ref, mid_ref, keep_ref, give_ref, res_acc, dx_acc
-):
-    c = pl.program_id(0)
-
-    @pl.when(c == 0)
-    def _():
-        res_acc[...] = jnp.zeros_like(res_acc)
-        dx_acc[...] = jnp.zeros_like(dx_acc)
-
-    x, dy = x_ref[...], dy_ref[...]
-    wg, wu, wo = wg_ref[...], wu_ref[...], wo_ref[...]
-    act, dg, du = gated(dot(x, wg), dot(x, wu), dot_nt(dy, wo))
-    act, dg, du = act.astype(BF16), dg.astype(BF16), du.astype(BF16)
-    res_acc[...] += dot(act, wo)
-    dx_acc[...] += dot_nt(dg, wg) + dot_nt(du, wu)
-    mid_ref[0] = dg
-    mid_ref[1] = du
-    store_shards(sc, c * CHUNK, dot_tn(act, dy).astype(BF16), keep_ref, give_ref)
-
-    @pl.when(c == pl.num_programs(0) - 1)
-    def _():
-        res_ref[...] = res_acc[...]
-        dx_ref[...] = dx_acc[...]
-
-
-def turn_shards(sc, x, raw, xt):
-    raw[...] = x.T
-    shard = raw.shape[0] // sc.shape[0]
-    for j in range(sc.shape[0]):
-        row = pl.multiple_of(sc[j] * shard, 16)
-        xt[j * shard : (j + 1) * shard, :] = raw[pl.ds(row, shard), :]
-
-
-def split_shards(value, keep_ref, give_ref):
-    half, shard, _ = keep_ref.shape
-    for j in range(half):
-        keep_ref[j] = value[j * shard : (j + 1) * shard]
-        give_ref[j] = value[(half + j) * shard : (half + j + 1) * shard]
-
-
-def shared_grad_kernel(sc, x_ref, mid_ref, keep_ref, give_ref, raw, xt):
-    @pl.when((pl.program_id(0) == 0) & (pl.program_id(1) == 0))
-    def _():
-        turn_shards(sc, x_ref[...], raw, xt)
-
-    split_shards(dot(xt[...], mid_ref[0]).astype(BF16), keep_ref, give_ref)
-
-
 def expert_kernel(
     x_ref, dy_ref, wg_ref, wu_ref, wt_ref, dx_ref, res_ref, mid_ref, dx_acc, res_acc, dgate
 ):
@@ -394,27 +328,236 @@
         dx_ref[:, D:] = part_lanes(dgate[:, 0:1], lanes_of(dgate.shape[0]))
 
 
-def combine_kernel(
+def ring_split(rows, columns, pieces):
+    down = 1
+    while 2 * down <= pieces and rows % (32 * down) == 0:
+        down *= 2
+    across = pieces // down
+    width = -(-columns // (LANES * across)) * LANES
+    return down, across, rows // down, width
+
+
+def ring_place(position, n):
+    half = n // 2
+    return jnp.where(position < half, 2 * position, 2 * (n - 1 - position) + 1)
+
+
+def flipped(index, mask):
+    for b in range(mask.bit_length()):
+        if mask >> b & 1:
+            index = index + (1 << b) - 2 * (1 << b) * (index // (1 << b) % 2)
+    return index
+
+
+def mirrored(members):
+    bits = members.bit_length() - 1
+    return [int(format(j, "b").zfill(bits)[::-1], 2) for j in range(members)]
+
+
+def shard_rows(members, shard):
+    fsdp = lax.axis_index("fsdp")
+    return [pl.multiple_of(flipped(fsdp, m) * shard, 16) for m in mirrored(members)]
+
+
+def remote(source, target, send_sem, recv_sem, peer):
+    return pltpu.make_async_remote_copy(
+        src_ref=source,
+        dst_ref=target,
+        send_sem=send_sem,
+        recv_sem=recv_sem,
+        device_id=peer,
+        device_id_type=pl.DeviceIdType.MESH,
+    )
+
+
+def greet(peers):
+    barrier = pltpu.get_barrier_semaphore()
+    for peer in peers:
+        pl.semaphore_signal(barrier, inc=1, device_id=peer, device_id_type=pl.DeviceIdType.MESH)
+    pl.semaphore_wait(barrier, len(peers))
+
+
+def mates_of(members):
+    ctx, fsdp = lax.axis_index("ctx"), lax.axis_index("fsdp")
+    return [(ctx, flipped(fsdp, 1 << b)) for b in range(members.bit_length() - 1)]
+
+
+def row_peers(n):
+    ctx, fsdp = lax.axis_index("ctx"), lax.axis_index("fsdp")
+    return [(lax.rem(ctx + d, n), fsdp) for d in range(1, n)]
+
+
+def loop(body, low, high):
+    lax.fori_loop(low, high, lambda s, carry: (body(s), carry)[1], 0)
+
+
+def add_into(target, j, other):
+    target[j] = (target[j].astype(F32) + other[j].astype(F32)).astype(BF16)
+
+
+def shared_kernel(
+    n,
+    members,
     heads,
     experts,
-    came_ref,
-    dx_ref,
+    send_ref,
+    in_ref,
+    dout_ref,
     residual_ref,
-    dout_ref,
     gates_ref,
     routes_ref,
     target_ref,
     tail_ref,
     w_ref,
-    send_ref,
+    wide_ref,
+    back_ref,
+    recv_ref,
+    res_ref,
     dres_ref,
     branch_ref,
     dlogits_ref,
     dgain_ref,
+    a_keep,
+    a_give,
+    b_keep,
+    b_give,
+    came,
+    packets,
+    mids,
+    dx_acc,
+    a_all,
+    b_all,
+    a_caught,
+    b_caught,
+    raw,
+    xt,
+    gate_buf,
+    up_buf,
+    back_buf,
+    send_sem,
+    recv_sem,
+    own_sem,
+    packet_send,
+    packet_recv,
+    a_sem,
+    b_sem,
+    w_sem,
 ):
-    pick = picks(target_ref, came_ref.shape[0])
+    ctx, fsdp = lax.axis_index("ctx"), lax.axis_index("fsdp")
+    bits = members.bit_length() - 1
+    peers = row_peers(n)
+    mate = mates_of(members)[0]
+    greet(peers + [mate])
+    block = send_ref.shape[0] // n
+
+    def block_at(p):
+        return pl.ds(pl.multiple_of(p * block, 16), block)
+
+    own = pltpu.make_async_copy(send_ref.at[block_at(ctx)], came.at[block_at(ctx)], own_sem.at[0])
+    own.start()
+    copies = [
+        remote(
+            send_ref.at[block_at(p[0])], came.at[block_at(ctx)], send_sem.at[d], recv_sem.at[d], p
+        )
+        for d, p in enumerate(peers)
+    ]
+    for c in copies:
+        c.start()
+
+    steps = FS // CHUNK
+
+    def fetch(c, slot):
+        at = pl.ds(pl.multiple_of(c * CHUNK, CHUNK), CHUNK)
+        up = pl.ds(pl.multiple_of(FS + c * CHUNK, CHUNK), CHUNK)
+        return [
+            pltpu.make_async_copy(wide_ref.at[:, at], gate_buf.at[slot], w_sem.at[slot, 0]),
+            pltpu.make_async_copy(wide_ref.at[:, up], up_buf.at[slot], w_sem.at[slot, 1]),
+            pltpu.make_async_copy(back_ref.at[at], back_buf.at[slot], w_sem.at[slot, 2]),
+        ]
+
+    for f in fetch(0, 0):
+        f.start()
+    res_ref[...] = jnp.zeros_like(res_ref)
+    dx_acc[...] = jnp.zeros_like(dx_acc)
+    b_shard = FS // members
+    piece = b_all.shape[2]
+
+    def ffn_step(c):
+        slot = lax.rem(c, 2)
+        for f in fetch(c, slot):
+            f.wait()
+
+        @pl.when(c + 1 < steps)
+        def _():
+            for f in fetch(c + 1, 1 - slot):
+                f.start()
+
+        x, dy = in_ref[...], dout_ref[...]
+        wg, wu, wo = gate_buf[slot], up_buf[slot], back_buf[slot]
+        act, dg, du = gated(dot(x, wg), dot(x, wu), dot_nt(dy, wo))
+        act, dg, du = act.astype(BF16), dg.astype(BF16), du.astype(BF16)
+        res_ref[...] += dot(act, wo)
+        dx_acc[...] += dot_nt(dg, wg) + dot_nt(du, wu)
+        mids[c] = dg
+        mids[steps + c] = du
+        value = dot_tn(act, dy).astype(BF16)
+        span = min(piece, CHUNK)
+        for u in range(CHUNK // span):
+            row = c * CHUNK + u * span
+            t = row // b_shard
+            j = sum(
+                lax.rem(fsdp // (1 << b) + t // (1 << b), 2) * (1 << (bits - 1 - b))
+                for b in range(bits)
+            )
+            inside = lax.rem(row, b_shard)
+            top = pl.multiple_of(lax.rem(inside, piece), 16)
+            b_all[inside // piece, j, pl.ds(top, span), :] = value[u * span : (u + 1) * span]
+
+    loop(ffn_step, 0, steps)
+    half, quarter = members // 2, members // 4
+
+    def a_swap(i):
+        return remote(
+            a_all.at[i, pl.ds(half, half)], a_caught.at[i], a_sem.at[i, 0], a_sem.at[i, 1], mate
+        )
+
+    def b_swap(i):
+        return remote(
+            b_all.at[i, pl.ds(half, half)], b_caught.at[i], b_sem.at[i, 0], b_sem.at[i, 1], mate
+        )
+
+    for i in range(2):
+        b_swap(i).start()
+    rows = shard_rows(members, D // members)
+    shard = D // members
+    raw[...] = in_ref[...].T
+    for j in range(members):
+        xt[j * shard : (j + 1) * shard, :] = raw[pl.ds(rows[j], shard), :]
+    for i in range(2):
+
+        def grad_step(c, i=i):
+            value = dot(xt[...], mids[i * steps + c]).astype(BF16)
+            column = pl.ds(pl.multiple_of(c * CHUNK, CHUNK), CHUNK)
+            for j in range(members):
+                a_all[i, j, :, column] = value[j * shard : (j + 1) * shard]
+
+        loop(grad_step, 0, steps)
+        a_swap(i).start()
+    for i in range(2):
+        b_swap(i).wait_recv()
+        for j in range(half):
+            total = (b_all[i, j].astype(F32) + b_caught[i, j].astype(F32)).astype(BF16)
+            if j < quarter:
+                b_keep[i, j] = total
+            else:
+                b_give[i, j - quarter] = total
+    for c in copies:
+        c.wait()
+    own.wait()
+
+    pick = picks(target_ref, came.shape[0])
     gates = [gates_ref[:, k : k + 1] for k in range(2)]
-    parts = came_ref[:, D:]
+    parts = came[:, D:]
     dgate = [jnp.sum(dot(pick[k], parts), axis=-1, keepdims=True) for k in range(2)]
     mean = gates[0] * dgate[0] + gates[1] * dgate[1]
     lane = lanes_of(pick[0].shape[0])
@@ -424,85 +567,40 @@
     ).astype(BF16)
     dlogits_ref[...] = dlogits
     tail = tail_ref[...]
-    dffn = dot(pick[0] + pick[1], came_ref[:, 0:D]) + dx_ref[...] + dot(dlogits, tail.astype(BF16))
+    dffn = dot(pick[0] + pick[1], came[:, 0:D]) + dx_acc[...] + dot(dlogits, tail.astype(BF16))
     residual = residual_ref[...]
     inv = lax.rsqrt(jnp.mean(residual * residual, axis=-1, keepdims=True) + norm_eps)
     scaled = dffn * tail[experts + 1 : experts + 2, :]
     total = jnp.mean(scaled * residual, axis=-1, keepdims=True)
     dres = dout_ref[...].astype(F32) + inv * scaled - residual * inv * inv * inv * total
-    dres_ref[...] = dres
-    dgain_ref[...] = jnp.sum(dffn * residual * inv, axis=0, keepdims=True)
     branch = dres.astype(BF16)
     branch_ref[...] = branch
     for d, head in enumerate(heads):
-        send_ref[d] = dot_nt(branch, w_ref[64 * head : 64 * head + LANES, :]).astype(BF16)
-
-
-def ring_split(rows, columns, pieces):
-    down = 1
-    while 2 * down <= pieces and rows % (32 * down) == 0:
-        down *= 2
-    across = pieces // down
-    width = -(-columns // (LANES * across)) * LANES
-    return down, across, rows // down, width
-
-
-def ring_place(position, n):
-    half = n // 2
-    return jnp.where(position < half, 2 * position, 2 * (n - 1 - position) + 1)
-
-
-def flipped(index, mask):
-    for b in range(mask.bit_length()):
-        if mask >> b & 1:
-            index = index + (1 << b) - 2 * (1 << b) * (index // (1 << b) % 2)
-    return index
-
-
-def mirrored(members):
-    bits = members.bit_length() - 1
-    return [int(format(j, "b").zfill(bits)[::-1], 2) for j in range(members)]
-
-
-def shard_rows(members, shard):
-    fsdp = lax.axis_index("fsdp")
-    return [pl.multiple_of(flipped(fsdp, m) * shard, 16) for m in mirrored(members)]
-
-
-def remote(source, target, send_sem, recv_sem, peer):
-    return pltpu.make_async_remote_copy(
-        src_ref=source,
-        dst_ref=target,
-        send_sem=send_sem,
-        recv_sem=recv_sem,
-        device_id=peer,
-        device_id_type=pl.DeviceIdType.MESH,
-    )
-
-
-def greet(peers):
-    barrier = pltpu.get_barrier_semaphore()
-    for peer in peers:
-        pl.semaphore_signal(barrier, inc=1, device_id=peer, device_id_type=pl.DeviceIdType.MESH)
-    pl.semaphore_wait(barrier, len(peers))
-
-
-def mates_of(members):
-    ctx, fsdp = lax.axis_index("ctx"), lax.axis_index("fsdp")
-    return [(ctx, flipped(fsdp, 1 << b)) for b in range(members.bit_length() - 1)]
-
-
-def row_peers(n):
-    ctx, fsdp = lax.axis_index("ctx"), lax.axis_index("fsdp")
-    return [(lax.rem(ctx + d, n), fsdp) for d in range(1, n)]
-
-
-def loop(body, low, high):
-    lax.fori_loop(low, high, lambda s, carry: (body(s), carry)[1], 0)
-
-
-def add_into(target, j, other):
-    target[j] = (target[j].astype(F32) + other[j].astype(F32)).astype(BF16)
+        packets[d] = dot_nt(branch, w_ref[64 * head : 64 * head + LANES, :]).astype(BF16)
+    own = pltpu.make_async_copy(packets.at[ctx], recv_ref.at[ctx], own_sem.at[1])
+    own.start()
+    copies = [
+        remote(packets.at[p[0]], recv_ref.at[ctx], packet_send.at[d], packet_recv.at[d], p)
+        for d, p in enumerate(peers)
+    ]
+    for c in copies:
+        c.start()
+    dres_ref[...] = dres
+    dgain_ref[...] = jnp.sum(dffn * residual * inv, axis=0, keepdims=True)
+    for i in range(2):
+        a_swap(i).wait_recv()
+        for j in range(half):
+            total = (a_all[i, j].astype(F32) + a_caught[i, j].astype(F32)).astype(BF16)
+            if j < quarter:
+                a_keep[i, j] = total
+            else:
+                a_give[i, j - quarter] = total
+    for c in copies:
+        c.wait()
+    own.wait()
+    for i in range(2):
+        a_swap(i).wait_send()
+        b_swap(i).wait_send()
 
 
 def back_exchange_kernel(
@@ -516,11 +614,18 @@
     branch_ref,
     in_ref,
     dlogits_ref,
+    residual_ref,
+    shared_ref,
+    gates_ref,
+    target_ref,
+    live_ref,
+    res_ref,
     mid_ref,
     recv_ref,
     sum_ref,
     out_grad_ref,
     router_ref,
+    output_ref,
     give,
     caught,
     crossed,
@@ -615,6 +720,10 @@
     for j in range(members):
         out_grad_ref[j] = acc[pl.ds(rows[j], shard), :].astype(BF16)
     router_ref[...] = dot_tn(in_ref[...], dlogits_ref[...])
+    pick = picks(target_ref, res_ref.shape[0])
+    came = res_ref[...]
+    mixture = gates_ref[:, 0:1] * dot(pick[0], came) + gates_ref[:, 1:2] * dot(pick[1], came)
+    output_ref[...] = (live_ref[...] * (residual_ref[...] + shared_ref[...] + mixture)).astype(BF16)
     swap(parts - 1).wait_recv()
     for j in range(half):
         add_into(sum_ref.at[parts - 1], j, caught.at[parts - 1])
@@ -659,11 +768,15 @@
 ):
     bits = members.bit_length() - 1
     streams = len(splits)
-    own, back, full = (scratch[k * streams : (k + 1) * streams] for k in range(3))
-    scratch = scratch[3 * streams :]
-    caught, e_caught = scratch[0:bits], scratch[bits : 2 * bits - 1]
-    dproj, raw, turned, small, pack = scratch[2 * bits - 1 : 2 * bits + 4]
-    send_sem, recv_sem, level_send, level_recv, e_send, e_recv = scratch[2 * bits + 4 :]
+    own, full, back_up, back_down = (scratch[k * streams : (k + 1) * streams] for k in range(4))
+    back = (back_up, back_down)
+    scratch = scratch[4 * streams :]
+    packs, scratch = scratch[0:4], scratch[4:]
+    caught = [scratch[4 * b : 4 * b + 4] for b in range(bits)]
+    scratch = scratch[4 * bits :]
+    e_caught, scratch = scratch[0 : bits - 1], scratch[bits - 1 :]
+    dproj, raw, turned, small = scratch[0:4]
+    send_sem, recv_sem, level_send, level_recv, e_send, e_recv = scratch[4:]
     ctx, fsdp = lax.axis_index("ctx"), lax.axis_index("fsdp")
     here = jnp.where(ctx % 2 == 0, ctx // 2, n - 1 - ctx // 2)
     ahead = (ring_place(lax.rem(here + 1, n), n), fsdp)
@@ -673,16 +786,24 @@
     shard = D // members
     parts = e_ref.shape[0]
 
-    def level_copy(b):
+    def level_copy(p, b):
         count = members >> (b + 1)
         return remote(
-            pack.at[pl.ds(count, count)], caught[b], level_send.at[b], level_recv.at[b], mates[b]
+            packs[p].at[pl.ds(count, count)],
+            caught[b][p],
+            level_send.at[p, b],
+            level_recv.at[p, b],
+            mates[b],
         )
 
-    def level_add(b):
-        level_copy(b).wait_recv()
+    def level_add(p, b):
+        level_copy(p, b).wait_recv()
         for j in range(members >> (b + 1)):
-            add_into(pack, j, caught[b])
+            add_into(packs[p], j, caught[b][p])
+
+    def level_next(p):
+        level_add(p, 0)
+        level_copy(p, 1).start()
 
     def e_copy(i, b):
         count = members >> (b + 1)
@@ -728,15 +849,18 @@
             if have > 0:
                 ref[top : top + height, skip + start : skip + start + have] = full[i][p, :, 0:have]
 
-    def chunk(direction, steps):
-        if direction == 0:
-            return lax.rem(here + 4 * n - steps, n)
-        return n + lax.rem(here + steps, n)
+    long, short = n // 2, n - 1 - n // 2
+
+    def hops(i, direction):
+        return long if direction == i % 2 else short
+
+    def place(direction, steps):
+        return lax.rem(here + (steps if direction == 0 else 2 * n - steps), n)
 
     def copy(i, direction, step, source, target, slot):
         return remote(
-            source[i].at[slot],
-            target[i].at[slot],
+            source.at[slot],
+            target.at[slot],
             send_sem.at[i, direction, step],
             recv_sem.at[i, direction, step],
             ahead if direction == 0 else behind,
@@ -744,39 +868,75 @@
 
     def first(i):
         for direction in range(2):
-            copy(i, direction, 0, own, back, chunk(direction, 1)).start()
+            slot = place(direction, hops(i, direction))
+            copy(i, direction, 0, own[i], back[direction][i], slot).start()
 
     def reduce_step(i, s):
         for direction in range(2):
-            slot = chunk(direction, 1 + s)
-            copy(i, direction, s - 1, own, back, slot).wait_recv()
-            add_into(back[i], slot, own[i])
-            copy(i, direction, s, back, back, slot).start()
+            count = hops(i, direction)
+            if s < count:
+                slot = place(direction, count - s)
+                buffer = back[direction][i]
+                copy(i, direction, s - 1, buffer, buffer, slot).wait_recv()
+                add_into(buffer, slot, own[i])
+                copy(i, direction, s, buffer, buffer, slot).start()
 
     def turn(i):
         for direction in range(2):
-            slot = chunk(direction, n)
-            copy(i, direction, n - 2, own, back, slot).wait_recv()
-            full[i][slot] = (back[i][slot].astype(F32) + own[i][slot].astype(F32)).astype(BF16)
-            copy(i, direction, n - 1, full, full, slot).start()
+            buffer = back[direction][i]
+            copy(i, direction, hops(i, direction) - 1, buffer, buffer, here).wait_recv()
+        full[i][here] = (
+            own[i][here].astype(F32) + back_up[i][here].astype(F32) + back_down[i][here].astype(F32)
+        ).astype(BF16)
+        for direction in range(2):
+            copy(i, direction, long, full[i], full[i], here).start()
 
     def gather_step(i, s):
         for direction in range(2):
-            slot = chunk(direction, s)
-            copy(i, direction, n - 2 + s, full, full, slot).wait_recv()
-            copy(i, direction, n - 1 + s, full, full, slot).start()
+            if s < hops(i, direction):
+                slot = place(1 - direction, s)
+                copy(i, direction, long + s - 1, full[i], full[i], slot).wait_recv()
+                copy(i, direction, long + s, full[i], full[i], slot).start()
 
     def end(i):
         for direction in range(2):
-            copy(i, direction, 2 * n - 3, full, full, chunk(direction, n - 1)).wait_recv()
-
-    dense, late = [0, 1], list(range(2, streams))
-    e_copy(1, 1).start()
-    load(0, a_ref, other=a_other)
-    first(0)
-    load(1, b_ref, other=b_other)
-    first(1)
-
+            count = hops(i, direction)
+            slot = place(1 - direction, count)
+            copy(i, direction, long + count - 1, full[i], full[i], slot).wait_recv()
+
+    def drain(i):
+        for direction in range(2):
+
+            def sent(step, direction=direction):
+                copy(i, direction, step, own[i], full[i], 0).wait_send()
+
+            loop(sent, 0, hops(i, direction))
+            loop(sent, long, long + hops(i, direction))
+
+    def steps_of(i):
+        done = [functools.partial(reduce_step, i, s) for s in range(1, long)]
+        done.append(functools.partial(turn, i))
+        done += [functools.partial(gather_step, i, s) for s in range(1, long)]
+        done.append(functools.partial(end, i))
+        return done
+
+    for i in range(2):
+        load(i, a_ref.at[i], 0, a_other.at[i])
+        first(i)
+    for i in range(2):
+        load(2 + i, b_ref.at[i], 0, b_other.at[i])
+        first(2 + i)
+    waiting = [steps_of(i) for i in range(4)]
+
+    def dense_step():
+        for queue in waiting[0:4]:
+            if queue:
+                queue.pop(0)()
+
+    rows = shard_rows(members, shard)
+    raw[...] = in_ref[...].T
+    for j in range(members):
+        turned[j * shard : (j + 1) * shard, :] = raw[pl.ds(rows[j], shard), :]
     lane = lanes_of(x_ref.shape[0])
     cos, sin = cos_ref[...], sin_ref[...]
     for part in range(3):
@@ -795,14 +955,13 @@
                 t = t.astype(BF16).astype(F32)
                 t = t * cos - partner(t, lane) * sin
             dproj[:, part * D + g * LANES : part * D + (g + 1) * LANES] = t.astype(BF16)
-    rows = shard_rows(members, shard)
-    raw[...] = in_ref[...].T
-    for j in range(members):
-        turned[j * shard : (j + 1) * shard, :] = raw[pl.ds(rows[j], shard), :]
-    for part in range(3):
         value = dot(turned[...], dproj[:, part * D : (part + 1) * D]).astype(BF16)
         for j in range(members):
-            pack[j, :, part * D : (part + 1) * D] = value[j * shard : (j + 1) * shard]
+            packs[part][j] = value[j * shard : (j + 1) * shard]
+        level_copy(part, 0).start()
+        if part > 0:
+            level_next(part - 1)
+    dense_step()
     dnorm = dot_nt(dproj[...], w_ref[:, 0 : 3 * D])
     x = x_ref[...].astype(F32)
     gain = tail_ref[experts : experts + 1, :]
@@ -812,72 +971,44 @@
     gains = jnp.where(row == experts, dgain_one, jnp.where(row == experts + 1, dgain_ref[...], 0.0))
     small[...] = router_ref[...] + gains.T
     for j in range(members):
-        pack[j, :, 3 * D : PACKED] = small[pl.ds(rows[j], shard), :].astype(BF16)
-        pack[j, :, PACKED:] = out_grad_ref[j]
-    level_copy(0).start()
+        packs[3][j, :, 0:LANES] = small[pl.ds(rows[j], shard), :].astype(BF16)
+        packs[3][j, :, LANES:] = out_grad_ref[j]
+    level_copy(3, 0).start()
+    level_next(2)
     scaled = dnorm * gain
     total = jnp.mean(scaled * x, axis=-1, keepdims=True)
     x_out[...] = dres_ref[...] + inv * scaled - x * inv * inv * inv * total
-
-    def early(s):
-        for i in dense:
-            reduce_step(i, s)
-
-    def dense_gather(s):
-        for i in dense:
-            gather_step(i, s)
-
-    loop(early, 1, 3)
-    level_add(0)
-    level_copy(1).start()
-    loop(early, 3, n - 1)
-    for i in dense:
-        turn(i)
-    loop(dense_gather, 1, n // 2 + 1)
-    for b in range(1, bits):
-        level_add(b)
-        if b + 1 < bits:
-            level_copy(b + 1).start()
-    for i in range(2, parts):
+    level_next(3)
+    for i in range(1, parts):
         e_copy(i, 1).start()
-    skip = 0
-    for i in late:
-        load(i, pack.at[0], skip)
-        skip += splits[i][4]
-        first(i)
-    rest = n - 2 - n // 2
-
-    def joint(s):
-        for i in late:
-            reduce_step(i, s)
-        for i in dense:
-            gather_step(i, s + n // 2)
-
-    def late_reduce(s):
-        for i in late:
-            reduce_step(i, s)
-
-    loop(joint, 1, rest + 1)
-    for i in dense:
-        end(i)
-    loop(late_reduce, rest + 1, n - 1)
-    for i in late:
-        turn(i)
-    save(0, a_out)
-    save(1, b_out)
-    e_add(1, 1)
-
-    def finish(s):
-        for i in late:
-            gather_step(i, s)
-
-    loop(finish, 1, n - 1)
-    for i in late:
-        end(i)
-    skip = 0
-    for i in late:
-        save(i, c_out, skip)
-        skip += splits[i][4]
+
+    for p in range(4):
+        for b in range(1, bits):
+            level_add(p, b)
+            if b + 1 < bits:
+                level_copy(p, b + 1).start()
+        load(4 + p, packs[p].at[0])
+        first(4 + p)
+        dense_step()
+        for queue in waiting[4:]:
+            queue.pop(0)()
+        waiting.append(steps_of(4 + p))
+    while any(waiting):
+        for i, queue in enumerate(waiting):
+            if queue:
+                queue.pop(0)()
+                if not queue and i < 4:
+                    if i < 2:
+                        save(i, a_out, i * splits[0][4])
+                    else:
+                        height = splits[2][0] * splits[2][2]
+                        save(i, b_out.at[pl.ds((i - 2) * height, height)])
+        if not any(waiting[0:4]) and parts > 1:
+            e_add(1, 1)
+            parts = min(parts, 1)
+    for p in range(4):
+        save(4 + p, c_out, p * D)
+    parts = e_ref.shape[0]
     for i in range(2, parts):
         e_add(i, 1)
     if bits == 2:
@@ -888,34 +1019,49 @@
         for i in range(parts):
             e_add(i, b)
     for b in range(bits):
-        level_copy(b).wait_send()
+        for p in range(4):
+            level_copy(p, b).wait_send()
     for b in range(1, bits):
         for i in range(1 if b == 1 else 0, parts):
             e_copy(i, b).wait_send()
 
-    def drain(s):
-        for i in range(streams):
-            for direction in range(2):
-                copy(i, direction, s, own, back, 0).wait_send()
-
-    loop(drain, 0, 2 * n - 2)
-
-
-def widen_kernel(late_ref, a_ref, b_ref, e_ref, qkv_out, w_out, a_out, b_out, in_out, back_out):
+    for i in range(streams):
+        drain(i)
+
+
+def widen_kernel(
+    experts,
+    late_ref,
+    a_ref,
+    b_ref,
+    in_ref,
+    back_ref,
+    x_ref,
+    small_ref,
+    qkv_out,
+    w_out,
+    a_out,
+    b_out,
+    in_out,
+    back_out,
+    x_out,
+    router_out,
+    gains_out,
+):
     qkv_out[...] = late_ref[:, 0 : 3 * D].astype(F32)
     w_out[...] = late_ref[:, PACKED:].astype(F32)
     a_out[...] = a_ref[...].astype(F32)
     b_out[...] = b_ref[...].astype(F32)
-    in_out[:, 0:FF] = e_ref[0].astype(F32)
-    in_out[:, FF:] = e_ref[1].astype(F32)
-    back_out[...] = e_ref[2].astype(F32).T
-
-
-def output_kernel(residual_ref, shared_ref, gates_ref, target_ref, live_ref, came_ref, out_ref):
-    pick = picks(target_ref, came_ref.shape[0])
-    came = came_ref[...]
-    mixture = gates_ref[:, 0:1] * dot(pick[0], came) + gates_ref[:, 1:2] * dot(pick[1], came)
-    out_ref[...] = (live_ref[...] * (residual_ref[...] + shared_ref[...] + mixture)).astype(BF16)
+    in_out[:, 0:FF] = in_ref[0].astype(F32)
+    in_out[:, FF:] = in_ref[1].astype(F32)
+    back_out[...] = back_ref[0].astype(F32)
+    x_out[...] = x_ref[...]
+
+    @pl.when(pl.program_id(0) == 0)
+    def _():
+        small = small_ref[...].astype(F32).T
+        router_out[...] = small[0:experts]
+        gains_out[...] = small[experts : experts + 2]
 
 
 def on_device(
@@ -967,11 +1113,7 @@
         jnp.concatenate([w_shared_in, w_expert_in[0], w_expert_out[0].T], axis=1)
     )
     shared_out = gather(w_shared_out)
-    fsdp_index = lax.axis_index("fsdp")
     bits = members.bit_length() - 1
-    shard_at = fsdp_index ^ jnp.array(mirrored(members), jnp.int32)
-    spots = fsdp_index ^ jnp.arange(members, dtype=jnp.int32)
-    spot_of = sum(((spots >> b) & 1) << (bits - 1 - b) for b in range(bits))
 
     query_pos = position_block[ctx_index] * rows + jnp.arange(rows, dtype=jnp.int32)
     live = (query_pos < length).astype(F32)[:, None]
@@ -1080,60 +1222,8 @@
     )(came, out_weight, x, tail, routes[0], target)
     x_rows = exchange(outgoing.reshape(n_ctx, -1, D + LANES)).reshape(places, D + LANES)
 
+    half, quarter = members // 2, members // 4
     steps = FS // CHUNK
-    half = members // 2
-
-    def split(rows_each, columns):
-        return (shape((half, rows_each, columns), BF16),) * 2
-
-    shared_res, shared_dx, shared_mid, so_keep, so_give = call(
-        shared_kernel,
-        (
-            shape((rows, D), F32),
-            shape((rows, D), F32),
-            shape((2, rows, FS), BF16),
-        )
-        + split(FS // members, D),
-        flops=2 * rows * D * FS * 7,
-        nbytes=14 << 20,
-        grid_spec=pltpu.PrefetchScalarGridSpec(
-            num_scalar_prefetch=1,
-            grid=(steps,),
-            in_specs=[
-                full(rows, D),
-                full(rows, D),
-                pl.BlockSpec((D, CHUNK), lambda c, sc: (0, c)),
-                pl.BlockSpec((D, CHUNK), lambda c, sc: (0, steps + c)),
-                pl.BlockSpec((CHUNK, D), lambda c, sc: (c, 0)),
-            ],
-            out_specs=[
-                full(rows, D),
-                full(rows, D),
-                pl.BlockSpec((2, rows, CHUNK), lambda c, sc: (0, 0, c)),
-                full(half, FS // members, D),
-                full(half, FS // members, D),
-            ],
-            scratch_shapes=[pltpu.VMEM((rows, D), F32), pltpu.VMEM((rows, D), F32)],
-        ),
-    )(spot_of, ffn_in, dout, weights, weights, shared_out)
-    column = pl.BlockSpec((half, local, CHUNK), lambda i, c, sc: (0, 0, i * steps + c))
-    dense_keep, dense_give = call(
-        shared_grad_kernel,
-        split(local, 2 * FS),
-        flops=2 * rows * D * FS * 2,
-        nbytes=9 << 20,
-        grid_spec=pltpu.PrefetchScalarGridSpec(
-            num_scalar_prefetch=1,
-            grid=(2, steps),
-            in_specs=[
-                full(rows, D),
-                pl.BlockSpec((1, rows, CHUNK), lambda i, c, sc: (i, 0, c)),
-            ],
-            out_specs=[column, column],
-            scratch_shapes=[pltpu.VMEM((D, rows), BF16), pltpu.VMEM((D, rows), BF16)],
-        ),
-    )(shard_at, ffn_in, shared_mid)
-
     wide = FF // CHUNK
     expert_dx, expert_res, expert_mid = call(
         expert_kernel,
@@ -1163,75 +1253,87 @@
             pltpu.VMEM((places, LANES), F32),
         ],
     )(x_rows, dy_rows, weights, weights, weights)
-    dx_came = exchange(expert_dx.reshape(n_ctx, -1, D + LANES)).reshape(places, D + LANES)
-    shared_dx, dense_keep, dense_give, so_keep, so_give = lax.optimization_barrier(
-        (shared_dx, dense_keep, dense_give, so_keep, so_give)
-    )
-    branch_send, dres, branch, dlogits, dgain_two = call(
-        functools.partial(combine_kernel, heads, experts),
+    b_rows = FS // members // 2
+    anywhere = pl.BlockSpec(memory_space=pl.ANY)
+    (
+        branch_recv,
+        shared_res,
+        dres,
+        branch,
+        dlogits,
+        dgain_two,
+        dense_keep,
+        dense_give,
+        so_keep,
+        so_give,
+    ) = comm_call(
+        functools.partial(shared_kernel, n_ctx, members, heads, experts),
         (
             shape((n_ctx, rows, LANES), BF16),
+            shape((rows, D), F32),
             shape((rows, D), F32),
             shape((rows, D), BF16),
             shape((rows, LANES), BF16),
             shape((1, D), F32),
-        ),
-        flops=2 * rows * D * (places + 1024),
-        nbytes=6 << 20,
-        grid=(1,),
-        in_specs=[
-            full(places, D + LANES),
-            full(rows, D),
-            full(rows, D),
-            full(rows, D),
-            full(rows, LANES),
-            full(rows, 2),
-            full(rows, 2),
-            full(LANES, D),
-            out_block,
+        )
+        + (shape((2, quarter, local, FS), BF16),) * 2
+        + (shape((2, quarter, b_rows, D), BF16),) * 2,
+        2,
+        in_specs=[whole] * 9 + [anywhere] * 2,
+        out_specs=[whole] * 10,
+        scratch_shapes=[
+            pltpu.VMEM((places, D + LANES), BF16),
+            pltpu.VMEM((n_ctx, rows, LANES), BF16),
+            pltpu.VMEM((2 * steps, rows, CHUNK), BF16),
+            pltpu.VMEM((rows, D), F32),
+            pltpu.VMEM((2, members, local, FS), BF16),
+            pltpu.VMEM((2, members, b_rows, D), BF16),
+            pltpu.VMEM((2, half, local, FS), BF16),
+            pltpu.VMEM((2, half, b_rows, D), BF16),
+            pltpu.VMEM((D, rows), BF16),
+            pltpu.VMEM((D, rows), BF16),
+            pltpu.VMEM((2, D, CHUNK), BF16),
+            pltpu.VMEM((2, D, CHUNK), BF16),
+            pltpu.VMEM((2, CHUNK, D), BF16),
+            pltpu.SemaphoreType.DMA((n_ctx - 1,)),
+            pltpu.SemaphoreType.DMA((n_ctx - 1,)),
+            pltpu.SemaphoreType.DMA((2,)),
+            pltpu.SemaphoreType.DMA((n_ctx - 1,)),
+            pltpu.SemaphoreType.DMA((n_ctx - 1,)),
+            pltpu.SemaphoreType.DMA((2, 2)),
+            pltpu.SemaphoreType.DMA((2, 2)),
+            pltpu.SemaphoreType.DMA((2, 3)),
         ],
-        out_specs=[
-            full(n_ctx, rows, LANES),
-            full(rows, D),
-            full(rows, D),
-            full(rows, LANES),
-            full(1, D),
-        ],
-    )(dx_came, shared_dx, residual, dout, gates, routes[0], target, tail, out_weight)
-    branch_recv = exchange(branch_send)
-
-    def halve(terms, give, b):
-        count = members >> (b + 1)
-        if give is None:
-            give = sum(t[count:].astype(F32) for t in terms).astype(BF16)
-            terms = [t[:count] for t in terms]
-        came_in = lax.ppermute(give, "fsdp", [(i, i ^ (1 << b)) for i in range(members)])
-        return terms + [came_in]
-
-    def upper(terms, b):
-        count = members >> (b + 1)
-        give = sum(t[count:].astype(F32) for t in terms).astype(BF16)
-        return [t[:count] for t in terms], give
+        nbytes=150 << 20,
+    )(
+        expert_dx,
+        ffn_in,
+        dout,
+        residual,
+        gates,
+        routes[0],
+        target,
+        tail,
+        out_weight,
+        weights,
+        shared_out,
+    )
 
     def gathered(terms):
         return sum(t.astype(F32) for t in terms).astype(BF16)
 
-    def rest_of(terms, give):
-        keep = gathered(terms)
+    def rest_of(keep, give):
         for b in range(1, bits):
-            came_in = halve([], give, b)[0]
+            came_in = lax.ppermute(give, "fsdp", [(i, i ^ (1 << b)) for i in range(members)])
             if b + 1 < bits:
-                keep, give = (
-                    gathered(t) for t in zip(*[(u[: u.shape[0] // 2], u[u.shape[0] // 2 :]) for u in (keep, came_in)])
-                )
-        return keep[0], came_in[0]
-
-    dense_terms, dense_give = upper(halve([dense_keep], dense_give, 0), 1)
-    so_terms, so_give = upper(halve([so_keep], so_give, 0), 1)
+                count = keep.shape[1] // 2
+                give = gathered([keep[:, count:], came_in[:, count:]])
+                keep = gathered([keep[:, :count], came_in[:, :count]])
+        return keep[:, 0], came_in[:, 0]
+
     branch_recv, expert_res = lax.optimization_barrier((branch_recv, expert_res))
-    recv, dense_give, so_give = lax.optimization_barrier((recv, dense_give, so_give))
-    dense_part, dense_other = rest_of(dense_terms, dense_give)
-    so_part, so_other = rest_of(so_terms, so_give)
+    dense_part, dense_other = rest_of(dense_keep, dense_give)
+    so_part, so_other = rest_of(so_keep, so_give)
 
     dsend = call(
         functools.partial(attend_back_kernel, n_ctx, share),
@@ -1257,17 +1359,19 @@
             ],
         ),
     )(scalars, recv, branch_recv, kept, lse)
-    drecv, expert_sum, out_grad, grad_router = comm_call(
+    res_came = exchange(expert_res.reshape(n_ctx, -1, D)).reshape(places, D)
+    drecv, expert_sum, out_grad, grad_router, output = comm_call(
         functools.partial(back_exchange_kernel, n_ctx, members, heads),
         (
             shape((n_ctx, rows, 3 * LANES), BF16),
             shape((3, half, local, FF), BF16),
             shape((members, local, D), BF16),
             shape((D, LANES), F32),
+            shape((rows, D), BF16),
         ),
         1,
-        in_specs=[whole] * 7 + [pl.BlockSpec(memory_space=pl.ANY)],
-        out_specs=[whole] * 4,
+        in_specs=[whole] * 13 + [pl.BlockSpec(memory_space=pl.ANY)],
+        out_specs=[whole] * 5,
         scratch_shapes=[
             pltpu.VMEM((3, half, local, FF), BF16),
             pltpu.VMEM((3, half, local, FF), BF16),
@@ -1286,14 +1390,29 @@
             pltpu.SemaphoreType.DMA((2,)),
         ],
         nbytes=120 << 20,
-    )(dsend, x_rows, dy_rows, came, branch, ffn_in, dlogits, expert_mid)
+    )(
+        dsend,
+        x_rows,
+        dy_rows,
+        came,
+        branch,
+        ffn_in,
+        dlogits,
+        residual,
+        shared_res,
+        gates,
+        target,
+        live,
+        res_came,
+        expert_mid,
+    )
 
     late_width = PACKED + D
-    first_width = late_width // 2 // LANES * LANES
-    sizes = [(local, 2 * FS), (FS // members, D)]
-    sizes += [(local, first_width), (local, late_width - first_width)]
-    splits = [ring_split(r, c, 2 * n_ctx) + (c,) for r, c in sizes]
-    tiles = [(2 * n_ctx, t[2], t[3]) for t in splits]
+    late_widths = [D, D, D, D + LANES]
+    sizes = [(local, FS)] * 2 + [(FS // members // 2, D)] * 2
+    sizes += [(local, width) for width in late_widths]
+    splits = [ring_split(r, c, n_ctx) + (c,) for r, c in sizes]
+    tiles = [(n_ctx, t[2], t[3]) for t in splits]
     grad_x, dense_sum, so_sum, last_sum, expert_sum = comm_call(
         functools.partial(last_kernel, n_ctx, members, heads, experts, splits),
         (
@@ -1306,19 +1425,23 @@
         0,
         in_specs=[whole] * 16,
         out_specs=[whole] * 5,
-        scratch_shapes=[pltpu.VMEM(t, BF16) for t in tiles * 3]
-        + [pltpu.VMEM((members >> (b + 1), local, late_width), BF16) for b in range(bits)]
+        scratch_shapes=[pltpu.VMEM(t, BF16) for t in tiles * 4]
+        + [pltpu.VMEM((members, local, width), BF16) for width in late_widths]
+        + [
+            pltpu.VMEM((members >> (b + 1), local, width), BF16)
+            for b in range(bits)
+            for width in late_widths
+        ]
         + [pltpu.VMEM((3, members >> (b + 1), local, FF), BF16) for b in range(1, bits)]
         + [
             pltpu.VMEM((rows, 3 * D), BF16),
             pltpu.VMEM((D, rows), BF16),
             pltpu.VMEM((D, rows), BF16),
             pltpu.VMEM((D, LANES), F32),
-            pltpu.VMEM((members, local, late_width), BF16),
-            pltpu.SemaphoreType.DMA((4, 2, 2 * n_ctx - 2)),
-            pltpu.SemaphoreType.DMA((4, 2, 2 * n_ctx - 2)),
-            pltpu.SemaphoreType.DMA((bits,)),
-            pltpu.SemaphoreType.DMA((bits,)),
+            pltpu.SemaphoreType.DMA((8, 2, n_ctx)),
+            pltpu.SemaphoreType.DMA((8, 2, n_ctx)),
+            pltpu.SemaphoreType.DMA((4, bits)),
+            pltpu.SemaphoreType.DMA((4, bits)),
             pltpu.SemaphoreType.DMA((3, max(1, bits - 1))),
             pltpu.SemaphoreType.DMA((3, max(1, bits - 1))),
         ],
@@ -1342,40 +1465,60 @@
         expert_sum,
     )
 
-    res_came = exchange(expert_res.reshape(n_ctx, -1, D)).reshape(places, D)
-    output = call(
-        output_kernel,
-        shape((rows, D), BF16),
-        flops=2 * rows * D * places * 2,
-        nbytes=5 << 20,
-    )(residual, shared_res, gates, target, live, res_came)
-
-    small = last_sum[:, 3 * D : PACKED].astype(F32)
-    grad_qkv, grad_out, grad_si, grad_so, grad_ei, grad_eo = call(
-        widen_kernel,
+    quarters = 4 if local % 64 == 0 else 1
+
+    def rows_of(count, width):
+        return pl.BlockSpec((count // quarters, width), lambda i: (i, 0))
+
+    grad_qkv, grad_out, grad_si, grad_so, grad_ei, grad_eo, grad_x, grad_router, gains = call(
+        functools.partial(widen_kernel, experts),
         (
             shape((local, 3 * D), F32),
             shape((local, D), F32),
             shape((local, 2 * FS), F32),
             shape((FS // members, D), F32),
             shape((local, 2 * FF), F32),
-            shape((FF, local), F32),
+            shape((local, FF), F32),
+            shape((rows, D), F32),
+            shape((experts, local), F32),
+            shape((2, local), F32),
         ),
         flops=0,
-        nbytes=21 << 20,
-    )(last_sum, dense_sum, so_sum, expert_sum)
+        nbytes=22 << 20,
+        grid=(quarters,),
+        in_specs=[
+            rows_of(local, late_width),
+            rows_of(local, 2 * FS),
+            rows_of(FS // members, D),
+            pl.BlockSpec((2, local // quarters, FF), lambda i: (0, i, 0)),
+            pl.BlockSpec((1, local // quarters, FF), lambda i: (2, i, 0)),
+            rows_of(rows, D),
+            pl.BlockSpec((local, LANES), lambda i: (0, 3 * D // LANES)),
+        ],
+        out_specs=[
+            rows_of(local, 3 * D),
+            rows_of(local, D),
+            rows_of(local, 2 * FS),
+            rows_of(FS // members, D),
+            rows_of(local, 2 * FF),
+            rows_of(local, FF),
+            rows_of(rows, D),
+            full(experts, local),
+            full(2, local),
+        ],
+    )(last_sum, dense_sum, so_sum, expert_sum, expert_sum, grad_x, last_sum)
     return (
         output[None],
         grad_x[None],
-        small[:, experts],
+        gains[0],
         grad_qkv,
         grad_out,
-        small[:, experts + 1],
-        small[:, 0:experts],
+        gains[1],
+        grad_router.T,
         grad_si,
         grad_so,
         grad_ei[None],
-        grad_eo[None],
+        grad_eo.T[None],
     )
 
 

time: 491 us -> 448 us (0.912); the launches traced: 492 us -> 443 us
  waiting for transfers between devices: 123 us -> 74.2 us
  blocking collectives: 0 us -> 36.5 us
  Pallas kernels: 287 us -> 275 us
  other arithmetic: 16 us -> 5.92 us
  starting transfers between devices: 32.7 us -> 22.9 us
  local copies, waits for them, and re-layouts: 18.3 us -> 13.3 us
    all_to_all x3 -> x0, waiting for transfers between devices: 49.5 us -> none  [the longest x1 32.4 us: on_device(): exchange(outgoing.reshape(n_ctx, -1, D + LANES)).reshape(places, D + LANES)]
    all_to_all x0 -> x1, blocking collectives: none -> 36.5 us  [on_device(): exchange(outgoing.reshape(n_ctx, -1, D + LANES)).reshape(places, D + LANES)]
    pallas_call x1, Pallas kernels: 113 us -> 91.9 us  [on_device(): comm_call(functools.partial(last_kernel, n_ctx, members, heads, experts,...]
    pallas_call x5 -> x2, Pallas kernels: 44.2 us -> 60.6 us  [the longest x1 52.6 us: on_device(): comm_call(functools.partial(shared_kernel, n_ctx, members, heads, experts...]
    all_to_all x3 -> x0, starting transfers between devices: 11.2 us -> none  [the longest x1 3.77 us: on_device(): exchange(outgoing.reshape(n_ctx, -1, D + LANES)).reshape(places, D + LANES)]
    squeeze x2 -> x0, other arithmetic: 8.73 us -> none  [rest_of(): return (keep[0], came_in[0])]
    unnamed x35 -> x25, local copies, waits for them, and re-layouts: 13.2 us -> 7.72 us
  transfers between devices with their start and end apart: 15 -> 10, of which waited for: 7 -> 5; matrix products, arithmetic and copies ran while one was open for 4% -> 2% of each run, Pallas kernels for 58% -> 28%
where the time goes in v4:
time: 448 us; the launch traced here: 443 us
  Pallas kernels  275 us (61%)
  waiting for transfers between devices  74.2 us (17%)
  blocking collectives  36.5 us (8%)
  starting transfers between devices  22.9 us (5%)
  between operations  15.3 us (3%)
  local copies, waits for them, and re-layouts  13.3 us (3%)
  other arithmetic  5.92 us (1%)
    pallas_call x1, Pallas kernels, on_device(): comm_call(functools.partial(last_kernel, n_ctx, members, heads, experts,...  91.9 us
    pallas_call x1, Pallas kernels, on_device(): comm_call(functools.partial(shared_kernel, n_ctx, members, heads, experts...  52.6 us
    pallas_call x1, Pallas kernels, on_device(): comm_call(functools.partial(back_exchange_kernel, n_ctx, members, heads),...  45.2 us
    all_to_all x1, waiting for transfers between devices, on_device(): recv = exchange(send)  36.5 us
    all_to_all x1, blocking collectives, on_device(): exchange(outgoing.reshape(n_ctx, -1, D + LANES)).reshape(places, D + LANES)  36.5 us
    pallas_call x1, Pallas kernels, on_device(): call(expert_kernel, (shape((places, D + LANES), BF16), shape((places, D),...  23.5 us
    pallas_call x1, Pallas kernels, on_device(): call(functools.partial(attend_back_kernel, n_ctx, share), shape((n_ctx, r...  21.8 us
    pallas_call x1, Pallas kernels, on_device(): call(functools.partial(attend_kernel, n_ctx, share), (shape((n_ctx, rows,...  18.6 us
  transfers between devices with their start and end apart: 10, of which 5 were waited for; matrix products, arithmetic and copies ran while one was open for 2% of the time, Pallas kernels for 28%

profile of v4, /device:TPU:0, one launch (start us, length us, event | category | flops | bytes accessed | tf_op | source)
XLA Modules:
  0.0 442.9 jit_solution(11796706988967045063)
XLA Ops:
  7.2 0.0 all-gather.5.cloned.1.call-start
  7.2 0.7 broadcast_in_dim.48
  8.0 0.7 broadcast_in_dim.49
  8.7 0.8 copy.41
  9.6 0.0 copy-start.5
  9.6 0.0 copy-start.6
  9.6 2.2 concatenate.16
  11.8 0.0 all-gather.5.cloned.1.call-update
  11.8 0.0 all-gather.7.cloned.1.call-start
  11.9 0.7 all-gather.7.cloned.1.call-update
  12.6 0.0 all-gather.9.cloned.1.call-start
  12.6 0.0 copy-done.5
  12.6 0.0 copy-done.6
  12.6 3.0 pad_maximum_fusion
  15.6 0.0 copy-start.9
  15.6 0.0 all-gather.9.cloned.1.call-update
  16.3 0.0 copy-done.9
  16.3 0.8 copy.45
  17.1 0.0 copy-done.10
  17.1 0.6 dynamic_slice.3
  18.4 0.7 fusion.live_ref
  19.0 3.2 shard_map.222
  22.2 7.3 %all-to-all-start = ((bf16[8,96,768]{2,1,0:T(8,128)(2,1)}), bf16[8,96,768]{2,1,0:T(8,128)(2,1)S(1)}, u32[]{:S(2)}, u32[]{:S(2)}) async-start(bf16[8,96,768]{2,1,0:T(8,128)(2,1)} %bitcast.44), calls=%async_computation | async-start | bytes 2359296 | tf_op jit(solution)/shard_map/all_to_all | solution.py:1147
  29.6 0.5 fusion.1
  30.1 1.0 pad_maximum_fusion.1
  31.1 15.4 %all-gather.5.cloned.1.call-done.w_ref = bf16[768,2432]{1,0:T(8,128)(2,1)} async-done(((bf16[192,2432]{1,0:T(8,128)(2,1)}), bf16[768,2432]{1,0:T(8,128)(2,1)}) %all-gather.5.cloned.1.call-update) | async-done | bytes 3735568 | tf_op jit(solution)/shard_map/all_gather | solution.py:1110
  46.5 5.0 %shard_map.221 = (bf16[8,256,384]{2,1,0:T(8,128)(2,1)}, bf16[256,768]{1,0:T(8,128)(2,1)}, f32[128,768]{1,0:T(8,128)}) custom-call(bf16[256,768]{1,0:T(8,128)(2,1)} %bitcast.40, bf16[768,2432]{1,0:T(8,128)(2,1)} %all-gather.5.cloned.1.call-done.w_ref, f32[256,128]{1,0:T(8,128)} %get-tuple-element.114.cos_ref, f32[256,128]{1,0:T(8,128)} %get-tuple-element.115.sin_ref), custom_call_target="tpu_custom_call" | custom-call | flops 905969664 | bytes 6291456 | tf_op jit(solution)/shard_map/pallas_call | solution.py:1149
  51.5 6.6 %all-to-all-done = bf16[8,96,768]{2,1,0:T(8,128)(2,1)S(1)} async-done(((bf16[8,96,768]{2,1,0:T(8,128)(2,1)}), bf16[8,96,768]{2,1,0:T(8,128)(2,1)S(1)}, u32[]{:S(2)}, u32[]{:S(2)}) %all-to-all-start) | async-done | bytes 1179680 | tf_op jit(solution)/shard_map/all_to_all | solution.py:1147
  58.2 1.0 copy-done
  59.2 3.6 all-to-all-start.1
  62.8 0.1 select_reduce_fusion
  62.9 0.6 pad_add_fusion.sc
  63.5 36.5 %all-to-all-done.1.recv_ref = bf16[8,256,384]{2,1,0:T(8,128)(2,1)S(1)} async-done(((bf16[8,256,384]{2,1,0:T(8,128)(2,1)}), bf16[8,256,384]{2,1,0:T(8,128)(2,1)S(1)}, u32[]{:S(2)}, u32[]{:S(2)}) %all-to-all-start.1) | async-done | bytes 1572896 | tf_op jit(solution)/shard_map/all_to_all | solution.py:1160
  100.0 1.1 copy-done.4
  101.1 18.6 %shard_map.223 = (bf16[8,256,128]{2,1,0:T(8,128)(2,1)}, f32[8,128,384]{2,1,0:T(8,128)}, f32[8,1,384]{2,1,0:T(1,128)}) custom-call(s32[10]{0:T(128)} %pad_add_fusion.sc, bf16[8,256,384]{2,1,0:T(8,128)(2,1)} %copy-done.4), custom_call_target="tpu_custom_call" | custom-call | flops 3221225472 | bytes 5242880 | tf_op jit(solution)/shard_map/pallas_call | solution.py:1164
  119.8 3.6 all-to-all-start.2
  123.4 0.0 all-gather.11.cloned.1.call-start
  123.4 0.5 all-gather.11.cloned.1.call-update
  124.0 0.0 all-gather.7.cloned.1.call-done.w_ref
  124.0 12.2 %all-to-all-done.2.came_ref = bf16[8,256,128]{2,1,0:T(8,128)(2,1)S(1)} async-done(((bf16[8,256,128]{2,1,0:T(8,128)(2,1)}), bf16[8,256,128]{2,1,0:T(8,128)(2,1)S(1)}, u32[]{:S(2)}, u32[]{:S(2)}) %all-to-all-start.2) | async-done | bytes 524320 | tf_op jit(solution)/shard_map/all_to_all | solution.py:1189
  136.2 0.8 copy-done.2
  137.0 5.2 %shard_map.224 = (f32[256,768]{1,0:T(8,128)}, bf16[256,768]{1,0:T(8,128)(2,1)}, f32[256,128]{1,0:T(8,128)}, bf16[768,896]{1,0:T(8,128)(2,1)}) custom-call(bf16[8,256,128]{2,1,0:T(8,128)(2,1)} %copy-done.2, bf16[768,768]{1,0:T(8,128)(2,1)} %all-gather.7.cloned.1.call-done.w_ref, bf16[256,768]{1,0:T(8,128)(2,1)} %bitcast.41, ...), custom_call_target="tpu_custom_call" | custom-call | flops 1308622848 | bytes 5242880 | tf_op jit(solution)/shard_map/pallas_call | solution.py:1197
  142.2 36.5 %all_to_all.25 = bf16[8,96,896]{2,1,0:T(8,128)(2,1)} all-to-all(bf16[8,96,896]{2,1,0:T(8,128)(2,1)} %bitcast.43), channel_id=1, replica_groups=mesh['ctx'=8,'fsdp'=4] {'ctx'}, dimensions={0} | all-to-all | bytes 2752512 | tf_op jit(solution)/shard_map/all_to_all | solution.py:1223
  178.6 23.5 %shard_map.225 = (bf16[768,896]{1,0:T(8,128)(2,1)}, bf16[768,768]{1,0:T(8,128)(2,1)}, bf16[3,768,2048]{2,1,0:T(8,128)(2,1)}) custom-call(bf16[768,896]{1,0:T(8,128)(2,1)} %bitcast.32, bf16[768,768]{1,0:T(8,128)(2,1)} %bitcast.34, bf16[768,10240]{1,0:T(8,128)(2,1)} %all-gather.9.cloned.1.call-done.wg_ref.wu_ref.wt_ref.wide_ref, ...), custom_call_target="tpu_custom_call" | custom-call | flops 14495514624 | bytes 25165824 | tf_op jit(solution)/shard_map/pallas_call | solution.py:1228
  202.1 52.6 %shard_map.226 = (bf16[8,256,128]{2,1,0:T(8,128)(2,1)}, f32[256,768]{1,0:T(8,128)}, f32[256,768]{1,0:T(8,128)}, bf16[256,768]{1,0:T(8,128)(2,1)}, bf16[256,128]{...) custom-call(bf16[768,896]{1,0:T(8,128)(2,1)} %get-tuple-element.68.s, ...), custom_call_target="tpu_custom_call" | custom-call | bytes 157286400 | tf_op jit(solution)/shard_map/pallas_call | solution.py:1269
  254.7 6.1 %all-to-all-start.4 = ((bf16[8,96,768]{2,1,0:T(8,128)(2,1)}), bf16[8,96,768]{2,1,0:T(8,128)(2,1)S(1)}, u32[]{:S(2)}, u32[]{:S(2)}) async-start(bf16[8,96,768]{2,1,0:T(8,128)(2,1)} %bitcast.13), calls=%async_computation.4 | async-start | bytes 2359296 | tf_op jit(solution)/shard_map/all_to_all | solution.py:1362
  260.8 0.0 collective-permute-start
  260.8 2.0 collective-permute-start.1
  262.8 21.8 %shard_map.227.send_ref = bf16[8,256,384]{2,1,0:T(8,128)(2,1)} custom-call(s32[10]{0:T(128)} %pad_add_fusion.sc, bf16[8,256,384]{2,1,0:T(8,128)(2,1)} %copy-done.4, bf16[8,256,128]{2,1,0:T(8,128)(2,1)} %get-tuple-element.75.grad_ref, f32[8,128,384]{2,1,0:T(8,128)} %get-tuple-element.76.keep_ref, f32[8,1,384]{2,1,0:T(1,128)} %get-tuple-element.77.lse_ref), custom_call_target="tpu_custom_call" | custom-call | flops 4831838208 | bytes 8388608 | tf_op jit(solution)/shard_map/pallas_call | solution.py:1338
  284.6 2.2 all-to-all-done.4
  286.8 1.0 copy-done.1
  287.8 45.2 %shard_map.228 = (bf16[8,256,384]{2,1,0:T(8,128)(2,1)}, bf16[3,2,192,2048]{3,2,1,0:T(8,128)(2,1)}, bf16[4,192,768]{2,1,0:T(8,128)(2,1)}, f32[768,128]{1,0:T(8,128)}, bf16[256,768]{1,0:T(8,128)(2,1)}) custom-call(bf16[8,256,384]{2,1,0:T(8,128)(2,1)} %shard_map.227.send_ref, bf16[768,896]{1,0:T(8,128)(2,1)} %bitcast.33, bf16[768,768]{1,0:T(8,128)(2,1)} %bitcast.35, ...), custom_call_target="tpu_custom_call" | custom-call | bytes 125829120 | tf_op jit(solution)/shard_map/pallas_call | solution.py:1363
  333.0 0.0 collective-permute-done.1
  333.0 0.0 copy-start.7
  333.0 0.0 collective-permute-done
  333.0 0.0 copy-start.3
  333.1 0.8 copy-done.7
  333.9 0.5 copy-done.3
  334.4 91.9 %shard_map.229 = (f32[256,768]{1,0:T(8,128)}, bf16[192,4096]{1,0:T(8,128)(2,1)}, bf16[512,768]{1,0:T(8,128)(2,1)}, bf16[192,3200]{1,0:T(8,128)(2,1)}, bf16[3,192,2048]{2,1,0:T(8,128)(2,1)}) custom-call(bf16[8,256,384]{2,1,0:T(8,128)(2,1)} %get-tuple-element.84.recv_ref, f32[256,128]{1,0:T(8,128)} %get-tuple-element.114.cos_ref, ...), custom_call_target="tpu_custom_call" | custom-call | bytes 209715200 | tf_op jit(solution)/shard_map/pallas_call | solution.py:1416
  426.3 0.0 copy-start.8
  426.3 8.0 %shard_map.230 = (f32[192,2304]{1,0:T(8,128)}, f32[192,768]{1,0:T(8,128)}, f32[192,4096]{1,0:T(8,128)}, f32[512,768]{1,0:T(8,128)}, f32[192,4096]{1,0:T(8,128)},...) custom-call(bf16[192,3200]{1,0:T(8,128)(2,1)} %get-tuple-element.95.late_ref.small_ref, ...), custom_call_target="tpu_custom_call" | custom-call | bytes 23068672 | tf_op jit(solution)/shard_map/pallas_call | solution.py:1473
  434.3 1.3 fusion.2
  435.6 0.0 copy-done.8
  435.6 0.7 copy.50
  (10 shorter events, 0.0 us)
Async XLA Ops:
  7.2 39.4 %all-gather.5.cloned.1.call-start = ((), (), s32[]{:S(2)}) async-start(), calls=%async_computation.5 | async-start | bytes 4669440 | tf_op jit(solution)/shard_map/all_gather | solution.py:1110
  9.6 3.0 copy-start.5
  9.6 3.0 copy-start.6
  11.8 112.2 %all-gather.7.cloned.1.call-start = ((), (), s32[]{:S(2)}) async-start(), calls=%async_computation.6 | async-start | bytes 1474560 | tf_op jit(solution)/shard_map/all_gather | solution.py:1111
  12.6 166.1 %all-gather.9.cloned.1.call-start = ((), (), s32[]{:S(2)}) async-start(), calls=%async_computation.7 | async-start | bytes 19660800 | tf_op jit(solution)/shard_map/all_gather | solution.py:1112
  15.6 0.7 copy-start.9
  15.6 1.5 copy-start.10
  22.2 35.9 %all-to-all-start = ((bf16[8,96,768]{2,1,0:T(8,128)(2,1)}), bf16[8,96,768]{2,1,0:T(8,128)(2,1)S(1)}, u32[]{:S(2)}, u32[]{:S(2)}) async-start(bf16[8,96,768]{2,1,0:T(8,128)(2,1)} %bitcast.44), calls=%async_computation | async-start | bytes 2359296 | tf_op jit(solution)/shard_map/all_to_all | solution.py:1147
  58.1 1.0 copy-start
  59.2 40.8 %all-to-all-start.1 = ((bf16[8,256,384]{2,1,0:T(8,128)(2,1)}), bf16[8,256,384]{2,1,0:T(8,128)(2,1)S(1)}, u32[]{:S(2)}, u32[]{:S(2)}) async-start(bf16[8,256,384]{2,1,0:T(8,128)(2,1)} %get-tuple-element.62), calls=%async_computation.1 | async-start | bytes 3145728 | tf_op jit(solution)/shard_map/all_to_all | solution.py:1160
  100.0 1.1 copy-start.4
  119.8 16.4 %all-to-all-start.2 = ((bf16[8,256,128]{2,1,0:T(8,128)(2,1)}), bf16[8,256,128]{2,1,0:T(8,128)(2,1)S(1)}, u32[]{:S(2)}, u32[]{:S(2)}) async-start(bf16[8,256,128]{2,1,0:T(8,128)(2,1)} %get-tuple-element.63), calls=%async_computation.2 | async-start | bytes 1048576 | tf_op jit(solution)/shard_map/all_to_all | solution.py:1189
  123.4 78.7 %all-gather.11.cloned.1.call-start = ((), (), s32[]{:S(2)}) async-start(), calls=%async_computation.8 | async-start | bytes 3932160 | tf_op jit(solution)/shard_map/all_gather | solution.py:1115
  136.2 0.8 copy-start.2
  254.7 32.0 %all-to-all-start.4 = ((bf16[8,96,768]{2,1,0:T(8,128)(2,1)}), bf16[8,96,768]{2,1,0:T(8,128)(2,1)S(1)}, u32[]{:S(2)}, u32[]{:S(2)}) async-start(bf16[8,96,768]{2,1,0:T(8,128)(2,1)} %bitcast.13), calls=%async_computation.4 | async-start | bytes 2359296 | tf_op jit(solution)/shard_map/all_to_all | solution.py:1362
  260.8 72.2 %collective-permute-start = (bf16[2,1,192,2048]{3,2,0,1:T(8,128)(2,1)}, bf16[2,1,192,2048]{3,2,0,1:T(8,128)(2,1)S(1)}, u32[]{:S(2)}, u32[]{:S(2)}) collective-permute-start(bf16[2,1,192,2048]{3,2,0,1:T(8,128)(2,1)} %bitcast.55), channel_id=1, source_target_pairs={{0,2},{1,3},{2,0},{3,1},{4,6},{5,7},{6,4},{7,5},{8,10},{9,11},{10,... | collective-permute-start | bytes 4718600 | tf_op jit(solution)/shard_map/ppermute | solution.py:1327
  260.8 72.2 %collective-permute-start.1 = (bf16[2,1,256,768]{3,2,0,1:T(8,128)(2,1)}, bf16[2,1,256,768]{3,2,0,1:T(8,128)(2,1)S(1)}, u32[]{:S(2)}, u32[]{:S(2)}) collective-permute-start(bf16[2,1,256,768]{3,2,0,1:T(8,128)(2,1)} %bitcast.57), channel_id=1, source_target_pairs={{0,2},{1,3},{2,0},{3,1},{4,6},{5,7},{6,4},{7,5},{8,10},{9,11},{10,... | collective-permute-start | bytes 2359304 | tf_op jit(solution)/shard_map/ppermute | solution.py:1327
  286.8 1.0 copy-start.1
  333.0 0.9 copy-start.7
  333.0 1.4 copy-start.3
  426.3 9.3 %copy-start.8 = (bf16[256,768]{1,0:T(8,128)(2,1)S(1)}, bf16[256,768]{1,0:T(8,128)(2,1)}, u32[]{:S(2)}) copy-start(bf16[256,768]{1,0:T(8,128)(2,1)} %get-tuple-element.83) | copy-start | bytes 1179652
Sparse Core Ops, SparseCore 0:
  11.9 34.5 all-gather.4
  48.1 17.4 all-gather.6
  67.2 99.9 all-gather.8
  168.6 28.5 all-gather.10

commit v5 on v4

--- a/solution.py
+++ b/solution.py
@@ -97,39 +97,197 @@
     )
 
 
-def start_kernel(experts, capacity, routes_ref, cot_ref, live_ref, target_ref, dout_ref, send_ref):
-    rows = routes_ref.shape[0]
+def flipped(index, mask):
+    for b in range(mask.bit_length()):
+        if mask >> b & 1:
+            index = index + (1 << b) - 2 * (1 << b) * (index // (1 << b) % 2)
+    return index
+
+
+def mirrored(members):
+    bits = members.bit_length() - 1
+    return [int(format(j, "b").zfill(bits)[::-1], 2) for j in range(members)]
+
+
+def shard_rows(members, shard):
+    fsdp = lax.axis_index("fsdp")
+    return [pl.multiple_of(flipped(fsdp, m) * shard, 16) for m in mirrored(members)]
+
+
+def remote(source, target, send_sem, recv_sem, peer):
+    return pltpu.make_async_remote_copy(
+        src_ref=source,
+        dst_ref=target,
+        send_sem=send_sem,
+        recv_sem=recv_sem,
+        device_id=peer,
+        device_id_type=pl.DeviceIdType.MESH,
+    )
+
+
+def greet(peers):
+    barrier = pltpu.get_barrier_semaphore()
+    for peer in peers:
+        pl.semaphore_signal(barrier, inc=1, device_id=peer, device_id_type=pl.DeviceIdType.MESH)
+    pl.semaphore_wait(barrier, len(peers))
+
+
+def mates_of(members):
+    ctx, fsdp = lax.axis_index("ctx"), lax.axis_index("fsdp")
+    return [(ctx, flipped(fsdp, 1 << b)) for b in range(members.bit_length() - 1)]
+
+
+def row_peers(n):
+    ctx, fsdp = lax.axis_index("ctx"), lax.axis_index("fsdp")
+    return [(lax.rem(ctx + d, n), fsdp) for d in range(1, n)]
+
+
+def loop(body, low, high):
+    lax.fori_loop(low, high, lambda s, carry: (body(s), carry)[1], 0)
+
+
+def add_into(target, j, other):
+    target[j] = (target[j].astype(F32) + other[j].astype(F32)).astype(BF16)
+
+
+def open_kernel(
+    n,
+    members,
+    heads,
+    experts,
+    capacity,
+    early,
+    where_ref,
+    length_ref,
+    routes_ref,
+    cot_ref,
+    x_ref,
+    w_ref,
+    router_ref,
+    gain_one_ref,
+    gain_two_ref,
+    cos_ref,
+    sin_ref,
+    recv_ref,
+    in_ref,
+    tail_ref,
+    target_ref,
+    dout_ref,
+    dy_ref,
+    dy_rest_ref,
+    w_all,
+    send,
+    dy_send,
+    small,
+    small_all,
+    gather_send,
+    gather_recv,
+    packet_send,
+    packet_recv,
+    dy_send_sem,
+    dy_recv_sem,
+    own_sem,
+):
+    ctx, fsdp = lax.axis_index("ctx"), lax.axis_index("fsdp")
+    bits = members.bit_length() - 1
+    peers = row_peers(n)
+    mates = mates_of(members)
+    shard = w_ref.shape[0]
+    rows = x_ref.shape[0]
+    row = lax.broadcasted_iota(jnp.int32, (LANES, shard), 0)
+    gains = jnp.where(
+        row == experts,
+        gain_one_ref[...].astype(F32),
+        jnp.where(row == experts + 1, gain_two_ref[...].astype(F32), 0.0),
+    )
+    small[...] = gains.T
+    small[:, 0:experts] = router_ref[...].astype(F32)
+    small_all[fsdp] = small[...].astype(BF16)
+    for part in range(3):
+        w_all[part, fsdp] = w_ref[:, part * D : (part + 1) * D]
+    greet(peers + mates)
+
+    def gather_copy(p, b, mask):
+        buffer = small_all if p == 3 else w_all.at[p]
+        spot = flipped(fsdp, mask)
+        return remote(
+            buffer.at[spot],
+            buffer.at[spot],
+            gather_send.at[p, b, mask],
+            gather_recv.at[p, b, mask],
+            mates[b],
+        )
+
+    def gather_wait(p, b, mask):
+        buffer = small_all if p == 3 else w_all.at[p]
+        spot = flipped(fsdp, mask | 1 << b)
+        remote(
+            buffer.at[spot],
+            buffer.at[spot],
+            gather_send.at[p, b, mask],
+            gather_recv.at[p, b, mask],
+            mates[b],
+        ).wait_recv()
+
+    for p in (3, 0, 1, 2):
+        for b in reversed(range(bits)):
+            gather_copy(p, b, 0).start()
+
+    def gather_rest(p):
+        masks = [0]
+        for b in reversed(range(bits)):
+            for mask in masks[1:]:
+                gather_copy(p, b, mask).start()
+            for mask in masks:
+                gather_wait(p, b, mask)
+            masks = masks + [mask | 1 << b for mask in masks]
+
     lane = lanes_of(rows)
     hot = [jnp.where(lane == routes_ref[:, k : k + 1], 1.0, 0.0) for k in range(2)]
     below = jnp.where(
         lanes_of(rows, rows) < lax.broadcasted_iota(jnp.int32, (rows, rows), 0), 1.0, 0.0
     )
-    earlier = dot(below.astype(BF16), (hot[0] + hot[1]).astype(BF16))
+    before = dot(below.astype(BF16), (hot[0] + hot[1]).astype(BF16))
     place = [
         routes_ref[:, k : k + 1] * capacity
-        + jnp.sum(hot[k] * earlier, axis=-1, keepdims=True).astype(jnp.int32)
+        + jnp.sum(hot[k] * before, axis=-1, keepdims=True).astype(jnp.int32)
         for k in range(2)
     ]
     for k in range(2):
         target_ref[:, k : k + 1] = place[k]
-    dout = (cot_ref[...].astype(F32) * live_ref[...]).astype(BF16)
+    position = where_ref[ctx] * rows + lax.broadcasted_iota(jnp.int32, (rows, D), 0)
+    dout = jnp.where(position < length_ref[0], cot_ref[...].astype(F32), 0.0).astype(BF16)
     dout_ref[...] = dout
-    spot = lanes_of(rows, send_ref.shape[0])
+    places = experts * capacity
+    spot = lanes_of(rows, places)
     pick = jnp.where((spot == place[0]) | (spot == place[1]), 1.0, 0.0).astype(BF16)
-    send_ref[...] = dot_tn(pick, dout).astype(BF16)
-
-
-def qkv_kernel(heads, experts, x_ref, w_ref, cos_ref, sin_ref, send_ref, in_ref, tail_ref):
+    packed = dot_tn(pick, dout).astype(BF16)
+    block = places // n
+    for p in range(n):
+        dy_send[p] = packed[p * block : p * block + early]
+        dy_rest_ref[p] = packed[p * block + early : (p + 1) * block]
+    own = [
+        pltpu.make_async_copy(dy_send.at[ctx], dy_ref.at[ctx], own_sem.at[3]),
+    ]
+    own[0].start()
+    copies = [
+        remote(dy_send.at[p[0]], dy_ref.at[ctx], dy_send_sem.at[d], dy_recv_sem.at[d], p)
+        for d, p in enumerate(peers)
+    ]
+    for c in copies:
+        c.start()
+
     x = x_ref[...].astype(F32)
-    tail = w_ref[:, 3 * D :].astype(F32).T
+    inv = lax.rsqrt(jnp.mean(x * x, axis=-1, keepdims=True) + norm_eps)
+    gather_rest(3)
+    tail = small_all[...].reshape(D, LANES).astype(F32).T
     tail_ref[...] = tail
-    inv = lax.rsqrt(jnp.mean(x * x, axis=-1, keepdims=True) + norm_eps)
     attn_in = (x * inv * tail[experts : experts + 1, :]).astype(BF16)
     in_ref[...] = attn_in
-    lane = lanes_of(x.shape[0])
     cos, sin = cos_ref[...], sin_ref[...]
     for part in range(3):
-        y = dot(attn_in, w_ref[:, part * D : (part + 1) * D])
+        gather_rest(part)
+        y = dot(attn_in, w_all[part].reshape(D, D))
         groups = []
         for g in range(D // LANES):
             t = y[:, g * LANES : (g + 1) * LANES]
@@ -143,7 +301,32 @@
                 packet = groups[g]
             else:
                 packet = jnp.where(lane < 64, turned[g], turned[g + 1])
-            send_ref[d, :, part * LANES : (part + 1) * LANES] = packet.astype(BF16)
+            send[part, d] = packet.astype(BF16)
+        own.append(
+            pltpu.make_async_copy(
+                send.at[part, ctx], recv_ref.at[part, ctx], own_sem.at[part]
+            )
+        )
+        own[-1].start()
+        for d, p in enumerate(peers):
+            copies.append(
+                remote(
+                    send.at[part, p[0]],
+                    recv_ref.at[part, ctx],
+                    packet_send.at[part, d],
+                    packet_recv.at[part, d],
+                    p,
+                )
+            )
+            copies[-1].start()
+    for c in copies + own:
+        c.wait()
+    for p in range(4):
+        masks = [0]
+        for b in reversed(range(bits)):
+            for mask in masks:
+                gather_copy(p, b, mask).wait_send()
+            masks = masks + [mask | 1 << b for mask in masks]
 
 
 def stack_rows(stack_ref, block, lane):
@@ -168,18 +351,18 @@
 
 def attend_kernel(n, share, sc, recv_ref, out_ref, keep_ref, lse_ref, stack, scores, back):
     q_block = pl.program_id(0)
-    rows = recv_ref.shape[1]
+    rows = recv_ref.shape[2]
     offset = pl.multiple_of(sc[n], 64)
     length = sc[n + 1]
     lane = lanes_of(rows)
-    stack_rows(stack, recv_ref[sc[q_block], :, 0:LANES] * 0.125, lane)
+    stack_rows(stack, recv_ref[0, sc[q_block]] * 0.125, lane)
     query = stack[pl.ds(offset, share), :]
     limit = key_limits(share, rows, q_block, offset, length)
     key_row = lax.broadcasted_iota(jnp.int32, (rows, share), 0)
     blocks = jnp.minimum(q_block + 1, (length + rows - 1) // rows)
 
     def score_step(j, top):
-        keys = recv_ref[sc[j], :, LANES : 2 * LANES]
+        keys = recv_ref[1, sc[j]]
         s = dot_nt(keys, query)
         s = jnp.where(key_row < limit - j * rows, s, -1e30)
         scores[j] = s
@@ -191,7 +374,7 @@
         total, acc = carry
         weights = jnp.exp(scores[j] - top)
         total = total + jnp.sum(weights, axis=0, keepdims=True)
-        values = recv_ref[sc[j], :, 2 * LANES : 3 * LANES]
+        values = recv_ref[2, sc[j]]
         return total, acc + dot_tn(values, weights.astype(BF16))
 
     total, acc = lax.fori_loop(
@@ -207,7 +390,7 @@
     n, share, sc, recv_ref, grad_ref, keep_ref, lse_ref, out_ref, stack, gstack, dkeys, dvalues, back
 ):
     q_block = pl.program_id(0)
-    rows = recv_ref.shape[1]
+    rows = recv_ref.shape[2]
     offset = pl.multiple_of(sc[n], 64)
     length = sc[n + 1]
     lane = lanes_of(rows)
@@ -218,7 +401,7 @@
         dkeys[...] = jnp.zeros_like(dkeys)
         dvalues[...] = jnp.zeros_like(dvalues)
 
-    stack_rows(stack, recv_ref[source, :, 0:LANES] * 0.125, lane)
+    stack_rows(stack, recv_ref[0, source] * 0.125, lane)
     query = stack[pl.ds(offset, share), :]
     stack_rows(gstack, grad_ref[source], lane)
     grad = gstack[pl.ds(offset, share), :]
@@ -229,8 +412,8 @@
     blocks = jnp.minimum(q_block + 1, (length + rows - 1) // rows)
 
     def step(j, acc):
-        keys = recv_ref[sc[j], :, LANES : 2 * LANES]
-        values = recv_ref[sc[j], :, 2 * LANES : 3 * LANES]
+        keys = recv_ref[1, sc[j]]
+        values = recv_ref[2, sc[j]]
         s = dot_nt(keys, query)
         weights = jnp.exp(jnp.where(key_row < limit - j * rows, s, -1e30) - lse)
         dweights = dot_nt(values, grad)
@@ -241,33 +424,57 @@
 
     acc = lax.fori_loop(0, blocks, step, jnp.zeros((LANES, share), F32))
     dquery = unstack_rows(back, acc.T * 0.125, offset, lane)
-    out_ref[source, :, 0:LANES] = dquery.astype(BF16)
+    out_ref[0, source] = dquery.astype(BF16)
 
     @pl.when(q_block == n - 1)
     def _():
         def flush(j, carry):
-            out_ref[sc[j], :, LANES : 2 * LANES] = dkeys[j].astype(BF16)
-            out_ref[sc[j], :, 2 * LANES : 3 * LANES] = dvalues[j].astype(BF16)
+            out_ref[1, sc[j]] = dkeys[j].astype(BF16)
+            out_ref[2, sc[j]] = dvalues[j].astype(BF16)
             return carry
 
         lax.fori_loop(0, n, flush, 0)
 
 
 def middle_kernel(
+    n,
     heads,
     experts,
-    came_ref,
+    attended_ref,
     w_ref,
     x_ref,
     tail_ref,
     routes_ref,
     target_ref,
+    came_ref,
     residual_ref,
     in_ref,
     gates_ref,
-    send_ref,
+    rows_ref,
+    outgoing,
+    came_send,
+    came_recv,
+    send_sem,
+    recv_sem,
+    own_sem,
 ):
+    ctx = lax.axis_index("ctx")
+    peers = row_peers(n)
+    greet(peers)
+    own = pltpu.make_async_copy(attended_ref.at[ctx], came_ref.at[ctx], own_sem.at[0])
+    own.start()
+    copies = [
+        remote(attended_ref.at[p[0]], came_ref.at[ctx], came_send.at[d], came_recv.at[d], p)
+        for d, p in enumerate(peers)
+    ]
+    for c in copies:
+        c.start()
+    pick = picks(target_ref, rows_ref.shape[0])
+    lane = lanes_of(x_ref.shape[0])
     total = x_ref[...].astype(F32)
+    for c in copies:
+        c.wait()
+    own.wait()
     for d, head in enumerate(heads):
         total = total + dot(came_ref[d], w_ref[64 * head : 64 * head + LANES, :])
     residual_ref[...] = total
@@ -275,7 +482,6 @@
     ffn_in = (total * inv * tail_ref[experts + 1 : experts + 2, :]).astype(BF16)
     in_ref[...] = ffn_in
     logits = dot_nt(ffn_in, tail_ref[...].astype(BF16))
-    lane = lanes_of(logits.shape[0])
     chosen = [
         jnp.sum(jnp.where(lane == routes_ref[:, k : k + 1], logits, 0.0), axis=-1, keepdims=True)
         for k in range(2)
@@ -284,11 +490,34 @@
     raised = [jnp.exp(c - top) for c in chosen]
     gates = [r / (raised[0] + raised[1]) for r in raised]
     gates_ref[...] = jnp.where(lane == 0, gates[0], gates[1])
-    pick = picks(target_ref, send_ref.shape[0])
-    send_ref[:, 0:D] = dot_tn(pick[0] + pick[1], ffn_in).astype(BF16)
-    send_ref[:, D:] = (
+    outgoing[:, 0:D] = dot_tn(pick[0] + pick[1], ffn_in).astype(BF16)
+    outgoing[:, D:] = (
         dot_tn(pick[0], part_lanes(gates[0], lane)) + dot_tn(pick[1], part_lanes(gates[1], lane))
     ).astype(BF16)
+    block = outgoing.shape[0] // n
+
+    def block_at(p):
+        return pl.ds(pl.multiple_of(p * block, 16), block)
+
+    own = pltpu.make_async_copy(
+        outgoing.at[block_at(ctx)], rows_ref.at[block_at(ctx)], own_sem.at[1]
+    )
+    own.start()
+    copies = [
+        remote(
+            outgoing.at[block_at(p[0])],
+            rows_ref.at[block_at(ctx)],
+            send_sem.at[d],
+            recv_sem.at[d],
+            p,
+        )
+        for d, p in enumerate(peers)
+    ]
+    for c in copies:
+        c.start()
+    for c in copies:
+        c.wait()
+    own.wait()
 
 
 def gated(g, u, da):
@@ -298,7 +527,19 @@
 
 
 def expert_kernel(
-    x_ref, dy_ref, wg_ref, wu_ref, wt_ref, dx_ref, res_ref, mid_ref, dx_acc, res_acc, dgate
+    x_ref,
+    first_ref,
+    rest_ref,
+    wg_ref,
+    wu_ref,
+    wt_ref,
+    dx_ref,
+    res_ref,
+    mid_ref,
+    dy_ref,
+    dx_acc,
+    res_acc,
+    dgate,
 ):
     c = pl.program_id(0)
 
@@ -307,6 +548,11 @@
         res_acc[...] = jnp.zeros_like(res_acc)
         dx_acc[...] = jnp.zeros_like(dx_acc)
         dgate[...] = jnp.zeros_like(dgate)
+        n, early = first_ref.shape[0:2]
+        block = early + rest_ref.shape[1]
+        for p in range(n):
+            dy_ref[p * block : p * block + early] = first_ref[p]
+            dy_ref[p * block + early : (p + 1) * block] = rest_ref[p]
 
     x, dy = x_ref[:, 0:D], dy_ref[...]
     gate = jnp.sum(x_ref[:, D:].astype(F32), axis=-1, keepdims=True)
@@ -340,59 +586,6 @@
 def ring_place(position, n):
     half = n // 2
     return jnp.where(position < half, 2 * position, 2 * (n - 1 - position) + 1)
-
-
-def flipped(index, mask):
-    for b in range(mask.bit_length()):
-        if mask >> b & 1:
-            index = index + (1 << b) - 2 * (1 << b) * (index // (1 << b) % 2)
-    return index
-
-
-def mirrored(members):
-    bits = members.bit_length() - 1
-    return [int(format(j, "b").zfill(bits)[::-1], 2) for j in range(members)]
-
-
-def shard_rows(members, shard):
-    fsdp = lax.axis_index("fsdp")
-    return [pl.multiple_of(flipped(fsdp, m) * shard, 16) for m in mirrored(members)]
-
-
-def remote(source, target, send_sem, recv_sem, peer):
-    return pltpu.make_async_remote_copy(
-        src_ref=source,
-        dst_ref=target,
-        send_sem=send_sem,
-        recv_sem=recv_sem,
-        device_id=peer,
-        device_id_type=pl.DeviceIdType.MESH,
-    )
-
-
-def greet(peers):
-    barrier = pltpu.get_barrier_semaphore()
-    for peer in peers:
-        pl.semaphore_signal(barrier, inc=1, device_id=peer, device_id_type=pl.DeviceIdType.MESH)
-    pl.semaphore_wait(barrier, len(peers))
-
-
-def mates_of(members):
-    ctx, fsdp = lax.axis_index("ctx"), lax.axis_index("fsdp")
-    return [(ctx, flipped(fsdp, 1 << b)) for b in range(members.bit_length() - 1)]
-
-
-def row_peers(n):
-    ctx, fsdp = lax.axis_index("ctx"), lax.axis_index("fsdp")
-    return [(lax.rem(ctx + d, n), fsdp) for d in range(1, n)]
-
-
-def loop(body, low, high):
-    lax.fori_loop(low, high, lambda s, carry: (body(s), carry)[1], 0)
-
-
-def add_into(target, j, other):
-    target[j] = (target[j].astype(F32) + other[j].astype(F32)).astype(BF16)
 
 
 def shared_kernel(
@@ -647,10 +840,10 @@
     mates = mates_of(members)
     mate, far = mates[0], mates[1]
     greet(peers + [mate, far])
-    own = pltpu.make_async_copy(send_ref.at[ctx], recv_ref.at[ctx], own_sem)
+    own = pltpu.make_async_copy(send_ref.at[:, ctx], recv_ref.at[:, ctx], own_sem)
     own.start()
     copies = [
-        remote(send_ref.at[p[0]], recv_ref.at[ctx], send_sem.at[d], recv_sem.at[d], p)
+        remote(send_ref.at[:, p[0]], recv_ref.at[:, ctx], send_sem.at[d], recv_sem.at[d], p)
         for d, p in enumerate(peers)
     ]
     for c in copies:
@@ -943,7 +1136,7 @@
         groups = [jnp.zeros(lane.shape, F32) for _ in range(D // LANES)]
         for d, head in enumerate(heads):
             g = head // 2
-            packet = recv_ref[d, :, part * LANES : (part + 1) * LANES].astype(F32)
+            packet = recv_ref[part, d].astype(F32)
             if head % 2 == 0:
                 groups[g] = groups[g] + packet
             else:
@@ -962,7 +1155,9 @@
         if part > 0:
             level_next(part - 1)
     dense_step()
-    dnorm = dot_nt(dproj[...], w_ref[:, 0 : 3 * D])
+    dnorm = sum(
+        dot_nt(dproj[:, part * D : (part + 1) * D], w_ref[part].reshape(D, D)) for part in range(3)
+    )
     x = x_ref[...].astype(F32)
     gain = tail_ref[experts : experts + 1, :]
     inv = lax.rsqrt(jnp.mean(x * x, axis=-1, keepdims=True) + norm_eps)
@@ -1097,17 +1292,6 @@
     x = tokens[0]
     length = lengths[0]
 
-    first_pack = jnp.concatenate(
-        [
-            w_qkv,
-            w_router,
-            gain_attn[:, None],
-            gain_ffn[:, None],
-            jnp.zeros((local, LANES - experts - 2), BF16),
-        ],
-        axis=1,
-    )
-    qkv_pack = gather(first_pack)
     out_weight = gather(w_out)
     weights = gather(
         jnp.concatenate([w_shared_in, w_expert_in[0], w_expert_out[0].T], axis=1)
@@ -1138,28 +1322,55 @@
         [order, jnp.stack([offset.astype(jnp.int32), length.astype(jnp.int32)])]
     )
 
-    target, dout, dy_send = call(
-        functools.partial(start_kernel, experts, capacity),
-        (shape((rows, 2), jnp.int32), shape((rows, D), BF16), shape((places, D), BF16)),
-        flops=2 * rows * D * places,
-        nbytes=3 << 20,
-    )(routes[0], cotangent[0], live)
-    dy_rows = exchange(dy_send.reshape(n_ctx, -1, D)).reshape(places, D)
-
-    send, attn_in, tail = call(
-        functools.partial(qkv_kernel, heads, experts),
+    whole = pl.BlockSpec(memory_space=pltpu.VMEM)
+    scalar = pl.BlockSpec(memory_space=pltpu.SMEM)
+    block = places // n_ctx
+    early = block // 32 * 16
+    recv, attn_in, tail, target, dout, dy_first, dy_rest, qkv_weight = comm_call(
+        functools.partial(open_kernel, n_ctx, members, heads, experts, capacity, early),
         (
-            shape((n_ctx, rows, 3 * LANES), BF16),
+            shape((3, n_ctx, rows, LANES), BF16),
             shape((rows, D), BF16),
             shape((LANES, D), F32),
+            shape((rows, 2), jnp.int32),
+            shape((rows, D), BF16),
+            shape((n_ctx, early, D), BF16),
+            shape((n_ctx, block - early, D), BF16),
+            shape((3, members, local, D), BF16),
         ),
-        flops=2 * rows * D * 3 * D,
-        nbytes=6 << 20,
-    )(x, qkv_pack, cos, sin)
-    send, dy_rows = lax.optimization_barrier((send, dy_rows))
-    recv = exchange(send)
-
-    packet = pl.BlockSpec((n_ctx, rows, 3 * LANES), lambda i, sc: (0, 0, 0))
+        3,
+        in_specs=[scalar] * 2 + [whole] * 9,
+        out_specs=[whole] * 8,
+        scratch_shapes=[
+            pltpu.VMEM((3, n_ctx, rows, LANES), BF16),
+            pltpu.VMEM((n_ctx, early, D), BF16),
+            pltpu.VMEM((local, LANES), F32),
+            pltpu.VMEM((members, local, LANES), BF16),
+            pltpu.SemaphoreType.DMA((4, bits, members)),
+            pltpu.SemaphoreType.DMA((4, bits, members)),
+            pltpu.SemaphoreType.DMA((3, n_ctx - 1)),
+            pltpu.SemaphoreType.DMA((3, n_ctx - 1)),
+            pltpu.SemaphoreType.DMA((n_ctx - 1,)),
+            pltpu.SemaphoreType.DMA((n_ctx - 1,)),
+            pltpu.SemaphoreType.DMA((4,)),
+        ],
+        nbytes=150 << 20,
+    )(
+        position_block,
+        lengths,
+        routes[0],
+        cotangent[0],
+        x,
+        w_qkv,
+        w_router,
+        gain_attn[None],
+        gain_ffn[None],
+        cos,
+        sin,
+    )
+    dy_rest = exchange(dy_rest)
+
+    packet = pl.BlockSpec((3, n_ctx, rows, LANES), lambda i, sc: (0, 0, 0, 0))
     block_of = lambda i, sc: (i, 0, 0)
     attended, kept, lse = call(
         functools.partial(attend_kernel, n_ctx, share),
@@ -1186,58 +1397,47 @@
             ],
         ),
     )(scalars, recv)
-    came = exchange(attended)
-
-    whole = pl.BlockSpec(memory_space=pltpu.VMEM)
-    out_block = pl.BlockSpec((D, D), lambda *at: (0, 0))
+    attended, dy_rest = lax.optimization_barrier((attended, dy_rest))
 
     def full(*dims):
         return pl.BlockSpec(dims, lambda *at: (0,) * len(dims))
 
-    residual, ffn_in, gates, outgoing = call(
-        functools.partial(middle_kernel, heads, experts),
+    came, residual, ffn_in, gates, x_rows = comm_call(
+        functools.partial(middle_kernel, n_ctx, heads, experts),
         (
+            shape((n_ctx, rows, LANES), BF16),
             shape((rows, D), F32),
             shape((rows, D), BF16),
             shape((rows, LANES), F32),
             shape((places, D + LANES), BF16),
         ),
-        flops=2 * rows * D * (D + 1024 + 2 * places),
-        nbytes=5 << 20,
-        grid=(1,),
-        in_specs=[
-            full(n_ctx, rows, LANES),
-            out_block,
-            full(rows, D),
-            full(LANES, D),
-            full(rows, 2),
-            full(rows, 2),
-        ],
-        out_specs=[
-            full(rows, D),
-            full(rows, D),
-            full(rows, LANES),
-            full(places, D + LANES),
-        ],
-    )(came, out_weight, x, tail, routes[0], target)
-    x_rows = exchange(outgoing.reshape(n_ctx, -1, D + LANES)).reshape(places, D + LANES)
+        4,
+        in_specs=[whole] * 6,
+        out_specs=[whole] * 5,
+        scratch_shapes=[pltpu.VMEM((places, D + LANES), BF16)]
+        + [pltpu.SemaphoreType.DMA((n_ctx - 1,)) for _ in range(4)]
+        + [pltpu.SemaphoreType.DMA((2,))],
+        nbytes=100 << 20,
+    )(attended, out_weight, x, tail, routes[0], target)
 
     half, quarter = members // 2, members // 4
     steps = FS // CHUNK
     wide = FF // CHUNK
-    expert_dx, expert_res, expert_mid = call(
+    expert_dx, expert_res, expert_mid, dy_rows = call(
         expert_kernel,
         (
             shape((places, D + LANES), BF16),
             shape((places, D), BF16),
             shape((3, places, FF), BF16),
+            shape((places, D), BF16),
         ),
         flops=2 * places * D * FF * 6,
         nbytes=24 << 20,
         grid=(wide,),
         in_specs=[
             full(places, D + LANES),
-            full(places, D),
+            full(n_ctx, early, D),
+            full(n_ctx, block - early, D),
             pl.BlockSpec((D, CHUNK), lambda c: (0, 2 * steps + c)),
             pl.BlockSpec((D, CHUNK), lambda c: (0, 2 * steps + wide + c)),
             pl.BlockSpec((D, CHUNK), lambda c: (0, 2 * steps + 2 * wide + c)),
@@ -1246,13 +1446,14 @@
             full(places, D + LANES),
             full(places, D),
             pl.BlockSpec((3, places, CHUNK), lambda c: (0, 0, c)),
+            full(places, D),
         ],
         scratch_shapes=[
             pltpu.VMEM((places, D), F32),
             pltpu.VMEM((places, D), F32),
             pltpu.VMEM((places, LANES), F32),
         ],
-    )(x_rows, dy_rows, weights, weights, weights)
+    )(x_rows, dy_first, dy_rest, weights, weights, weights)
     b_rows = FS // members // 2
     anywhere = pl.BlockSpec(memory_space=pl.ANY)
     (
@@ -1337,7 +1538,7 @@
 
     dsend = call(
         functools.partial(attend_back_kernel, n_ctx, share),
-        shape((n_ctx, rows, 3 * LANES), BF16),
+        shape((3, n_ctx, rows, LANES), BF16),
         flops=2 * share * rows * n_ctx * n_ctx * LANES * 3,
         nbytes=8 << 20,
         grid_spec=pltpu.PrefetchScalarGridSpec(
@@ -1363,7 +1564,7 @@
     drecv, expert_sum, out_grad, grad_router, output = comm_call(
         functools.partial(back_exchange_kernel, n_ctx, members, heads),
         (
-            shape((n_ctx, rows, 3 * LANES), BF16),
+            shape((3, n_ctx, rows, LANES), BF16),
             shape((3, half, local, FF), BF16),
             shape((members, local, D), BF16),
             shape((D, LANES), F32),
@@ -1452,7 +1653,7 @@
         sin,
         attn_in,
         x,
-        qkv_pack,
+        qkv_weight,
         tail,
         dres,
         out_grad,

time: 448 us -> 427 us (0.953); the launches traced: 443 us -> 427 us
  Pallas kernels: 275 us -> 380 us
  waiting for transfers between devices: 74.2 us -> 1.44 us
  blocking collectives: 36.5 us -> 0 us
  starting transfers between devices: 22.9 us -> 16.3 us
  local copies, waits for them, and re-layouts: 13.3 us -> 7.75 us
    pallas_call x4 -> x3, Pallas kernels: 35.1 us -> 126 us  [the longest x1 57.5 us: on_device(): comm_call(functools.partial(open_kernel, n_ctx, members, heads, experts,...]
    all_to_all x3 -> x1, waiting for transfers between devices: 55.3 us -> 0.01 us  [on_device(): dy_rest = exchange(dy_rest)]
    all_to_all x1 -> x0, blocking collectives: 36.5 us -> none  [on_device(): exchange(outgoing.reshape(n_ctx, -1, D + LANES)).reshape(places, D + LANES)]
    all_gather x1 -> x0, waiting for transfers between devices: 15.4 us -> none  [on_device(): qkv_pack = gather(first_pack)]
    pallas_call x1, Pallas kernels: 52.6 us -> 63.9 us  [on_device(): comm_call(functools.partial(shared_kernel, n_ctx, members, heads, experts...]
    all_to_all x3 -> x1, starting transfers between devices: 14.6 us -> 7.68 us  [on_device(): dy_rest = exchange(dy_rest)]
  transfers between devices with their start and end apart: 10 -> 7, of which waited for: 5 -> 0; matrix products, arithmetic and copies ran while one was open for 2% -> 2% of each run, Pallas kernels for 28% -> 50%
where the time goes in v5:
time: 427 us
  Pallas kernels  380 us (89%)
  starting transfers between devices  16.3 us (4%)
  between operations  15.3 us (4%)
  local copies, waits for them, and re-layouts  7.75 us (2%)
  other arithmetic  6.42 us (2%)
    pallas_call x1, Pallas kernels, on_device(): comm_call(functools.partial(last_kernel, n_ctx, members, heads, experts,...  94.2 us
    pallas_call x1, Pallas kernels, on_device(): comm_call(functools.partial(shared_kernel, n_ctx, members, heads, experts...  63.9 us
    pallas_call x1, Pallas kernels, on_device(): comm_call(functools.partial(open_kernel, n_ctx, members, heads, experts,...  57.5 us
    pallas_call x1, Pallas kernels, on_device(): comm_call(functools.partial(middle_kernel, n_ctx, heads, experts), (shape...  44.1 us
    pallas_call x1, Pallas kernels, on_device(): comm_call(functools.partial(back_exchange_kernel, n_ctx, members, heads),...  42.5 us
    pallas_call x1, Pallas kernels, on_device(): call(functools.partial(attend_back_kernel, n_ctx, share), shape((3, n_ctx...  24.8 us
    pallas_call x1, Pallas kernels, on_device(): call(expert_kernel, (shape((places, D + LANES), BF16), shape((places, D),...  23.9 us
    pallas_call x1, Pallas kernels, on_device(): call(functools.partial(attend_kernel, n_ctx, share), (shape((n_ctx, rows,...  21.4 us
  transfers between devices with their start and end apart: 7, of which 0 were waited for; matrix products, arithmetic and copies ran while one was open for 2% of the time, Pallas kernels for 50%

profile of v5, /device:TPU:0, one launch (start us, length us, event | category | flops | bytes accessed | tf_op | source)
XLA Modules:
  0.0 427.4 jit_solution(3427716770717304395)
XLA Ops:
  7.2 0.0 all-gather.4.cloned.1.call-start
  7.2 0.7 all-gather.4.cloned.1.call-update
  7.9 0.0 all-gather.6.cloned.1.call-start
  8.0 3.5 pad_maximum_fusion
  11.5 0.0 copy-start.6
  11.5 0.0 copy-start.5
  11.5 0.0 copy-start.9
  11.5 0.0 copy-start.10
  11.5 0.0 copy-start.7
  11.5 0.0 all-gather.6.cloned.1.call-update
  11.5 0.0 all-gather.8.cloned.1.call-start
  11.6 0.7 all-gather.8.cloned.1.call-update
  12.9 0.0 copy-done.6
  12.9 0.8 copy.33
  13.7 0.0 copy-done.5
  13.7 0.7 copy.35.router_ref
  14.5 0.0 copy-done.9
  14.5 0.6 broadcast_in_dim.38.gain_one_ref
  15.0 0.0 copy-done.10
  15.1 0.6 broadcast_in_dim.39.gain_two_ref
  15.6 0.0 copy-done.7
  15.6 0.6 dynamic_slice.3
  16.9 0.5 fusion.1
  17.4 1.0 pad_maximum_fusion.1
  18.4 0.0 copy-start.8
  18.4 57.5 %shard_map.221 = (bf16[3,8,256,128]{3,2,1,0:T(8,128)(2,1)}, bf16[256,768]{1,0:T(8,128)(2,1)}, f32[128,768]{1,0:T(8,128)}, s32[256,2]{1,0:T(8,128)}, bf16[256,768...) custom-call(s32[8]{0:T(128)} %where_ref.1, ...), custom_call_target="tpu_custom_call" | custom-call | bytes 157286400 | tf_op jit(solution)/shard_map/pallas_call | solution.py:1329
  75.9 7.7 %all-to-all-start = ((bf16[8,48,768]{2,1,0:T(8,128)(2,1)}), bf16[8,48,768]{2,1,0:T(8,128)(2,1)S(1)}, u32[]{:S(2)}, u32[]{:S(2)}) async-start(bf16[8,48,768]{2,1,0:T(8,128)(2,1)} %get-tuple-element.66), calls=%async_computation | async-start | bytes 1179648 | tf_op jit(solution)/shard_map/all_to_all | solution.py:1371
  83.6 0.0 copy-done.8
  83.6 0.1 select_reduce_fusion
  83.7 0.6 pad_add_fusion.sc
  84.3 21.4 %shard_map.222 = (bf16[8,256,128]{2,1,0:T(8,128)(2,1)}, f32[8,128,384]{2,1,0:T(8,128)}, f32[8,1,384]{2,1,0:T(1,128)}) custom-call(s32[10]{0:T(128)} %pad_add_fusion.sc, bf16[3,8,256,128]{3,2,1,0:T(8,128)(2,1)} %get-tuple-element.64.recv_ref), custom_call_target="tpu_custom_call" | custom-call | flops 3221225472 | bytes 5242880 | tf_op jit(solution)/shard_map/pallas_call | solution.py:1375
  105.7 0.0 all-to-all-done.rest_ref
  105.7 0.0 copy-start.3
  105.7 0.0 all-gather.4.cloned.1.call-done.w_ref
  105.7 44.1 %shard_map.223 = (bf16[8,256,128]{2,1,0:T(8,128)(2,1)}, f32[256,768]{1,0:T(8,128)}, bf16[256,768]{1,0:T(8,128)(2,1)}, f32[256,128]{1,0:T(8,128)}, bf16[768,896]{1,0:T(8,128)(2,1)}) custom-call(bf16[8,256,128]{2,1,0:T(8,128)(2,1)} %get-tuple-element.67.attended_ref, bf16[768,768]{1,0:T(8,128)(2,1)} %all-gather.4.cloned.1.call-done.w_ref, ...), custom_call_target="tpu_custom_call" | custom-call | bytes 104857600 | tf_op jit(solution)/shard_map/pallas_call | solution.py:1405
  149.8 0.0 all-gather.6.cloned.1.call-done.wg_ref.wu_ref.wt_ref.wide_ref
  149.8 0.0 copy-done.3
  149.9 23.9 %shard_map.224 = (bf16[768,896]{1,0:T(8,128)(2,1)}, bf16[768,768]{1,0:T(8,128)(2,1)}, bf16[3,768,2048]{2,1,0:T(8,128)(2,1)}, bf16[768,768]{1,0:T(8,128)(2,1)}) custom-call(bf16[768,896]{1,0:T(8,128)(2,1)} %get-tuple-element.70.x_ref, bf16[8,48,768]{2,1,0:T(8,128)(2,1)} %get-tuple-element.71.first_ref, bf16[8,48,768]{2,1,0:T(8,128)(2,1)} %copy-done.3, ...), custom_call_target="tpu_custom_call" | custom-call | flops 14495514624 | bytes 25165824 | tf_op jit(solution)/shard_map/pallas_call | solution.py:1426
  173.8 0.0 all-gather.8.cloned.1.call-done.back_ref
  173.8 63.9 %shard_map.225 = (bf16[8,256,128]{2,1,0:T(8,128)(2,1)}, f32[256,768]{1,0:T(8,128)}, f32[256,768]{1,0:T(8,128)}, bf16[256,768]{1,0:T(8,128)(2,1)}, bf16[256,128]{...) custom-call(bf16[768,896]{1,0:T(8,128)(2,1)} %get-tuple-element.73.s, ...), custom_call_target="tpu_custom_call" | custom-call | bytes 157286400 | tf_op jit(solution)/shard_map/pallas_call | solution.py:1470
  237.7 6.5 %all-to-all-start.1 = ((bf16[8,96,768]{2,1,0:T(8,128)(2,1)}), bf16[8,96,768]{2,1,0:T(8,128)(2,1)S(1)}, u32[]{:S(2)}, u32[]{:S(2)}) async-start(bf16[8,96,768]{2,1,0:T(8,128)(2,1)} %bitcast.9), calls=%async_computation.1 | async-start | bytes 2359296 | tf_op jit(solution)/shard_map/all_to_all | solution.py:1563
  244.2 0.0 collective-permute-start
  244.2 2.0 collective-permute-start.1
  246.2 0.7 fusion.live_ref
  246.9 24.8 %shard_map.226.send_ref = bf16[3,8,256,128]{3,2,1,0:T(8,128)(2,1)} custom-call(s32[10]{0:T(128)} %pad_add_fusion.sc, bf16[3,8,256,128]{3,2,1,0:T(8,128)(2,1)} %get-tuple-element.64.recv_ref, bf16[8,256,128]{2,1,0:T(8,128)(2,1)} %get-tuple-element.80.grad_ref, f32[8,128,384]{2,1,0:T(8,128)} %get-tuple-element.81.keep_ref, f32[8,1,384]{2,1,0:T(1,128)} %get-tuple-element.82.lse_ref), custom_call_target="tpu_custom_call" | custom-call | flops 4831838208 | bytes 8388608 | tf_op jit(solution)/shard_map/pallas_call | solution.py:1539
  271.7 0.0 all-to-all-done.1
  271.7 0.0 copy-start
  271.7 1.0 copy-done
  272.7 42.5 %shard_map.227 = (bf16[3,8,256,128]{3,2,1,0:T(8,128)(2,1)}, bf16[3,2,192,2048]{3,2,1,0:T(8,128)(2,1)}, bf16[4,192,768]{2,1,0:T(8,128)(2,1)}, f32[768,128]{1,0:T(8,128)}, bf16[256,768]{1,0:T(8,128)(2,1)}) custom-call(bf16[3,8,256,128]{3,2,1,0:T(8,128)(2,1)} %shard_map.226.send_ref, bf16[768,896]{1,0:T(8,128)(2,1)} %get-tuple-element.70.x_ref, ...), custom_call_target="tpu_custom_call" | custom-call | bytes 125829120 | tf_op jit(solution)/shard_map/pallas_call | solution.py:1564
  315.2 0.0 collective-permute-done.1
  315.2 0.0 copy-start.2
  315.2 0.0 collective-permute-done
  315.3 0.0 copy-start.1
  315.3 0.8 copy-done.2
  316.1 0.5 copy-done.1
  316.6 94.2 %shard_map.228 = (f32[256,768]{1,0:T(8,128)}, bf16[192,4096]{1,0:T(8,128)(2,1)}, bf16[512,768]{1,0:T(8,128)(2,1)}, bf16[192,3200]{1,0:T(8,128)(2,1)}, bf16[3,192,2048]{2,1,0:T(8,128)(2,1)}) custom-call(bf16[3,8,256,128]{3,2,1,0:T(8,128)(2,1)} %get-tuple-element.91.recv_ref, f32[256,128]{1,0:T(8,128)} %get-tuple-element.122.cos_ref, ...), custom_call_target="tpu_custom_call" | custom-call | bytes 209715200 | tf_op jit(solution)/shard_map/pallas_call | solution.py:1617
  410.8 0.0 copy-start.4
  410.8 8.0 %shard_map.229 = (f32[192,2304]{1,0:T(8,128)}, f32[192,768]{1,0:T(8,128)}, f32[192,4096]{1,0:T(8,128)}, f32[512,768]{1,0:T(8,128)}, f32[192,4096]{1,0:T(8,128)},...) custom-call(bf16[192,3200]{1,0:T(8,128)(2,1)} %get-tuple-element.103.late_ref.small_ref, ...), custom_call_target="tpu_custom_call" | custom-call | bytes 23068672 | tf_op jit(solution)/shard_map/pallas_call | solution.py:1674
  418.8 1.3 fusion.2
  420.1 0.0 copy-done.4
  420.1 0.7 copy.41
  (2 shorter events, 0.0 us)
Async XLA Ops:
  7.2 98.5 %all-gather.4.cloned.1.call-start = ((), (), s32[]{:S(2)}) async-start(), calls=%async_computation.2 | async-start | bytes 1474560 | tf_op jit(solution)/shard_map/all_gather | solution.py:1295
  7.9 141.9 %all-gather.6.cloned.1.call-start = ((), (), s32[]{:S(2)}) async-start(), calls=%async_computation.3 | async-start | bytes 19660800 | tf_op jit(solution)/shard_map/all_gather | solution.py:1296
  11.5 1.4 copy-start.6
  11.5 2.3 copy-start.5
  11.5 3.0 copy-start.9
  11.5 3.6 copy-start.10
  11.5 4.1 copy-start.7
  11.5 162.2 %all-gather.8.cloned.1.call-start = ((), (), s32[]{:S(2)}) async-start(), calls=%async_computation.4 | async-start | bytes 3932160 | tf_op jit(solution)/shard_map/all_gather | solution.py:1299
  18.4 65.2 %copy-start.8 = (s32[8]{0:T(128)S(1)}, s32[8]{0:T(128)}, u32[]{:S(2)}) copy-start(s32[8]{0:T(128)} %where_ref.1) | copy-start | bytes 100
  75.9 29.8 %all-to-all-start = ((bf16[8,48,768]{2,1,0:T(8,128)(2,1)}), bf16[8,48,768]{2,1,0:T(8,128)(2,1)S(1)}, u32[]{:S(2)}, u32[]{:S(2)}) async-start(bf16[8,48,768]{2,1,0:T(8,128)(2,1)} %get-tuple-element.66), calls=%async_computation | async-start | bytes 1179648 | tf_op jit(solution)/shard_map/all_to_all | solution.py:1371
  105.7 44.2 %copy-start.3 = (bf16[8,48,768]{2,1,0:T(8,128)(2,1)}, bf16[8,48,768]{2,1,0:T(8,128)(2,1)S(1)}, u32[]{:S(2)}) copy-start(bf16[8,48,768]{2,1,0:T(8,128)(2,1)S(1)} %all-to-all-done.rest_ref) | copy-start | bytes 1769476
  237.7 33.9 %all-to-all-start.1 = ((bf16[8,96,768]{2,1,0:T(8,128)(2,1)}), bf16[8,96,768]{2,1,0:T(8,128)(2,1)S(1)}, u32[]{:S(2)}, u32[]{:S(2)}) async-start(bf16[8,96,768]{2,1,0:T(8,128)(2,1)} %bitcast.9), calls=%async_computation.1 | async-start | bytes 2359296 | tf_op jit(solution)/shard_map/all_to_all | solution.py:1563
  244.2 71.0 %collective-permute-start = (bf16[2,1,192,2048]{3,2,0,1:T(8,128)(2,1)}, bf16[2,1,192,2048]{3,2,0,1:T(8,128)(2,1)S(1)}, u32[]{:S(2)}, u32[]{:S(2)}) collective-permute-start(bf16[2,1,192,2048]{3,2,0,1:T(8,128)(2,1)} %bitcast.46), channel_id=1, source_target_pairs={{0,2},{1,3},{2,0},{3,1},{4,6},{5,7},{6,4},{7,5},{8,10},{9,11},{10,... | collective-permute-start | bytes 4718600 | tf_op jit(solution)/shard_map/ppermute | solution.py:1528
  244.2 71.0 %collective-permute-start.1 = (bf16[2,1,256,768]{3,2,0,1:T(8,128)(2,1)}, bf16[2,1,256,768]{3,2,0,1:T(8,128)(2,1)S(1)}, u32[]{:S(2)}, u32[]{:S(2)}) collective-permute-start(bf16[2,1,256,768]{3,2,0,1:T(8,128)(2,1)} %bitcast.48), channel_id=1, source_target_pairs={{0,2},{1,3},{2,0},{3,1},{4,6},{5,7},{6,4},{7,5},{8,10},{9,11},{10,... | collective-permute-start | bytes 2359304 | tf_op jit(solution)/shard_map/ppermute | solution.py:1528
  271.7 1.0 copy-start
  315.2 0.9 copy-start.2
  315.3 1.4 copy-start.1
  410.8 9.3 %copy-start.4 = (bf16[256,768]{1,0:T(8,128)(2,1)S(1)}, bf16[256,768]{1,0:T(8,128)(2,1)}, u32[]{:S(2)}) copy-start(bf16[256,768]{1,0:T(8,128)(2,1)} %get-tuple-element.90) | copy-start | bytes 1179652
Sparse Core Ops, SparseCore 0:
  9.6 20.3 all-gather.3
  31.6 103.2 all-gather.5
  136.5 28.5 all-gather.7

commit v6 on v5

--- a/solution.py
+++ b/solution.py
@@ -2,6 +2,7 @@
 
 import jax
 import jax.numpy as jnp
+import numpy as np
 from jax import lax
 from jax.experimental import pallas as pl
 from jax.experimental.pallas import tpu as pltpu
@@ -14,6 +15,7 @@
 FS = 2048
 LANES = 128
 CHUNK = 256
+BROAD = 512
 PACKED = 3 * D + LANES
 norm_eps = 1e-06
 F32 = jnp.float32
@@ -71,22 +73,6 @@
 
 def partner(t, lane):
     return jnp.where(lane % 64 < 32, pltpu.roll(t, 96, 1), pltpu.roll(t, 32, 1))
-
-
-def in_parts(v):
-    high = v.astype(BF16)
-    rest = v - high.astype(F32)
-    mid = rest.astype(BF16)
-    low = (rest - mid.astype(F32)).astype(BF16)
-    return high.astype(F32), mid.astype(F32), low.astype(F32)
-
-
-def part_lanes(v, lane):
-    high, mid, low = in_parts(v)
-    zero = jnp.zeros((), F32)
-    return jnp.where(
-        lane == 0, high, jnp.where(lane == 1, mid, jnp.where(lane == 2, low, zero))
-    ).astype(BF16)
 
 
 def picks(target_ref, places):
@@ -164,10 +150,8 @@
     x_ref,
     w_ref,
     router_ref,
-    gain_one_ref,
-    gain_two_ref,
-    cos_ref,
-    sin_ref,
+    gains_ref,
+    turn_ref,
     recv_ref,
     in_ref,
     tail_ref,
@@ -176,6 +160,8 @@
     dy_ref,
     dy_rest_ref,
     w_all,
+    cos_ref,
+    sin_ref,
     send,
     dy_send,
     small,
@@ -194,15 +180,10 @@
     mates = mates_of(members)
     shard = w_ref.shape[0]
     rows = x_ref.shape[0]
-    row = lax.broadcasted_iota(jnp.int32, (LANES, shard), 0)
-    gains = jnp.where(
-        row == experts,
-        gain_one_ref[...].astype(F32),
-        jnp.where(row == experts + 1, gain_two_ref[...].astype(F32), 0.0),
-    )
-    small[...] = gains.T
-    small[:, 0:experts] = router_ref[...].astype(F32)
-    small_all[fsdp] = small[...].astype(BF16)
+    small[...] = jnp.zeros_like(small)
+    small[0:experts] = router_ref[...].astype(F32)
+    small[experts : experts + 2] = gains_ref[...].astype(F32)
+    small_all[fsdp] = small[...].T.astype(BF16)
     for part in range(3):
         w_all[part, fsdp] = w_ref[:, part * D : (part + 1) * D]
     greet(peers + mates)
@@ -284,7 +265,12 @@
     tail_ref[...] = tail
     attn_in = (x * inv * tail[experts : experts + 1, :]).astype(BF16)
     in_ref[...] = attn_in
-    cos, sin = cos_ref[...], sin_ref[...]
+    position = where_ref[ctx] * rows + lax.broadcasted_iota(jnp.int32, (rows, LANES), 0)
+    angles = position.astype(F32) * turn_ref[...]
+    cos, sin = jnp.cos(angles), jnp.sin(angles)
+    sin = jnp.where(lane % 64 < 32, -sin, sin)
+    cos_ref[...] = cos
+    sin_ref[...] = sin
     for part in range(3):
         gather_rest(part)
         y = dot(attn_in, w_all[part].reshape(D, D))
@@ -361,24 +347,28 @@
     key_row = lax.broadcasted_iota(jnp.int32, (rows, share), 0)
     blocks = jnp.minimum(q_block + 1, (length + rows - 1) // rows)
 
-    def score_step(j, top):
-        keys = recv_ref[1, sc[j]]
-        s = dot_nt(keys, query)
-        s = jnp.where(key_row < limit - j * rows, s, -1e30)
-        scores[j] = s
-        return jnp.maximum(top, jnp.max(s, axis=0, keepdims=True))
-
-    top = lax.fori_loop(0, blocks, score_step, jnp.full((1, share), -1e30, F32))
-
-    def value_step(j, carry):
+    def score_step(pair, top):
+        found = []
+        for j in (2 * pair, 2 * pair + 1):
+            s = dot_nt(recv_ref[1, sc[j]], query)
+            s = jnp.where(key_row < limit - j * rows, s, -1e30)
+            scores[j] = s
+            found.append(jnp.max(s, axis=0, keepdims=True))
+        return jnp.maximum(top, jnp.maximum(found[0], found[1]))
+
+    pairs = (blocks + 1) // 2
+    top = lax.fori_loop(0, pairs, score_step, jnp.full((1, share), -1e30, F32))
+
+    def value_step(pair, carry):
         total, acc = carry
-        weights = jnp.exp(scores[j] - top)
-        total = total + jnp.sum(weights, axis=0, keepdims=True)
-        values = recv_ref[2, sc[j]]
-        return total, acc + dot_tn(values, weights.astype(BF16))
+        for j in (2 * pair, 2 * pair + 1):
+            weights = jnp.exp(scores[j] - top)
+            total = total + jnp.sum(weights, axis=0, keepdims=True)
+            acc = acc + dot_tn(recv_ref[2, sc[j]], weights.astype(BF16))
+        return total, acc
 
     total, acc = lax.fori_loop(
-        0, blocks, value_step, (jnp.zeros((1, share), F32), jnp.zeros((LANES, share), F32))
+        0, pairs, value_step, (jnp.zeros((1, share), F32), jnp.zeros((LANES, share), F32))
     )
     acc = acc / total
     keep_ref[0] = acc
@@ -411,18 +401,20 @@
     key_row = lax.broadcasted_iota(jnp.int32, (rows, share), 0)
     blocks = jnp.minimum(q_block + 1, (length + rows - 1) // rows)
 
-    def step(j, acc):
-        keys = recv_ref[1, sc[j]]
-        values = recv_ref[2, sc[j]]
-        s = dot_nt(keys, query)
-        weights = jnp.exp(jnp.where(key_row < limit - j * rows, s, -1e30) - lse)
-        dweights = dot_nt(values, grad)
-        dscores = (weights * (dweights - delta)).astype(BF16)
-        dkeys[j] += dot(dscores, query)
-        dvalues[j] += dot(weights.astype(BF16), grad)
-        return acc + dot_tn(keys, dscores)
-
-    acc = lax.fori_loop(0, blocks, step, jnp.zeros((LANES, share), F32))
+    def step(pair, acc):
+        for j in (2 * pair, 2 * pair + 1):
+            keys = recv_ref[1, sc[j]]
+            values = recv_ref[2, sc[j]]
+            s = dot_nt(keys, query)
+            weights = jnp.exp(jnp.where(key_row < limit - j * rows, s, -1e30) - lse)
+            dweights = dot_nt(values, grad)
+            dscores = (weights * (dweights - delta)).astype(BF16)
+            dkeys[j] += dot(dscores, query)
+            dvalues[j] += dot(weights.astype(BF16), grad)
+            acc = acc + dot_tn(keys, dscores)
+        return acc
+
+    acc = lax.fori_loop(0, (blocks + 1) // 2, step, jnp.zeros((LANES, share), F32))
     dquery = unstack_rows(back, acc.T * 0.125, offset, lane)
     out_ref[0, source] = dquery.astype(BF16)
 
@@ -451,11 +443,15 @@
     in_ref,
     gates_ref,
     rows_ref,
+    row_gates_ref,
     outgoing,
+    outgates,
     came_send,
     came_recv,
     send_sem,
     recv_sem,
+    gate_send,
+    gate_recv,
     own_sem,
 ):
     ctx = lax.axis_index("ctx")
@@ -490,19 +486,17 @@
     raised = [jnp.exp(c - top) for c in chosen]
     gates = [r / (raised[0] + raised[1]) for r in raised]
     gates_ref[...] = jnp.where(lane == 0, gates[0], gates[1])
-    outgoing[:, 0:D] = dot_tn(pick[0] + pick[1], ffn_in).astype(BF16)
-    outgoing[:, D:] = (
-        dot_tn(pick[0], part_lanes(gates[0], lane)) + dot_tn(pick[1], part_lanes(gates[1], lane))
-    ).astype(BF16)
+    outgoing[...] = dot_tn(pick[0] + pick[1], ffn_in).astype(BF16)
     block = outgoing.shape[0] // n
 
     def block_at(p):
         return pl.ds(pl.multiple_of(p * block, 16), block)
 
-    own = pltpu.make_async_copy(
-        outgoing.at[block_at(ctx)], rows_ref.at[block_at(ctx)], own_sem.at[1]
-    )
-    own.start()
+    own = [
+        pltpu.make_async_copy(
+            outgoing.at[block_at(ctx)], rows_ref.at[block_at(ctx)], own_sem.at[1]
+        )
+    ]
     copies = [
         remote(
             outgoing.at[block_at(p[0])],
@@ -513,11 +507,29 @@
         )
         for d, p in enumerate(peers)
     ]
-    for c in copies:
+    for c in own + copies:
         c.start()
-    for c in copies:
+    for p in range(n):
+        row = sum(
+            jnp.sum(
+                jnp.where(lane == target_ref[:, k : k + 1] - p * block, gates[k], 0.0),
+                axis=0,
+                keepdims=True,
+            )
+            for k in range(2)
+        )
+        outgates[p] = jnp.broadcast_to(row, outgates.shape[1:])
+    own.append(pltpu.make_async_copy(outgates.at[ctx], row_gates_ref.at[ctx], own_sem.at[2]))
+    own[-1].start()
+    for d, p in enumerate(peers):
+        copies.append(
+            remote(
+                outgates.at[p[0]], row_gates_ref.at[ctx], gate_send.at[d], gate_recv.at[d], p
+            )
+        )
+        copies[-1].start()
+    for c in copies + own:
         c.wait()
-    own.wait()
 
 
 def gated(g, u, da):
@@ -528,18 +540,21 @@
 
 def expert_kernel(
     x_ref,
+    gates_ref,
     first_ref,
     rest_ref,
     wg_ref,
     wu_ref,
     wt_ref,
     dx_ref,
+    dgate_ref,
     res_ref,
     mid_ref,
     dy_ref,
     dx_acc,
     res_acc,
     dgate,
+    gate_rows,
 ):
     c = pl.program_id(0)
 
@@ -553,9 +568,11 @@
         for p in range(n):
             dy_ref[p * block : p * block + early] = first_ref[p]
             dy_ref[p * block + early : (p + 1) * block] = rest_ref[p]
-
-    x, dy = x_ref[:, 0:D], dy_ref[...]
-    gate = jnp.sum(x_ref[:, D:].astype(F32), axis=-1, keepdims=True)
+            column = gates_ref[p].T[0:block, 0:1]
+            gate_rows[p * block : (p + 1) * block] = jnp.broadcast_to(column, (block, LANES))
+
+    x, dy = x_ref[...], dy_ref[...]
+    gate = gate_rows[:, 0:1]
     wg, wu, wt = wg_ref[...], wu_ref[...], wt_ref[...]
     da = dot(dy, wt)
     act, dg, du = gated(dot(x, wg), dot(x, wu), da * gate)
@@ -570,8 +587,12 @@
     @pl.when(c == pl.num_programs(0) - 1)
     def _():
         res_ref[...] = res_acc[...].astype(BF16)
-        dx_ref[:, 0:D] = dx_acc[...].astype(BF16)
-        dx_ref[:, D:] = part_lanes(dgate[:, 0:1], lanes_of(dgate.shape[0]))
+        dx_ref[...] = dx_acc[...].astype(BF16)
+        n, early = first_ref.shape[0:2]
+        block = early + rest_ref.shape[1]
+        dgate_ref[...] = jnp.zeros_like(dgate_ref)
+        for p in range(n):
+            dgate_ref[p, :, 0:block] = dgate[p * block : (p + 1) * block].T[0:8]
 
 
 def ring_split(rows, columns, pieces):
@@ -594,6 +615,7 @@
     heads,
     experts,
     send_ref,
+    row_dgates_ref,
     in_ref,
     dout_ref,
     residual_ref,
@@ -613,9 +635,11 @@
     a_keep,
     a_give,
     b_keep,
+    b_other,
+    came,
+    came_dgates,
+    packets,
     b_give,
-    came,
-    packets,
     mids,
     dx_acc,
     a_all,
@@ -632,28 +656,46 @@
     own_sem,
     packet_send,
     packet_recv,
+    dgate_send,
+    dgate_recv,
     a_sem,
     b_sem,
+    far_sem,
     w_sem,
 ):
     ctx, fsdp = lax.axis_index("ctx"), lax.axis_index("fsdp")
     bits = members.bit_length() - 1
     peers = row_peers(n)
-    mate = mates_of(members)[0]
-    greet(peers + [mate])
+    mate, far = mates_of(members)[0:2]
+    greet(peers + [mate, far])
     block = send_ref.shape[0] // n
 
     def block_at(p):
         return pl.ds(pl.multiple_of(p * block, 16), block)
 
-    own = pltpu.make_async_copy(send_ref.at[block_at(ctx)], came.at[block_at(ctx)], own_sem.at[0])
-    own.start()
     copies = [
-        remote(
-            send_ref.at[block_at(p[0])], came.at[block_at(ctx)], send_sem.at[d], recv_sem.at[d], p
+        pltpu.make_async_copy(send_ref.at[block_at(ctx)], came.at[block_at(ctx)], own_sem.at[0]),
+        pltpu.make_async_copy(row_dgates_ref.at[ctx], came_dgates.at[ctx], own_sem.at[2]),
+    ]
+    for d, p in enumerate(peers):
+        copies.append(
+            remote(
+                row_dgates_ref.at[p[0]],
+                came_dgates.at[ctx],
+                dgate_send.at[d],
+                dgate_recv.at[d],
+                p,
+            )
         )
-        for d, p in enumerate(peers)
-    ]
+        copies.append(
+            remote(
+                send_ref.at[block_at(p[0])],
+                came.at[block_at(ctx)],
+                send_sem.at[d],
+                recv_sem.at[d],
+                p,
+            )
+        )
     for c in copies:
         c.start()
 
@@ -691,8 +733,9 @@
         act, dg, du = act.astype(BF16), dg.astype(BF16), du.astype(BF16)
         res_ref[...] += dot(act, wo)
         dx_acc[...] += dot_nt(dg, wg) + dot_nt(du, wu)
-        mids[c] = dg
-        mids[steps + c] = du
+        column = pl.ds(pl.multiple_of(c * CHUNK, CHUNK), CHUNK)
+        mids[0, :, column] = dg
+        mids[1, :, column] = du
         value = dot_tn(act, dy).astype(BF16)
         span = min(piece, CHUNK)
         for u in range(CHUNK // span):
@@ -719,6 +762,9 @@
             b_all.at[i, pl.ds(half, half)], b_caught.at[i], b_sem.at[i, 0], b_sem.at[i, 1], mate
         )
 
+    def b_cross(i):
+        return remote(b_give.at[i], b_other.at[i], far_sem.at[i, 0], far_sem.at[i, 1], far)
+
     for i in range(2):
         b_swap(i).start()
     rows = shard_rows(members, D // members)
@@ -729,14 +775,13 @@
     for i in range(2):
 
         def grad_step(c, i=i):
-            value = dot(xt[...], mids[i * steps + c]).astype(BF16)
-            column = pl.ds(pl.multiple_of(c * CHUNK, CHUNK), CHUNK)
+            column = pl.ds(pl.multiple_of(c * BROAD, BROAD), BROAD)
+            value = dot(xt[...], mids[i, :, column]).astype(BF16)
             for j in range(members):
                 a_all[i, j, :, column] = value[j * shard : (j + 1) * shard]
 
-        loop(grad_step, 0, steps)
+        loop(grad_step, 0, FS // BROAD)
         a_swap(i).start()
-    for i in range(2):
         b_swap(i).wait_recv()
         for j in range(half):
             total = (b_all[i, j].astype(F32) + b_caught[i, j].astype(F32)).astype(BF16)
@@ -744,23 +789,34 @@
                 b_keep[i, j] = total
             else:
                 b_give[i, j - quarter] = total
+        b_cross(i).start()
     for c in copies:
         c.wait()
-    own.wait()
 
     pick = picks(target_ref, came.shape[0])
     gates = [gates_ref[:, k : k + 1] for k in range(2)]
-    parts = came[:, D:]
-    dgate = [jnp.sum(dot(pick[k], parts), axis=-1, keepdims=True) for k in range(2)]
+    lane = lanes_of(pick[0].shape[0])
+    dgate = [
+        jnp.sum(
+            sum(
+                jnp.where(
+                    lane == target_ref[:, k : k + 1] - p * block, came_dgates[p, 0:1, :], 0.0
+                )
+                for p in range(n)
+            ),
+            axis=-1,
+            keepdims=True,
+        )
+        for k in range(2)
+    ]
     mean = gates[0] * dgate[0] + gates[1] * dgate[1]
-    lane = lanes_of(pick[0].shape[0])
     dlogits = sum(
         jnp.where(lane == routes_ref[:, k : k + 1], gates[k] * (dgate[k] - mean), 0.0)
         for k in range(2)
     ).astype(BF16)
     dlogits_ref[...] = dlogits
     tail = tail_ref[...]
-    dffn = dot(pick[0] + pick[1], came[:, 0:D]) + dx_acc[...] + dot(dlogits, tail.astype(BF16))
+    dffn = dot(pick[0] + pick[1], came[...]) + dx_acc[...] + dot(dlogits, tail.astype(BF16))
     residual = residual_ref[...]
     inv = lax.rsqrt(jnp.mean(residual * residual, axis=-1, keepdims=True) + norm_eps)
     scaled = dffn * tail[experts + 1 : experts + 2, :]
@@ -794,6 +850,7 @@
     for i in range(2):
         a_swap(i).wait_send()
         b_swap(i).wait_send()
+        b_cross(i).wait()
 
 
 def back_exchange_kernel(
@@ -816,12 +873,15 @@
     mid_ref,
     recv_ref,
     sum_ref,
-    out_grad_ref,
+    out_keep,
+    out_other,
     router_ref,
     output_ref,
     give,
     caught,
     crossed,
+    out_all,
+    out_caught,
     raw,
     xt,
     dyt,
@@ -833,6 +893,7 @@
     give_sem,
     caught_sem,
     cross_sem,
+    out_sem,
     mid_sem,
 ):
     ctx = lax.axis_index("ctx")
@@ -849,13 +910,13 @@
     for c in copies:
         c.start()
 
-    steps = mid_ref.shape[2] // CHUNK
+    steps = mid_ref.shape[2] // BROAD
     parts = mid_ref.shape[0]
 
     def fetch(i, c, slot):
-        column = pl.multiple_of(c * CHUNK, CHUNK)
+        column = pl.multiple_of(c * BROAD, BROAD)
         return pltpu.make_async_copy(
-            mid_ref.at[i, :, pl.ds(column, CHUNK)], mids.at[slot], mid_sem.at[slot]
+            mid_ref.at[i, :, pl.ds(column, BROAD)], mids.at[slot], mid_sem.at[slot]
         )
 
     fetch(0, 0, 0).start()
@@ -868,13 +929,32 @@
         for j in range(members):
             target[j * shard : (j + 1) * shard, :] = raw[pl.ds(rows[j], shard), :]
 
-    turned(x_ref[:, 0:D], xt)
+    acc[...] = jnp.zeros_like(acc)
+    branch = branch_ref[...]
+    for d, head in enumerate(heads):
+        acc[64 * head : 64 * head + LANES, :] += dot_tn(came_ref[d], branch)
+    for j in range(members):
+        out_all[j] = acc[pl.ds(rows[j], shard), :].astype(BF16)
+    quarter = members // 4
+    out_swap = remote(
+        out_all.at[pl.ds(half, half)], out_caught, out_sem.at[0], out_sem.at[1], mate
+    )
+    out_swap.start()
+    turned(x_ref[...], xt)
     turned(dy_ref[...], dyt)
+    out_swap.wait_recv()
+    for j in range(half):
+        add_into(out_all, j, out_caught)
+    for j in range(quarter):
+        out_keep[j] = out_all[j]
+    out_cross = remote(
+        out_all.at[pl.ds(quarter, quarter)], out_other, out_sem.at[2], out_sem.at[3], far
+    )
+    out_cross.start()
 
     def swap(i):
         return remote(give.at[i], caught.at[i], give_sem.at[i], caught_sem.at[i], mate)
 
-    quarter = members // 4
     cross = remote(
         sum_ref.at[0, pl.ds(quarter, quarter)], crossed, cross_sem.at[0], cross_sem.at[1], far
     )
@@ -890,7 +970,7 @@
                 fetch(i, c + 1, 1 - slot).start()
 
             value = dot(left[...], mids[slot]).astype(BF16)
-            column = pl.ds(pl.multiple_of(c * CHUNK, CHUNK), CHUNK)
+            column = pl.ds(pl.multiple_of(c * BROAD, BROAD), BROAD)
             for j in range(half):
                 sum_ref[i, j, :, column] = value[j * shard : (j + 1) * shard]
                 give[i, j, :, column] = value[(half + j) * shard : (half + j + 1) * shard]
@@ -906,12 +986,6 @@
         if i == 1:
             cross.start()
 
-    acc[...] = jnp.zeros_like(acc)
-    branch = branch_ref[...]
-    for d, head in enumerate(heads):
-        acc[64 * head : 64 * head + LANES, :] += dot_tn(came_ref[d], branch)
-    for j in range(members):
-        out_grad_ref[j] = acc[pl.ds(rows[j], shard), :].astype(BF16)
     router_ref[...] = dot_tn(in_ref[...], dlogits_ref[...])
     pick = picks(target_ref, res_ref.shape[0])
     came = res_ref[...]
@@ -928,6 +1002,8 @@
         add_into(sum_ref.at[0], j, crossed)
     for i in range(parts):
         swap(i).wait_send()
+    out_swap.wait_send()
+    out_cross.wait()
 
 
 def last_kernel(
@@ -944,13 +1020,14 @@
     w_ref,
     tail_ref,
     dres_ref,
-    out_grad_ref,
     router_ref,
     dgain_ref,
     a_ref,
     a_other,
     b_ref,
     b_other,
+    o_ref,
+    o_other,
     e_ref,
     x_out,
     a_out,
@@ -1119,10 +1196,12 @@
     for i in range(2):
         load(2 + i, b_ref.at[i], 0, b_other.at[i])
         first(2 + i)
-    waiting = [steps_of(i) for i in range(4)]
+    load(4, o_ref, 0, o_other)
+    first(4)
+    waiting = [steps_of(i) for i in range(5)]
 
     def dense_step():
-        for queue in waiting[0:4]:
+        for queue in waiting[0:5]:
             if queue:
                 queue.pop(0)()
 
@@ -1166,8 +1245,7 @@
     gains = jnp.where(row == experts, dgain_one, jnp.where(row == experts + 1, dgain_ref[...], 0.0))
     small[...] = router_ref[...] + gains.T
     for j in range(members):
-        packs[3][j, :, 0:LANES] = small[pl.ds(rows[j], shard), :].astype(BF16)
-        packs[3][j, :, LANES:] = out_grad_ref[j]
+        packs[3][j] = small[pl.ds(rows[j], shard), :].astype(BF16)
     level_copy(3, 0).start()
     level_next(2)
     scaled = dnorm * gain
@@ -1182,27 +1260,32 @@
             level_add(p, b)
             if b + 1 < bits:
                 level_copy(p, b + 1).start()
-        load(4 + p, packs[p].at[0])
-        first(4 + p)
-        dense_step()
-        for queue in waiting[4:]:
+        load(5 + p, packs[p].at[0])
+        first(5 + p)
+        for queue in waiting[5:]:
             queue.pop(0)()
-        waiting.append(steps_of(4 + p))
+        if p < 3:
+            dense_step()
+        waiting.append(steps_of(5 + p))
+    turns = 0
     while any(waiting):
-        for i, queue in enumerate(waiting):
-            if queue:
+        turns += 1
+        for i, queue in reversed(list(enumerate(waiting))):
+            if queue and (i >= 5 or turns % 2 == 0 or not any(waiting[5:])):
                 queue.pop(0)()
-                if not queue and i < 4:
-                    if i < 2:
+                if not queue and i < 5:
+                    if i == 4:
+                        save(i, c_out, PACKED)
+                    elif i < 2:
                         save(i, a_out, i * splits[0][4])
                     else:
                         height = splits[2][0] * splits[2][2]
                         save(i, b_out.at[pl.ds((i - 2) * height, height)])
-        if not any(waiting[0:4]) and parts > 1:
+        if not any(waiting[0:5]) and parts > 1:
             e_add(1, 1)
             parts = min(parts, 1)
     for p in range(4):
-        save(4 + p, c_out, p * D)
+        save(5 + p, c_out, p * D)
     parts = e_ref.shape[0]
     for i in range(2, parts):
         e_add(i, 1)
@@ -1301,12 +1384,8 @@
 
     query_pos = position_block[ctx_index] * rows + jnp.arange(rows, dtype=jnp.int32)
     live = (query_pos < length).astype(F32)[:, None]
-    halves = HEAD_DIM // 2
-    inverse = 10000.0 ** (-(jnp.arange(halves, dtype=F32) * 2.0 / HEAD_DIM))
-    angles = query_pos.astype(F32)[:, None] * inverse[None, :]
-    cos, sin = jnp.cos(angles), jnp.sin(angles)
-    cos = jnp.concatenate([cos, cos, cos, cos], axis=1)
-    sin = jnp.concatenate([-sin, sin, -sin, sin], axis=1)
+    rates = 10000.0 ** (-(np.arange(HEAD_DIM // 2) * 2.0 / HEAD_DIM))
+    rates = jnp.asarray(np.tile(rates.astype(np.float32), 4)[None])
 
     order = jnp.sum(
         jnp.where(
@@ -1325,8 +1404,8 @@
     whole = pl.BlockSpec(memory_space=pltpu.VMEM)
     scalar = pl.BlockSpec(memory_space=pltpu.SMEM)
     block = places // n_ctx
-    early = block // 32 * 16
-    recv, attn_in, tail, target, dout, dy_first, dy_rest, qkv_weight = comm_call(
+    early = block // 48 * 16
+    recv, attn_in, tail, target, dout, dy_first, dy_rest, qkv_weight, cos, sin = comm_call(
         functools.partial(open_kernel, n_ctx, members, heads, experts, capacity, early),
         (
             shape((3, n_ctx, rows, LANES), BF16),
@@ -1337,14 +1416,16 @@
             shape((n_ctx, early, D), BF16),
             shape((n_ctx, block - early, D), BF16),
             shape((3, members, local, D), BF16),
+            shape((rows, LANES), F32),
+            shape((rows, LANES), F32),
         ),
         3,
-        in_specs=[scalar] * 2 + [whole] * 9,
-        out_specs=[whole] * 8,
+        in_specs=[scalar] * 2 + [whole] * 7,
+        out_specs=[whole] * 10,
         scratch_shapes=[
             pltpu.VMEM((3, n_ctx, rows, LANES), BF16),
             pltpu.VMEM((n_ctx, early, D), BF16),
-            pltpu.VMEM((local, LANES), F32),
+            pltpu.VMEM((LANES, local), F32),
             pltpu.VMEM((members, local, LANES), BF16),
             pltpu.SemaphoreType.DMA((4, bits, members)),
             pltpu.SemaphoreType.DMA((4, bits, members)),
@@ -1362,11 +1443,9 @@
         cotangent[0],
         x,
         w_qkv,
-        w_router,
-        gain_attn[None],
-        gain_ffn[None],
-        cos,
-        sin,
+        w_router.T,
+        jnp.stack([gain_attn, gain_ffn]),
+        rates,
     )
     dy_rest = exchange(dy_rest)
 
@@ -1402,31 +1481,37 @@
     def full(*dims):
         return pl.BlockSpec(dims, lambda *at: (0,) * len(dims))
 
-    came, residual, ffn_in, gates, x_rows = comm_call(
+    came, residual, ffn_in, gates, x_rows, row_gates = comm_call(
         functools.partial(middle_kernel, n_ctx, heads, experts),
         (
             shape((n_ctx, rows, LANES), BF16),
             shape((rows, D), F32),
             shape((rows, D), BF16),
             shape((rows, LANES), F32),
-            shape((places, D + LANES), BF16),
+            shape((places, D), BF16),
+            shape((n_ctx, 8, LANES), F32),
         ),
         4,
         in_specs=[whole] * 6,
-        out_specs=[whole] * 5,
-        scratch_shapes=[pltpu.VMEM((places, D + LANES), BF16)]
-        + [pltpu.SemaphoreType.DMA((n_ctx - 1,)) for _ in range(4)]
-        + [pltpu.SemaphoreType.DMA((2,))],
+        out_specs=[whole] * 6,
+        scratch_shapes=[
+            pltpu.VMEM((places, D), BF16),
+            pltpu.VMEM((n_ctx, 8, LANES), F32),
+        ]
+        + [pltpu.SemaphoreType.DMA((n_ctx - 1,)) for _ in range(6)]
+        + [pltpu.SemaphoreType.DMA((3,))],
         nbytes=100 << 20,
     )(attended, out_weight, x, tail, routes[0], target)
 
     half, quarter = members // 2, members // 4
     steps = FS // CHUNK
-    wide = FF // CHUNK
-    expert_dx, expert_res, expert_mid, dy_rows = call(
+    wide = FF // BROAD
+    base = 2 * FS // BROAD
+    expert_dx, row_dgates, expert_res, expert_mid, dy_rows = call(
         expert_kernel,
         (
-            shape((places, D + LANES), BF16),
+            shape((places, D), BF16),
+            shape((n_ctx, 8, LANES), F32),
             shape((places, D), BF16),
             shape((3, places, FF), BF16),
             shape((places, D), BF16),
@@ -1435,25 +1520,28 @@
         nbytes=24 << 20,
         grid=(wide,),
         in_specs=[
-            full(places, D + LANES),
+            full(places, D),
+            full(n_ctx, 8, LANES),
             full(n_ctx, early, D),
             full(n_ctx, block - early, D),
-            pl.BlockSpec((D, CHUNK), lambda c: (0, 2 * steps + c)),
-            pl.BlockSpec((D, CHUNK), lambda c: (0, 2 * steps + wide + c)),
-            pl.BlockSpec((D, CHUNK), lambda c: (0, 2 * steps + 2 * wide + c)),
+            pl.BlockSpec((D, BROAD), lambda c: (0, base + c)),
+            pl.BlockSpec((D, BROAD), lambda c: (0, base + wide + c)),
+            pl.BlockSpec((D, BROAD), lambda c: (0, base + 2 * wide + c)),
         ],
         out_specs=[
-            full(places, D + LANES),
             full(places, D),
-            pl.BlockSpec((3, places, CHUNK), lambda c: (0, 0, c)),
+            full(n_ctx, 8, LANES),
+            full(places, D),
+            pl.BlockSpec((3, places, BROAD), lambda c: (0, 0, c)),
             full(places, D),
         ],
         scratch_shapes=[
             pltpu.VMEM((places, D), F32),
             pltpu.VMEM((places, D), F32),
             pltpu.VMEM((places, LANES), F32),
+            pltpu.VMEM((places, LANES), F32),
         ],
-    )(x_rows, dy_first, dy_rest, weights, weights, weights)
+    )(x_rows, row_gates, dy_first, dy_rest, weights, weights, weights)
     b_rows = FS // members // 2
     anywhere = pl.BlockSpec(memory_space=pl.ANY)
     (
@@ -1466,7 +1554,7 @@
         dense_keep,
         dense_give,
         so_keep,
-        so_give,
+        so_came,
     ) = comm_call(
         functools.partial(shared_kernel, n_ctx, members, heads, experts),
         (
@@ -1480,12 +1568,14 @@
         + (shape((2, quarter, local, FS), BF16),) * 2
         + (shape((2, quarter, b_rows, D), BF16),) * 2,
         2,
-        in_specs=[whole] * 9 + [anywhere] * 2,
+        in_specs=[whole] * 10 + [anywhere] * 2,
         out_specs=[whole] * 10,
         scratch_shapes=[
-            pltpu.VMEM((places, D + LANES), BF16),
+            pltpu.VMEM((places, D), BF16),
+            pltpu.VMEM((n_ctx, 8, LANES), F32),
             pltpu.VMEM((n_ctx, rows, LANES), BF16),
-            pltpu.VMEM((2 * steps, rows, CHUNK), BF16),
+            pltpu.VMEM((2, quarter, b_rows, D), BF16),
+            pltpu.VMEM((2, rows, FS), BF16),
             pltpu.VMEM((rows, D), F32),
             pltpu.VMEM((2, members, local, FS), BF16),
             pltpu.VMEM((2, members, b_rows, D), BF16),
@@ -1498,9 +1588,12 @@
             pltpu.VMEM((2, CHUNK, D), BF16),
             pltpu.SemaphoreType.DMA((n_ctx - 1,)),
             pltpu.SemaphoreType.DMA((n_ctx - 1,)),
-            pltpu.SemaphoreType.DMA((2,)),
+            pltpu.SemaphoreType.DMA((3,)),
             pltpu.SemaphoreType.DMA((n_ctx - 1,)),
             pltpu.SemaphoreType.DMA((n_ctx - 1,)),
+            pltpu.SemaphoreType.DMA((n_ctx - 1,)),
+            pltpu.SemaphoreType.DMA((n_ctx - 1,)),
+            pltpu.SemaphoreType.DMA((2, 2)),
             pltpu.SemaphoreType.DMA((2, 2)),
             pltpu.SemaphoreType.DMA((2, 2)),
             pltpu.SemaphoreType.DMA((2, 3)),
@@ -1508,6 +1601,7 @@
         nbytes=150 << 20,
     )(
         expert_dx,
+        row_dgates,
         ffn_in,
         dout,
         residual,
@@ -1523,18 +1617,20 @@
     def gathered(terms):
         return sum(t.astype(F32) for t in terms).astype(BF16)
 
-    def rest_of(keep, give):
-        for b in range(1, bits):
-            came_in = lax.ppermute(give, "fsdp", [(i, i ^ (1 << b)) for i in range(members)])
-            if b + 1 < bits:
-                count = keep.shape[1] // 2
-                give = gathered([keep[:, count:], came_in[:, count:]])
-                keep = gathered([keep[:, :count], came_in[:, :count]])
+    def cross(give, b):
+        return lax.ppermute(give, "fsdp", [(i, i ^ (1 << b)) for i in range(members)])
+
+    def rest_of(keep, came_in):
+        for b in range(2, bits):
+            count = keep.shape[1] // 2
+            give = gathered([keep[:, count:], came_in[:, count:]])
+            keep = gathered([keep[:, :count], came_in[:, :count]])
+            came_in = cross(give, b)
         return keep[:, 0], came_in[:, 0]
 
     branch_recv, expert_res = lax.optimization_barrier((branch_recv, expert_res))
-    dense_part, dense_other = rest_of(dense_keep, dense_give)
-    so_part, so_other = rest_of(so_keep, so_give)
+    dense_part, dense_other = rest_of(dense_keep, cross(dense_give, 1))
+    so_part, so_other = rest_of(so_keep, so_came)
 
     dsend = call(
         functools.partial(attend_back_kernel, n_ctx, share),
@@ -1561,33 +1657,37 @@
         ),
     )(scalars, recv, branch_recv, kept, lse)
     res_came = exchange(expert_res.reshape(n_ctx, -1, D)).reshape(places, D)
-    drecv, expert_sum, out_grad, grad_router, output = comm_call(
+    drecv, expert_sum, out_keep, out_came, grad_router, output = comm_call(
         functools.partial(back_exchange_kernel, n_ctx, members, heads),
         (
             shape((3, n_ctx, rows, LANES), BF16),
             shape((3, half, local, FF), BF16),
-            shape((members, local, D), BF16),
+            shape((quarter, local, D), BF16),
+            shape((quarter, local, D), BF16),
             shape((D, LANES), F32),
             shape((rows, D), BF16),
         ),
         1,
-        in_specs=[whole] * 13 + [pl.BlockSpec(memory_space=pl.ANY)],
-        out_specs=[whole] * 5,
+        in_specs=[whole] * 13 + [anywhere],
+        out_specs=[whole] * 6,
         scratch_shapes=[
             pltpu.VMEM((3, half, local, FF), BF16),
             pltpu.VMEM((3, half, local, FF), BF16),
-            pltpu.VMEM((members // 4, local, FF), BF16),
+            pltpu.VMEM((quarter, local, FF), BF16),
+            pltpu.VMEM((members, local, D), BF16),
+            pltpu.VMEM((half, local, D), BF16),
             pltpu.VMEM((D, places), BF16),
             pltpu.VMEM((D, places), BF16),
             pltpu.VMEM((D, places), BF16),
             pltpu.VMEM((D, D), F32),
-            pltpu.VMEM((2, places, CHUNK), BF16),
+            pltpu.VMEM((2, places, BROAD), BF16),
             pltpu.SemaphoreType.DMA((n_ctx - 1,)),
             pltpu.SemaphoreType.DMA((n_ctx - 1,)),
             pltpu.SemaphoreType.DMA,
             pltpu.SemaphoreType.DMA((3,)),
             pltpu.SemaphoreType.DMA((3,)),
             pltpu.SemaphoreType.DMA((2,)),
+            pltpu.SemaphoreType.DMA((4,)),
             pltpu.SemaphoreType.DMA((2,)),
         ],
         nbytes=120 << 20,
@@ -1609,8 +1709,9 @@
     )
 
     late_width = PACKED + D
-    late_widths = [D, D, D, D + LANES]
-    sizes = [(local, FS)] * 2 + [(FS // members // 2, D)] * 2
+    out_part, out_other = rest_of(out_keep[None], out_came[None])
+    late_widths = [D, D, D, LANES]
+    sizes = [(local, FS)] * 2 + [(FS // members // 2, D)] * 2 + [(local, D)]
     sizes += [(local, width) for width in late_widths]
     splits = [ring_split(r, c, n_ctx) + (c,) for r, c in sizes]
     tiles = [(n_ctx, t[2], t[3]) for t in splits]
@@ -1624,7 +1725,7 @@
             shape((3, local, FF), BF16),
         ),
         0,
-        in_specs=[whole] * 16,
+        in_specs=[whole] * 17,
         out_specs=[whole] * 5,
         scratch_shapes=[pltpu.VMEM(t, BF16) for t in tiles * 4]
         + [pltpu.VMEM((members, local, width), BF16) for width in late_widths]
@@ -1639,8 +1740,8 @@
             pltpu.VMEM((D, rows), BF16),
             pltpu.VMEM((D, rows), BF16),
             pltpu.VMEM((D, LANES), F32),
-            pltpu.SemaphoreType.DMA((8, 2, n_ctx)),
-            pltpu.SemaphoreType.DMA((8, 2, n_ctx)),
+            pltpu.SemaphoreType.DMA((9, 2, n_ctx)),
+            pltpu.SemaphoreType.DMA((9, 2, n_ctx)),
             pltpu.SemaphoreType.DMA((4, bits)),
             pltpu.SemaphoreType.DMA((4, bits)),
             pltpu.SemaphoreType.DMA((3, max(1, bits - 1))),
@@ -1656,13 +1757,14 @@
         qkv_weight,
         tail,
         dres,
-        out_grad,
         grad_router,
         dgain_two,
         dense_part,
         dense_other,
         so_part,
         so_other,
+        out_part[0],
+        out_other[0],
         expert_sum,
     )
 

time: 427 us -> 408 us (0.956)
  Pallas kernels: 380 us -> 363 us
    pallas_call x1, Pallas kernels: 63.9 us -> 51.2 us  [on_device(): comm_call(functools.partial(shared_kernel, n_ctx, members, heads, experts...]
    pallas_call x1, Pallas kernels: 21.4 us -> 16.4 us  [on_device(): call(functools.partial(attend_kernel, n_ctx, share), (shape((n_ctx, rows,...]
  transfers between devices with their start and end apart: 7 -> 6, of which waited for: 0 -> 1; matrix products, arithmetic and copies ran while one was open for 2% -> 2% of each run, Pallas kernels for 50% -> 52%
where the time goes in v6:
time: 408 us
  Pallas kernels  363 us (89%)
  between operations  15.2 us (4%)
  starting transfers between devices  14.1 us (3%)
  local copies, waits for them, and re-layouts  5.64 us (1%)
  other arithmetic  5.46 us (1%)
  waiting for transfers between devices  4.73 us (1%)
    pallas_call x1, Pallas kernels, on_device(): comm_call(functools.partial(last_kernel, n_ctx, members, heads, experts,...  92.4 us
    pallas_call x1, Pallas kernels, on_device(): comm_call(functools.partial(open_kernel, n_ctx, members, heads, experts,...  61 us
    pallas_call x1, Pallas kernels, on_device(): comm_call(functools.partial(shared_kernel, n_ctx, members, heads, experts...  51.2 us
    pallas_call x1, Pallas kernels, on_device(): comm_call(functools.partial(middle_kernel, n_ctx, heads, experts), (shape...  46.4 us
    pallas_call x1, Pallas kernels, on_device(): comm_call(functools.partial(back_exchange_kernel, n_ctx, members, heads),...  40.4 us
    pallas_call x1, Pallas kernels, on_device(): call(expert_kernel, (shape((places, D), BF16), shape((n_ctx, 8, LANES), F...  23.8 us
    pallas_call x1, Pallas kernels, on_device(): call(functools.partial(attend_back_kernel, n_ctx, share), shape((3, n_ctx...  23.3 us
    pallas_call x1, Pallas kernels, on_device(): call(functools.partial(attend_kernel, n_ctx, share), (shape((n_ctx, rows,...  16.4 us
  transfers between devices with their start and end apart: 6, of which 1 were waited for; matrix products, arithmetic and copies ran while one was open for 2% of the time, Pallas kernels for 52%

profile of v6, /device:TPU:0, one launch (start us, length us, event | category | flops | bytes accessed | tf_op | source)
XLA Modules:
  0.0 407.9 jit_solution(10607812931698010640)
XLA Ops:
  7.2 0.0 all-gather.4.cloned.1.call-start
  7.2 0.7 all-gather.4.cloned.1.call-update
  7.9 0.0 all-gather.6.cloned.1.call-start
  8.0 3.5 pad_maximum_fusion
  11.5 0.0 copy-start.4
  11.5 0.0 copy-start.6
  11.5 0.0 copy-start.7
  11.5 0.0 all-gather.6.cloned.1.call-update
  11.5 0.0 all-gather.8.cloned.1.call-start
  11.5 0.7 all-gather.8.cloned.1.call-update
  12.9 0.0 copy-done.4
  12.9 0.8 copy.30
  13.7 0.0 copy-done.6
  13.7 0.0 copy-done.7
  13.7 0.6 pad_maximum_fusion.1.gains_ref
  14.3 0.0 copy-start.5
  14.3 61.0 %shard_map.230 = (bf16[3,8,256,128]{3,2,1,0:T(8,128)(2,1)}, bf16[256,768]{1,0:T(8,128)(2,1)}, f32[128,768]{1,0:T(8,128)}, s32[256,2]{1,0:T(8,128)}, bf16[256,768...) custom-call(s32[8]{0:T(128)} %where_ref.1, ...), custom_call_target="tpu_custom_call" | custom-call | bytes 157286400 | tf_op jit(solution)/shard_map/pallas_call | solution.py:1408
  75.3 7.8 %all-to-all-start = ((bf16[8,64,768]{2,1,0:T(8,128)(2,1)}), bf16[8,64,768]{2,1,0:T(8,128)(2,1)S(1)}, u32[]{:S(2)}, u32[]{:S(2)}) async-start(bf16[8,64,768]{2,1,0:T(8,128)(2,1)} %get-tuple-element.71), calls=%async_computation | async-start | bytes 1572864 | tf_op jit(solution)/shard_map/all_to_all | solution.py:1450
  83.1 0.0 copy-done.5
  83.1 0.1 select_reduce_fusion
  83.2 0.6 pad_add_fusion.sc
  83.8 16.4 %shard_map.231 = (bf16[8,256,128]{2,1,0:T(8,128)(2,1)}, f32[8,128,384]{2,1,0:T(8,128)}, f32[8,1,384]{2,1,0:T(1,128)}) custom-call(s32[10]{0:T(128)} %pad_add_fusion.sc, bf16[3,8,256,128]{3,2,1,0:T(8,128)(2,1)} %get-tuple-element.69.recv_ref), custom_call_target="tpu_custom_call" | custom-call | flops 3221225472 | bytes 5242880 | tf_op jit(solution)/shard_map/pallas_call | solution.py:1454
  100.2 3.3 all-to-all-done.rest_ref
  103.5 0.0 copy-start.2
  103.5 0.0 all-gather.4.cloned.1.call-done.w_ref
  103.5 46.4 %shard_map.232 = (bf16[8,256,128]{2,1,0:T(8,128)(2,1)}, f32[256,768]{1,0:T(8,128)}, bf16[256,768]{1,0:T(8,128)(2,1)}, f32[256,128]{1,0:T(8,128)}, bf16[768,768]{1,0:T(8,128)(2,1)}, /*index=5*/f32[8,8,128]{2,1,0:T(8,128)}) custom-call(bf16[8,256,128]{2,1,0:T(8,128)(2,1)} %get-tuple-element.72.attended_ref, ...), custom_call_target="tpu_custom_call" | custom-call | bytes 104857600 | tf_op jit(solution)/shard_map/pallas_call | solution.py:1484
  149.9 0.0 all-gather.6.cloned.1.call-done.wg_ref.wu_ref.wt_ref.wide_ref
  149.9 0.0 copy-done.2
  149.9 23.8 %shard_map.233 = (bf16[768,768]{1,0:T(8,128)(2,1)}, f32[8,8,128]{2,1,0:T(8,128)}, bf16[768,768]{1,0:T(8,128)(2,1)}, bf16[3,768,2048]{2,1,0:T(8,128)(2,1)}, bf16[768,768]{1,0:T(8,128)(2,1)}) custom-call(bf16[768,768]{1,0:T(8,128)(2,1)} %get-tuple-element.75.x_ref, f32[8,8,128]{2,1,0:T(8,128)} %get-tuple-element.76.gates_ref, ...), custom_call_target="tpu_custom_call" | custom-call | flops 14495514624 | bytes 25165824 | tf_op jit(solution)/shard_map/pallas_call | solution.py:1510
  173.7 0.0 all-gather.8.cloned.1.call-done.back_ref
  173.7 51.2 %shard_map.234 = (bf16[8,256,128]{2,1,0:T(8,128)(2,1)}, f32[256,768]{1,0:T(8,128)}, f32[256,768]{1,0:T(8,128)}, bf16[256,768]{1,0:T(8,128)(2,1)}, bf16[256,128]{...) custom-call(bf16[768,768]{1,0:T(8,128)(2,1)} %get-tuple-element.79.s, ...), custom_call_target="tpu_custom_call" | custom-call | bytes 157286400 | tf_op jit(solution)/shard_map/pallas_call | solution.py:1558
  225.0 5.3 %all-to-all-start.1 = ((bf16[8,96,768]{2,1,0:T(8,128)(2,1)}), bf16[8,96,768]{2,1,0:T(8,128)(2,1)S(1)}, u32[]{:S(2)}, u32[]{:S(2)}) async-start(bf16[8,96,768]{2,1,0:T(8,128)(2,1)} %bitcast.10), calls=%async_computation.1 | async-start | bytes 2359296 | tf_op jit(solution)/shard_map/all_to_all | solution.py:1659
  230.3 0.9 collective-permute-start
  231.2 0.6 dynamic_slice.3
  232.5 0.7 fusion.live_ref
  233.2 23.3 %shard_map.235.send_ref = bf16[3,8,256,128]{3,2,1,0:T(8,128)(2,1)} custom-call(s32[10]{0:T(128)} %pad_add_fusion.sc, bf16[3,8,256,128]{3,2,1,0:T(8,128)(2,1)} %get-tuple-element.69.recv_ref, bf16[8,256,128]{2,1,0:T(8,128)(2,1)} %get-tuple-element.87.grad_ref, f32[8,128,384]{2,1,0:T(8,128)} %get-tuple-element.88.keep_ref, f32[8,1,384]{2,1,0:T(1,128)} %get-tuple-element.89.lse_ref), custom_call_target="tpu_custom_call" | custom-call | flops 4831838208 | bytes 8388608 | tf_op jit(solution)/shard_map/pallas_call | solution.py:1635
  256.4 0.0 all-to-all-done.1
  256.4 0.0 copy-start
  256.4 1.0 copy-done
  257.4 40.4 %shard_map.236 = (bf16[3,8,256,128]{3,2,1,0:T(8,128)(2,1)}, bf16[3,2,192,2048]{3,2,1,0:T(8,128)(2,1)}, bf16[1,192,768]{2,1,0:T(8,128)(2,1)}, bf16[1,192,768]{2,1...) custom-call(bf16[3,8,256,128]{3,2,1,0:T(8,128)(2,1)} %shard_map.235.send_ref, ...), custom_call_target="tpu_custom_call" | custom-call | bytes 125829120 | tf_op jit(solution)/shard_map/pallas_call | solution.py:1660
  297.8 0.0 collective-permute-done
  297.8 0.0 copy-start.1
  297.8 1.1 copy-done.1
  299.0 92.4 %shard_map.237 = (f32[256,768]{1,0:T(8,128)}, bf16[192,4096]{1,0:T(8,128)(2,1)}, bf16[512,768]{1,0:T(8,128)(2,1)}, bf16[192,3200]{1,0:T(8,128)(2,1)}, bf16[3,192,2048]{2,1,0:T(8,128)(2,1)}) custom-call(bf16[3,8,256,128]{3,2,1,0:T(8,128)(2,1)} %get-tuple-element.98.recv_ref, f32[256,128]{1,0:T(8,128)} %get-tuple-element.99.cos_ref, ...), custom_call_target="tpu_custom_call" | custom-call | bytes 209715200 | tf_op jit(solution)/shard_map/pallas_call | solution.py:1718
  391.3 0.0 copy-start.3
  391.4 8.0 %shard_map.238 = (f32[192,2304]{1,0:T(8,128)}, f32[192,768]{1,0:T(8,128)}, f32[192,4096]{1,0:T(8,128)}, f32[512,768]{1,0:T(8,128)}, f32[192,4096]{1,0:T(8,128)},...) custom-call(bf16[192,3200]{1,0:T(8,128)(2,1)} %get-tuple-element.113.late_ref.small_ref, ...), custom_call_target="tpu_custom_call" | custom-call | bytes 23068672 | tf_op jit(solution)/shard_map/pallas_call | solution.py:1776
  399.3 1.3 fusion.1
  400.7 0.0 copy-done.3
  400.7 0.7 copy.35
  (2 shorter events, 0.0 us)
Async XLA Ops:
  7.2 96.3 %all-gather.4.cloned.1.call-start = ((), (), s32[]{:S(2)}) async-start(), calls=%async_computation.2 | async-start | bytes 1474560 | tf_op jit(solution)/shard_map/all_gather | solution.py:1378
  7.9 142.0 %all-gather.6.cloned.1.call-start = ((), (), s32[]{:S(2)}) async-start(), calls=%async_computation.3 | async-start | bytes 19660800 | tf_op jit(solution)/shard_map/all_gather | solution.py:1379
  11.5 1.4 copy-start.4
  11.5 2.2 copy-start.6
  11.5 2.2 copy-start.7
  11.5 162.2 %all-gather.8.cloned.1.call-start = ((), (), s32[]{:S(2)}) async-start(), calls=%async_computation.4 | async-start | bytes 3932160 | tf_op jit(solution)/shard_map/all_gather | solution.py:1382
  14.3 68.8 %copy-start.5 = (s32[8]{0:T(128)S(1)}, s32[8]{0:T(128)}, u32[]{:S(2)}) copy-start(s32[8]{0:T(128)} %where_ref.1) | copy-start | bytes 100
  75.3 28.2 %all-to-all-start = ((bf16[8,64,768]{2,1,0:T(8,128)(2,1)}), bf16[8,64,768]{2,1,0:T(8,128)(2,1)S(1)}, u32[]{:S(2)}, u32[]{:S(2)}) async-start(bf16[8,64,768]{2,1,0:T(8,128)(2,1)} %get-tuple-element.71), calls=%async_computation | async-start | bytes 1572864 | tf_op jit(solution)/shard_map/all_to_all | solution.py:1450
  103.5 46.4 %copy-start.2 = (bf16[8,64,768]{2,1,0:T(8,128)(2,1)}, bf16[8,64,768]{2,1,0:T(8,128)(2,1)S(1)}, u32[]{:S(2)}) copy-start(bf16[8,64,768]{2,1,0:T(8,128)(2,1)S(1)} %all-to-all-done.rest_ref) | copy-start | bytes 2359300
  225.0 31.4 %all-to-all-start.1 = ((bf16[8,96,768]{2,1,0:T(8,128)(2,1)}), bf16[8,96,768]{2,1,0:T(8,128)(2,1)S(1)}, u32[]{:S(2)}, u32[]{:S(2)}) async-start(bf16[8,96,768]{2,1,0:T(8,128)(2,1)} %bitcast.10), calls=%async_computation.1 | async-start | bytes 2359296 | tf_op jit(solution)/shard_map/all_to_all | solution.py:1659
  230.3 67.5 %collective-permute-start = (bf16[2,1,192,2048]{3,2,0,1:T(8,128)(2,1)}, bf16[2,1,192,2048]{3,2,0,1:T(8,128)(2,1)S(1)}, u32[]{:S(2)}, u32[]{:S(2)}) collective-permute-start(bf16[2,1,192,2048]{3,2,0,1:T(8,128)(2,1)} %bitcast.51), channel_id=1, source_target_pairs={{0,2},{1,3},{2,0},{3,1},{4,6},{5,7},{6,4},{7,5},{8,10},{9,11},{10,... | collective-permute-start | bytes 4718600 | tf_op jit(solution)/shard_map/ppermute | solution.py:1621
  256.4 1.0 copy-start
  297.8 1.1 copy-start.1
  391.3 9.3 %copy-start.3 = (bf16[256,768]{1,0:T(8,128)(2,1)S(1)}, bf16[256,768]{1,0:T(8,128)(2,1)}, u32[]{:S(2)}) copy-start(bf16[256,768]{1,0:T(8,128)(2,1)} %get-tuple-element.97) | copy-start | bytes 1179652
Sparse Core Ops, SparseCore 0:
  9.6 24.5 all-gather.3
  35.7 101.8 all-gather.5
  139.2 28.5 all-gather.7

commit v7 on v6

--- a/solution.py
+++ b/solution.py
@@ -152,6 +152,7 @@
     router_ref,
     gains_ref,
     turn_ref,
+    query_ref,
     recv_ref,
     in_ref,
     tail_ref,
@@ -162,6 +163,7 @@
     w_all,
     cos_ref,
     sin_ref,
+    query_send,
     send,
     dy_send,
     small,
@@ -287,18 +289,21 @@
                 packet = groups[g]
             else:
                 packet = jnp.where(lane < 64, turned[g], turned[g + 1])
-            send[part, d] = packet.astype(BF16)
+            if part == 0:
+                query_send[d] = fold(n, d, packet).astype(BF16)
+            else:
+                send[part - 1, d] = packet.astype(BF16)
+        source = query_send if part == 0 else send.at[part - 1]
+        target = query_ref if part == 0 else recv_ref.at[part - 1]
         own.append(
-            pltpu.make_async_copy(
-                send.at[part, ctx], recv_ref.at[part, ctx], own_sem.at[part]
-            )
+            pltpu.make_async_copy(source.at[ctx], target.at[ctx], own_sem.at[part])
         )
         own[-1].start()
         for d, p in enumerate(peers):
             copies.append(
                 remote(
-                    send.at[part, p[0]],
-                    recv_ref.at[part, ctx],
+                    source.at[p[0]],
+                    target.at[ctx],
                     packet_send.at[part, d],
                     packet_recv.at[part, d],
                     p,
@@ -315,6 +320,72 @@
             masks = masks + [mask | 1 << b for mask in masks]
 
 
+def folds(n, rows):
+    return 2 * HEADS * rows == 3 * n * rows
+
+
+def packet_rows(n, rows):
+    return rows * 3 // 4 if folds(n, rows) else rows
+
+
+def fold(n, d, block):
+    rows = block.shape[0]
+    if not folds(n, rows):
+        return block
+    half, quarter = rows // 2, rows // 4
+    lane = lanes_of(quarter)
+    if d % 2 == 0:
+        both, one = block[0:half], block[half:]
+        lone = jnp.where(lane < 64, one[0:quarter], pltpu.roll(one[quarter:], 64, 1))
+    else:
+        both, one = block[half:], block[0:half]
+        lone = jnp.where(lane < 64, pltpu.roll(one[0:quarter], 64, 1), one[quarter:])
+    return jnp.concatenate([both, lone], axis=0)
+
+
+def unfold(n, d, block, rows):
+    if not folds(n, rows):
+        return block
+    half, quarter = rows // 2, rows // 4
+    both, lone = block[0:half], block[half:]
+    turned = pltpu.roll(lone, 64, 1)
+    lane = lanes_of(quarter)
+    zero = jnp.zeros((), block.dtype)
+    if d % 2 == 0:
+        pieces = [both, jnp.where(lane < 64, lone, zero), jnp.where(lane < 64, turned, zero)]
+    else:
+        pieces = [jnp.where(lane < 64, zero, turned), jnp.where(lane < 64, zero, lone), both]
+    return jnp.concatenate(pieces, axis=0)
+
+
+def stack_folded(stack_ref, block, odd):
+    count = block.shape[0]
+    half, quarter = count * 2 // 3, count // 3
+    lane = lanes_of(half)
+    zero = jnp.zeros((), block.dtype)
+    both, lone = block[0:half], block[half:]
+    stack_ref[0:half, :] = jnp.where(lane < 64, both, zero)
+    stack_ref[half : 2 * half, :] = jnp.where(lane < 64, zero, both)
+    turned = pltpu.roll(lone, 64, 1)
+    lane = lanes_of(quarter)
+    low = jnp.where(odd, turned, lone)
+    high = jnp.where(odd, lone, turned)
+    keep = (lane < 64) != odd
+    stack_ref[2 * half : 2 * half + quarter, :] = jnp.where(keep, low, zero)
+    stack_ref[2 * half + quarter : 2 * half + 2 * quarter, :] = jnp.where(keep, high, zero)
+
+
+def fold_stack(block, odd):
+    half = block.shape[0] // 3
+    quarter = half // 2
+    both = jnp.where(lanes_of(half) < 64, block[0:half], block[half : 2 * half])
+    low, high = block[2 * half : 2 * half + quarter], block[2 * half + quarter :]
+    lane = lanes_of(quarter)
+    even_way = jnp.where(lane < 64, low, pltpu.roll(high, 64, 1))
+    odd_way = jnp.where(lane < 64, pltpu.roll(low, 64, 1), high)
+    return jnp.concatenate([both, jnp.where(odd, odd_way, even_way)], axis=0)
+
+
 def stack_rows(stack_ref, block, lane):
     rows = block.shape[0]
     zero = jnp.zeros((), block.dtype)
@@ -329,28 +400,41 @@
     return jnp.where(lane < 64, stack_ref[0:rows, :], stack_ref[rows : 2 * rows, :])
 
 
-def key_limits(share, rows, q_block, offset, length):
-    row = lax.broadcasted_iota(jnp.int32, (1, share), 1) + offset
-    row = jnp.where(row >= rows, row - rows, row)
+def key_limits(n, share, rows, q_block, offset, length):
+    row = lax.broadcasted_iota(jnp.int32, (1, share), 1)
+    if folds(n, rows):
+        half = rows // 2
+        odd = jnp.where(offset > 0, half, 0)
+        row = jnp.where(
+            row < half, row + odd, jnp.where(row < rows, row - half + odd, row - half - odd)
+        )
+    else:
+        row = row + offset
+        row = jnp.where(row >= rows, row - rows, row)
     return jnp.minimum(q_block * rows + row + 1, length)
 
 
-def attend_kernel(n, share, sc, recv_ref, out_ref, keep_ref, lse_ref, stack, scores, back):
+def attend_kernel(n, share, sc, query_ref, recv_ref, out_ref, keep_ref, lse_ref, stack, scores, back):
     q_block = pl.program_id(0)
     rows = recv_ref.shape[2]
     offset = pl.multiple_of(sc[n], 64)
     length = sc[n + 1]
     lane = lanes_of(rows)
-    stack_rows(stack, recv_ref[0, sc[q_block]] * 0.125, lane)
-    query = stack[pl.ds(offset, share), :]
-    limit = key_limits(share, rows, q_block, offset, length)
+    block = query_ref[sc[q_block]] * 0.125
+    if folds(n, rows):
+        stack_folded(stack, block, offset > 0)
+        query = stack[0:share, :]
+    else:
+        stack_rows(stack, block, lane)
+        query = stack[pl.ds(offset, share), :]
+    limit = key_limits(n, share, rows, q_block, offset, length)
     key_row = lax.broadcasted_iota(jnp.int32, (rows, share), 0)
     blocks = jnp.minimum(q_block + 1, (length + rows - 1) // rows)
 
     def score_step(pair, top):
         found = []
         for j in (2 * pair, 2 * pair + 1):
-            s = dot_nt(recv_ref[1, sc[j]], query)
+            s = dot_nt(recv_ref[0, sc[j]], query)
             s = jnp.where(key_row < limit - j * rows, s, -1e30)
             scores[j] = s
             found.append(jnp.max(s, axis=0, keepdims=True))
@@ -364,7 +448,7 @@
         for j in (2 * pair, 2 * pair + 1):
             weights = jnp.exp(scores[j] - top)
             total = total + jnp.sum(weights, axis=0, keepdims=True)
-            acc = acc + dot_tn(recv_ref[2, sc[j]], weights.astype(BF16))
+            acc = acc + dot_tn(recv_ref[1, sc[j]], weights.astype(BF16))
         return total, acc
 
     total, acc = lax.fori_loop(
@@ -373,11 +457,28 @@
     acc = acc / total
     keep_ref[0] = acc
     lse_ref[0] = top + jnp.log(total)
-    out_ref[0] = unstack_rows(back, acc.T, offset, lane).astype(BF16)
+    if folds(n, rows):
+        out_ref[0] = fold_stack(acc.T, offset > 0).astype(BF16)
+    else:
+        out_ref[0] = unstack_rows(back, acc.T, offset, lane).astype(BF16)
 
 
 def attend_back_kernel(
-    n, share, sc, recv_ref, grad_ref, keep_ref, lse_ref, out_ref, stack, gstack, dkeys, dvalues, back
+    n,
+    share,
+    sc,
+    query_ref,
+    recv_ref,
+    grad_ref,
+    keep_ref,
+    lse_ref,
+    query_out,
+    out_ref,
+    stack,
+    gstack,
+    dkeys,
+    dvalues,
+    back,
 ):
     q_block = pl.program_id(0)
     rows = recv_ref.shape[2]
@@ -391,20 +492,27 @@
         dkeys[...] = jnp.zeros_like(dkeys)
         dvalues[...] = jnp.zeros_like(dvalues)
 
-    stack_rows(stack, recv_ref[0, source] * 0.125, lane)
-    query = stack[pl.ds(offset, share), :]
-    stack_rows(gstack, grad_ref[source], lane)
-    grad = gstack[pl.ds(offset, share), :]
+    block = query_ref[source] * 0.125
+    if folds(n, rows):
+        stack_folded(stack, block, offset > 0)
+        query = stack[0:share, :]
+        stack_folded(gstack, grad_ref[source], offset > 0)
+        grad = gstack[0:share, :]
+    else:
+        stack_rows(stack, block, lane)
+        query = stack[pl.ds(offset, share), :]
+        stack_rows(gstack, grad_ref[source], lane)
+        grad = gstack[pl.ds(offset, share), :]
     lse = lse_ref[0]
     delta = jnp.sum(grad.astype(F32).T * keep_ref[0], axis=0, keepdims=True)
-    limit = key_limits(share, rows, q_block, offset, length)
+    limit = key_limits(n, share, rows, q_block, offset, length)
     key_row = lax.broadcasted_iota(jnp.int32, (rows, share), 0)
     blocks = jnp.minimum(q_block + 1, (length + rows - 1) // rows)
 
     def step(pair, acc):
         for j in (2 * pair, 2 * pair + 1):
-            keys = recv_ref[1, sc[j]]
-            values = recv_ref[2, sc[j]]
+            keys = recv_ref[0, sc[j]]
+            values = recv_ref[1, sc[j]]
             s = dot_nt(keys, query)
             weights = jnp.exp(jnp.where(key_row < limit - j * rows, s, -1e30) - lse)
             dweights = dot_nt(values, grad)
@@ -415,14 +523,17 @@
         return acc
 
     acc = lax.fori_loop(0, (blocks + 1) // 2, step, jnp.zeros((LANES, share), F32))
-    dquery = unstack_rows(back, acc.T * 0.125, offset, lane)
-    out_ref[0, source] = dquery.astype(BF16)
+    if folds(n, rows):
+        dquery = fold_stack(acc.T * 0.125, offset > 0)
+    else:
+        dquery = unstack_rows(back, acc.T * 0.125, offset, lane)
+    query_out[source] = dquery.astype(BF16)
 
     @pl.when(q_block == n - 1)
     def _():
         def flush(j, carry):
-            out_ref[1, sc[j]] = dkeys[j].astype(BF16)
-            out_ref[2, sc[j]] = dvalues[j].astype(BF16)
+            out_ref[0, sc[j]] = dkeys[j].astype(BF16)
+            out_ref[1, sc[j]] = dvalues[j].astype(BF16)
             return carry
 
         lax.fori_loop(0, n, flush, 0)
@@ -444,6 +555,7 @@
     gates_ref,
     rows_ref,
     row_gates_ref,
+    packets,
     outgoing,
     outgates,
     came_send,
@@ -457,10 +569,10 @@
     ctx = lax.axis_index("ctx")
     peers = row_peers(n)
     greet(peers)
-    own = pltpu.make_async_copy(attended_ref.at[ctx], came_ref.at[ctx], own_sem.at[0])
+    own = pltpu.make_async_copy(attended_ref.at[ctx], packets.at[ctx], own_sem.at[0])
     own.start()
     copies = [
-        remote(attended_ref.at[p[0]], came_ref.at[ctx], came_send.at[d], came_recv.at[d], p)
+        remote(attended_ref.at[p[0]], packets.at[ctx], came_send.at[d], came_recv.at[d], p)
         for d, p in enumerate(peers)
     ]
     for c in copies:
@@ -472,7 +584,9 @@
         c.wait()
     own.wait()
     for d, head in enumerate(heads):
-        total = total + dot(came_ref[d], w_ref[64 * head : 64 * head + LANES, :])
+        came = unfold(n, d, packets[d], total.shape[0])
+        came_ref[d] = came
+        total = total + dot(came, w_ref[64 * head : 64 * head + LANES, :])
     residual_ref[...] = total
     inv = lax.rsqrt(jnp.mean(total * total, axis=-1, keepdims=True) + norm_eps)
     ffn_in = (total * inv * tail_ref[experts + 1 : experts + 2, :]).astype(BF16)
@@ -533,7 +647,7 @@
 
 
 def gated(g, u, da):
-    sig = 1.0 / (1.0 + jnp.exp(-g))
+    sig = 0.5 * jnp.tanh(0.5 * g) + 0.5
     silu = g * sig
     return silu * u, da * u * sig * (1.0 + g * (1.0 - sig)), da * silu
 
@@ -825,7 +939,8 @@
     branch = dres.astype(BF16)
     branch_ref[...] = branch
     for d, head in enumerate(heads):
-        packets[d] = dot_nt(branch, w_ref[64 * head : 64 * head + LANES, :]).astype(BF16)
+        packet = dot_nt(branch, w_ref[64 * head : 64 * head + LANES, :])
+        packets[d] = fold(n, d, packet).astype(BF16)
     own = pltpu.make_async_copy(packets.at[ctx], recv_ref.at[ctx], own_sem.at[1])
     own.start()
     copies = [
@@ -857,6 +972,7 @@
     n,
     members,
     heads,
+    query_ref,
     send_ref,
     x_ref,
     dy_ref,
@@ -868,9 +984,11 @@
     shared_ref,
     gates_ref,
     target_ref,
-    live_ref,
     res_ref,
+    where_ref,
+    length_ref,
     mid_ref,
+    query_out,
     recv_ref,
     sum_ref,
     out_keep,
@@ -887,6 +1005,8 @@
     dyt,
     acc,
     mids,
+    query_send,
+    query_recv,
     send_sem,
     recv_sem,
     own_sem,
@@ -901,9 +1021,17 @@
     mates = mates_of(members)
     mate, far = mates[0], mates[1]
     greet(peers + [mate, far])
-    own = pltpu.make_async_copy(send_ref.at[:, ctx], recv_ref.at[:, ctx], own_sem)
-    own.start()
+    own = [
+        pltpu.make_async_copy(send_ref.at[:, ctx], recv_ref.at[:, ctx], own_sem.at[0]),
+        pltpu.make_async_copy(query_ref.at[ctx], query_out.at[ctx], own_sem.at[1]),
+    ]
+    for c in own:
+        c.start()
     copies = [
+        remote(query_ref.at[p[0]], query_out.at[ctx], query_send.at[d], query_recv.at[d], p)
+        for d, p in enumerate(peers)
+    ]
+    copies += [
         remote(send_ref.at[:, p[0]], recv_ref.at[:, ctx], send_sem.at[d], recv_sem.at[d], p)
         for d, p in enumerate(peers)
     ]
@@ -990,13 +1118,14 @@
     pick = picks(target_ref, res_ref.shape[0])
     came = res_ref[...]
     mixture = gates_ref[:, 0:1] * dot(pick[0], came) + gates_ref[:, 1:2] * dot(pick[1], came)
-    output_ref[...] = (live_ref[...] * (residual_ref[...] + shared_ref[...] + mixture)).astype(BF16)
+    total = residual_ref[...] + shared_ref[...] + mixture
+    position = where_ref[ctx] * total.shape[0] + lax.broadcasted_iota(jnp.int32, total.shape, 0)
+    output_ref[...] = jnp.where(position < length_ref[0], total, 0.0).astype(BF16)
     swap(parts - 1).wait_recv()
     for j in range(half):
         add_into(sum_ref.at[parts - 1], j, caught.at[parts - 1])
-    for c in copies:
+    for c in copies + own:
         c.wait()
-    own.wait()
     cross.wait()
     for j in range(quarter):
         add_into(sum_ref.at[0], j, crossed)
@@ -1012,6 +1141,7 @@
     heads,
     experts,
     splits,
+    query_ref,
     recv_ref,
     cos_ref,
     sin_ref,
@@ -1052,7 +1182,9 @@
     ahead = (ring_place(lax.rem(here + 1, n), n), fsdp)
     behind = (ring_place(lax.rem(here + n - 1, n), n), fsdp)
     mates = mates_of(members)
-    greet([ahead, behind] + mates)
+    barrier = pltpu.get_barrier_semaphore()
+    for peer in [ahead, behind] + mates:
+        pl.semaphore_signal(barrier, inc=1, device_id=peer, device_id_type=pl.DeviceIdType.MESH)
     shard = D // members
     parts = e_ref.shape[0]
 
@@ -1192,7 +1324,9 @@
 
     for i in range(2):
         load(i, a_ref.at[i], 0, a_other.at[i])
-        first(i)
+    pl.semaphore_wait(barrier, 2 + bits)
+    first(0)
+    first(1)
     for i in range(2):
         load(2 + i, b_ref.at[i], 0, b_other.at[i])
         first(2 + i)
@@ -1200,10 +1334,10 @@
     first(4)
     waiting = [steps_of(i) for i in range(5)]
 
-    def dense_step():
-        for queue in waiting[0:5]:
-            if queue:
-                queue.pop(0)()
+    def dense_step(picked=range(5)):
+        for i in picked:
+            if waiting[i]:
+                waiting[i].pop(0)()
 
     rows = shard_rows(members, shard)
     raw[...] = in_ref[...].T
@@ -1215,7 +1349,10 @@
         groups = [jnp.zeros(lane.shape, F32) for _ in range(D // LANES)]
         for d, head in enumerate(heads):
             g = head // 2
-            packet = recv_ref[part, d].astype(F32)
+            if part == 0:
+                packet = unfold(n, d, query_ref[d].astype(F32), lane.shape[0])
+            else:
+                packet = recv_ref[part - 1, d].astype(F32)
             if head % 2 == 0:
                 groups[g] = groups[g] + packet
             else:
@@ -1256,6 +1393,8 @@
         e_copy(i, 1).start()
 
     for p in range(4):
+        if p < 3:
+            dense_step((0, 2))
         for b in range(1, bits):
             level_add(p, b)
             if b + 1 < bits:
@@ -1265,13 +1404,13 @@
         for queue in waiting[5:]:
             queue.pop(0)()
         if p < 3:
-            dense_step()
+            dense_step((1, 3, 4))
         waiting.append(steps_of(5 + p))
     turns = 0
     while any(waiting):
         turns += 1
         for i, queue in reversed(list(enumerate(waiting))):
-            if queue and (i >= 5 or turns % 2 == 0 or not any(waiting[5:])):
+            if queue and (i >= 5 or turns % 2 == (i in (1, 3, 4))):
                 queue.pop(0)()
                 if not queue and i < 5:
                     if i == 4:
@@ -1382,8 +1521,6 @@
     shared_out = gather(w_shared_out)
     bits = members.bit_length() - 1
 
-    query_pos = position_block[ctx_index] * rows + jnp.arange(rows, dtype=jnp.int32)
-    live = (query_pos < length).astype(F32)[:, None]
     rates = 10000.0 ** (-(np.arange(HEAD_DIM // 2) * 2.0 / HEAD_DIM))
     rates = jnp.asarray(np.tile(rates.astype(np.float32), 4)[None])
 
@@ -1405,10 +1542,12 @@
     scalar = pl.BlockSpec(memory_space=pltpu.SMEM)
     block = places // n_ctx
     early = block // 48 * 16
-    recv, attn_in, tail, target, dout, dy_first, dy_rest, qkv_weight, cos, sin = comm_call(
+    thin = packet_rows(n_ctx, rows)
+    queries, recv, attn_in, tail, target, dout, dy_first, dy_rest, qkv_weight, cos, sin = comm_call(
         functools.partial(open_kernel, n_ctx, members, heads, experts, capacity, early),
         (
-            shape((3, n_ctx, rows, LANES), BF16),
+            shape((n_ctx, thin, LANES), BF16),
+            shape((2, n_ctx, rows, LANES), BF16),
             shape((rows, D), BF16),
             shape((LANES, D), F32),
             shape((rows, 2), jnp.int32),
@@ -1421,9 +1560,10 @@
         ),
         3,
         in_specs=[scalar] * 2 + [whole] * 7,
-        out_specs=[whole] * 10,
+        out_specs=[whole] * 11,
         scratch_shapes=[
-            pltpu.VMEM((3, n_ctx, rows, LANES), BF16),
+            pltpu.VMEM((n_ctx, thin, LANES), BF16),
+            pltpu.VMEM((2, n_ctx, rows, LANES), BF16),
             pltpu.VMEM((n_ctx, early, D), BF16),
             pltpu.VMEM((LANES, local), F32),
             pltpu.VMEM((members, local, LANES), BF16),
@@ -1449,12 +1589,13 @@
     )
     dy_rest = exchange(dy_rest)
 
-    packet = pl.BlockSpec((3, n_ctx, rows, LANES), lambda i, sc: (0, 0, 0, 0))
+    packet = pl.BlockSpec((2, n_ctx, rows, LANES), lambda i, sc: (0, 0, 0, 0))
+    thin_packet = pl.BlockSpec((n_ctx, thin, LANES), lambda i, sc: (0, 0, 0))
     block_of = lambda i, sc: (i, 0, 0)
     attended, kept, lse = call(
         functools.partial(attend_kernel, n_ctx, share),
         (
-            shape((n_ctx, rows, LANES), BF16),
+            shape((n_ctx, thin, LANES), BF16),
             shape((n_ctx, LANES, share), F32),
             shape((n_ctx, 1, share), F32),
         ),
@@ -1463,9 +1604,9 @@
         grid_spec=pltpu.PrefetchScalarGridSpec(
             num_scalar_prefetch=1,
             grid=(n_ctx,),
-            in_specs=[packet],
+            in_specs=[thin_packet, packet],
             out_specs=[
-                pl.BlockSpec((1, rows, LANES), lambda i, sc: (sc[i], 0, 0)),
+                pl.BlockSpec((1, thin, LANES), lambda i, sc: (sc[i], 0, 0)),
                 pl.BlockSpec((1, LANES, share), block_of),
                 pl.BlockSpec((1, 1, share), block_of),
             ],
@@ -1475,7 +1616,7 @@
                 pltpu.VMEM((2 * rows, LANES), F32),
             ],
         ),
-    )(scalars, recv)
+    )(scalars, queries, recv)
     attended, dy_rest = lax.optimization_barrier((attended, dy_rest))
 
     def full(*dims):
@@ -1495,6 +1636,7 @@
         in_specs=[whole] * 6,
         out_specs=[whole] * 6,
         scratch_shapes=[
+            pltpu.VMEM((n_ctx, thin, LANES), BF16),
             pltpu.VMEM((places, D), BF16),
             pltpu.VMEM((n_ctx, 8, LANES), F32),
         ]
@@ -1558,7 +1700,7 @@
     ) = comm_call(
         functools.partial(shared_kernel, n_ctx, members, heads, experts),
         (
-            shape((n_ctx, rows, LANES), BF16),
+            shape((n_ctx, thin, LANES), BF16),
             shape((rows, D), F32),
             shape((rows, D), F32),
             shape((rows, D), BF16),
@@ -1573,7 +1715,7 @@
         scratch_shapes=[
             pltpu.VMEM((places, D), BF16),
             pltpu.VMEM((n_ctx, 8, LANES), F32),
-            pltpu.VMEM((n_ctx, rows, LANES), BF16),
+            pltpu.VMEM((n_ctx, thin, LANES), BF16),
             pltpu.VMEM((2, quarter, b_rows, D), BF16),
             pltpu.VMEM((2, rows, FS), BF16),
             pltpu.VMEM((rows, D), F32),
@@ -1632,21 +1774,22 @@
     dense_part, dense_other = rest_of(dense_keep, cross(dense_give, 1))
     so_part, so_other = rest_of(so_keep, so_came)
 
-    dsend = call(
+    dquery, dsend = call(
         functools.partial(attend_back_kernel, n_ctx, share),
-        shape((3, n_ctx, rows, LANES), BF16),
+        (shape((n_ctx, thin, LANES), BF16), shape((2, n_ctx, rows, LANES), BF16)),
         flops=2 * share * rows * n_ctx * n_ctx * LANES * 3,
         nbytes=8 << 20,
         grid_spec=pltpu.PrefetchScalarGridSpec(
             num_scalar_prefetch=1,
             grid=(n_ctx,),
             in_specs=[
+                thin_packet,
                 packet,
-                pl.BlockSpec((n_ctx, rows, LANES), lambda i, sc: (0, 0, 0)),
+                thin_packet,
                 pl.BlockSpec((1, LANES, share), block_of),
                 pl.BlockSpec((1, 1, share), block_of),
             ],
-            out_specs=packet,
+            out_specs=[thin_packet, packet],
             scratch_shapes=[
                 pltpu.VMEM((2 * rows, LANES), BF16),
                 pltpu.VMEM((2 * rows, LANES), BF16),
@@ -1655,12 +1798,13 @@
                 pltpu.VMEM((2 * rows, LANES), F32),
             ],
         ),
-    )(scalars, recv, branch_recv, kept, lse)
+    )(scalars, queries, recv, branch_recv, kept, lse)
     res_came = exchange(expert_res.reshape(n_ctx, -1, D)).reshape(places, D)
-    drecv, expert_sum, out_keep, out_came, grad_router, output = comm_call(
+    dquery, drecv, expert_sum, out_keep, out_came, grad_router, output = comm_call(
         functools.partial(back_exchange_kernel, n_ctx, members, heads),
         (
-            shape((3, n_ctx, rows, LANES), BF16),
+            shape((n_ctx, thin, LANES), BF16),
+            shape((2, n_ctx, rows, LANES), BF16),
             shape((3, half, local, FF), BF16),
             shape((quarter, local, D), BF16),
             shape((quarter, local, D), BF16),
@@ -1668,8 +1812,8 @@
             shape((rows, D), BF16),
         ),
         1,
-        in_specs=[whole] * 13 + [anywhere],
-        out_specs=[whole] * 6,
+        in_specs=[whole] * 13 + [scalar] * 2 + [anywhere],
+        out_specs=[whole] * 7,
         scratch_shapes=[
             pltpu.VMEM((3, half, local, FF), BF16),
             pltpu.VMEM((3, half, local, FF), BF16),
@@ -1683,7 +1827,9 @@
             pltpu.VMEM((2, places, BROAD), BF16),
             pltpu.SemaphoreType.DMA((n_ctx - 1,)),
             pltpu.SemaphoreType.DMA((n_ctx - 1,)),
-            pltpu.SemaphoreType.DMA,
+            pltpu.SemaphoreType.DMA((n_ctx - 1,)),
+            pltpu.SemaphoreType.DMA((n_ctx - 1,)),
+            pltpu.SemaphoreType.DMA((2,)),
             pltpu.SemaphoreType.DMA((3,)),
             pltpu.SemaphoreType.DMA((3,)),
             pltpu.SemaphoreType.DMA((2,)),
@@ -1692,6 +1838,7 @@
         ],
         nbytes=120 << 20,
     )(
+        dquery,
         dsend,
         x_rows,
         dy_rows,
@@ -1703,8 +1850,9 @@
         shared_res,
         gates,
         target,
-        live,
         res_came,
+        position_block,
+        lengths,
         expert_mid,
     )
 
@@ -1725,7 +1873,7 @@
             shape((3, local, FF), BF16),
         ),
         0,
-        in_specs=[whole] * 17,
+        in_specs=[whole] * 18,
         out_specs=[whole] * 5,
         scratch_shapes=[pltpu.VMEM(t, BF16) for t in tiles * 4]
         + [pltpu.VMEM((members, local, width), BF16) for width in late_widths]
@@ -1749,6 +1897,7 @@
         ],
         nbytes=200 << 20,
     )(
+        dquery,
         drecv,
         cos,
         sin,

time: 408 us -> 396 us (0.971)
  Pallas kernels: 363 us -> 350 us
    pallas_call x1, Pallas kernels: 92.4 us -> 87.7 us  [on_device(): comm_call(functools.partial(last_kernel, n_ctx, members, heads, experts,...]
  transfers between devices with their start and end apart: 6 -> 6, of which waited for: 1 -> 2; matrix products, arithmetic and copies ran while one was open for 2% -> 1% of each run, Pallas kernels for 52% -> 52%
where the time goes in v7:
time: 396 us; the launch traced here: 393 us
  Pallas kernels  350 us (88%)
  between operations  14.6 us (4%)
  starting transfers between devices  12.6 us (3%)
  waiting for transfers between devices  6.06 us (2%)
  local copies, waits for them, and re-layouts  5.06 us (1%)
  other arithmetic  4.79 us (1%)
    pallas_call x1, Pallas kernels, on_device(): comm_call(functools.partial(last_kernel, n_ctx, members, heads, experts,...  87.7 us
    pallas_call x1, Pallas kernels, on_device(): comm_call(functools.partial(open_kernel, n_ctx, members, heads, experts,...  58.1 us
    pallas_call x1, Pallas kernels, on_device(): comm_call(functools.partial(shared_kernel, n_ctx, members, heads, experts...  50.7 us
    pallas_call x1, Pallas kernels, on_device(): comm_call(functools.partial(middle_kernel, n_ctx, heads, experts), (shape...  43.6 us
    pallas_call x1, Pallas kernels, on_device(): comm_call(functools.partial(back_exchange_kernel, n_ctx, members, heads),...  40.1 us
    pallas_call x1, Pallas kernels, on_device(): call(expert_kernel, (shape((places, D), BF16), shape((n_ctx, 8, LANES), F...  24.7 us
    pallas_call x1, Pallas kernels, on_device(): call(functools.partial(attend_back_kernel, n_ctx, share), (shape((n_ctx,...  21.8 us
    pallas_call x1, Pallas kernels, on_device(): call(functools.partial(attend_kernel, n_ctx, share), (shape((n_ctx, thin,...  15.6 us
  transfers between devices with their start and end apart: 6, of which 2 were waited for; matrix products, arithmetic and copies ran while one was open for 1% of the time, Pallas kernels for 52%

profile of v7, /device:TPU:0, one launch (start us, length us, event | category | flops | bytes accessed | tf_op | source)
XLA Modules:
  0.0 393.2 jit_solution(9627679564758483461)
XLA Ops:
  7.2 0.0 all-gather.4.cloned.1.call-start
  7.2 0.7 all-gather.4.cloned.1.call-update
  7.9 0.0 all-gather.6.cloned.1.call-start
  8.0 3.5 pad_maximum_fusion
  11.5 0.0 copy-start.6
  11.5 0.0 copy-start.7
  11.5 0.0 copy-start.4
  11.5 0.0 all-gather.6.cloned.1.call-update
  11.5 0.0 all-gather.8.cloned.1.call-start
  11.6 0.7 all-gather.8.cloned.1.call-update
  12.9 0.0 copy-done.6
  12.9 0.0 copy-done.7
  12.9 0.0 copy-done.4
  12.9 0.0 copy-start.5
  13.0 0.8 copy.28
  13.8 0.6 pad_maximum_fusion.1.gains_ref
  14.3 58.1 %shard_map.230 = (bf16[8,192,128]{2,1,0:T(8,128)(2,1)}, bf16[2,8,256,128]{3,2,1,0:T(8,128)(2,1)}, bf16[256,768]{1,0:T(8,128)(2,1)}, f32[128,768]{1,0:T(8,128)}, ...) custom-call(s32[8]{0:T(128)} %where_ref.3, ...), custom_call_target="tpu_custom_call" | custom-call | bytes 157286400 | tf_op jit(solution)/shard_map/pallas_call | solution.py:1546
  72.5 7.6 %all-to-all-start = ((bf16[8,64,768]{2,1,0:T(8,128)(2,1)}), bf16[8,64,768]{2,1,0:T(8,128)(2,1)S(1)}, u32[]{:S(2)}, u32[]{:S(2)}) async-start(bf16[8,64,768]{2,1,0:T(8,128)(2,1)} %get-tuple-element.76), calls=%async_computation | async-start | bytes 1572864 | tf_op jit(solution)/shard_map/all_to_all | solution.py:1590
  80.0 0.0 copy-done.5
  80.0 0.1 select_reduce_fusion
  80.2 0.6 pad_add_fusion.sc
  80.8 15.6 %shard_map.231 = (bf16[8,192,128]{2,1,0:T(8,128)(2,1)}, f32[8,128,384]{2,1,0:T(8,128)}, f32[8,1,384]{2,1,0:T(1,128)}) custom-call(s32[10]{0:T(128)} %pad_add_fusion.sc, bf16[8,192,128]{2,1,0:T(8,128)(2,1)} %get-tuple-element.73.query_ref, bf16[2,8,256,128]{3,2,1,0:T(8,128)(2,1)} %get-tuple-element.74.recv_ref), custom_call_target="tpu_custom_call" | custom-call | flops 3221225472 | bytes 5242880 | tf_op jit(solution)/shard_map/pallas_call | solution.py:1595
  96.4 4.2 %all-to-all-done.rest_ref = bf16[8,64,768]{2,1,0:T(8,128)(2,1)S(1)} async-done(((bf16[8,64,768]{2,1,0:T(8,128)(2,1)}), bf16[8,64,768]{2,1,0:T(8,128)(2,1)S(1)}, u32[]{:S(2)}, u32[]{:S(2)}) %all-to-all-start) | async-done | bytes 786464 | tf_op jit(solution)/shard_map/all_to_all | solution.py:1590
  100.6 0.0 copy-start.2
  100.6 0.0 all-gather.4.cloned.1.call-done.w_ref
  100.6 43.6 %shard_map.232 = (bf16[8,256,128]{2,1,0:T(8,128)(2,1)}, f32[256,768]{1,0:T(8,128)}, bf16[256,768]{1,0:T(8,128)(2,1)}, f32[256,128]{1,0:T(8,128)}, bf16[768,768]{1,0:T(8,128)(2,1)}, /*index=5*/f32[8,8,128]{2,1,0:T(8,128)}) custom-call(bf16[8,192,128]{2,1,0:T(8,128)(2,1)} %get-tuple-element.77.attended_ref, ...), custom_call_target="tpu_custom_call" | custom-call | bytes 104857600 | tf_op jit(solution)/shard_map/pallas_call | solution.py:1625
  144.1 0.0 all-gather.6.cloned.1.call-done.wg_ref.wu_ref.wt_ref.wide_ref
  144.2 0.0 copy-done.2
  144.2 24.7 %shard_map.233 = (bf16[768,768]{1,0:T(8,128)(2,1)}, f32[8,8,128]{2,1,0:T(8,128)}, bf16[768,768]{1,0:T(8,128)(2,1)}, bf16[3,768,2048]{2,1,0:T(8,128)(2,1)}, bf16[768,768]{1,0:T(8,128)(2,1)}) custom-call(bf16[768,768]{1,0:T(8,128)(2,1)} %get-tuple-element.80.x_ref, f32[8,8,128]{2,1,0:T(8,128)} %get-tuple-element.81.gates_ref, ...), custom_call_target="tpu_custom_call" | custom-call | flops 14495514624 | bytes 25165824 | tf_op jit(solution)/shard_map/pallas_call | solution.py:1652
  168.8 0.0 all-gather.8.cloned.1.call-done.back_ref
  168.9 50.7 %shard_map.234 = (bf16[8,192,128]{2,1,0:T(8,128)(2,1)}, f32[256,768]{1,0:T(8,128)}, f32[256,768]{1,0:T(8,128)}, bf16[256,768]{1,0:T(8,128)(2,1)}, bf16[256,128]{...) custom-call(bf16[768,768]{1,0:T(8,128)(2,1)} %get-tuple-element.84.s, ...), custom_call_target="tpu_custom_call" | custom-call | bytes 157286400 | tf_op jit(solution)/shard_map/pallas_call | solution.py:1700
  219.5 4.5 %all-to-all-start.1 = ((bf16[8,96,768]{2,1,0:T(8,128)(2,1)}), bf16[8,96,768]{2,1,0:T(8,128)(2,1)S(1)}, u32[]{:S(2)}, u32[]{:S(2)}) async-start(bf16[8,96,768]{2,1,0:T(8,128)(2,1)} %bitcast.8), calls=%async_computation.1 | async-start | bytes 2359296 | tf_op jit(solution)/shard_map/all_to_all | solution.py:1802
  224.0 0.4 collective-permute-start
  224.4 21.8 %shard_map.235 = (bf16[8,192,128]{2,1,0:T(8,128)(2,1)}, bf16[2,8,256,128]{3,2,1,0:T(8,128)(2,1)}) custom-call(s32[10]{0:T(128)} %pad_add_fusion.sc, bf16[8,192,128]{2,1,0:T(8,128)(2,1)} %get-tuple-element.73.query_ref, bf16[2,8,256,128]{3,2,1,0:T(8,128)(2,1)} %get-tuple-element.74.recv_ref, bf16[8,192,128]{2,1,0:T(8,128)(2,1)} %get-tuple-element.92.grad_ref, ...), custom_call_target="tpu_custom_call" | custom-call | flops 4831838208 | bytes 8388608 | tf_op jit(solution)/shard_map/pallas_call | solution.py:1777
  246.2 0.5 all-to-all-done.1
  246.7 0.0 copy-start
  246.7 1.0 copy-done
  247.7 40.1 %shard_map.236 = (bf16[8,192,128]{2,1,0:T(8,128)(2,1)}, bf16[2,8,256,128]{3,2,1,0:T(8,128)(2,1)}, bf16[3,2,192,2048]{3,2,1,0:T(8,128)(2,1)}, bf16[1,192,768]{2,1...) custom-call(bf16[8,192,128]{2,1,0:T(8,128)(2,1)} %get-tuple-element.95.query_ref, ...), custom_call_target="tpu_custom_call" | custom-call | bytes 125829120 | tf_op jit(solution)/shard_map/pallas_call | solution.py:1803
  287.8 0.0 collective-permute-done
  287.8 0.0 copy-start.1
  287.8 1.1 copy-done.1
  289.0 87.7 %shard_map.237 = (f32[256,768]{1,0:T(8,128)}, bf16[192,4096]{1,0:T(8,128)(2,1)}, bf16[512,768]{1,0:T(8,128)(2,1)}, bf16[192,3200]{1,0:T(8,128)(2,1)}, bf16[3,192,2048]{2,1,0:T(8,128)(2,1)}) custom-call(bf16[8,192,128]{2,1,0:T(8,128)(2,1)} %get-tuple-element.105.query_ref, bf16[2,8,256,128]{3,2,1,0:T(8,128)(2,1)} %get-tuple-element.106.recv_ref, ...), custom_call_target="tpu_custom_call" | custom-call | bytes 209715200 | tf_op jit(solution)/shard_map/pallas_call | solution.py:1866
  376.6 0.0 copy-start.3
  376.6 8.0 %shard_map.238 = (f32[192,2304]{1,0:T(8,128)}, f32[192,768]{1,0:T(8,128)}, f32[192,4096]{1,0:T(8,128)}, f32[512,768]{1,0:T(8,128)}, f32[192,4096]{1,0:T(8,128)},...) custom-call(bf16[192,3200]{1,0:T(8,128)(2,1)} %get-tuple-element.121.late_ref.small_ref, ...), custom_call_target="tpu_custom_call" | custom-call | bytes 23068672 | tf_op jit(solution)/shard_map/pallas_call | solution.py:1925
  384.6 1.3 fusion
  385.9 0.0 copy-done.3
  385.9 0.7 copy.32
  (2 shorter events, 0.0 us)
Async XLA Ops:
  7.2 93.4 %all-gather.4.cloned.1.call-start = ((), (), s32[]{:S(2)}) async-start(), calls=%async_computation.2 | async-start | bytes 1474560 | tf_op jit(solution)/shard_map/all_gather | solution.py:1517
  7.9 136.3 %all-gather.6.cloned.1.call-start = ((), (), s32[]{:S(2)}) async-start(), calls=%async_computation.3 | async-start | bytes 19660800 | tf_op jit(solution)/shard_map/all_gather | solution.py:1518
  11.5 1.4 copy-start.6
  11.5 1.4 copy-start.7
  11.5 1.5 copy-start.4
  11.5 157.4 %all-gather.8.cloned.1.call-start = ((), (), s32[]{:S(2)}) async-start(), calls=%async_computation.4 | async-start | bytes 3932160 | tf_op jit(solution)/shard_map/all_gather | solution.py:1521
  12.9 67.1 %copy-start.5 = (s32[8]{0:T(128)S(1)}, s32[8]{0:T(128)}, u32[]{:S(2)}) copy-start(s32[8]{0:T(128)} %where_ref.3) | copy-start | bytes 100
  72.5 28.1 %all-to-all-start = ((bf16[8,64,768]{2,1,0:T(8,128)(2,1)}), bf16[8,64,768]{2,1,0:T(8,128)(2,1)S(1)}, u32[]{:S(2)}, u32[]{:S(2)}) async-start(bf16[8,64,768]{2,1,0:T(8,128)(2,1)} %get-tuple-element.76), calls=%async_computation | async-start | bytes 1572864 | tf_op jit(solution)/shard_map/all_to_all | solution.py:1590
  100.6 43.6 %copy-start.2 = (bf16[8,64,768]{2,1,0:T(8,128)(2,1)}, bf16[8,64,768]{2,1,0:T(8,128)(2,1)S(1)}, u32[]{:S(2)}) copy-start(bf16[8,64,768]{2,1,0:T(8,128)(2,1)S(1)} %all-to-all-done.rest_ref) | copy-start | bytes 2359300
  219.5 27.2 %all-to-all-start.1 = ((bf16[8,96,768]{2,1,0:T(8,128)(2,1)}), bf16[8,96,768]{2,1,0:T(8,128)(2,1)S(1)}, u32[]{:S(2)}, u32[]{:S(2)}) async-start(bf16[8,96,768]{2,1,0:T(8,128)(2,1)} %bitcast.8), calls=%async_computation.1 | async-start | bytes 2359296 | tf_op jit(solution)/shard_map/all_to_all | solution.py:1802
  224.0 63.8 %collective-permute-start = (bf16[2,1,192,2048]{3,2,0,1:T(8,128)(2,1)}, bf16[2,1,192,2048]{3,2,0,1:T(8,128)(2,1)S(1)}, u32[]{:S(2)}, u32[]{:S(2)}) collective-permute-start(bf16[2,1,192,2048]{3,2,0,1:T(8,128)(2,1)} %bitcast.48), channel_id=1, source_target_pairs={{0,2},{1,3},{2,0},{3,1},{4,6},{5,7},{6,4},{7,5},{8,10},{9,11},{10,... | collective-permute-start | bytes 4718600 | tf_op jit(solution)/shard_map/ppermute | solution.py:1763
  246.7 1.0 copy-start
  287.8 1.1 copy-start.1
  376.6 9.3 %copy-start.3 = (bf16[256,768]{1,0:T(8,128)(2,1)S(1)}, bf16[256,768]{1,0:T(8,128)(2,1)}, u32[]{:S(2)}) copy-start(bf16[256,768]{1,0:T(8,128)(2,1)} %get-tuple-element.104) | copy-start | bytes 1179652
Sparse Core Ops, SparseCore 0:
  9.6 24.4 all-gather.3
  35.7 101.9 all-gather.5
  139.2 28.5 all-gather.7

commit v8 on v7

--- a/solution.py
+++ b/solution.py
@@ -1455,6 +1455,7 @@
     back_ref,
     x_ref,
     small_ref,
+    output_ref,
     qkv_out,
     w_out,
     a_out,
@@ -1463,7 +1464,9 @@
     back_out,
     x_out,
     router_out,
-    gains_out,
+    gain_one_out,
+    gain_two_out,
+    output_out,
 ):
     qkv_out[...] = late_ref[:, 0 : 3 * D].astype(F32)
     w_out[...] = late_ref[:, PACKED:].astype(F32)
@@ -1473,12 +1476,14 @@
     in_out[:, FF:] = in_ref[1].astype(F32)
     back_out[...] = back_ref[0].astype(F32)
     x_out[...] = x_ref[...]
+    output_out[...] = output_ref[...]
 
     @pl.when(pl.program_id(0) == 0)
     def _():
         small = small_ref[...].astype(F32).T
         router_out[...] = small[0:experts]
-        gains_out[...] = small[experts : experts + 2]
+        gain_one_out[...] = small[experts]
+        gain_two_out[...] = small[experts + 1]
 
 
 def on_device(
@@ -1922,7 +1927,7 @@
     def rows_of(count, width):
         return pl.BlockSpec((count // quarters, width), lambda i: (i, 0))
 
-    grad_qkv, grad_out, grad_si, grad_so, grad_ei, grad_eo, grad_x, grad_router, gains = call(
+    grad_qkv, grad_out, grad_si, grad_so, grad_ei, grad_eo, grad_x, grad_router, gain_one, gain_two, output = call(
         functools.partial(widen_kernel, experts),
         (
             shape((local, 3 * D), F32),
@@ -1933,7 +1938,9 @@
             shape((local, FF), F32),
             shape((rows, D), F32),
             shape((experts, local), F32),
-            shape((2, local), F32),
+            shape((local,), F32),
+            shape((local,), F32),
+            shape((rows, D), BF16),
         ),
         flops=0,
         nbytes=22 << 20,
@@ -1946,6 +1953,7 @@
             pl.BlockSpec((1, local // quarters, FF), lambda i: (2, i, 0)),
             rows_of(rows, D),
             pl.BlockSpec((local, LANES), lambda i: (0, 3 * D // LANES)),
+            rows_of(rows, D),
         ],
         out_specs=[
             rows_of(local, 3 * D),
@@ -1956,16 +1964,18 @@
             rows_of(local, FF),
             rows_of(rows, D),
             full(experts, local),
-            full(2, local),
+            full(local),
+            full(local),
+            rows_of(rows, D),
         ],
-    )(last_sum, dense_sum, so_sum, expert_sum, expert_sum, grad_x, last_sum)
+    )(last_sum, dense_sum, so_sum, expert_sum, expert_sum, grad_x, last_sum, output)
     return (
         output[None],
         grad_x[None],
-        gains[0],
+        gain_one,
         grad_qkv,
         grad_out,
-        gains[1],
+        gain_two,
         grad_router.T,
         grad_si,
         grad_so,

time: 396 us -> 394 us (level)
  transfers between devices with their start and end apart: 6 -> 6, of which waited for: 2 -> 2; matrix products, arithmetic and copies ran while one was open for 1% -> 1% of each run, Pallas kernels for 52% -> 53%
where the time goes in v8:
time: 394 us; the launch traced here: 392 us
  Pallas kernels  351 us (89%)
  between operations  14.6 us (4%)
  starting transfers between devices  12.6 us (3%)
  waiting for transfers between devices  6.07 us (2%)
  other arithmetic  4.79 us (1%)
    pallas_call x1, Pallas kernels, on_device(): comm_call(functools.partial(last_kernel, n_ctx, members, heads, experts,...  86.4 us
    pallas_call x1, Pallas kernels, on_device(): comm_call(functools.partial(open_kernel, n_ctx, members, heads, experts,...  58.2 us
    pallas_call x1, Pallas kernels, on_device(): comm_call(functools.partial(shared_kernel, n_ctx, members, heads, experts...  50.7 us
    pallas_call x1, Pallas kernels, on_device(): comm_call(functools.partial(middle_kernel, n_ctx, heads, experts), (shape...  43.5 us
    pallas_call x1, Pallas kernels, on_device(): comm_call(functools.partial(back_exchange_kernel, n_ctx, members, heads),...  42.1 us
    pallas_call x1, Pallas kernels, on_device(): call(expert_kernel, (shape((places, D), BF16), shape((n_ctx, 8, LANES), F...  24.7 us
    pallas_call x1, Pallas kernels, on_device(): call(functools.partial(attend_back_kernel, n_ctx, share), (shape((n_ctx,...  21.8 us
    pallas_call x1, Pallas kernels, on_device(): call(functools.partial(attend_kernel, n_ctx, share), (shape((n_ctx, thin,...  15.6 us
  transfers between devices with their start and end apart: 6, of which 2 were waited for; matrix products, arithmetic and copies ran while one was open for 1% of the time, Pallas kernels for 53%

profile of v8, /device:TPU:0, one launch (start us, length us, event | category | flops | bytes accessed | tf_op | source)
XLA Modules:
  0.0 392.2 jit_solution(15911127251112986801)
XLA Ops:
  7.2 0.0 all-gather.4.cloned.1.call-start
  7.2 0.7 all-gather.4.cloned.1.call-update
  7.9 0.0 all-gather.6.cloned.1.call-start
  8.0 3.5 pad_maximum_fusion
  11.5 0.0 copy-start.5
  11.5 0.0 copy-start.6
  11.5 0.0 copy-start.3
  11.5 0.0 all-gather.6.cloned.1.call-update
  11.5 0.0 all-gather.8.cloned.1.call-start
  11.6 0.7 all-gather.8.cloned.1.call-update
  12.9 0.0 copy-done.5
  12.9 0.0 copy-done.6
  12.9 0.0 copy-done.3
  12.9 0.0 copy-start.4
  13.0 0.8 copy.28
  13.8 0.6 pad_maximum_fusion.1.gains_ref
  14.3 58.2 %shard_map.230 = (bf16[8,192,128]{2,1,0:T(8,128)(2,1)}, bf16[2,8,256,128]{3,2,1,0:T(8,128)(2,1)}, bf16[256,768]{1,0:T(8,128)(2,1)}, f32[128,768]{1,0:T(8,128)}, ...) custom-call(s32[8]{0:T(128)} %where_ref.3, ...), custom_call_target="tpu_custom_call" | custom-call | bytes 157286400 | tf_op jit(solution)/shard_map/pallas_call | solution.py:1551
  72.5 7.6 %all-to-all-start = ((bf16[8,64,768]{2,1,0:T(8,128)(2,1)}), bf16[8,64,768]{2,1,0:T(8,128)(2,1)S(1)}, u32[]{:S(2)}, u32[]{:S(2)}) async-start(bf16[8,64,768]{2,1,0:T(8,128)(2,1)} %get-tuple-element.78), calls=%async_computation | async-start | bytes 1572864 | tf_op jit(solution)/shard_map/all_to_all | solution.py:1595
  80.1 0.0 copy-done.4
  80.1 0.1 select_reduce_fusion
  80.2 0.6 pad_add_fusion.sc
  80.8 15.6 %shard_map.231 = (bf16[8,192,128]{2,1,0:T(8,128)(2,1)}, f32[8,128,384]{2,1,0:T(8,128)}, f32[8,1,384]{2,1,0:T(1,128)}) custom-call(s32[10]{0:T(128)} %pad_add_fusion.sc, bf16[8,192,128]{2,1,0:T(8,128)(2,1)} %get-tuple-element.75.query_ref, bf16[2,8,256,128]{3,2,1,0:T(8,128)(2,1)} %get-tuple-element.76.recv_ref), custom_call_target="tpu_custom_call" | custom-call | flops 3221225472 | bytes 5242880 | tf_op jit(solution)/shard_map/pallas_call | solution.py:1600
  96.4 4.2 %all-to-all-done.rest_ref = bf16[8,64,768]{2,1,0:T(8,128)(2,1)S(1)} async-done(((bf16[8,64,768]{2,1,0:T(8,128)(2,1)}), bf16[8,64,768]{2,1,0:T(8,128)(2,1)S(1)}, u32[]{:S(2)}, u32[]{:S(2)}) %all-to-all-start) | async-done | bytes 786464 | tf_op jit(solution)/shard_map/all_to_all | solution.py:1595
  100.6 0.0 copy-start.2
  100.6 0.0 all-gather.4.cloned.1.call-done.w_ref
  100.6 43.5 %shard_map.232 = (bf16[8,256,128]{2,1,0:T(8,128)(2,1)}, f32[256,768]{1,0:T(8,128)}, bf16[256,768]{1,0:T(8,128)(2,1)}, f32[256,128]{1,0:T(8,128)}, bf16[768,768]{1,0:T(8,128)(2,1)}, /*index=5*/f32[8,8,128]{2,1,0:T(8,128)}) custom-call(bf16[8,192,128]{2,1,0:T(8,128)(2,1)} %get-tuple-element.79.attended_ref, ...), custom_call_target="tpu_custom_call" | custom-call | bytes 104857600 | tf_op jit(solution)/shard_map/pallas_call | solution.py:1630
  144.1 0.0 all-gather.6.cloned.1.call-done.wg_ref.wu_ref.wt_ref.wide_ref
  144.2 0.0 copy-done.2
  144.2 24.7 %shard_map.233 = (bf16[768,768]{1,0:T(8,128)(2,1)}, f32[8,8,128]{2,1,0:T(8,128)}, bf16[768,768]{1,0:T(8,128)(2,1)}, bf16[3,768,2048]{2,1,0:T(8,128)(2,1)}, bf16[768,768]{1,0:T(8,128)(2,1)}) custom-call(bf16[768,768]{1,0:T(8,128)(2,1)} %get-tuple-element.82.x_ref, f32[8,8,128]{2,1,0:T(8,128)} %get-tuple-element.83.gates_ref, ...), custom_call_target="tpu_custom_call" | custom-call | flops 14495514624 | bytes 25165824 | tf_op jit(solution)/shard_map/pallas_call | solution.py:1657
  168.8 0.0 all-gather.8.cloned.1.call-done.back_ref
  168.9 50.7 %shard_map.234 = (bf16[8,192,128]{2,1,0:T(8,128)(2,1)}, f32[256,768]{1,0:T(8,128)}, f32[256,768]{1,0:T(8,128)}, bf16[256,768]{1,0:T(8,128)(2,1)}, bf16[256,128]{...) custom-call(bf16[768,768]{1,0:T(8,128)(2,1)} %get-tuple-element.86.s, ...), custom_call_target="tpu_custom_call" | custom-call | bytes 157286400 | tf_op jit(solution)/shard_map/pallas_call | solution.py:1705
  219.5 4.5 %all-to-all-start.1 = ((bf16[8,96,768]{2,1,0:T(8,128)(2,1)}), bf16[8,96,768]{2,1,0:T(8,128)(2,1)S(1)}, u32[]{:S(2)}, u32[]{:S(2)}) async-start(bf16[8,96,768]{2,1,0:T(8,128)(2,1)} %bitcast.8), calls=%async_computation.1 | async-start | bytes 2359296 | tf_op jit(solution)/shard_map/all_to_all | solution.py:1807
  224.0 0.4 collective-permute-start
  224.4 21.8 %shard_map.235 = (bf16[8,192,128]{2,1,0:T(8,128)(2,1)}, bf16[2,8,256,128]{3,2,1,0:T(8,128)(2,1)}) custom-call(s32[10]{0:T(128)} %pad_add_fusion.sc, bf16[8,192,128]{2,1,0:T(8,128)(2,1)} %get-tuple-element.75.query_ref, bf16[2,8,256,128]{3,2,1,0:T(8,128)(2,1)} %get-tuple-element.76.recv_ref, bf16[8,192,128]{2,1,0:T(8,128)(2,1)} %get-tuple-element.94.grad_ref, ...), custom_call_target="tpu_custom_call" | custom-call | flops 4831838208 | bytes 8388608 | tf_op jit(solution)/shard_map/pallas_call | solution.py:1782
  246.2 0.5 all-to-all-done.1
  246.7 0.0 copy-start
  246.7 1.0 copy-done
  247.7 42.1 %shard_map.236 = (bf16[8,192,128]{2,1,0:T(8,128)(2,1)}, bf16[2,8,256,128]{3,2,1,0:T(8,128)(2,1)}, bf16[3,2,192,2048]{3,2,1,0:T(8,128)(2,1)}, bf16[1,192,768]{2,1...) custom-call(bf16[8,192,128]{2,1,0:T(8,128)(2,1)} %get-tuple-element.97.query_ref, ...), custom_call_target="tpu_custom_call" | custom-call | bytes 125829120 | tf_op jit(solution)/shard_map/pallas_call | solution.py:1808
  289.8 0.0 collective-permute-done
  289.8 0.0 copy-start.1
  289.8 1.1 copy-done.1
  291.0 86.4 %shard_map.237 = (f32[256,768]{1,0:T(8,128)}, bf16[192,4096]{1,0:T(8,128)(2,1)}, bf16[512,768]{1,0:T(8,128)(2,1)}, bf16[192,3200]{1,0:T(8,128)(2,1)}, bf16[3,192,2048]{2,1,0:T(8,128)(2,1)}) custom-call(bf16[8,192,128]{2,1,0:T(8,128)(2,1)} %get-tuple-element.106.query_ref, bf16[2,8,256,128]{3,2,1,0:T(8,128)(2,1)} %get-tuple-element.107.recv_ref, ...), custom_call_target="tpu_custom_call" | custom-call | bytes 209715200 | tf_op jit(solution)/shard_map/pallas_call | solution.py:1871
  377.4 8.3 %shard_map.238 = (f32[192,2304]{1,0:T(8,128)}, f32[192,768]{1,0:T(8,128)}, f32[192,4096]{1,0:T(8,128)}, f32[512,768]{1,0:T(8,128)}, f32[192,4096]{1,0:T(8,128)},...) custom-call(bf16[192,3200]{1,0:T(8,128)(2,1)} %get-tuple-element.122, ...), custom_call_target="tpu_custom_call" | custom-call | bytes 23068672 | tf_op jit(solution)/shard_map/pallas_call | solution.py:1930
  (2 shorter events, 0.0 us)
Async XLA Ops:
  7.2 93.4 %all-gather.4.cloned.1.call-start = ((), (), s32[]{:S(2)}) async-start(), calls=%async_computation.2 | async-start | bytes 1474560 | tf_op jit(solution)/shard_map/all_gather | solution.py:1522
  7.9 136.2 %all-gather.6.cloned.1.call-start = ((), (), s32[]{:S(2)}) async-start(), calls=%async_computation.3 | async-start | bytes 19660800 | tf_op jit(solution)/shard_map/all_gather | solution.py:1523
  11.5 1.4 copy-start.5
  11.5 1.4 copy-start.6
  11.5 1.5 copy-start.3
  11.5 157.4 %all-gather.8.cloned.1.call-start = ((), (), s32[]{:S(2)}) async-start(), calls=%async_computation.4 | async-start | bytes 3932160 | tf_op jit(solution)/shard_map/all_gather | solution.py:1526
  12.9 67.1 %copy-start.4 = (s32[8]{0:T(128)S(1)}, s32[8]{0:T(128)}, u32[]{:S(2)}) copy-start(s32[8]{0:T(128)} %where_ref.3) | copy-start | bytes 100
  72.5 28.1 %all-to-all-start = ((bf16[8,64,768]{2,1,0:T(8,128)(2,1)}), bf16[8,64,768]{2,1,0:T(8,128)(2,1)S(1)}, u32[]{:S(2)}, u32[]{:S(2)}) async-start(bf16[8,64,768]{2,1,0:T(8,128)(2,1)} %get-tuple-element.78), calls=%async_computation | async-start | bytes 1572864 | tf_op jit(solution)/shard_map/all_to_all | solution.py:1595
  100.6 43.6 %copy-start.2 = (bf16[8,64,768]{2,1,0:T(8,128)(2,1)}, bf16[8,64,768]{2,1,0:T(8,128)(2,1)S(1)}, u32[]{:S(2)}) copy-start(bf16[8,64,768]{2,1,0:T(8,128)(2,1)S(1)} %all-to-all-done.rest_ref) | copy-start | bytes 2359300
  219.5 27.2 %all-to-all-start.1 = ((bf16[8,96,768]{2,1,0:T(8,128)(2,1)}), bf16[8,96,768]{2,1,0:T(8,128)(2,1)S(1)}, u32[]{:S(2)}, u32[]{:S(2)}) async-start(bf16[8,96,768]{2,1,0:T(8,128)(2,1)} %bitcast.8), calls=%async_computation.1 | async-start | bytes 2359296 | tf_op jit(solution)/shard_map/all_to_all | solution.py:1807
  224.0 65.8 %collective-permute-start = (bf16[2,1,192,2048]{3,2,0,1:T(8,128)(2,1)}, bf16[2,1,192,2048]{3,2,0,1:T(8,128)(2,1)S(1)}, u32[]{:S(2)}, u32[]{:S(2)}) collective-permute-start(bf16[2,1,192,2048]{3,2,0,1:T(8,128)(2,1)} %bitcast.43), channel_id=1, source_target_pairs={{0,2},{1,3},{2,0},{3,1},{4,6},{5,7},{6,4},{7,5},{8,10},{9,11},{10,... | collective-permute-start | bytes 4718600 | tf_op jit(solution)/shard_map/ppermute | solution.py:1768
  246.7 1.0 copy-start
  289.8 1.1 copy-start.1
Sparse Core Ops, SparseCore 0:
  9.6 24.4 all-gather.3
  35.7 101.9 all-gather.5
  139.2 28.5 all-gather.7
